TPU v7x, 256 devices: a whole 4x4x8 slice. The times are simulated.
256 devices in a mesh: dp: 32 (over x_lo, z, core), expert: 8 (over x_hi, y).
Axes of the slice: x: 4 (x_hi: 2, x_lo: 2; x = x_hi * 2 + x_lo), y: 4, z: 8, core: 2. Of those that a mesh axis runs over, the one named last changes fastest.
Arguments:
- tokens: bfloat16 [49152, 4096], P(('dp', 'expert')), may hold values from -24 to 24
- routes: int32 [49152, 2], P(('dp', 'expert')), may hold values from 0 to 7, all different within a row; in each aligned block of 192 rows (0 to 191, 192 to 383, ...) at most 64 rows name the same one
- positives: int32 [512], P(('dp', 'expert')), may hold values from 0 to 511, each once
- expert_out: bfloat16 [32, 8, 8, 64, 4096], P('dp', 'expert'), may hold values from -6 to 6
- router: bfloat16 [4096, 8], replicated, may hold values from -0.09375 to 0.09375
- norm_gain: float32 [4096], replicated, may hold values from 0.25 to 1.75
- loss_scale: float32 [], replicated, may hold values from 8192 to 65536
Outputs:
- token_grad: bfloat16 [49152, 4096], P(('dp', 'expert'))
- expert_grad: bfloat16 [32, 8, 8, 64, 4096], P('dp', 'expert')
- router_grad: float32 [4096, 8], replicated
- loss: float32 [], replicated
Inputs may be any that keep to these rules, and one draw needn't show every extreme that they name: `routes`: each row names 2 different experts; among the rows of one device no expert is named by more than 64 rows, a bound that some block reaches. `positives`: A permutation of the records.
All inputs are finite; a program needn't handle non-finite values.
Results may differ from a plain program's by a relative error of at most 0.0061.
Values may be sent and summed in bfloat16 or wider, within the bound.
No kernel may reach another device: no remote copies, remote signals or barrier semaphores. Data moves between devices by JAX's collectives and lax.ppermute only.
A program may use at most 128 MiB of HBM per device.

v0:
```python
import math

import jax
import jax.numpy as jnp
from jax import lax
from jax.sharding import PartitionSpec as P

PAIR_DEV = 2
SEQ = 48


norm_eps = 1e-05


def slot_where(routes, experts, capacity):
    hit_table = (routes[:, :, None] == jnp.arange(experts, dtype=jnp.int32)[None, None, :]).astype(
        jnp.int32
    )
    flat_hits = hit_table.reshape(-1, experts)
    before = jnp.cumsum(flat_hits, axis=0) - flat_hits
    slot_rank = jnp.sum(before * flat_hits, axis=1).reshape(routes.shape)
    return routes * capacity + slot_rank


def forward_rows(tokens, routes, received, router, norm_gain):
    experts = received.shape[0]
    capacity = received.shape[1]
    hidden_width = received.shape[2]
    logits = jnp.dot(tokens, router, preferred_element_type=jnp.float32)
    one_hot = (routes[:, :, None] == jnp.arange(experts, dtype=jnp.int32)[None, None, :]).astype(
        jnp.float32
    )
    chosen = jnp.sum(one_hot * logits[:, None, :], axis=2)
    gate_mix = jax.nn.softmax(chosen, axis=1)
    slot_rows = slot_where(routes, experts, capacity)
    fetched = received.reshape(experts * capacity, hidden_width)[slot_rows]
    summed_rows = (
        tokens.astype(jnp.float32)
        + gate_mix[:, 0:1] * fetched[:, 0].astype(jnp.float32)
        + gate_mix[:, 1:2] * fetched[:, 1].astype(jnp.float32)
    )
    inverse = lax.rsqrt(jnp.mean(summed_rows * summed_rows, axis=1, keepdims=True) + norm_eps)
    normed = summed_rows * inverse * norm_gain
    pooled = jnp.mean(normed.reshape(-1, SEQ, hidden_width), axis=1).astype(jnp.bfloat16)
    return (pooled, (gate_mix, one_hot, slot_rows, fetched, summed_rows, inverse))


def backward_rows(tokens, router, norm_gain, saved, grad_pool, experts, capacity):
    gate_mix, one_hot, slot_rows, fetched, summed_rows, inverse = saved
    hidden_width = tokens.shape[1]
    grad_rows = jnp.broadcast_to(
        grad_pool[:, None, :] / SEQ, (grad_pool.shape[0], SEQ, hidden_width)
    ).reshape(-1, hidden_width)
    weighted = grad_rows * norm_gain
    grad_summed = inverse * weighted - summed_rows * inverse**3 * jnp.mean(
        weighted * summed_rows, axis=1, keepdims=True
    )
    grad_gate = jnp.sum(grad_summed[:, None, :] * fetched.astype(jnp.float32), axis=2)
    grad_chosen = gate_mix * (grad_gate - jnp.sum(gate_mix * grad_gate, axis=1, keepdims=True))
    grad_logits = jnp.sum(one_hot * grad_chosen[:, :, None], axis=1).astype(jnp.bfloat16)
    router_part = lax.dot_general(
        tokens, grad_logits, (((0,), (0,)), ((), ())), preferred_element_type=jnp.float32
    )
    through_router = lax.dot_general(
        grad_logits, router, (((1,), (1,)), ((), ())), preferred_element_type=jnp.float32
    )
    token_grad = (grad_summed + through_router).astype(jnp.bfloat16)
    outgoing = (
        (gate_mix[:, :, None] * grad_summed[:, None, :])
        .astype(jnp.bfloat16)
        .reshape(-1, hidden_width)
    )
    sendback = (
        jnp.zeros((experts * capacity, hidden_width), jnp.bfloat16)
        .at[slot_rows.reshape(-1)]
        .set(outgoing)
    )
    return (token_grad, sendback.reshape(experts, capacity, hidden_width), router_part)


def score_rows(queries, records_all, positives, loss_scale, pair_total, score_scale):
    scores = (
        lax.dot_general(
            queries, records_all, (((1,), (1,)), ((), ())), preferred_element_type=jnp.float32
        )
        * score_scale
    )
    highest = jnp.max(scores, axis=1, keepdims=True)
    log_total = highest[:, 0] + jnp.log(jnp.sum(jnp.exp(scores - highest), axis=1))
    is_positive = jnp.arange(pair_total, dtype=jnp.int32)[None, :] == positives[:, None]
    positive_score = jnp.sum(jnp.where(is_positive, scores, jnp.zeros_like(scores)), axis=1)
    row_loss = log_total - positive_score
    softmax_rows = jnp.exp(scores - log_total[:, None])
    score_grad = (
        (softmax_rows - is_positive.astype(jnp.float32)) * (loss_scale / pair_total)
    ).astype(jnp.bfloat16)
    return (row_loss, score_grad)


def shards(tokens, routes, positives, expert_out, router, norm_gain, loss_scale):
    experts = expert_out.shape[2]
    capacity = expert_out.shape[3]
    hidden_width = expert_out.shape[4]
    received = lax.all_to_all(
        expert_out.reshape(experts, capacity, hidden_width),
        "expert",
        split_axis=0,
        concat_axis=0,
        tiled=True,
    )
    pooled, saved = forward_rows(tokens, routes, received, router, norm_gain)
    queries = pooled[:PAIR_DEV]
    records = pooled[PAIR_DEV:]
    loop_size = lax.axis_size("dp")
    column_size = lax.axis_size("expert")
    device_count = loop_size * column_size
    pair_total = PAIR_DEV * device_count
    score_scale = 4.0 / math.sqrt(hidden_width)
    records_all = lax.all_gather(records, ("dp", "expert"), axis=0, tiled=True)
    row_loss, score_grad = score_rows(
        queries, records_all, positives, loss_scale, pair_total, score_scale
    )
    loss_local = jnp.sum(row_loss)
    grad_queries = (
        jnp.dot(score_grad, records_all, preferred_element_type=jnp.float32) * score_scale
    )
    grad_records = lax.psum_scatter(
        lax.dot_general(
            score_grad, queries, (((0,), (0,)), ((), ())), preferred_element_type=jnp.float32
        )
        * score_scale,
        ("dp", "expert"),
        scatter_dimension=0,
        tiled=True,
    )
    grad_pool = jnp.concatenate([grad_queries, grad_records], axis=0)
    token_grad, sendback, router_part = backward_rows(
        tokens, router, norm_gain, saved, grad_pool, experts, capacity
    )
    returned = lax.all_to_all(sendback, "expert", split_axis=0, concat_axis=0, tiled=True)
    router_grad, loss_total = lax.psum((router_part, loss_local), ("dp", "expert"))
    expert_grad = returned.reshape(1, 1, experts, capacity, hidden_width)
    return (token_grad, expert_grad, router_grad, loss_total / pair_total)


def solution(mesh):
    placed = (
        P(("dp", "expert"), None),
        P(("dp", "expert"), None),
        P(("dp", "expert")),
        P("dp", "expert", None, None, None),
        P(),
        P(),
        P(),
    )
    return jax.shard_map(
        shards,
        mesh=mesh,
        in_specs=placed,
        out_specs=(P(("dp", "expert"), None), P("dp", "expert", None, None, None), P(), P()),
        check_vma=False,
    )
```

profile of v0, /device:TPU:1, one launch (start us, length us, event | category | flops | bytes accessed | tf_op | source)
XLA Modules:
  0.0 1506.2 jit_solution(1943185011051784695)
XLA Ops:
  7.2 7.6 all-to-all-start
  17.7 45.8 %all-to-all-done = bf16[8,64,4096]{2,1,0:T(8,128)(2,1)} async-done(((bf16[8,64,4096]{2,1,0:T(8,128)(2,1)}), bf16[8,64,4096]{2,1,0:T(8,128)(2,1)}, u32[]{:S(2)}, u32[]{:S(2)}) %all-to-all-start) | async-done | bytes 4194336 | tf_op jit(solution)/shard_map/all_to_all | solution.py:104
  63.5 11.0 gather_fusion
  74.5 4.6 reshape.220
  79.1 7.0 fusion.17
  86.2 4.0 multiply_reduce_fusion.2
  90.2 2.4 multiply_multiply_fusion
  92.8 2.2 reduce_sum.112
  96.6 707.9 %all-gather.3.cloned.1.call-done = bf16[256,2,4096]{2,1,0:T(2,128)(2,1)} async-done(((bf16[1,2,4096]{2,1,0:T(2,128)(2,1)}), bf16[256,2,4096]{2,1,0:T(2,128)(2,1)}) %all-gather.3.cloned.1.call-update) | async-done | bytes 4194320 | tf_op jit(solution)/shard_map/all_gather | solution.py:119
  804.5 7.2 reshape.238
  811.6 3.5 fusion.19
  816.0 4.6 convolution_multiply_fusion
  821.2 2.9 convolution_multiply_fusion.1
  824.1 273.2 %all-reduce.6.cloned.1.call-done = f32[512,4096]{1,0:T(8,128)} async-done(((f32[512,4096]{1,0:T(8,128)}), f32[512,4096]{1,0:T(8,128)}) %all-reduce.6.cloned.1.call-update) | async-done | bytes 8388624
  1102.0 5.3 mul.182
  1107.3 8.4 mul.189
  1115.7 9.7 scatter_custom_fusion
  1125.4 6.0 all-to-all-start.1
  1131.4 115.8 %psum.15 = f32[]{:T(128)} all-reduce(f32[]{:T(128)} %get-tuple-element.6), channel_id=1, replica_groups=mesh['dp'=32,'expert'=8] {'dp','expert'}, use_global_device_ids=true, to_apply=%region_19.20 | all-reduce | flops 1 | bytes 8 | tf_op jit(solution)/shard_map/psum | solution.py:141
  1247.8 5.7 multiply_reduce_fusion
  1253.7 2.4 convolution_bitcast_fusion
  1256.1 3.6 fusion
  1259.8 233.4 %all-reduce.4.cloned.1.call-done = f32[4096,8]{0,1:T(8,128)} async-done(((f32[4096,8]{0,1:T(8,128)}), f32[4096,8]{0,1:T(8,128)}) %all-reduce.4.cloned.1.call-update) | async-done | bytes 131088 | tf_op jit(solution)/shard_map/psum | solution.py:141
  1493.1 4.7 copy.69
  (68 shorter events, 10.8 us)
Async XLA Ops:
  7.2 9.9 copy-start
  7.2 7.7 copy-start.8
  7.2 9.9 copy-start.4
  7.2 56.3 %all-to-all-start = ((bf16[8,64,4096]{2,1,0:T(8,128)(2,1)}), bf16[8,64,4096]{2,1,0:T(8,128)(2,1)}, u32[]{:S(2)}, u32[]{:S(2)}) async-start(bf16[8,64,4096]{2,1,0:T(8,128)(2,1)} %bitcast.46), calls=%async_computation | async-start | bytes 8388608 | tf_op jit(solution)/shard_map/all_to_all | solution.py:104
  14.8 789.6 %all-gather.3.cloned.1.call-start = ((), (), s32[]{:S(2)}) async-start(), calls=%async_computation.3 | async-start | bytes 4210688 | tf_op jit(solution)/shard_map/all_gather | solution.py:119
  79.1 7.0 copy-start.5
  86.1 4.1 copy-start.6
  90.2 2.6 copy-start.2
  95.7 1001.6 %all-reduce.6.cloned.1.call-start = ((), (), s32[]{:S(2)}) async-start(), calls=%async_computation.4 | async-start | bytes 16777216
  811.6 3.5 copy-start.9
  1097.2 2.0 copy-start.3
  1100.3 1.7 copy-start.1
  1125.4 134.4 %all-to-all-start.1 = ((bf16[8,64,4096]{2,1,0:T(8,128)(2,1)}), bf16[8,64,4096]{2,1,0:T(8,128)(2,1)}, u32[]{:S(2)}, u32[]{:S(2)}) async-start(bf16[8,64,4096]{2,1,0:T(8,128)(2,1)} %bitcast.44), calls=%async_computation.1 | async-start | bytes 8388608 | tf_op jit(solution)/shard_map/all_to_all | solution.py:140
  1131.4 361.8 %all-reduce.4.cloned.1.call-start = ((), (), s32[]{:S(2)}) async-start(), calls=%async_computation.2 | async-start | bytes 262144 | tf_op jit(solution)/shard_map/psum | solution.py:141
  1493.1 4.7 copy-start.7
Sparse Core Ops, SparseCore 0:
  95.8 708.6 all-gather.2
  820.7 276.4 all-reduce.5
  1256.2 236.8 all-reduce.3
where the time goes:
time: 1510 us
  waiting for transfers between devices  1260 us (83%)
  blocking collectives  116 us (8%)
  local copies, waits for them, and re-layouts  54.7 us (4%)
  other arithmetic  27.5 us (2%)
  matrix products  17.5 us (1%)
  between operations  16.5 us (1%)
    all_gather x1, waiting for transfers between devices, shards(): records_all = lax.all_gather(records, ('dp', 'expert'), axis=0, tiled=True)  708 us
    unnamed x4, waiting for transfers between devices  273 us
    psum x1, waiting for transfers between devices, shards(): lax.psum((router_part, loss_local), ('dp', 'expert'))  233 us
    psum x1, blocking collectives, shards(): lax.psum((router_part, loss_local), ('dp', 'expert'))  116 us
    all_to_all x1, waiting for transfers between devices, shards(): lax.all_to_all(expert_out.reshape(experts, capacity, hidden_width), 'expe...  45.8 us
  transfers between devices with their start and end apart: 5, of which 4 were waited for; matrix products, arithmetic and copies ran while one was open for 1% of the time, Pallas kernels for 0%

commit v1 on v0

v1 whole, which is shorter than its diff:
```python
import math

import jax
import jax.numpy as jnp
from jax import lax
from jax.sharding import Mesh, PartitionSpec as P

PAIR_DEV = 2
SEQ = 48
EPS = 1e-05
CORES = 2
F32 = jnp.float32
BF16 = jnp.bfloat16


def swap_core(x):
    return lax.ppermute(x, "c", [(0, 1), (1, 0)])


def spread(x, axes, size):
    return lax.all_to_all(
        jnp.broadcast_to(x[None], (size,) + x.shape), axes, split_axis=0, concat_axis=0, tiled=True
    )


def routing(tokens, routes, router, experts, capacity):
    logits = jnp.dot(tokens, router, preferred_element_type=F32)
    lanes = jnp.arange(experts, dtype=jnp.int32)[None, None, :]
    one_hot = (routes[:, :, None] == lanes).astype(F32)
    chosen = jnp.sum(one_hot * logits[:, None, :], axis=2)
    gates = jax.nn.softmax(chosen, axis=1)
    rows = routes.shape[0]
    hits = jnp.sum(one_hot, axis=1)
    order = jnp.arange(rows, dtype=jnp.int32)
    earlier = (order[None, :] < order[:, None]).astype(BF16)
    before = jnp.dot(earlier, hits.astype(BF16), preferred_element_type=F32)
    rank = jnp.sum(one_hot * before[:, None, :], axis=2).astype(jnp.int32)
    return gates, one_hot, routes * capacity + rank


def split_bf16(x):
    high = x.astype(BF16)
    rest = x - high.astype(F32)
    mid = rest.astype(BF16)
    low = (rest - mid.astype(F32)).astype(BF16)
    return jnp.concatenate([high, mid, low], axis=0)


def shards(tokens, routes, positives, expert_out, router, norm_gain, loss_scale):
    experts, capacity, width = expert_out.shape[2:]
    rows = tokens.shape[0]
    slots = experts * capacity
    outer = lax.axis_size("u")
    place = lax.axis_index("u")
    core = lax.axis_index("c")
    mine = lax.axis_index("expert")
    wide = outer * experts
    part = width // experts
    group = PAIR_DEV * experts
    pairs = group * outer * CORES
    scale = 4.0 / math.sqrt(width)

    received = lax.all_to_all(
        expert_out.reshape(experts, capacity, width), "expert", split_axis=0, concat_axis=0, tiled=True
    ).reshape(slots, width)
    gates, one_hot, slot = routing(tokens, routes, router, experts, capacity)

    slot_ids = jnp.arange(slots, dtype=jnp.int32)[None, :]
    picks = [(slot[:, k : k + 1] == slot_ids) for k in range(2)]
    fetched = [jnp.dot(p.astype(BF16), received, preferred_element_type=F32) for p in picks]
    summed = tokens.astype(F32) + gates[:, 0:1] * fetched[0] + gates[:, 1:2] * fetched[1]
    inverse = lax.rsqrt(jnp.mean(summed * summed, axis=1, keepdims=True) + EPS)
    overlap = jnp.concatenate([jnp.sum(summed * f, axis=1, keepdims=True) for f in fetched], axis=1)
    normed = summed * inverse * norm_gain
    pooled = jnp.mean(normed.reshape(-1, SEQ, width), axis=1).astype(BF16)
    taken = picks[0] | picks[1]
    sendback = lax.dot_general(
        taken.astype(BF16), summed.astype(BF16), (((0,), (0,)), ((), ())), preferred_element_type=F32
    ).astype(BF16)
    gate_slot = jnp.sum(
        jnp.where(picks[0], gates[:, 0:1], 0.0) + jnp.where(picks[1], gates[:, 1:2], 0.0), axis=0
    )
    inverse_slot = jnp.sum(jnp.where(taken, inverse, 0.0), axis=0)
    sequence = (jnp.arange(rows, dtype=jnp.int32) // SEQ).astype(F32)
    sequence_slot = jnp.sum(jnp.where(taken, sequence[:, None], 0.0), axis=0)

    sliced = jnp.transpose(pooled.reshape(2 * PAIR_DEV, experts, part), (1, 0, 2))
    offered = jnp.broadcast_to(sliced[None], (outer,) + sliced.shape).reshape(wide, 2 * PAIR_DEV, part)
    near = lax.all_to_all(offered, ("u", "expert"), split_axis=0, concat_axis=0, tiled=True)
    returned = lax.all_to_all(
        sendback.reshape(experts, capacity, width), "expert", split_axis=0, concat_axis=0, tiled=True
    )
    far = swap_core(near)
    queries = jnp.concatenate([x[:, :PAIR_DEV].reshape(-1, part) for x in (near, far)], axis=0)
    records = jnp.concatenate([x[:, PAIR_DEV:].reshape(-1, part) for x in (near, far)], axis=0)
    own = lax.dynamic_slice_in_dim(near, place * experts, experts, axis=0)
    own_queries = own[:, :PAIR_DEV].reshape(group, part)
    own_records = own[:, PAIR_DEV:].reshape(group, part)
    contract = (((1,), (1,)), ((), ()))
    by_query = lax.dot_general(own_queries, records, contract, preferred_element_type=F32)
    by_record = lax.dot_general(own_records, queries, contract, preferred_element_type=F32)
    notes = jnp.stack(
        [gate_slot, inverse_slot, sequence_slot, jnp.pad(positives.astype(F32), (0, slots - PAIR_DEV))]
        + [jnp.zeros_like(gate_slot)] * 4
    )
    gathered = spread(jnp.concatenate([by_query, by_record, notes], axis=0), "expert", experts)
    scores = jnp.sum(gathered[:, : 2 * group], axis=0) * scale
    by_query, by_record = scores[:group], scores[group:]
    own_positive = gathered[:, 2 * group + 3, :PAIR_DEV].reshape(group)

    column = jnp.arange(pairs // CORES, dtype=jnp.int32)
    column = (column // group) * (CORES * group) + column % group
    names = jnp.concatenate([column + core * group, column + (1 - core) * group]).astype(F32)
    hit = own_positive[:, None] == names[None, :]
    highest = jnp.max(by_query, axis=1, keepdims=True)
    log_total = highest + jnp.log(jnp.sum(jnp.exp(by_query - highest), axis=1, keepdims=True))
    row_loss = log_total[:, 0] - jnp.sum(jnp.where(hit, by_query, 0.0), axis=1)
    told = jnp.concatenate([log_total[:, 0], own_positive, jnp.sum(row_loss)[None]])
    told = jnp.pad(told, (0, 128 - told.shape[0]))
    heard = spread(told[None], ("u", "c"), outer * CORES).reshape(outer, CORES, 128)
    loss = jnp.sum(heard[:, :, 2 * group]) / pairs
    heard = jnp.concatenate(
        [lax.dynamic_index_in_dim(heard, i, axis=1, keepdims=False) for i in (core, 1 - core)], axis=0
    )
    all_total = heard[:, :group].reshape(1, pairs)
    all_positive = heard[:, group : 2 * group].reshape(1, pairs)
    own_names = ((place * CORES + core) * group + jnp.arange(group, dtype=jnp.int32)).astype(F32)
    factor = loss_scale / pairs
    grad_by_query = ((jnp.exp(by_query - log_total) - hit.astype(F32)) * factor).astype(BF16)
    hit_record = (all_positive == own_names[:, None]).astype(F32)
    grad_by_record = ((jnp.exp(by_record - all_total) - hit_record) * factor).astype(BF16)
    grad_sliced = scale * jnp.concatenate(
        [
            jnp.dot(grad_by_query, records, preferred_element_type=F32),
            jnp.dot(grad_by_record, queries, preferred_element_type=F32),
        ],
        axis=0,
    )
    grads = spread(grad_sliced, "expert", experts)
    grads = jnp.transpose(grads, (1, 0, 2)).reshape(2 * group, width)
    weighted_all = grads * (norm_gain / SEQ)[None, :]

    by_source = weighted_all.reshape(2, experts, PAIR_DEV, width)
    weighted = lax.dynamic_index_in_dim(by_source, mine, axis=1, keepdims=False).reshape(-1, width)
    count = weighted.shape[0]
    on_slots = jnp.dot(split_bf16(weighted), received.T, preferred_element_type=F32)
    on_slots = jnp.sum(on_slots.reshape(3, count, slots), axis=0)
    on_rows = jnp.repeat(on_slots, SEQ, axis=0)
    along = jnp.concatenate(
        [jnp.sum(jnp.where(p, on_rows, 0.0), axis=1, keepdims=True) for p in picks], axis=1
    )
    weighted_rows = jnp.repeat(weighted, SEQ, axis=0)
    shrink = inverse**3 * jnp.mean(weighted_rows * summed, axis=1, keepdims=True)
    grad_gate = inverse * along - shrink * overlap
    grad_chosen = gates * (grad_gate - jnp.sum(gates * grad_gate, axis=1, keepdims=True))
    grad_logits = jnp.sum(one_hot * grad_chosen[:, :, None], axis=1).astype(BF16)
    router_part = lax.dot_general(
        grad_logits, tokens, (((0,), (0,)), ((), ())), preferred_element_type=F32
    )
    router_part = router_part + swap_core(router_part)
    router_part = router_part.reshape(wide, 1, -1)
    router_part = lax.all_to_all(
        router_part, ("u", "expert"), split_axis=0, concat_axis=0, tiled=True
    )
    router_sum = jnp.sum(router_part, axis=0)
    router_grad = spread(router_sum, ("u", "expert"), wide).reshape(experts, width).T
    through = lax.dot_general(
        grad_logits, router, (((1,), (1,)), ((), ())), preferred_element_type=F32
    )
    token_grad = (inverse * weighted_rows - shrink * summed + through).astype(BF16)

    held = lax.dynamic_slice_in_dim(gathered[:, 2 * group : 2 * group + 3], mine * capacity, capacity, axis=2)
    gate_here, inverse_here, sequence_here = held[:, 0], held[:, 1], held[:, 2].astype(jnp.int32)
    by_slot = jnp.zeros((experts, capacity, width), F32)
    per_source = jnp.transpose(by_source, (1, 0, 2, 3)).reshape(experts, 2 * PAIR_DEV, width)
    for s in range(2 * PAIR_DEV):
        by_slot = jnp.where((sequence_here == s)[:, :, None], per_source[:, s : s + 1], by_slot)
    back = returned.astype(F32)
    shrink_here = inverse_here**3 * jnp.mean(by_slot * back, axis=2)
    expert_grad = gate_here[:, :, None] * (inverse_here[:, :, None] * by_slot - shrink_here[:, :, None] * back)
    expert_grad = expert_grad.astype(BF16).reshape(1, 1, experts, capacity, width)
    return token_grad, expert_grad, router_grad, loss


def solution(mesh):
    outer = mesh.shape["dp"] // CORES
    fine = Mesh(
        mesh.devices.reshape(outer, CORES, mesh.shape["expert"]), ("u", "c", "expert")
    )
    everywhere = ("u", "c", "expert")
    placed = (
        P(everywhere, None),
        P(everywhere, None),
        P(everywhere),
        P(("u", "c"), "expert", None, None, None),
        P(),
        P(),
        P(),
    )
    return jax.shard_map(
        shards,
        mesh=fine,
        in_specs=placed,
        out_specs=(P(everywhere, None), P(("u", "c"), "expert", None, None, None), P(), P()),
        check_vma=False,
    )
```

time: 1510 us -> 299 us (0.20)
  waiting for transfers between devices: 1260 us -> 135 us
  blocking collectives: 116 us -> 16.5 us
  starting transfers between devices: 13.9 us -> 52.6 us
  local copies, waits for them, and re-layouts: 54.7 us -> 34.3 us
    all_gather x1 -> x0, waiting for transfers between devices: 708 us -> none  [shards(): records_all = lax.all_gather(records, ('dp', 'expert'), axis=0, tiled=True)]
    unnamed x4 -> x0, waiting for transfers between devices: 273 us -> none
    psum x1 -> x0, waiting for transfers between devices: 233 us -> none  [shards(): lax.psum((router_part, loss_local), ('dp', 'expert'))]
    psum x1 -> x0, blocking collectives: 116 us -> none  [shards(): lax.psum((router_part, loss_local), ('dp', 'expert'))]
    all_to_all x2 -> x7, waiting for transfers between devices: 45.9 us -> 134 us  [the longest x1 46.7 us: shards(): lax.all_to_all(expert_out.reshape(experts, capacity, width), 'expert', sp...]
    all_to_all x2 -> x7, starting transfers between devices: 13.6 us -> 47.1 us  [the longest x4 20.1 us: spread(): lax.all_to_all(jnp.broadcast_to(x[None], (size,) + x.shape), axes, split_...]
    all_to_all x0 -> x1, blocking collectives: none -> 16.5 us  [shards(): lax.all_to_all(router_part, ('u', 'expert'), split_axis=0, concat_axis=0,...]
    gather x2 -> x0, local copies, waits for them, and re-layouts: 15.5 us -> none  [forward_rows(): fetched = received.reshape(experts * capacity, hidden_width)[slot_rows]]
  transfers between devices with their start and end apart: 5 -> 9, of which waited for: 4 -> 8; matrix products, arithmetic and copies ran while one was open for 1% -> 9% of each run, Pallas kernels for 0% -> 0%
where the time goes in v1:
time: 299 us; the launch traced here: 297 us
  waiting for transfers between devices  135 us (45%)
  starting transfers between devices  52.6 us (18%)
  local copies, waits for them, and re-layouts  34.3 us (11%)
  other arithmetic  28.2 us (9%)
  matrix products  26.5 us (9%)
  blocking collectives  16.5 us (6%)
  between operations  3.6 us (1%)
    all_to_all x1, waiting for transfers between devices, shards(): lax.all_to_all(expert_out.reshape(experts, capacity, width), 'expert', sp...  46.7 us
    all_to_all x1, waiting for transfers between devices, shards(): lax.all_to_all(sendback.reshape(experts, capacity, width), 'expert', spli...  39.5 us
    all_to_all x4, waiting for transfers between devices, spread(): lax.all_to_all(jnp.broadcast_to(x[None], (size,) + x.shape), axes, split_...  32.2 us
    all_to_all x4, starting transfers between devices, spread(): lax.all_to_all(jnp.broadcast_to(x[None], (size,) + x.shape), axes, split_...  20.1 us
    all_to_all x1, blocking collectives, shards(): lax.all_to_all(router_part, ('u', 'expert'), split_axis=0, concat_axis=0,...  16.5 us
    all_to_all x1, waiting for transfers between devices, shards(): lax.all_to_all(offered, ('u', 'expert'), split_axis=0, concat_axis=0, til...  16 us
    all_to_all x1, starting transfers between devices, shards(): lax.all_to_all(offered, ('u', 'expert'), split_axis=0, concat_axis=0, til...  14.6 us
    dot_general x2, matrix products, shards(): jnp.dot(p.astype(BF16), received, preferred_element_type=F32)  9.8 us
  transfers between devices with their start and end apart: 9, of which 8 were waited for; matrix products, arithmetic and copies ran while one was open for 9% of the time, Pallas kernels for 0%

profile of v1, /device:TPU:1, one launch (start us, length us, event | category | flops | bytes accessed | tf_op | source)
XLA Modules:
  0.0 297.1 jit_solution(4309982716655843103)
XLA Ops:
  0.7 7.6 %all-to-all-start = ((bf16[8,64,4096]{2,1,0:T(8,128)(2,1)}), bf16[8,64,4096]{2,1,0:T(8,128)(2,1)}, u32[]{:S(2)}, u32[]{:S(2)}) async-start(bf16[8,64,4096]{2,1,0:T(8,128)(2,1)} %bitcast.80), calls=%async_computation | async-start | bytes 8388608 | tf_op jit(solution)/shard_map/all_to_all | solution.py:63
  10.3 46.7 %all-to-all-done = bf16[8,64,4096]{2,1,0:T(8,128)(2,1)} async-done(((bf16[8,64,4096]{2,1,0:T(8,128)(2,1)}), bf16[8,64,4096]{2,1,0:T(8,128)(2,1)}, u32[]{:S(2)}, u32[]{:S(2)}) %all-to-all-start) | async-done | bytes 4194336 | tf_op jit(solution)/shard_map/all_to_all | solution.py:63
  57.0 3.3 %fusion.9 = f32[192,4096]{1,0:T(8,128)S(1)} fusion(bf16[512,4096]{1,0:T(8,128)(2,1)} %bitcast.3, s32[192]{0:T(256)S(1)} %bitcast.97), kind=kOutput, calls=%fused_computation.31 | convolution fusion | flops 805404672 | bytes 7340800 | tf_op jit(solution)/shard_map/dot_general | solution.py:70
  60.4 6.5 %multiply_reduce_fusion.3 = (f32[192]{0:T(256)S(1)}, f32[192,4096]{1,0:T(8,128)S(1)}, f32[192,4096]{1,0:T(8,128)}) fusion(f32[192]{0:T(256)S(1)} %bitcast.93, f32[192,4096]{1,0:T(8,128)S(1)} %fusion.9, f32[192]{0:T(256)S(1)} %bitcast.91, bf16[192,4096]{1,0:T(8,128)(2,1)S(1)} %copy-done.5, bf16[512,4096]{1,0:T(8,128)(2,1)} %bitcast.3, s32[192]{0:T(256)S(1)} %bitcast.88), kind=kOutput, calls=%fused_computation.15 | convolution fusion | flops 810909504 | bytes 15207424 | tf_op jit(solution)/shard_map/dot_general | solution.py:70
  72.4 14.6 %all-to-all-start.1 = ((bf16[128,4,512]{2,1,0:T(4,128)(2,1)}), bf16[128,4,512]{2,1,0:T(4,128)(2,1)}, u32[]{:S(2)}, u32[]{:S(2)}) async-start(bf16[128,4,512]{2,1,0:T(4,128)(2,1)} %bitcast.81), calls=%async_computation.1 | async-start | bytes 1048576 | tf_op jit(solution)/shard_map/all_to_all | solution.py:89
  88.4 16.0 %all-to-all-done.1 = bf16[128,4,512]{2,1,0:T(4,128)(2,1)} async-done(((bf16[128,4,512]{2,1,0:T(4,128)(2,1)}), bf16[128,4,512]{2,1,0:T(4,128)(2,1)}, u32[]{:S(2)}, u32[]{:S(2)}) %all-to-all-start.1) | async-done | bytes 524320 | tf_op jit(solution)/shard_map/all_to_all | solution.py:89
  126.1 4.2 %all-to-all-start.2 = ((f32[8,40,512]{2,1,0:T(8,128)}), f32[8,40,512]{2,1,0:T(8,128)}, u32[]{:S(2)}, u32[]{:S(2)}) async-start(f32[8,40,512]{2,1,0:T(8,128)} %broadcast_in_dim.169), calls=%async_computation.2 | async-start | bytes 1310720 | tf_op jit(solution)/shard_map/all_to_all | solution.py:21
  131.1 10.7 %all-to-all-done.2 = f32[8,40,512]{2,1,0:T(8,128)} async-done(((f32[8,40,512]{2,1,0:T(8,128)}), f32[8,40,512]{2,1,0:T(8,128)}, u32[]{:S(2)}, u32[]{:S(2)}) %all-to-all-start.2) | async-done | bytes 655392 | tf_op jit(solution)/shard_map/all_to_all | solution.py:21
  146.0 4.9 %all-to-all-start.3 = ((f32[32,1,128]{2,1,0:T(1,128)}), f32[32,1,128]{2,1,0:T(1,128)S(1)}, u32[]{:S(2)}, u32[]{:S(2)}) async-start(f32[32,1,128]{2,1,0:T(1,128)} %broadcast_in_dim.172), calls=%async_computation.3 | async-start | bytes 32768 | tf_op jit(solution)/shard_map/all_to_all | solution.py:21
  152.2 6.5 %all-to-all-done.3 = f32[32,1,128]{2,1,0:T(1,128)S(1)} async-done(((f32[32,1,128]{2,1,0:T(1,128)}), f32[32,1,128]{2,1,0:T(1,128)S(1)}, u32[]{:S(2)}, u32[]{:S(2)}) %all-to-all-start.3) | async-done | bytes 16416 | tf_op jit(solution)/shard_map/all_to_all | solution.py:21
  161.1 4.3 %all-to-all-start.4 = ((f32[8,32,512]{2,1,0:T(8,128)}), f32[8,32,512]{2,1,0:T(8,128)}, u32[]{:S(2)}, u32[]{:S(2)}) async-start(f32[8,32,512]{2,1,0:T(8,128)} %broadcast_in_dim.173), calls=%async_computation.4 | async-start | bytes 1048576 | tf_op jit(solution)/shard_map/all_to_all | solution.py:21
  166.8 7.4 %all-to-all-done.4 = f32[8,32,512]{2,1,0:T(8,128)} async-done(((f32[8,32,512]{2,1,0:T(8,128)}), f32[8,32,512]{2,1,0:T(8,128)}, u32[]{:S(2)}, u32[]{:S(2)}) %all-to-all-start.4) | async-done | bytes 524320 | tf_op jit(solution)/shard_map/all_to_all | solution.py:21
  180.2 3.4 %convolution_reduce_fusion = f32[4,512]{1,0:T(4,128)S(1)} fusion(bf16[3,4,4096]{2,1,0:T(4,128)(2,1)S(1)} %dot_general.46, bf16[512,4096,1]{1,0,2:T(8,128)(2,1)} %bitcast.19), kind=kOutput, calls=%fused_computation.18 | convolution fusion | flops 50335744 | bytes 4300800 | tf_op jit(solution)/shard_map/dot_general | solution.py:146
  187.8 2.8 multiply_reduce_fusion.1
  191.0 3.2 %collective-permute-start.1 = (f32[8,4096]{1,0:T(8,128)S(1)}, f32[8,4096]{1,0:T(8,128)S(1)}, u32[]{:S(2)}, u32[]{:S(2)}) collective-permute-start(f32[8,4096]{1,0:T(8,128)S(1)} %fusion.63), channel_id=1, source_target_pairs={{0,8},{8,0},{1,9},{9,1},{2,10},{10,2},{3,11},{11,3},{4,12},{12,4},... | collective-permute-start | bytes 393224 | tf_op jit(solution)/shard_map/ppermute | solution.py:17
  195.5 16.5 %all_to_all.40 = f32[128,1,256]{2,1,0:T(1,128)S(1)} all-to-all(f32[128,1,256]{2,1,0:T(1,128)S(1)} %reshape.372), channel_id=1, replica_groups=mesh['u'=16,'c'=2,'expert'=8] {'u','expert'}, dimensions={0} | all-to-all | bytes 262144 | tf_op jit(solution)/shard_map/all_to_all | solution.py:162
  212.8 6.7 %all-to-all-start.7 = ((f32[128,1,256]{2,1,0:T(1,128)}), f32[128,1,256]{2,1,0:T(1,128)S(1)}, u32[]{:S(2)}, u32[]{:S(2)}) async-start(f32[128,1,256]{2,1,0:T(1,128)} %broadcast_in_dim.190), calls=%async_computation.7 | async-start | bytes 262144 | tf_op jit(solution)/shard_map/all_to_all | solution.py:21
  219.5 3.4 %convolution_convert_fusion = bf16[512,4096]{1,0:T(8,128)(2,1)} fusion(f32[192,4096]{1,0:T(8,128)S(1)} %get-tuple-element.23, s32[192]{0:T(256)S(1)} %bitcast.90, s32[192]{0:T(256)S(1)} %bitcast.99), kind=kOutput, calls=%fused_computation.7 | convolution fusion | flops 808484864 | bytes 7341568 | tf_op jit(solution)/shard_map/dot_general | solution.py:77
  222.9 7.5 %all-to-all-done.7 = f32[128,1,256]{2,1,0:T(1,128)S(1)} async-done(((f32[128,1,256]{2,1,0:T(1,128)}), f32[128,1,256]{2,1,0:T(1,128)S(1)}, u32[]{:S(2)}, u32[]{:S(2)}) %all-to-all-start.7) | async-done | bytes 131104 | tf_op jit(solution)/shard_map/all_to_all | solution.py:21
  230.4 4.8 %all-to-all-start.5 = ((bf16[8,64,4096]{2,1,0:T(8,128)(2,1)}), bf16[8,64,4096]{2,1,0:T(8,128)(2,1)}, u32[]{:S(2)}, u32[]{:S(2)}) async-start(bf16[8,64,4096]{2,1,0:T(8,128)(2,1)} %bitcast.78), calls=%async_computation.5 | async-start | bytes 8388608 | tf_op jit(solution)/shard_map/all_to_all | solution.py:90
  239.2 3.8 %fusion.4 = bf16[192,4096]{1,0:T(8,128)(2,1)} fusion(bf16[4096,8]{0,1:T(8,128)(2,1)S(1)} %copy-done, f32[192,4096]{1,0:T(8,128)S(1)} %get-tuple-element.23, f32[192,4096]{1,0:T(8,128)} %bitcast.77, f32[192]{0:T(256)S(1)} %fusion.52, f32[192]{0:T(256)S(1)} %copy-done.13, bf16[192,8]{0,1:T(8,128)(2,1)S(1)} %select_reduce_fusion.4), kind=kOutput, calls=%fused_computation.9 | convolution fusion | flops 16515072 | bytes 7934464 | tf_op jit(solution)/shard_map/dot_general | solution.py:167
  244.0 39.5 %all-to-all-done.5 = bf16[8,64,4096]{2,1,0:T(8,128)(2,1)} async-done(((bf16[8,64,4096]{2,1,0:T(8,128)(2,1)}), bf16[8,64,4096]{2,1,0:T(8,128)(2,1)}, u32[]{:S(2)}, u32[]{:S(2)}) %all-to-all-start.5) | async-done | bytes 4194336 | tf_op jit(solution)/shard_map/all_to_all | solution.py:90
  283.6 4.0 %fusion = f32[8,64]{1,0:T(8,128)S(1)} fusion(bf16[8,64,4096]{2,1,0:T(8,128)(2,1)} %all-to-all-done.5, f32[8,4096]{1,0:T(8,128)S(1)} %get-tuple-element.25, f32[8,4096]{1,0:T(8,128)S(1)} %get-tuple-element.26, f32[8,4096]{1,0:T(8,128)S(1)} %get-tuple-element.27, f32[8,4096]{1,0:T(8,128)S(1)} %get-tuple-element.24, pred[8,64]{1,0:T(8,128)(4,1)S(1)} %get-tuple-element.47, ...), kind=kLoop, calls=%fused_computation.2 | loop fusion | flops 14679552 | bytes 4722688 | tf_op jit(solution)/shard_map/reduce_sum | solution.py:179
  287.6 8.4 %fusion.5 = bf16[1,1,8,64,4096]{4,3,2,1,0:T(8,128)(2,1)} fusion(bf16[8,64,4096]{2,1,0:T(8,128)(2,1)} %all-to-all-done.5, f32[8,64]{1,0:T(8,128)S(1)} %fusion.37, f32[8,4096]{1,0:T(8,128)S(1)} %get-tuple-element.25, f32[8,4096]{1,0:T(8,128)S(1)} %get-tuple-element.26, f32[8,4096]{1,0:T(8,128)S(1)} %get-tuple-element.27, f32[8,4096]{1,0:T(8,128)S(1)} %get-tuple-element.24, ...), kind=kLoop, calls=%fused_computation.10 | loop fusion | flops 20971520 | bytes 8921088 | tf_op jit(solution)/shard_map/reshape | solution.py:181
  (138 shorter events, 56.6 us)
Async XLA Ops:
  0.6 7.8 %copy-start = (bf16[4096,8]{0,1:T(8,128)(2,1)S(1)}, bf16[4096,8]{0,1:T(8,128)(2,1)}, u32[]{:S(2)}) copy-start(bf16[4096,8]{0,1:T(8,128)(2,1)} %param.11) | copy-start | bytes 196612
  0.6 7.6 %copy-start.9 = (s32[192,2]{0,1:T(2,128)S(1)}, s32[192,2]{0,1:T(2,128)}, u32[]{:S(2)}) copy-start(s32[192,2]{0,1:T(2,128)} %param.8) | copy-start | bytes 4612
  0.7 7.8 %copy-start.4 = (bf16[192,4096]{1,0:T(8,128)(2,1)S(1)}, bf16[192,4096]{1,0:T(8,128)(2,1)}, u32[]{:S(2)}) copy-start(bf16[192,4096]{1,0:T(8,128)(2,1)} %param.7) | copy-start | bytes 4718596
  0.7 56.3 %all-to-all-start = ((bf16[8,64,4096]{2,1,0:T(8,128)(2,1)}), bf16[8,64,4096]{2,1,0:T(8,128)(2,1)}, u32[]{:S(2)}, u32[]{:S(2)}) async-start(bf16[8,64,4096]{2,1,0:T(8,128)(2,1)} %bitcast.80), calls=%async_computation | async-start | bytes 8388608 | tf_op jit(solution)/shard_map/all_to_all | solution.py:63
  57.0 3.4 %copy-start.5 = (bf16[192,4096]{1,0:T(8,128)(2,1)S(1)}, bf16[192,4096]{1,0:T(8,128)(2,1)}, u32[]{:S(2)}) copy-start(bf16[192,4096]{1,0:T(8,128)(2,1)} %param.7) | copy-start | bytes 4718596
  60.4 6.5 %copy-start.1 = (f32[192,4096]{1,0:T(8,128)}, f32[192,4096]{1,0:T(8,128)S(1)}, u32[]{:S(2)}) copy-start(f32[192,4096]{1,0:T(8,128)S(1)} %fusion.9) | copy-start | bytes 9437188
  60.4 6.5 %copy-start.7 = (f32[4096]{0:T(1024)S(1)}, f32[4096]{0:T(1024)}, u32[]{:S(2)}) copy-start(f32[4096]{0:T(1024)} %param.12) | copy-start | bytes 49156
  66.9 20.7 %copy-start.12 = (f32[192]{0:T(256)}, f32[192]{0:T(256)S(1)}, u32[]{:S(2)}) copy-start(f32[192]{0:T(256)S(1)} %add_rsqrt_fusion) | copy-start | bytes 2308
  69.1 17.9 %copy-start.20 = (s32[2]{0:T(128)S(1)}, s32[2]{0:T(128)}, u32[]{:S(2)}) copy-start(s32[2]{0:T(128)} %param.9) | copy-start | bytes 28
  72.4 32.0 %all-to-all-start.1 = ((bf16[128,4,512]{2,1,0:T(4,128)(2,1)}), bf16[128,4,512]{2,1,0:T(4,128)(2,1)}, u32[]{:S(2)}, u32[]{:S(2)}) async-start(bf16[128,4,512]{2,1,0:T(4,128)(2,1)} %bitcast.81), calls=%async_computation.1 | async-start | bytes 1048576 | tf_op jit(solution)/shard_map/all_to_all | solution.py:89
  104.4 10.9 %collective-permute-start = (bf16[128,4,512]{2,1,0:T(4,128)(2,1)}, bf16[128,4,512]{2,1,0:T(4,128)(2,1)}, u32[]{:S(2)}, u32[]{:S(2)}) collective-permute-start(bf16[128,4,512]{2,1,0:T(4,128)(2,1)} %all-to-all-done.1), channel_id=1, source_target_pairs={{0,8},{8,0},{1,9},{9,1},{2,10},{10,2},{3,11},{11,3},{4,12},{12,4},... | collective-permute-start | bytes 1572872 | tf_op jit(solution)/shard_map/ppermute | solution.py:17
  124.5 41.0 %copy-start.19 = (s32[192]{0:T(256)S(1)}, s32[192]{0:T(256)}, u32[]{:S(2)}) copy-start(s32[192]{0:T(256)} %get-tuple-element.11) | copy-start | bytes 2308
  124.5 41.6 %copy-start.18 = (s32[192]{0:T(256)S(1)}, s32[192]{0:T(256)}, u32[]{:S(2)}) copy-start(s32[192]{0:T(256)} %get-tuple-element.12) | copy-start | bytes 2308
  124.5 42.3 %copy-start.8 = (f32[4096]{0:T(1024)S(1)}, f32[4096]{0:T(1024)}, u32[]{:S(2)}) copy-start(f32[4096]{0:T(1024)} %param.12) | copy-start | bytes 49156
  126.1 15.6 %all-to-all-start.2 = ((f32[8,40,512]{2,1,0:T(8,128)}), f32[8,40,512]{2,1,0:T(8,128)}, u32[]{:S(2)}, u32[]{:S(2)}) async-start(f32[8,40,512]{2,1,0:T(8,128)} %broadcast_in_dim.169), calls=%async_computation.2 | async-start | bytes 1310720 | tf_op jit(solution)/shard_map/all_to_all | solution.py:21
  146.0 12.7 %all-to-all-start.3 = ((f32[32,1,128]{2,1,0:T(1,128)}), f32[32,1,128]{2,1,0:T(1,128)S(1)}, u32[]{:S(2)}, u32[]{:S(2)}) async-start(f32[32,1,128]{2,1,0:T(1,128)} %broadcast_in_dim.172), calls=%async_computation.3 | async-start | bytes 32768 | tf_op jit(solution)/shard_map/all_to_all | solution.py:21
  161.1 13.1 %all-to-all-start.4 = ((f32[8,32,512]{2,1,0:T(8,128)}), f32[8,32,512]{2,1,0:T(8,128)}, u32[]{:S(2)}, u32[]{:S(2)}) async-start(f32[8,32,512]{2,1,0:T(8,128)} %broadcast_in_dim.173), calls=%async_computation.4 | async-start | bytes 1048576 | tf_op jit(solution)/shard_map/all_to_all | solution.py:21
  184.7 3.0 %copy-start.2 = (f32[192,4096]{1,0:T(8,128)S(1)}, f32[192,4096]{1,0:T(8,128)}, u32[]{:S(2)}) copy-start(f32[192,4096]{1,0:T(8,128)} %copy-done.1) | copy-start | bytes 9437188
  185.1 5.5 %copy-start.3 = (f32[4,48,4096]{2,1,0:T(8,128)}, f32[4,48,4096]{2,1,0:T(8,128)S(1)}, u32[]{:S(2)}) copy-start(f32[4,48,4096]{2,1,0:T(8,128)S(1)} %broadcast_in_dim.174) | copy-start | bytes 9437188
  187.8 2.9 copy-start.15
  187.8 2.9 copy-start.6
  191.0 4.2 %collective-permute-start.1 = (f32[8,4096]{1,0:T(8,128)S(1)}, f32[8,4096]{1,0:T(8,128)S(1)}, u32[]{:S(2)}, u32[]{:S(2)}) collective-permute-start(f32[8,4096]{1,0:T(8,128)S(1)} %fusion.63), channel_id=1, source_target_pairs={{0,8},{8,0},{1,9},{9,1},{2,10},{10,2},{3,11},{11,3},{4,12},{12,4},... | collective-permute-start | bytes 393224 | tf_op jit(solution)/shard_map/ppermute | solution.py:17
  212.8 17.6 %all-to-all-start.7 = ((f32[128,1,256]{2,1,0:T(1,128)}), f32[128,1,256]{2,1,0:T(1,128)S(1)}, u32[]{:S(2)}, u32[]{:S(2)}) async-start(f32[128,1,256]{2,1,0:T(1,128)} %broadcast_in_dim.190), calls=%async_computation.7 | async-start | bytes 262144 | tf_op jit(solution)/shard_map/all_to_all | solution.py:21
  230.4 53.2 %all-to-all-start.5 = ((bf16[8,64,4096]{2,1,0:T(8,128)(2,1)}), bf16[8,64,4096]{2,1,0:T(8,128)(2,1)}, u32[]{:S(2)}, u32[]{:S(2)}) async-start(bf16[8,64,4096]{2,1,0:T(8,128)(2,1)} %bitcast.78), calls=%async_computation.5 | async-start | bytes 8388608 | tf_op jit(solution)/shard_map/all_to_all | solution.py:90
  (6 other events, 11.9 us)

commit v2 on v1

v2 whole, which is shorter than its diff:
```python
import functools
import math

import jax
import jax.numpy as jnp
from jax import lax
from jax.experimental import pallas as pl
from jax.experimental.pallas import tpu as pltpu
from jax.sharding import Mesh, PartitionSpec as P

PAIR_DEV = 2
SEQ = 48
EPS = 1e-05
CORES = 2
ROWS_DEV = 2 * PAIR_DEV
F32 = jnp.float32
BF16 = jnp.bfloat16
I32 = jnp.int32
VMEM = pl.BlockSpec(memory_space=pltpu.VMEM)
SMEM = pl.BlockSpec(memory_space=pltpu.SMEM)
NT = (((1,), (1,)), ((), ()))


def iota(shape, dim):
    return lax.broadcasted_iota(I32, shape, dim)


def params(**more):
    return pltpu.CompilerParams(vmem_limit_bytes=40 << 20, **more)


def cost(flops, moved):
    return pl.CostEstimate(flops=flops, bytes_accessed=moved, transcendentals=0)


def fold(x):
    total = x[:, :128]
    for k in range(1, x.shape[1] // 128):
        total = total + x[:, 128 * k : 128 * (k + 1)]
    return total


def swap_core(x):
    return lax.ppermute(x, "c", [(0, 1), (1, 0)])


def exchange(x, axes):
    return lax.all_to_all(x, axes, split_axis=0, concat_axis=0, tiled=True)


def routing(tokens, routes, router, experts, capacity):
    logits = jnp.dot(tokens, router, preferred_element_type=F32)
    lanes = jnp.arange(experts, dtype=I32)[None, None, :]
    one_hot = (routes[:, :, None] == lanes).astype(F32)
    chosen = jnp.sum(one_hot * logits[:, None, :], axis=2)
    gates = jax.nn.softmax(chosen, axis=1)
    rows = routes.shape[0]
    hits = jnp.sum(one_hot, axis=1)
    order = jnp.arange(rows, dtype=I32)
    earlier = (order[None, :] < order[:, None]).astype(BF16)
    before = jnp.dot(earlier, hits.astype(BF16), preferred_element_type=F32)
    rank = jnp.sum(one_hot * before[:, None, :], axis=2).astype(I32)
    return gates, routes * capacity + rank


def forward_kernel(steps, outer, tok, rec, slot, gate, gain, summed, offered, inverse, held, square):
    step = pl.program_id(0)
    part = tok.shape[1]
    rows, slots = tok.shape[0], rec.shape[0]
    ids = iota((rows, slots), 1)
    first = (slot[:, 0:1] == ids).astype(BF16)
    second = (slot[:, 1:2] == ids).astype(BF16)

    @pl.when(step == 0)
    def _():
        square[...] = jnp.zeros_like(square)

    for k in range(part // 256):
        cols = slice(256 * k, 256 * (k + 1))
        block = rec[:, cols]
        x = (
            tok[:, cols].astype(F32)
            + gate[:, 0:1] * jnp.dot(first, block, preferred_element_type=F32)
            + gate[:, 1:2] * jnp.dot(second, block, preferred_element_type=F32)
        )
        summed[:, cols] = x
        held[step, :, cols] = x
        square[...] += fold(x * x)

    @pl.when(step == steps - 1)
    def _():
        mean = jnp.sum(square[...], axis=1, keepdims=True) / (steps * part)
        scale = lax.rsqrt(mean + EPS)
        inverse[...] = scale
        count = rows // SEQ
        for e in range(steps):
            x = held[e] * scale
            x = jnp.sum(x.reshape(count, SEQ, part), axis=1) / SEQ
            x = (x * gain[:, part * e : part * (e + 1)]).astype(BF16)
            for u in range(outer):
                offered[u * steps + e] = x


def forward(tokens, received, slot, gates, gain, experts, outer):
    rows, width = tokens.shape
    slots = received.shape[0]
    part = width // experts
    whole = lambda shape: pl.BlockSpec(shape, lambda i: (0,) * len(shape))
    return pl.pallas_call(
        functools.partial(forward_kernel, experts, outer),
        grid=(experts,),
        in_specs=[
            pl.BlockSpec((rows, part), lambda i: (0, i)),
            pl.BlockSpec((slots, part), lambda i: (0, i)),
            whole((rows, 2)),
            whole((rows, 2)),
            whole((1, width)),
        ],
        out_specs=[
            pl.BlockSpec((rows, part), lambda i: (0, i)),
            whole((outer * experts, rows // SEQ, part)),
            whole((rows, 1)),
        ],
        out_shape=[
            jax.ShapeDtypeStruct((rows, width), F32),
            jax.ShapeDtypeStruct((outer * experts, rows // SEQ, part), BF16),
            jax.ShapeDtypeStruct((rows, 1), F32),
        ],
        scratch_shapes=[pltpu.VMEM((experts, rows, part), F32), pltpu.VMEM((rows, 128), F32)],
        compiler_params=params(),
        cost_estimate=cost(4 * rows * slots * width, 10 << 20),
    )(tokens, received, slot, gates, gain)


def pack_kernel(steps, place, x, rec, slot, turned, overlap, *rest):
    outs, dots = rest[:-1], rest[-1]
    step = pl.program_id(0)
    rows, part = x.shape
    slots = rec.shape[0]
    capacity = slots // len(outs)
    ids = iota((rows, slots), 1)
    first = (slot[:, 0:1] == ids).astype(BF16)
    second = (slot[:, 1:2] == ids).astype(BF16)
    target = lax.rem(iota((slots, rows), 0) + place[0] * capacity, slots)
    spot = ((turned[0:1, :] == target) | (turned[1:2, :] == target)).astype(BF16)

    @pl.when(step == 0)
    def _():
        dots[...] = jnp.zeros_like(dots)

    for k in range(part // 256):
        cols = slice(256 * k, 256 * (k + 1))
        value = x[:, cols]
        block = rec[:, cols]
        dots[0] += fold(value * jnp.dot(first, block, preferred_element_type=F32))
        dots[1] += fold(value * jnp.dot(second, block, preferred_element_type=F32))
        moved = jnp.dot(spot, value.astype(BF16), preferred_element_type=F32).astype(BF16)
        for r, out in enumerate(outs):
            out[:, cols] = moved[capacity * r : capacity * (r + 1)]

    @pl.when(step == steps - 1)
    def _():
        overlap[...] = jnp.concatenate(
            [jnp.sum(dots[k], axis=1, keepdims=True) for k in range(2)], axis=1
        )


def pack(place, summed, received, slot, experts, capacity):
    rows, width = summed.shape
    slots = received.shape[0]
    part = width // experts
    whole = lambda shape: pl.BlockSpec(shape, lambda i: (0,) * len(shape))
    return pl.pallas_call(
        functools.partial(pack_kernel, experts),
        grid=(experts,),
        in_specs=[
            SMEM,
            pl.BlockSpec((rows, part), lambda i: (0, i)),
            pl.BlockSpec((slots, part), lambda i: (0, i)),
            whole((rows, 2)),
            whole((2, rows)),
        ],
        out_specs=[whole((rows, 2))] + [pl.BlockSpec((capacity, part), lambda i: (0, i))] * experts,
        out_shape=[jax.ShapeDtypeStruct((rows, 2), F32)]
        + [jax.ShapeDtypeStruct((capacity, width), BF16)] * experts,
        scratch_shapes=[pltpu.VMEM((2, rows, 128), F32)],
        compiler_params=params(),
        cost_estimate=cost(6 * rows * slots * width, 11 << 20),
    )(place, summed, received, slot, slot.T)


def lanes_of(shape, dim):
    lane = iota(shape, dim)
    kind = lax.rem(lane, ROWS_DEV)
    return lane, kind, kind >= PAIR_DEV


def picker(group, kind, turned=False):
    wide = 2 * group
    shape, pair, row = ((wide, group), 1, 0) if turned else ((group, wide), 0, 1)
    a = iota(shape, pair)
    b = iota(shape, row)
    source = (a // PAIR_DEV) * ROWS_DEV + lax.rem(a, PAIR_DEV) + PAIR_DEV * kind
    return (source == b).astype(BF16)


def scores_kernel(place, near, far, notes, offered):
    experts, total, columns = offered.shape
    group = experts * PAIR_DEV
    wide = 2 * group
    own = near[pl.ds(pl.multiple_of(place[0] * wide, wide), wide), :]
    queries, records = [
        jnp.dot(picker(group, kind), own, preferred_element_type=F32).astype(BF16) for kind in (0, 1)
    ]
    at_record = lanes_of((group, columns), 1)[2]
    blocks = []
    for side in (near, far):
        every = side[...]
        by_query = lax.dot_general(queries, every, NT, preferred_element_type=F32)
        by_record = lax.dot_general(records, every, NT, preferred_element_type=F32)
        blocks.append(jnp.where(at_record, by_query, by_record))
    blocks.append(notes[...])
    for e in range(experts):
        for k, block in enumerate(blocks):
            offered[e, group * k : group * k + block.shape[0], :] = block


def totals_kernel(scale, devices, place, gathered, offered, kept, own_total, own_positive, loss_row):
    experts, total, columns = gathered.shape
    group = experts * PAIR_DEV
    outer_size = columns // (2 * group)
    both = gathered[0]
    for e in range(1, experts):
        both = both + gathered[e]
    positive_lane = both[2 * group + 3 : 2 * group + 4, :]
    near, far = both[:group] * scale, both[group : 2 * group] * scale
    kept[0:group] = near
    kept[group : 2 * group] = far

    shape = (group, columns)
    lane, kind, at_record = lanes_of(shape, 1)
    pair = iota(shape, 0)
    within = lax.rem(lane, 2 * group)
    matching = (within // ROWS_DEV == pair // PAIR_DEV) & (kind == lax.rem(pair, PAIR_DEV))
    here = matching & (lane // (2 * group) == place[0])
    positive = jnp.sum(jnp.where(here, positive_lane, 0.0), axis=1, keepdims=True)

    low = jnp.float32(-jnp.inf)
    near_records = jnp.where(at_record, near, low)
    far_records = jnp.where(at_record, far, low)
    highest = jnp.maximum(
        jnp.max(near_records, axis=1, keepdims=True), jnp.max(far_records, axis=1, keepdims=True)
    )
    weight = jnp.sum(jnp.exp(near_records - highest), axis=1, keepdims=True) + jnp.sum(
        jnp.exp(far_records - highest), axis=1, keepdims=True
    )
    log_total = highest + jnp.log(weight)
    chosen = jnp.zeros((group, 1), F32)
    for side, core in ((near, place[1]), (far, 1 - place[1])):
        name = column_names(lane, kind, group, core)
        hit = at_record & (name.astype(F32) == positive)
        chosen = chosen + jnp.sum(jnp.where(hit, side, 0.0), axis=1, keepdims=True)
    own_total[...] = log_total
    own_positive[...] = positive
    row_loss = log_total - chosen

    total_lane = jnp.sum(jnp.where(here, log_total, 0.0), axis=0, keepdims=True)
    loss_lane = jnp.sum(
        jnp.where(matching & (lane // (2 * group) == place[0]), row_loss, 0.0), axis=0, keepdims=True
    )
    own_lane = jnp.where(lane[0:1] // (2 * group) == place[0], positive_lane, 0.0)
    loss_row[...] = loss_lane
    pieces = [x[:, 128 * k : 128 * (k + 1)] for x in (total_lane, own_lane) for k in range(columns // 128)]
    loss_pieces = [
        pltpu.roll(loss_lane, PAIR_DEV, 1)[:, 128 * k : 128 * (k + 1)] for k in range(columns // 128)
    ]
    pieces = [a + b for a, b in zip(pieces, loss_pieces)] + pieces[columns // 128 :]
    message = jnp.concatenate(pieces, axis=0)
    for d in range(devices):
        offered[d] = message


def column_names(lane, kind, group, core):
    wide = 2 * group
    block = (lane // wide) * CORES + core
    return block * group + (lax.rem(lane, wide) // ROWS_DEV) * PAIR_DEV + lax.rem(kind, PAIR_DEV)


def gradient_kernel(scale, place, factor, heard, kept, own_total, own_positive, near, far, offered, loss):
    experts, wide, columns = offered.shape
    group = wide // 2
    outer_size = heard.shape[0] // CORES
    pieces = columns // 128
    shape = (group, columns)
    lane, kind, at_record = lanes_of(shape, 1)
    pair = iota(shape, 0)
    own_name = (place[0] * CORES + place[1]) * group + iota((group, 1), 0)
    row_lane = lane[0:1]
    result = jnp.zeros((wide, columns), F32)
    losses = jnp.zeros((1, columns), F32)
    for k, (side, core) in enumerate(((near, place[1]), (far, 1 - place[1]))):
        told = heard[core]
        for u in range(1, outer_size):
            told = told + heard[u * CORES + core]
        total = jnp.concatenate([told[i : i + 1] for i in range(pieces)], axis=1)
        positive = jnp.concatenate([told[pieces + i : pieces + i + 1] for i in range(pieces)], axis=1)
        losses = losses + jnp.where(at_record[0:1], total, 0.0)
        value = kept[group * k : group * (k + 1), :]
        name = column_names(lane, kind, group, core).astype(F32)
        hit = jnp.where(name == own_positive[...], 1.0, 0.0)
        by_query = (jnp.exp(value - own_total[...]) - hit) * factor[0]
        by_query = jnp.where(at_record, by_query, 0.0).astype(BF16)
        hit = jnp.where(positive == own_name.astype(F32), 1.0, 0.0)
        by_record = (jnp.exp(jnp.where(at_record, 0.0, value - total)) - hit) * factor[0]
        by_record = jnp.where(at_record, 0.0, by_record).astype(BF16)
        rows = jnp.dot(picker(group, 0, True), by_query, preferred_element_type=F32) + jnp.dot(
            picker(group, 1, True), by_record, preferred_element_type=F32
        )
        result = result + jnp.dot(rows.astype(BF16), side[...], preferred_element_type=F32)
    result = result * scale
    for e in range(experts):
        offered[e] = result
    loss[...] = jnp.sum(losses, axis=1, keepdims=True)


def rows_of(grads, e, index):
    tile = grads[e, pl.ds(pl.multiple_of((index // 2) * 8, 8), 8), :]
    return jnp.where(lax.rem(index, 2) == 0, tile[:ROWS_DEV], tile[ROWS_DEV:])


def split_bf16(x):
    high = x.astype(BF16)
    rest = x - high.astype(F32)
    mid = rest.astype(BF16)
    low = (rest - mid.astype(F32)).astype(BF16)
    return high, mid, low


def router_kernel(place, grads, gain, summed, rec, tok, slot, routes, gate, inverse, overlap, part_out, shrink_out, choice_out, weighted_out):
    experts, _, part = grads.shape
    rows = summed.shape[0]
    slots = rec.shape[0]
    count = rows // SEQ
    acc = [jnp.zeros((SEQ, 128), F32) for _ in range(count)]
    on_slots = jnp.zeros((16, slots), F32)
    for e in range(experts):
        cols = slice(part * e, part * (e + 1))
        w = rows_of(grads, e, place[0]) * (gain[:, cols] / SEQ)
        weighted_out[:, cols] = w
        lhs = jnp.concatenate(list(split_bf16(w)) + [jnp.zeros((count, part), BF16)], axis=0)
        on_slots = on_slots + lax.dot_general(lhs, rec[:, cols], NT, preferred_element_type=F32)
        for q in range(count):
            acc[q] = acc[q] + fold(summed[SEQ * q : SEQ * (q + 1), cols] * w[q : q + 1, :])
    on_slots = on_slots[0:count] + on_slots[count : 2 * count] + on_slots[2 * count : 3 * count]
    ids = iota((SEQ, slots), 1)
    lanes = iota((SEQ, 128), 1)
    choices = []
    for q in range(count):
        at = slice(SEQ * q, SEQ * (q + 1))
        inv = inverse[at]
        shrink = inv * inv * inv * (jnp.sum(acc[q], axis=1, keepdims=True) / (experts * part))
        shrink_out[at] = shrink
        row = on_slots[q : q + 1, :]
        grad_gate = []
        for k in range(2):
            along = jnp.sum(jnp.where(slot[at, k : k + 1] == ids, row, 0.0), axis=1, keepdims=True)
            grad_gate.append(inv * along - shrink * overlap[at, k : k + 1])
        gates = [gate[at, k : k + 1] for k in range(2)]
        mean = gates[0] * grad_gate[0] + gates[1] * grad_gate[1]
        choice = jnp.zeros((SEQ, 128), F32)
        for k in range(2):
            chosen = gates[k] * (grad_gate[k] - mean)
            choice = choice + jnp.where(routes[at, k : k + 1] == lanes, chosen, 0.0)
        choices.append(choice)
    choice = jnp.concatenate(choices, axis=0)
    choice_out[...] = choice.astype(BF16)
    lhs = jnp.transpose(choice)[:experts].astype(BF16)
    block = part_out.shape[1]
    for k in range(tok.shape[1] // block):
        cols = slice(block * k, block * (k + 1))
        part_out[experts * k : experts * (k + 1), :] = jnp.dot(
            lhs, tok[:, cols], preferred_element_type=F32
        )


def token_kernel(summed, weighted, inverse, shrink, choice, router, out):
    rows = summed.shape[0]
    through = jnp.dot(choice[...], router[...], preferred_element_type=F32)
    for q in range(rows // SEQ):
        at = slice(SEQ * q, SEQ * (q + 1))
        x = inverse[at] * weighted[q : q + 1, :] - shrink[at] * summed[at]
        out[at] = (x + through[SEQ * q : SEQ * (q + 1)]).astype(BF16)


def token_rows(summed, weighted, inverse, shrink, choice, router, parts):
    rows, width = summed.shape
    part = width // parts
    whole = lambda shape: pl.BlockSpec(shape, lambda i: (0, 0))
    split = lambda count: pl.BlockSpec((count, part), lambda i: (0, i))
    return pl.pallas_call(
        token_kernel,
        grid=(parts,),
        in_specs=[split(rows), split(weighted.shape[0]), whole((rows, 1)), whole((rows, 1)), whole((rows, 128)), split(128)],
        out_specs=split(rows),
        out_shape=jax.ShapeDtypeStruct((rows, width), BF16),
        compiler_params=params(),
        cost_estimate=cost(2 * rows * 128 * width, 5 << 20),
    )(summed, weighted, inverse, shrink, choice, router)


def expert_kernel(place, grads, gain, notes, *rest):
    experts = len(rest) - 1
    backs, out = rest[:experts], rest[experts]
    _, _, part = grads.shape
    step = pl.program_id(0)
    source = lax.rem(place[0] + experts - step, experts)
    gate, inv, seq = notes[0, :, 0:1], notes[0, :, 1:2], notes[0, :, 2:3]
    capacity = gate.shape[0]
    for r in range(experts):

        @pl.when(step == r)
        def _():
            back = backs[r]
            acc = jnp.zeros((capacity, 128), F32)
            rows = []
            for e in range(experts):
                cols = slice(part * e, part * (e + 1))
                w = rows_of(grads, e, source) * (gain[:, cols] / SEQ)
                x = jnp.broadcast_to(w[0:1], (capacity, part))
                for s in range(1, ROWS_DEV):
                    x = jnp.where(seq == s, w[s : s + 1], x)
                rows.append(w)
                acc = acc + fold(x * back[:, cols].astype(F32))
            shrink = inv * inv * inv * (jnp.sum(acc, axis=1, keepdims=True) / (experts * part))
            for e in range(experts):
                cols = slice(part * e, part * (e + 1))
                w = rows[e]
                x = jnp.broadcast_to(w[0:1], (capacity, part))
                for s in range(1, ROWS_DEV):
                    x = jnp.where(seq == s, w[s : s + 1], x)
                x = gate * (inv * x - shrink * back[:, cols].astype(F32))
                out[0, :, cols] = x.astype(BF16)


def expert_rows(place, grads, gain, notes, backs):
    experts, capacity = notes.shape[:2]
    width = gain.shape[1]
    whole = lambda shape: pl.BlockSpec(shape, lambda i, p: (0,) * len(shape))
    source = lambda i, p: (lax.rem(p[0] + experts - i, experts), 0, 0)
    return pl.pallas_call(
        expert_kernel,
        grid_spec=pltpu.PrefetchScalarGridSpec(
            num_scalar_prefetch=1,
            grid=(experts,),
            in_specs=[
                whole(grads.shape),
                whole((1, width)),
                pl.BlockSpec((1, capacity, notes.shape[2]), source),
            ]
            + [whole((capacity, width))] * experts,
            out_specs=pl.BlockSpec((1, capacity, width), source),
        ),
        out_shape=jax.ShapeDtypeStruct((experts, capacity, width), BF16),
        compiler_params=params(),
        cost_estimate=cost(12 * experts * capacity * width, 9 << 20),
    )(place, grads, gain, notes, *backs)


def turn_kernel(x, out):
    experts = out.shape[1]
    block = x.shape[1]
    for k in range(x.shape[0] // experts):
        out[block * k : block * (k + 1), :] = jnp.transpose(x[experts * k : experts * (k + 1), :])


def shards(tokens, routes, positives, expert_out, router, norm_gain, loss_scale):
    experts, capacity, width = expert_out.shape[2:]
    rows = tokens.shape[0]
    slots = experts * capacity
    outer = lax.axis_size("u")
    mine = lax.axis_index("expert").astype(I32)
    where = jnp.stack([lax.axis_index("u").astype(I32), lax.axis_index("c").astype(I32)])
    mine_at = mine[None]
    wide = outer * experts
    part = width // experts
    group = PAIR_DEV * experts
    pairs = group * outer * CORES
    scale = 4.0 / math.sqrt(width)
    gain = norm_gain[None, :]
    columns = outer * experts * ROWS_DEV

    received = exchange(expert_out.reshape(experts, capacity, width), "expert").reshape(slots, width)
    gates, slot = routing(tokens, routes, router, experts, capacity)
    lane = jnp.arange(columns, dtype=I32)
    spread_positive = jnp.where(
        (lane % (2 * group)) // ROWS_DEV == mine,
        jnp.where(lane % ROWS_DEV == 0, positives[0], positives[1]) * (lane % ROWS_DEV < PAIR_DEV),
        0,
    ).astype(F32)

    summed, offered, inverse = forward(tokens, received, slot, gates, gain, experts, outer)
    near = exchange(offered, ("u", "expert"))
    overlap, *outgoing = pack(mine_at, summed, received, slot, experts, capacity)
    backs = [outgoing[0]] + [
        lax.ppermute(outgoing[r], "expert", [(i, (i + r) % experts) for i in range(experts)])
        for r in range(1, experts)
    ]
    slot_ids = jnp.arange(slots, dtype=I32)[None, :]
    picks = [slot[:, k : k + 1] == slot_ids for k in range(2)]
    gate_slot = jnp.sum(
        jnp.where(picks[0], gates[:, 0:1], 0.0) + jnp.where(picks[1], gates[:, 1:2], 0.0), axis=0
    )
    taken = picks[0] | picks[1]
    inverse_slot = jnp.sum(jnp.where(taken, inverse, 0.0), axis=0)
    sequence = (jnp.arange(rows, dtype=I32) // SEQ).astype(F32)
    sequence_slot = jnp.sum(jnp.where(taken, sequence[:, None], 0.0), axis=0)
    notes = jnp.stack([gate_slot, inverse_slot, sequence_slot, spread_positive])
    notes = jnp.pad(notes, ((0, 4), (0, 0)))

    far = swap_core(near)
    near, far = near.reshape(columns, part), far.reshape(columns, part)
    offered = pl.pallas_call(
        scores_kernel,
        in_specs=[SMEM, VMEM, VMEM, VMEM],
        out_specs=VMEM,
        out_shape=jax.ShapeDtypeStruct((experts, 2 * group + 8, columns), F32),
        compiler_params=params(),
    )(where, near, far, notes)
    gathered = exchange(offered, "expert")
    column = jax.ShapeDtypeStruct((group, 1), F32)
    offered, kept, own_total, own_positive, _ = pl.pallas_call(
        functools.partial(totals_kernel, scale, outer * CORES),
        in_specs=[SMEM, VMEM],
        out_specs=[VMEM] * 5,
        out_shape=[
            jax.ShapeDtypeStruct((outer * CORES, 8, 128), F32),
            jax.ShapeDtypeStruct((2 * group, columns), F32),
            column,
            column,
            jax.ShapeDtypeStruct((1, columns), F32),
        ],
        compiler_params=params(),
    )(where, gathered)
    heard = exchange(offered, ("u", "c"))
    offered, loss = pl.pallas_call(
        functools.partial(gradient_kernel, scale),
        in_specs=[SMEM, SMEM] + [VMEM] * 6,
        out_specs=[VMEM, VMEM],
        out_shape=[
            jax.ShapeDtypeStruct((experts, 2 * group, part), F32),
            jax.ShapeDtypeStruct((1, 1), F32),
        ],
        compiler_params=params(),
    )(where, (loss_scale / pairs)[None], heard, kept, own_total, own_positive, near, far)
    grads = exchange(offered, "expert")

    router_part, shrink, choice, weighted = pl.pallas_call(
        router_kernel,
        in_specs=[SMEM] + [VMEM] * 10,
        out_specs=[VMEM] * 4,
        out_shape=[
            jax.ShapeDtypeStruct((wide, width * experts // wide), F32),
            jax.ShapeDtypeStruct((rows, 1), F32),
            jax.ShapeDtypeStruct((rows, 128), BF16),
            jax.ShapeDtypeStruct((rows // SEQ, width), F32),
        ],
        compiler_params=params(),
    )(mine_at, grads, gain, summed, received, tokens, slot, routes, gates, inverse, overlap)
    router_part = router_part + swap_core(router_part)
    router_part = exchange(router_part[:, None, :], ("u", "expert"))
    router_sum = jnp.sum(router_part, axis=0)
    router_all = exchange(jnp.broadcast_to(router_sum[None], (wide,) + router_sum.shape), ("u", "expert"))
    router_grad = pl.pallas_call(
        turn_kernel,
        in_specs=[VMEM],
        out_specs=VMEM,
        out_shape=jax.ShapeDtypeStruct((width, experts), F32),
        compiler_params=params(),
    )(router_all.reshape(wide, -1))

    turned = jnp.pad(router.T, ((0, 128 - experts), (0, 0)))
    token_grad = token_rows(summed, weighted, inverse, shrink, choice, turned, experts)
    held = lax.dynamic_slice_in_dim(gathered[:, 2 * group : 2 * group + 3], mine * capacity, capacity, axis=2)
    held = jnp.pad(jnp.transpose(held, (0, 2, 1)), ((0, 0), (0, 0), (0, 5)))
    expert_grad = expert_rows(mine_at, grads, gain, held, backs)
    return token_grad, expert_grad.reshape(1, 1, experts, capacity, width), router_grad, loss[0, 0] / pairs


def solution(mesh):
    outer = mesh.shape["dp"] // CORES
    fine = Mesh(mesh.devices.reshape(outer, CORES, mesh.shape["expert"]), ("u", "c", "expert"))
    everywhere = ("u", "c", "expert")
    return jax.shard_map(
        shards,
        mesh=fine,
        in_specs=(
            P(everywhere, None),
            P(everywhere, None),
            P(everywhere),
            P(("u", "c"), "expert", None, None, None),
            P(),
            P(),
            P(),
        ),
        out_specs=(P(everywhere, None), P(("u", "c"), "expert", None, None, None), P(), P()),
        check_vma=False,
    )
```

time: 299 us -> 272 us (0.910)
  waiting for transfers between devices: 135 us -> 80.3 us
  Pallas kernels: 0 us -> 39.9 us
  blocking collectives: 16.5 us -> 46.8 us
  other arithmetic: 28.2 us -> 2.29 us
  matrix products: 26.5 us -> 0.68 us
  starting transfers between devices: 52.6 us -> 78 us
  local copies, waits for them, and re-layouts: 34.3 us -> 19 us
    all_to_all x7 -> x5, waiting for transfers between devices: 134 us -> 71 us  [exchange(): return lax.all_to_all(x, axes, split_axis=0, concat_axis=0, tiled=True)]
    pallas_call x0 -> x9, Pallas kernels: none -> 39.9 us  [the longest x1 9.73 us: pack(): pl.pallas_call(functools.partial(pack_kernel, experts), grid=(experts,),...]
    all_to_all x1 -> x2, blocking collectives: 16.5 us -> 46.8 us  [exchange(): return lax.all_to_all(x, axes, split_axis=0, concat_axis=0, tiled=True)]
    ppermute x0 -> x7, starting transfers between devices: none -> 27.6 us  [shards(): lax.ppermute(outgoing[r], 'expert', [(i, (i + r) % experts) for i in rang...]
    dot_general x10 -> x0, matrix products: 25.8 us -> none  [the longest x2 9.8 us: shards(): jnp.dot(p.astype(BF16), received, preferred_element_type=F32)]
    reduce_sum x11 -> x1, other arithmetic: 13.4 us -> 0.25 us  [shards(): jnp.sum(jnp.where(picks[0], gates[:, 0:1], 0.0) + jnp.where(picks[1], gat...]
    unnamed x45 -> x60, local copies, waits for them, and re-layouts: 5.77 us -> 14.8 us
    ppermute x0 -> x7, waiting for transfers between devices: none -> 8.69 us  [shards(): lax.ppermute(outgoing[r], 'expert', [(i, (i + r) % experts) for i in rang...]
  transfers between devices with their start and end apart: 9 -> 14, of which waited for: 8 -> 6; matrix products, arithmetic and copies ran while one was open for 9% -> 3% of each run, Pallas kernels for 0% -> 10%
where the time goes in v2:
time: 272 us; the launch traced here: 270 us
  waiting for transfers between devices  80.3 us (30%)
  starting transfers between devices  78 us (29%)
  blocking collectives  46.8 us (17%)
  Pallas kernels  39.9 us (15%)
  local copies, waits for them, and re-layouts  19 us (7%)
  between operations  3.5 us (1%)
    all_to_all x5, waiting for transfers between devices, exchange(): return lax.all_to_all(x, axes, split_axis=0, concat_axis=0, tiled=True)  71 us
    all_to_all x2, blocking collectives, exchange(): return lax.all_to_all(x, axes, split_axis=0, concat_axis=0, tiled=True)  46.8 us
    all_to_all x5, starting transfers between devices, exchange(): return lax.all_to_all(x, axes, split_axis=0, concat_axis=0, tiled=True)  45.6 us
    ppermute x7, starting transfers between devices, shards(): lax.ppermute(outgoing[r], 'expert', [(i, (i + r) % experts) for i in rang...  27.6 us
    unnamed x60, local copies, waits for them, and re-layouts  14.8 us
    pallas_call x1, Pallas kernels, pack(): pl.pallas_call(functools.partial(pack_kernel, experts), grid=(experts,),...  9.73 us
    ppermute x7, waiting for transfers between devices, shards(): lax.ppermute(outgoing[r], 'expert', [(i, (i + r) % experts) for i in rang...  8.69 us
    pallas_call x1, Pallas kernels, forward(): pl.pallas_call(functools.partial(forward_kernel, experts, outer), grid=(e...  8.53 us
  transfers between devices with their start and end apart: 14, of which 6 were waited for; matrix products, arithmetic and copies ran while one was open for 3% of the time, Pallas kernels for 10%

profile of v2, /device:TPU:1, one launch (start us, length us, event | category | flops | bytes accessed | tf_op | source)
XLA Modules:
  0.0 270.4 jit_solution(4264394455861210039)
XLA Ops:
  0.7 7.6 %all-to-all-start = ((bf16[8,64,4096]{2,1,0:T(8,128)(2,1)}), bf16[8,64,4096]{2,1,0:T(8,128)(2,1)}, u32[]{:S(2)}, u32[]{:S(2)}) async-start(bf16[8,64,4096]{2,1,0:T(8,128)(2,1)} %bitcast.30), calls=%async_computation | async-start | bytes 8388608 | tf_op jit(solution)/shard_map/all_to_all | solution.py:48
  9.7 47.3 %all-to-all-done = bf16[8,64,4096]{2,1,0:T(8,128)(2,1)} async-done(((bf16[8,64,4096]{2,1,0:T(8,128)(2,1)}), bf16[8,64,4096]{2,1,0:T(8,128)(2,1)}, u32[]{:S(2)}, u32[]{:S(2)}) %all-to-all-start) | async-done | bytes 4194336 | tf_op jit(solution)/shard_map/all_to_all | solution.py:48
  57.0 8.5 %shard_map.102 = (f32[192,4096]{1,0:T(8,128)S(1)}, bf16[128,4,512]{2,1,0:T(4,128)(2,1)}, f32[192,1]{1,0:T(8,128)S(1)}) custom-call(bf16[192,4096]{1,0:T(8,128)(2,1)S(1)} %copy-done, bf16[512,4096]{1,0:T(8,128)(2,1)} %bitcast.1.rec, s32[192,2]{1,0:T(8,128)S(1)} %add.59.slot, f32[192,2]{1,0:T(8,128)S(1)} %exponential_divide_fusion.gate, f32[1,4096]{1,0:T(1,128)S(1)} %bitcast.27), custom_call_target="tpu_custom_call" | custom-call | flops 1610612736 | bytes 10485760 | tf_op jit(solution)/shard_map/pallas_call | solution.py:109
  67.2 14.0 %all-to-all-start.1 = ((bf16[128,4,512]{2,1,0:T(4,128)(2,1)}), bf16[128,4,512]{2,1,0:T(4,128)(2,1)S(1)}, u32[]{:S(2)}, u32[]{:S(2)}) async-start(bf16[128,4,512]{2,1,0:T(4,128)(2,1)} %get-tuple-element.27), calls=%async_computation.1 | async-start | bytes 1048576 | tf_op jit(solution)/shard_map/all_to_all | solution.py:48
  83.3 15.9 %all-to-all-done.1 = bf16[128,4,512]{2,1,0:T(4,128)(2,1)S(1)} async-done(((bf16[128,4,512]{2,1,0:T(4,128)(2,1)}), bf16[128,4,512]{2,1,0:T(4,128)(2,1)S(1)}, u32[]{:S(2)}, u32[]{:S(2)}) %all-to-all-start.1) | async-done | bytes 524320 | tf_op jit(solution)/shard_map/all_to_all | solution.py:48
  99.2 2.2 collective-permute-start
  104.4 15.6 %all_to_all.35.gathered = f32[8,40,512]{2,1,0:T(8,128)S(1)} all-to-all(f32[8,40,512]{2,1,0:T(8,128)S(1)} %shard_map.103), channel_id=1, replica_groups=mesh['u'=16,'c'=2,'expert'=8] {'expert'}, dimensions={0} | all-to-all | bytes 1310720 | tf_op jit(solution)/shard_map/all_to_all | solution.py:48
  123.8 6.0 %all-to-all-start.3 = ((f32[32,8,128]{2,1,0:T(8,128)}), f32[32,8,128]{2,1,0:T(8,128)}, u32[]{:S(2)}, u32[]{:S(2)}) async-start(f32[32,8,128]{2,1,0:T(8,128)} %copy-done.11), calls=%async_computation.3 | async-start | bytes 262144 | tf_op jit(solution)/shard_map/all_to_all | solution.py:48
  131.2 7.9 %all-to-all-done.3.heard = f32[32,8,128]{2,1,0:T(8,128)} async-done(((f32[32,8,128]{2,1,0:T(8,128)}), f32[32,8,128]{2,1,0:T(8,128)}, u32[]{:S(2)}, u32[]{:S(2)}) %all-to-all-start.3) | async-done | bytes 131104 | tf_op jit(solution)/shard_map/all_to_all | solution.py:48
  143.7 3.5 %all-to-all-start.4 = ((f32[8,32,512]{2,1,0:T(8,128)}), f32[8,32,512]{2,1,0:T(8,128)S(1)}, u32[]{:S(2)}, u32[]{:S(2)}) async-start(f32[8,32,512]{2,1,0:T(8,128)} %copy-done.9), calls=%async_computation.4 | async-start | bytes 1048576 | tf_op jit(solution)/shard_map/all_to_all | solution.py:48
  147.2 1.9 copy-done.2
  149.8 9.7 %shard_map.106 = (f32[192,2]{1,0:T(8,128)S(1)}, bf16[64,4096]{1,0:T(8,128)(2,1)S(1)}, bf16[64,4096]{1,0:T(8,128)(2,1)}, bf16[64,4096]{1,0:T(8,128)(2,1)}, bf16[6...) custom-call(s32[1]{0:T(128)} %bitcast.3.place, ...), custom_call_target="tpu_custom_call" | custom-call | flops 2415919104 | bytes 11534336 | tf_op jit(solution)/shard_map/pallas_call | solution.py:173
  161.7 2.4 collective-permute-start.2
  166.1 4.3 %shard_map.107 = (f32[128,256]{1,0:T(8,128)S(1)}, f32[192,1]{1,0:T(8,128)S(1)}, bf16[192,128]{1,0:T(8,128)(2,1)S(1)}, f32[4,4096]{1,0:T(4,128)S(1)}) custom-call(s32[1]{0:T(128)} %bitcast.3.place, f32[8,32,512]{2,1,0:T(8,128)S(1)} %all-to-all-done.4.grads, f32[1,4096]{1,0:T(1,128)S(1)} %bitcast.28, f32[192,4096]{1,0:T(8,128)S(1)} %copy-done.3, ...), custom_call_target="tpu_custom_call" | custom-call | tf_op jit(solution)/shard_map/pallas_call | solution.py:557
  170.4 2.6 collective-permute-start.8
  172.9 3.6 %collective-permute-start.3 = (bf16[64,4096]{1,0:T(8,128)(2,1)}, bf16[64,4096]{1,0:T(8,128)(2,1)}, u32[]{:S(2)}, u32[]{:S(2)}) collective-permute-start(bf16[64,4096]{1,0:T(8,128)(2,1)} %get-tuple-element.41), channel_id=1, source_target_pairs={{0,3},{1,4},{2,5},{3,6},{4,7},{5,0},{6,1},{7,2},{8,11},{9,12},{10,... | collective-permute-start | bytes 1572872 | tf_op jit(solution)/shard_map/ppermute | solution.py:505
  176.8 5.8 %collective-permute-done.1.rest_1_ = bf16[64,4096]{1,0:T(8,128)(2,1)} collective-permute-done((bf16[64,4096]{1,0:T(8,128)(2,1)}, bf16[64,4096]{1,0:T(8,128)(2,1)}, u32[]{:S(2)}, u32[]{:S(2)}) %collective-permute-start.1) | collective-permute-done | bytes 524320 | tf_op jit(solution)/shard_map/ppermute | solution.py:505
  182.6 2.8 %collective-permute-done.2.rest_2_ = bf16[64,4096]{1,0:T(8,128)(2,1)} collective-permute-done((bf16[64,4096]{1,0:T(8,128)(2,1)}, bf16[64,4096]{1,0:T(8,128)(2,1)}, u32[]{:S(2)}, u32[]{:S(2)}) %collective-permute-start.2) | collective-permute-done | bytes 524320 | tf_op jit(solution)/shard_map/ppermute | solution.py:505
  185.5 3.2 %collective-permute-start.6 = (bf16[64,4096]{1,0:T(8,128)(2,1)}, bf16[64,4096]{1,0:T(8,128)(2,1)}, u32[]{:S(2)}, u32[]{:S(2)}) collective-permute-start(bf16[64,4096]{1,0:T(8,128)(2,1)} %get-tuple-element.44), channel_id=1, source_target_pairs={{0,6},{1,7},{2,0},{3,1},{4,2},{5,3},{6,4},{7,5},{8,14},{9,15},{10,... | collective-permute-start | bytes 1572872 | tf_op jit(solution)/shard_map/ppermute | solution.py:505
  188.7 16.9 %collective-permute-start.7 = (bf16[64,4096]{1,0:T(8,128)(2,1)}, bf16[64,4096]{1,0:T(8,128)(2,1)}, u32[]{:S(2)}, u32[]{:S(2)}) collective-permute-start(bf16[64,4096]{1,0:T(8,128)(2,1)} %get-tuple-element.45), channel_id=1, source_target_pairs={{0,7},{1,0},{2,1},{3,2},{4,3},{5,4},{6,5},{7,6},{8,15},{9,8},{10,9... | collective-permute-start | bytes 1572872 | tf_op jit(solution)/shard_map/ppermute | solution.py:505
  205.7 31.2 %all_to_all.36 = f32[128,1,256]{2,1,0:T(1,128)S(1)} all-to-all(f32[128,1,256]{2,1,0:T(1,128)S(1)} %copy.57), channel_id=1, replica_groups=mesh['u'=16,'c'=2,'expert'=8] {'u','expert'}, dimensions={0} | all-to-all | bytes 262144 | tf_op jit(solution)/shard_map/all_to_all | solution.py:48
  237.8 14.4 %all-to-all-start.6 = ((f32[128,1,256]{2,1,0:T(1,128)}), f32[128,1,256]{2,1,0:T(1,128)}, u32[]{:S(2)}, u32[]{:S(2)}) async-start(f32[128,1,256]{2,1,0:T(1,128)} %broadcast_in_dim.88), calls=%async_computation.6 | async-start | bytes 262144 | tf_op jit(solution)/shard_map/all_to_all | solution.py:48
  254.2 8.4 %shard_map.109 = bf16[8,64,4096]{2,1,0:T(8,128)(2,1)} custom-call(s32[1]{0:T(128)} %bitcast.3.place, f32[8,32,512]{2,1,0:T(8,128)S(1)} %all-to-all-done.4.grads, f32[1,4096]{1,0:T(1,128)S(1)} %bitcast.29, f32[8,64,8]{2,1,0:T(8,128)S(1)} %pad.14.notes, bf16[64,4096]{1,0:T(8,128)(2,1)S(1)} %copy-done.8, bf16[64,4096]{1,0:T(8,128)(2,1)} %collective-permute-done.1.rest_1_, ...), custom_call_target="tpu_custom_call" | custom-call | flops 25165824 | bytes 9437184 | tf_op jit(solution)/shard_map/pallas_call | solution.py:450
  262.6 3.9 %shard_map.108 = bf16[192,4096]{1,0:T(8,128)(2,1)} custom-call(f32[192,4096]{1,0:T(8,128)S(1)} %copy-done.4, f32[4,4096]{1,0:T(4,128)S(1)} %get-tuple-element.35.weighted, f32[192,1]{1,0:T(8,128)S(1)} %copy-done.6, f32[192,1]{1,0:T(8,128)S(1)} %copy-done.13, bf16[192,128]{1,0:T(8,128)(2,1)S(1)} %copy-done.15, bf16[128,4096]{1,0:T(8,128)(2,1)S(1)} %pad.13.router), custom_call_target="tpu_custom_call" | custom-call | flops 201326592 | bytes 5242880 | tf_op jit(solution)/shard_map/pallas_call | solution.py:400
  (109 shorter events, 27.3 us)
Async XLA Ops:
  0.7 56.3 %all-to-all-start = ((bf16[8,64,4096]{2,1,0:T(8,128)(2,1)}), bf16[8,64,4096]{2,1,0:T(8,128)(2,1)}, u32[]{:S(2)}, u32[]{:S(2)}) async-start(bf16[8,64,4096]{2,1,0:T(8,128)(2,1)} %bitcast.30), calls=%async_computation | async-start | bytes 8388608 | tf_op jit(solution)/shard_map/all_to_all | solution.py:48
  8.3 48.7 %copy-start.10 = (f32[4096]{0:T(1024)S(1)}, f32[4096]{0:T(1024)}, u32[]{:S(2)}) copy-start(f32[4096]{0:T(1024)} %param.12) | copy-start | bytes 49156
  57.0 24.3 %copy-start.27 = (s32[2]{0:T(128)S(1)}, s32[2]{0:T(128)}, u32[]{:S(2)}) copy-start(s32[2]{0:T(128)} %param.9) | copy-start | bytes 28
  67.2 35.9 %copy-start.5 = (f32[192,1]{1,0:T(8,128)}, f32[192,1]{1,0:T(8,128)S(1)}, u32[]{:S(2)}) copy-start(f32[192,1]{1,0:T(8,128)S(1)} %get-tuple-element.28.inverse) | copy-start | bytes 2308
  67.2 31.9 %all-to-all-start.1 = ((bf16[128,4,512]{2,1,0:T(4,128)(2,1)}), bf16[128,4,512]{2,1,0:T(4,128)(2,1)S(1)}, u32[]{:S(2)}, u32[]{:S(2)}) async-start(bf16[128,4,512]{2,1,0:T(4,128)(2,1)} %get-tuple-element.27), calls=%async_computation.1 | async-start | bytes 1048576 | tf_op jit(solution)/shard_map/all_to_all | solution.py:48
  99.2 3.8 %collective-permute-start = (bf16[128,4,512]{2,1,0:T(4,128)(2,1)S(1)}, bf16[128,4,512]{2,1,0:T(4,128)(2,1)S(1)}, u32[]{:S(2)}, u32[]{:S(2)}) collective-permute-start(bf16[128,4,512]{2,1,0:T(4,128)(2,1)S(1)} %all-to-all-done.1), channel_id=1, source_target_pairs={{0,8},{8,0},{1,9},{9,1},{2,10},{10,2},{3,11},{11,3},{4,12},{12,4},... | collective-permute-start | bytes 1572872 | tf_op jit(solution)/shard_map/ppermute | solution.py:44
  123.8 15.3 %all-to-all-start.3 = ((f32[32,8,128]{2,1,0:T(8,128)}), f32[32,8,128]{2,1,0:T(8,128)}, u32[]{:S(2)}, u32[]{:S(2)}) async-start(f32[32,8,128]{2,1,0:T(8,128)} %copy-done.11), calls=%async_computation.3 | async-start | bytes 262144 | tf_op jit(solution)/shard_map/all_to_all | solution.py:48
  143.7 20.5 %all-to-all-start.4 = ((f32[8,32,512]{2,1,0:T(8,128)}), f32[8,32,512]{2,1,0:T(8,128)S(1)}, u32[]{:S(2)}, u32[]{:S(2)}) async-start(f32[8,32,512]{2,1,0:T(8,128)} %copy-done.9), calls=%async_computation.4 | async-start | bytes 1048576 | tf_op jit(solution)/shard_map/all_to_all | solution.py:48
  149.8 14.3 %copy-start.26 = (s32[192,2]{0,1:T(2,128)S(1)}, s32[192,2]{0,1:T(2,128)}, u32[]{:S(2)}) copy-start(s32[192,2]{0,1:T(2,128)} %param.8) | copy-start | bytes 4612
  149.8 14.4 %copy-start.6 = (f32[192,1]{1,0:T(8,128)S(1)}, f32[192,1]{1,0:T(8,128)}, u32[]{:S(2)}) copy-start(f32[192,1]{1,0:T(8,128)} %copy-done.5) | copy-start | bytes 2308
  160.3 22.3 %collective-permute-start.1 = (bf16[64,4096]{1,0:T(8,128)(2,1)}, bf16[64,4096]{1,0:T(8,128)(2,1)}, u32[]{:S(2)}, u32[]{:S(2)}) collective-permute-start(bf16[64,4096]{1,0:T(8,128)(2,1)} %get-tuple-element.39), channel_id=1, source_target_pairs={{0,1},{1,2},{2,3},{3,4},{4,5},{5,6},{6,7},{7,0},{8,9},{9,10},{10,1... | collective-permute-start | bytes 1572872 | tf_op jit(solution)/shard_map/ppermute | solution.py:505
  161.7 23.8 %collective-permute-start.2 = (bf16[64,4096]{1,0:T(8,128)(2,1)}, bf16[64,4096]{1,0:T(8,128)(2,1)}, u32[]{:S(2)}, u32[]{:S(2)}) collective-permute-start(bf16[64,4096]{1,0:T(8,128)(2,1)} %get-tuple-element.40), channel_id=1, source_target_pairs={{0,2},{1,3},{2,4},{3,5},{4,6},{5,7},{6,0},{7,1},{8,10},{9,11},{10,... | collective-permute-start | bytes 1572872 | tf_op jit(solution)/shard_map/ppermute | solution.py:505
  170.4 35.2 %copy-start.12 = (f32[192,1]{1,0:T(8,128)}, f32[192,1]{1,0:T(8,128)S(1)}, u32[]{:S(2)}) copy-start(f32[192,1]{1,0:T(8,128)S(1)} %get-tuple-element.36.shrink) | copy-start | bytes 2308
  170.4 35.3 %copy-start.14 = (bf16[192,128]{1,0:T(8,128)(2,1)}, bf16[192,128]{1,0:T(8,128)(2,1)S(1)}, u32[]{:S(2)}) copy-start(bf16[192,128]{1,0:T(8,128)(2,1)S(1)} %get-tuple-element.37.choice) | copy-start | bytes 147460
  170.4 83.7 %copy-start.8 = (bf16[64,4096]{1,0:T(8,128)(2,1)S(1)}, bf16[64,4096]{1,0:T(8,128)(2,1)}, u32[]{:S(2)}) copy-start(bf16[64,4096]{1,0:T(8,128)(2,1)} %copy-done.7) | copy-start | bytes 1572868
  170.4 18.3 %collective-permute-start.8 = (f32[128,256]{1,0:T(8,128)S(1)}, f32[128,256]{1,0:T(8,128)S(1)}, u32[]{:S(2)}, u32[]{:S(2)}) collective-permute-start(f32[128,256]{1,0:T(8,128)S(1)} %get-tuple-element.46), channel_id=1, source_target_pairs={{0,8},{8,0},{1,9},{9,1},{2,10},{10,2},{3,11},{11,3},{4,12},{12,4},... | collective-permute-start | bytes 393224 | tf_op jit(solution)/shard_map/ppermute | solution.py:44
  172.9 81.1 %collective-permute-start.3 = (bf16[64,4096]{1,0:T(8,128)(2,1)}, bf16[64,4096]{1,0:T(8,128)(2,1)}, u32[]{:S(2)}, u32[]{:S(2)}) collective-permute-start(bf16[64,4096]{1,0:T(8,128)(2,1)} %get-tuple-element.41), channel_id=1, source_target_pairs={{0,3},{1,4},{2,5},{3,6},{4,7},{5,0},{6,1},{7,2},{8,11},{9,12},{10,... | collective-permute-start | bytes 1572872 | tf_op jit(solution)/shard_map/ppermute | solution.py:505
  176.6 77.5 %collective-permute-start.4 = (bf16[64,4096]{1,0:T(8,128)(2,1)}, bf16[64,4096]{1,0:T(8,128)(2,1)}, u32[]{:S(2)}, u32[]{:S(2)}) collective-permute-start(bf16[64,4096]{1,0:T(8,128)(2,1)} %get-tuple-element.42), channel_id=1, source_target_pairs={{0,4},{1,5},{2,6},{3,7},{4,0},{5,1},{6,2},{7,3},{8,12},{9,13},{10,... | collective-permute-start | bytes 1572872 | tf_op jit(solution)/shard_map/ppermute | solution.py:505
  182.6 71.4 %collective-permute-start.5 = (bf16[64,4096]{1,0:T(8,128)(2,1)}, bf16[64,4096]{1,0:T(8,128)(2,1)}, u32[]{:S(2)}, u32[]{:S(2)}) collective-permute-start(bf16[64,4096]{1,0:T(8,128)(2,1)} %get-tuple-element.43), channel_id=1, source_target_pairs={{0,5},{1,6},{2,7},{3,0},{4,1},{5,2},{6,3},{7,4},{8,13},{9,14},{10,... | collective-permute-start | bytes 1572872 | tf_op jit(solution)/shard_map/ppermute | solution.py:505
  185.5 68.6 %collective-permute-start.6 = (bf16[64,4096]{1,0:T(8,128)(2,1)}, bf16[64,4096]{1,0:T(8,128)(2,1)}, u32[]{:S(2)}, u32[]{:S(2)}) collective-permute-start(bf16[64,4096]{1,0:T(8,128)(2,1)} %get-tuple-element.44), channel_id=1, source_target_pairs={{0,6},{1,7},{2,0},{3,1},{4,2},{5,3},{6,4},{7,5},{8,14},{9,15},{10,... | collective-permute-start | bytes 1572872 | tf_op jit(solution)/shard_map/ppermute | solution.py:505
  188.7 65.4 %collective-permute-start.7 = (bf16[64,4096]{1,0:T(8,128)(2,1)}, bf16[64,4096]{1,0:T(8,128)(2,1)}, u32[]{:S(2)}, u32[]{:S(2)}) collective-permute-start(bf16[64,4096]{1,0:T(8,128)(2,1)} %get-tuple-element.45), channel_id=1, source_target_pairs={{0,7},{1,0},{2,1},{3,2},{4,3},{5,4},{6,5},{7,6},{8,15},{9,8},{10,9... | collective-permute-start | bytes 1572872 | tf_op jit(solution)/shard_map/ppermute | solution.py:505
  237.8 28.7 %all-to-all-start.6 = ((f32[128,1,256]{2,1,0:T(1,128)}), f32[128,1,256]{2,1,0:T(1,128)}, u32[]{:S(2)}, u32[]{:S(2)}) async-start(f32[128,1,256]{2,1,0:T(1,128)} %broadcast_in_dim.88), calls=%async_computation.6 | async-start | bytes 262144 | tf_op jit(solution)/shard_map/all_to_all | solution.py:48
  254.1 8.4 %copy-start.4 = (f32[192,4096]{1,0:T(8,128)S(1)}, f32[192,4096]{1,0:T(8,128)}, u32[]{:S(2)}) copy-start(f32[192,4096]{1,0:T(8,128)} %copy-done.1) | copy-start | bytes 9437188
  254.1 8.4 %copy-start.13 = (f32[192,1]{1,0:T(8,128)S(1)}, f32[192,1]{1,0:T(8,128)}, u32[]{:S(2)}) copy-start(f32[192,1]{1,0:T(8,128)} %copy-done.12) | copy-start | bytes 2308
  (18 other events, 45.6 us)

commit v3 on v2

--- a/solution.py
+++ b/solution.py
@@ -18,6 +18,7 @@
 I32 = jnp.int32
 VMEM = pl.BlockSpec(memory_space=pltpu.VMEM)
 SMEM = pl.BlockSpec(memory_space=pltpu.SMEM)
+HBM = pl.BlockSpec(memory_space=pltpu.HBM)
 NT = (((1,), (1,)), ((), ()))
 
 
@@ -25,8 +26,8 @@
     return lax.broadcasted_iota(I32, shape, dim)
 
 
-def params(**more):
-    return pltpu.CompilerParams(vmem_limit_bytes=40 << 20, **more)
+def params(mib):
+    return pltpu.CompilerParams(vmem_limit_bytes=mib << 20)
 
 
 def cost(flops, moved):
@@ -63,9 +64,19 @@
     return gates, routes * capacity + rank
 
 
-def forward_kernel(steps, outer, tok, rec, slot, gate, gain, summed, offered, inverse, held, square):
+def forward_kernel(
+    steps, outer, tok, rec, slot, gate, gain, summed, offered, inverse, held, square, sliced, row_sem, slice_sem
+):
     step = pl.program_id(0)
     part = tok.shape[1]
+
+    def keep(e):
+        start = pl.multiple_of(e * part, part)
+        return pltpu.make_async_copy(held.at[e], summed.at[:, pl.ds(start, part)], row_sem.at[e])
+
+    def offer(u):
+        return pltpu.make_async_copy(sliced, offered.at[pl.ds(u * steps, steps)], slice_sem.at[u])
+
     rows, slots = tok.shape[0], rec.shape[0]
     ids = iota((rows, slots), 1)
     first = (slot[:, 0:1] == ids).astype(BF16)
@@ -83,9 +94,9 @@
             + gate[:, 0:1] * jnp.dot(first, block, preferred_element_type=F32)
             + gate[:, 1:2] * jnp.dot(second, block, preferred_element_type=F32)
         )
-        summed[:, cols] = x
         held[step, :, cols] = x
         square[...] += fold(x * x)
+    keep(step).start()
 
     @pl.when(step == steps - 1)
     def _():
@@ -96,9 +107,13 @@
         for e in range(steps):
             x = held[e] * scale
             x = jnp.sum(x.reshape(count, SEQ, part), axis=1) / SEQ
-            x = (x * gain[:, part * e : part * (e + 1)]).astype(BF16)
-            for u in range(outer):
-                offered[u * steps + e] = x
+            sliced[e] = (x * gain[:, part * e : part * (e + 1)]).astype(BF16)
+        for u in range(outer):
+            offer(u).start()
+        for e in range(steps):
+            keep(e).wait()
+        for u in range(outer):
+            offer(u).wait()
 
 
 def forward(tokens, received, slot, gates, gain, experts, outer):
@@ -116,26 +131,35 @@
             whole((rows, 2)),
             whole((1, width)),
         ],
-        out_specs=[
-            pl.BlockSpec((rows, part), lambda i: (0, i)),
-            whole((outer * experts, rows // SEQ, part)),
-            whole((rows, 1)),
-        ],
+        out_specs=[HBM, HBM, whole((rows, 1))],
         out_shape=[
-            jax.ShapeDtypeStruct((rows, width), F32),
-            jax.ShapeDtypeStruct((outer * experts, rows // SEQ, part), BF16),
+            pltpu.HBM((rows, width), F32),
+            pltpu.HBM((outer * experts, rows // SEQ, part), BF16),
             jax.ShapeDtypeStruct((rows, 1), F32),
         ],
-        scratch_shapes=[pltpu.VMEM((experts, rows, part), F32), pltpu.VMEM((rows, 128), F32)],
-        compiler_params=params(),
+        scratch_shapes=[
+            pltpu.VMEM((experts, rows, part), F32),
+            pltpu.VMEM((rows, 128), F32),
+            pltpu.VMEM((experts, rows // SEQ, part), BF16),
+            pltpu.SemaphoreType.DMA((experts,)),
+            pltpu.SemaphoreType.DMA((outer,)),
+        ],
+        compiler_params=params(14),
         cost_estimate=cost(4 * rows * slots * width, 10 << 20),
     )(tokens, received, slot, gates, gain)
 
 
 def pack_kernel(steps, place, x, rec, slot, turned, overlap, *rest):
-    outs, dots = rest[:-1], rest[-1]
+    *outs, dots, packed, sems = rest
     step = pl.program_id(0)
     rows, part = x.shape
+
+    def leave(e, r):
+        start = pl.multiple_of(e * part, part)
+        return pltpu.make_async_copy(
+            packed.at[e, pl.ds(r * capacity, capacity)], outs[r].at[:, pl.ds(start, part)], sems.at[e, r]
+        )
+
     slots = rec.shape[0]
     capacity = slots // len(outs)
     ids = iota((rows, slots), 1)
@@ -155,14 +179,18 @@
         dots[0] += fold(value * jnp.dot(first, block, preferred_element_type=F32))
         dots[1] += fold(value * jnp.dot(second, block, preferred_element_type=F32))
         moved = jnp.dot(spot, value.astype(BF16), preferred_element_type=F32).astype(BF16)
-        for r, out in enumerate(outs):
-            out[:, cols] = moved[capacity * r : capacity * (r + 1)]
+        packed[step, :, cols] = moved
+    for r in range(len(outs)):
+        leave(step, r).start()
 
     @pl.when(step == steps - 1)
     def _():
         overlap[...] = jnp.concatenate(
             [jnp.sum(dots[k], axis=1, keepdims=True) for k in range(2)], axis=1
         )
+        for e in range(steps):
+            for r in range(len(outs)):
+                leave(e, r).wait()
 
 
 def pack(place, summed, received, slot, experts, capacity):
@@ -180,11 +208,15 @@
             whole((rows, 2)),
             whole((2, rows)),
         ],
-        out_specs=[whole((rows, 2))] + [pl.BlockSpec((capacity, part), lambda i: (0, i))] * experts,
+        out_specs=[whole((rows, 2))] + [HBM] * experts,
         out_shape=[jax.ShapeDtypeStruct((rows, 2), F32)]
-        + [jax.ShapeDtypeStruct((capacity, width), BF16)] * experts,
-        scratch_shapes=[pltpu.VMEM((2, rows, 128), F32)],
-        compiler_params=params(),
+        + [pltpu.HBM((capacity, width), BF16)] * experts,
+        scratch_shapes=[
+            pltpu.VMEM((2, rows, 128), F32),
+            pltpu.VMEM((experts, slots, part), BF16),
+            pltpu.SemaphoreType.DMA((experts, experts)),
+        ],
+        compiler_params=params(12),
         cost_estimate=cost(6 * rows * slots * width, 11 << 20),
     )(place, summed, received, slot, slot.T)
 
@@ -204,11 +236,11 @@
     return (source == b).astype(BF16)
 
 
-def scores_kernel(place, near, far, notes, offered):
+def scores_kernel(near, far, notes, offered):
     experts, total, columns = offered.shape
     group = experts * PAIR_DEV
     wide = 2 * group
-    own = near[pl.ds(pl.multiple_of(place[0] * wide, wide), wide), :]
+    own = near[pl.ds(pl.multiple_of(lax.axis_index("u") * wide, wide), wide), :]
     queries, records = [
         jnp.dot(picker(group, kind), own, preferred_element_type=F32).astype(BF16) for kind in (0, 1)
     ]
@@ -225,10 +257,10 @@
             offered[e, group * k : group * k + block.shape[0], :] = block
 
 
-def totals_kernel(scale, devices, place, gathered, offered, kept, own_total, own_positive, loss_row):
+def totals_kernel(scale, devices, gathered, offered, kept):
+    place, core = lax.axis_index("u"), lax.axis_index("c")
     experts, total, columns = gathered.shape
     group = experts * PAIR_DEV
-    outer_size = columns // (2 * group)
     both = gathered[0]
     for e in range(1, experts):
         both = both + gathered[e]
@@ -242,7 +274,7 @@
     pair = iota(shape, 0)
     within = lax.rem(lane, 2 * group)
     matching = (within // ROWS_DEV == pair // PAIR_DEV) & (kind == lax.rem(pair, PAIR_DEV))
-    here = matching & (lane // (2 * group) == place[0])
+    here = matching & (lane // (2 * group) == place)
     positive = jnp.sum(jnp.where(here, positive_lane, 0.0), axis=1, keepdims=True)
 
     low = jnp.float32(-jnp.inf)
@@ -256,20 +288,17 @@
     )
     log_total = highest + jnp.log(weight)
     chosen = jnp.zeros((group, 1), F32)
-    for side, core in ((near, place[1]), (far, 1 - place[1])):
-        name = column_names(lane, kind, group, core)
+    for side, where in ((near, core), (far, 1 - core)):
+        name = column_names(lane, kind, group, where)
         hit = at_record & (name.astype(F32) == positive)
         chosen = chosen + jnp.sum(jnp.where(hit, side, 0.0), axis=1, keepdims=True)
-    own_total[...] = log_total
-    own_positive[...] = positive
+    kept[2 * group : 3 * group, :128] = jnp.broadcast_to(log_total, (group, 128))
+    kept[2 * group : 3 * group, 128:256] = jnp.broadcast_to(positive, (group, 128))
     row_loss = log_total - chosen
 
     total_lane = jnp.sum(jnp.where(here, log_total, 0.0), axis=0, keepdims=True)
-    loss_lane = jnp.sum(
-        jnp.where(matching & (lane // (2 * group) == place[0]), row_loss, 0.0), axis=0, keepdims=True
-    )
-    own_lane = jnp.where(lane[0:1] // (2 * group) == place[0], positive_lane, 0.0)
-    loss_row[...] = loss_lane
+    loss_lane = jnp.sum(jnp.where(here, row_loss, 0.0), axis=0, keepdims=True)
+    own_lane = jnp.where(lane[0:1] // (2 * group) == place, positive_lane, 0.0)
     pieces = [x[:, 128 * k : 128 * (k + 1)] for x in (total_lane, own_lane) for k in range(columns // 128)]
     loss_pieces = [
         pltpu.roll(loss_lane, PAIR_DEV, 1)[:, 128 * k : 128 * (k + 1)] for k in range(columns // 128)
@@ -286,7 +315,8 @@
     return block * group + (lax.rem(lane, wide) // ROWS_DEV) * PAIR_DEV + lax.rem(kind, PAIR_DEV)
 
 
-def gradient_kernel(scale, place, factor, heard, kept, own_total, own_positive, near, far, offered, loss):
+def gradient_kernel(scale, factor, heard, kept, near, far, offered, loss):
+    place, core = lax.axis_index("u"), lax.axis_index("c")
     experts, wide, columns = offered.shape
     group = wide // 2
     outer_size = heard.shape[0] // CORES
@@ -294,21 +324,22 @@
     shape = (group, columns)
     lane, kind, at_record = lanes_of(shape, 1)
     pair = iota(shape, 0)
-    own_name = (place[0] * CORES + place[1]) * group + iota((group, 1), 0)
-    row_lane = lane[0:1]
+    own_name = (place * CORES + core) * group + iota((group, 1), 0)
+    own_total = kept[2 * group : 3 * group, 0:1]
+    own_positive = kept[2 * group : 3 * group, 128:129]
     result = jnp.zeros((wide, columns), F32)
     losses = jnp.zeros((1, columns), F32)
-    for k, (side, core) in enumerate(((near, place[1]), (far, 1 - place[1]))):
-        told = heard[core]
+    for k, (side, where) in enumerate(((near, core), (far, 1 - core))):
+        told = heard[where]
         for u in range(1, outer_size):
-            told = told + heard[u * CORES + core]
+            told = told + heard[u * CORES + where]
         total = jnp.concatenate([told[i : i + 1] for i in range(pieces)], axis=1)
         positive = jnp.concatenate([told[pieces + i : pieces + i + 1] for i in range(pieces)], axis=1)
         losses = losses + jnp.where(at_record[0:1], total, 0.0)
         value = kept[group * k : group * (k + 1), :]
-        name = column_names(lane, kind, group, core).astype(F32)
-        hit = jnp.where(name == own_positive[...], 1.0, 0.0)
-        by_query = (jnp.exp(value - own_total[...]) - hit) * factor[0]
+        name = column_names(lane, kind, group, where).astype(F32)
+        hit = jnp.where(name == own_positive, 1.0, 0.0)
+        by_query = (jnp.exp(value - own_total) - hit) * factor[0]
         by_query = jnp.where(at_record, by_query, 0.0).astype(BF16)
         hit = jnp.where(positive == own_name.astype(F32), 1.0, 0.0)
         by_record = (jnp.exp(jnp.where(at_record, 0.0, value - total)) - hit) * factor[0]
@@ -336,7 +367,7 @@
     return high, mid, low
 
 
-def router_kernel(place, grads, gain, summed, rec, tok, slot, routes, gate, inverse, overlap, part_out, shrink_out, choice_out, weighted_out):
+def router_kernel(grads, gain, summed, rec, tok, slot, routes, gate, inverse, overlap, part_out, shrink_out, choice_out, weighted_out):
     experts, _, part = grads.shape
     rows = summed.shape[0]
     slots = rec.shape[0]
@@ -345,7 +376,7 @@
     on_slots = jnp.zeros((16, slots), F32)
     for e in range(experts):
         cols = slice(part * e, part * (e + 1))
-        w = rows_of(grads, e, place[0]) * (gain[:, cols] / SEQ)
+        w = rows_of(grads, e, lax.axis_index("expert")) * (gain[:, cols] / SEQ)
         weighted_out[:, cols] = w
         lhs = jnp.concatenate(list(split_bf16(w)) + [jnp.zeros((count, part), BF16)], axis=0)
         on_slots = on_slots + lax.dot_general(lhs, rec[:, cols], NT, preferred_element_type=F32)
@@ -375,12 +406,9 @@
     choice = jnp.concatenate(choices, axis=0)
     choice_out[...] = choice.astype(BF16)
     lhs = jnp.transpose(choice)[:experts].astype(BF16)
-    block = part_out.shape[1]
-    for k in range(tok.shape[1] // block):
-        cols = slice(block * k, block * (k + 1))
-        part_out[experts * k : experts * (k + 1), :] = jnp.dot(
-            lhs, tok[:, cols], preferred_element_type=F32
-        )
+    for k in range(experts):
+        cols = slice(part * k, part * (k + 1))
+        part_out[:, cols] = jnp.dot(lhs, tok[:, cols], preferred_element_type=F32)
 
 
 def token_kernel(summed, weighted, inverse, shrink, choice, router, out):
@@ -403,7 +431,7 @@
         in_specs=[split(rows), split(weighted.shape[0]), whole((rows, 1)), whole((rows, 1)), whole((rows, 128)), split(128)],
         out_specs=split(rows),
         out_shape=jax.ShapeDtypeStruct((rows, width), BF16),
-        compiler_params=params(),
+        compiler_params=params(10),
         cost_estimate=cost(2 * rows * 128 * width, 5 << 20),
     )(summed, weighted, inverse, shrink, choice, router)
 
@@ -461,16 +489,9 @@
             out_specs=pl.BlockSpec((1, capacity, width), source),
         ),
         out_shape=jax.ShapeDtypeStruct((experts, capacity, width), BF16),
-        compiler_params=params(),
+        compiler_params=params(24),
         cost_estimate=cost(12 * experts * capacity * width, 9 << 20),
     )(place, grads, gain, notes, *backs)
-
-
-def turn_kernel(x, out):
-    experts = out.shape[1]
-    block = x.shape[1]
-    for k in range(x.shape[0] // experts):
-        out[block * k : block * (k + 1), :] = jnp.transpose(x[experts * k : experts * (k + 1), :])
 
 
 def shards(tokens, routes, positives, expert_out, router, norm_gain, loss_scale):
@@ -479,7 +500,6 @@
     slots = experts * capacity
     outer = lax.axis_size("u")
     mine = lax.axis_index("expert").astype(I32)
-    where = jnp.stack([lax.axis_index("u").astype(I32), lax.axis_index("c").astype(I32)])
     mine_at = mine[None]
     wide = outer * experts
     part = width // experts
@@ -517,66 +537,60 @@
     notes = jnp.stack([gate_slot, inverse_slot, sequence_slot, spread_positive])
     notes = jnp.pad(notes, ((0, 4), (0, 0)))
 
+    near, overlap = lax.optimization_barrier((near, overlap))
     far = swap_core(near)
     near, far = near.reshape(columns, part), far.reshape(columns, part)
     offered = pl.pallas_call(
         scores_kernel,
-        in_specs=[SMEM, VMEM, VMEM, VMEM],
+        in_specs=[VMEM] * 3,
         out_specs=VMEM,
         out_shape=jax.ShapeDtypeStruct((experts, 2 * group + 8, columns), F32),
-        compiler_params=params(),
-    )(where, near, far, notes)
+        compiler_params=params(2),
+    )(near, far, notes)
     gathered = exchange(offered, "expert")
-    column = jax.ShapeDtypeStruct((group, 1), F32)
-    offered, kept, own_total, own_positive, _ = pl.pallas_call(
+    gathered, *backs[1:4] = lax.optimization_barrier((gathered, *backs[1:4]))
+    offered, kept = pl.pallas_call(
         functools.partial(totals_kernel, scale, outer * CORES),
-        in_specs=[SMEM, VMEM],
-        out_specs=[VMEM] * 5,
+        in_specs=[VMEM],
+        out_specs=[VMEM] * 2,
         out_shape=[
             jax.ShapeDtypeStruct((outer * CORES, 8, 128), F32),
-            jax.ShapeDtypeStruct((2 * group, columns), F32),
-            column,
-            column,
-            jax.ShapeDtypeStruct((1, columns), F32),
-        ],
-        compiler_params=params(),
-    )(where, gathered)
+            jax.ShapeDtypeStruct((3 * group, columns), F32),
+        ],
+        compiler_params=params(2),
+    )(gathered)
     heard = exchange(offered, ("u", "c"))
+    heard, *backs[4:6] = lax.optimization_barrier((heard, *backs[4:6]))
     offered, loss = pl.pallas_call(
         functools.partial(gradient_kernel, scale),
-        in_specs=[SMEM, SMEM] + [VMEM] * 6,
+        in_specs=[SMEM] + [VMEM] * 4,
         out_specs=[VMEM, VMEM],
         out_shape=[
             jax.ShapeDtypeStruct((experts, 2 * group, part), F32),
             jax.ShapeDtypeStruct((1, 1), F32),
         ],
-        compiler_params=params(),
-    )(where, (loss_scale / pairs)[None], heard, kept, own_total, own_positive, near, far)
+        compiler_params=params(2),
+    )((loss_scale / pairs)[None], heard, kept, near, far)
     grads = exchange(offered, "expert")
+    grads, *backs[6:8] = lax.optimization_barrier((grads, *backs[6:8]))
 
     router_part, shrink, choice, weighted = pl.pallas_call(
         router_kernel,
-        in_specs=[SMEM] + [VMEM] * 10,
+        in_specs=[VMEM] * 10,
         out_specs=[VMEM] * 4,
         out_shape=[
-            jax.ShapeDtypeStruct((wide, width * experts // wide), F32),
+            jax.ShapeDtypeStruct((experts, width), F32),
             jax.ShapeDtypeStruct((rows, 1), F32),
             jax.ShapeDtypeStruct((rows, 128), BF16),
             jax.ShapeDtypeStruct((rows // SEQ, width), F32),
         ],
-        compiler_params=params(),
-    )(mine_at, grads, gain, summed, received, tokens, slot, routes, gates, inverse, overlap)
+        compiler_params=params(6),
+    )(grads, gain, summed, received, tokens, slot, routes, gates, inverse, overlap)
     router_part = router_part + swap_core(router_part)
-    router_part = exchange(router_part[:, None, :], ("u", "expert"))
+    router_part = exchange(router_part.reshape(wide, 1, -1), ("u", "expert"))
     router_sum = jnp.sum(router_part, axis=0)
     router_all = exchange(jnp.broadcast_to(router_sum[None], (wide,) + router_sum.shape), ("u", "expert"))
-    router_grad = pl.pallas_call(
-        turn_kernel,
-        in_specs=[VMEM],
-        out_specs=VMEM,
-        out_shape=jax.ShapeDtypeStruct((width, experts), F32),
-        compiler_params=params(),
-    )(router_all.reshape(wide, -1))
+    router_grad = router_all.reshape(experts, width).T
 
     turned = jnp.pad(router.T, ((0, 128 - experts), (0, 0)))
     token_grad = token_rows(summed, weighted, inverse, shrink, choice, turned, experts)

time: 272 us -> 276 us (1.015)
  waiting for transfers between devices: 80.3 us -> 110 us
  blocking collectives: 46.8 us -> 21.3 us
    ppermute x7, waiting for transfers between devices: 8.69 us -> 50.1 us  [shards(): lax.ppermute(outgoing[r], 'expert', [(i, (i + r) % experts) for i in rang...]
    all_to_all x2 -> x1, blocking collectives: 46.8 us -> 21.3 us  [exchange(): return lax.all_to_all(x, axes, split_axis=0, concat_axis=0, tiled=True)]
    all_to_all x5 -> x6, waiting for transfers between devices: 71 us -> 58 us  [exchange(): return lax.all_to_all(x, axes, split_axis=0, concat_axis=0, tiled=True)]
    all_to_all x5 -> x6, starting transfers between devices: 45.6 us -> 49.7 us  [exchange(): return lax.all_to_all(x, axes, split_axis=0, concat_axis=0, tiled=True)]
    ppermute x7, starting transfers between devices: 27.6 us -> 23.9 us  [shards(): lax.ppermute(outgoing[r], 'expert', [(i, (i + r) % experts) for i in rang...]
    pallas_call x4 -> x3, Pallas kernels: 7.93 us -> 6.86 us  [the longest x1 4.27 us: shards(): pl.pallas_call(router_kernel, in_specs=[VMEM] * 10, out_specs=[VMEM] * 4,...]
  transfers between devices with their start and end apart: 14 -> 15, of which waited for: 6 -> 8; matrix products, arithmetic and copies ran while one was open for 3% -> 2% of each run, Pallas kernels for 10% -> 9%
where the time goes in v3:
time: 276 us; the launch traced here: 274 us
  waiting for transfers between devices  110 us (40%)
  starting transfers between devices  77.3 us (28%)
  Pallas kernels  38.1 us (14%)
  blocking collectives  21.3 us (8%)
  local copies, waits for them, and re-layouts  20.4 us (7%)
  between operations  3.48 us (1%)
  other arithmetic  3.39 us (1%)
    all_to_all x6, waiting for transfers between devices, exchange(): return lax.all_to_all(x, axes, split_axis=0, concat_axis=0, tiled=True)  58 us
    ppermute x7, waiting for transfers between devices, shards(): lax.ppermute(outgoing[r], 'expert', [(i, (i + r) % experts) for i in rang...  50.1 us
    all_to_all x6, starting transfers between devices, exchange(): return lax.all_to_all(x, axes, split_axis=0, concat_axis=0, tiled=True)  49.7 us
    ppermute x7, starting transfers between devices, shards(): lax.ppermute(outgoing[r], 'expert', [(i, (i + r) % experts) for i in rang...  23.9 us
    all_to_all x1, blocking collectives, exchange(): return lax.all_to_all(x, axes, split_axis=0, concat_axis=0, tiled=True)  21.3 us
    unnamed x60, local copies, waits for them, and re-layouts  16.1 us
    pallas_call x1, Pallas kernels, pack(): pl.pallas_call(functools.partial(pack_kernel, experts), grid=(experts,),...  10.2 us
    pallas_call x1, Pallas kernels, forward(): pl.pallas_call(functools.partial(forward_kernel, experts, outer), grid=(e...  8.94 us
  transfers between devices with their start and end apart: 15, of which 8 were waited for; matrix products, arithmetic and copies ran while one was open for 2% of the time, Pallas kernels for 9%

profile of v3, /device:TPU:1, one launch (start us, length us, event | category | flops | bytes accessed | tf_op | source)
XLA Modules:
  0.0 274.3 jit_solution(12823489319796481630)
XLA Ops:
  0.7 7.6 %all-to-all-start = ((bf16[8,64,4096]{2,1,0:T(8,128)(2,1)}), bf16[8,64,4096]{2,1,0:T(8,128)(2,1)}, u32[]{:S(2)}, u32[]{:S(2)}) async-start(bf16[8,64,4096]{2,1,0:T(8,128)(2,1)} %bitcast.23), calls=%async_computation | async-start | bytes 8388608 | tf_op jit(solution)/shard_map/all_to_all | solution.py:49
  9.7 47.3 %all-to-all-done = bf16[8,64,4096]{2,1,0:T(8,128)(2,1)} async-done(((bf16[8,64,4096]{2,1,0:T(8,128)(2,1)}), bf16[8,64,4096]{2,1,0:T(8,128)(2,1)}, u32[]{:S(2)}, u32[]{:S(2)}) %all-to-all-start) | async-done | bytes 4194336 | tf_op jit(solution)/shard_map/all_to_all | solution.py:49
  57.0 8.9 %shard_map.102 = (f32[192,4096]{1,0:T(8,128)}, bf16[128,4,512]{2,1,0:T(4,128)(2,1)}, f32[192,1]{1,0:T(8,128)S(1)}) custom-call(bf16[192,4096]{1,0:T(8,128)(2,1)S(1)} %copy-done, bf16[512,4096]{1,0:T(8,128)(2,1)} %bitcast.1.rec, s32[192,2]{1,0:T(8,128)S(1)} %add.59.slot, f32[192,2]{1,0:T(8,128)S(1)} %exponential_divide_fusion.gate, f32[1,4096]{1,0:T(1,128)S(1)} %bitcast.20), custom_call_target="tpu_custom_call" | custom-call | flops 1610612736 | bytes 10485760 | tf_op jit(solution)/shard_map/pallas_call | solution.py:124
  66.0 14.1 %all-to-all-start.1 = ((bf16[128,4,512]{2,1,0:T(4,128)(2,1)}), bf16[128,4,512]{2,1,0:T(4,128)(2,1)S(1)}, u32[]{:S(2)}, u32[]{:S(2)}) async-start(bf16[128,4,512]{2,1,0:T(4,128)(2,1)} %get-tuple-element.37), calls=%async_computation.1 | async-start | bytes 1048576 | tf_op jit(solution)/shard_map/all_to_all | solution.py:49
  83.9 10.2 %shard_map.103 = (f32[192,2]{1,0:T(8,128)S(1)}, bf16[64,4096]{1,0:T(8,128)(2,1)}, bf16[64,4096]{1,0:T(8,128)(2,1)}, bf16[64,4096]{1,0:T(8,128)(2,1)}, bf16[64,40...) custom-call(s32[1]{0:T(128)} %bitcast.4.place, ...), custom_call_target="tpu_custom_call" | custom-call | flops 2415919104 | bytes 11534336 | tf_op jit(solution)/shard_map/pallas_call | solution.py:201
  94.7 3.2 %all-to-all-done.1 = bf16[128,4,512]{2,1,0:T(4,128)(2,1)S(1)} async-done(((bf16[128,4,512]{2,1,0:T(4,128)(2,1)}), bf16[128,4,512]{2,1,0:T(4,128)(2,1)S(1)}, u32[]{:S(2)}, u32[]{:S(2)}) %all-to-all-start.1) | async-done | bytes 524320 | tf_op jit(solution)/shard_map/all_to_all | solution.py:49
  97.9 2.3 collective-permute-start
  103.4 3.7 %all-to-all-start.2 = ((f32[8,40,512]{2,1,0:T(8,128)}), f32[8,40,512]{2,1,0:T(8,128)S(1)}, u32[]{:S(2)}, u32[]{:S(2)}) async-start(f32[8,40,512]{2,1,0:T(8,128)} %copy-done.4), calls=%async_computation.2 | async-start | bytes 1310720 | tf_op jit(solution)/shard_map/all_to_all | solution.py:49
  108.6 2.4 collective-permute-start.2
  111.0 3.6 %collective-permute-start.3 = (bf16[64,4096]{1,0:T(8,128)(2,1)}, bf16[64,4096]{1,0:T(8,128)(2,1)S(1)}, u32[]{:S(2)}, u32[]{:S(2)}) collective-permute-start(bf16[64,4096]{1,0:T(8,128)(2,1)} %get-tuple-element.43), channel_id=1, source_target_pairs={{0,3},{1,4},{2,5},{3,6},{4,7},{5,0},{6,1},{7,2},{8,11},{9,12},{10,... | collective-permute-start | bytes 1572872 | tf_op jit(solution)/shard_map/ppermute | solution.py:525
  114.9 2.7 collective-permute-start.5
  117.5 21.5 %collective-permute-done.1.rest_1_ = bf16[64,4096]{1,0:T(8,128)(2,1)S(1)} collective-permute-done((bf16[64,4096]{1,0:T(8,128)(2,1)}, bf16[64,4096]{1,0:T(8,128)(2,1)S(1)}, u32[]{:S(2)}, u32[]{:S(2)}) %collective-permute-start.1) | collective-permute-done | bytes 524320 | tf_op jit(solution)/shard_map/ppermute | solution.py:525
  139.9 17.4 %collective-permute-done.2.rest_2_ = bf16[64,4096]{1,0:T(8,128)(2,1)S(1)} collective-permute-done((bf16[64,4096]{1,0:T(8,128)(2,1)}, bf16[64,4096]{1,0:T(8,128)(2,1)S(1)}, u32[]{:S(2)}, u32[]{:S(2)}) %collective-permute-start.2) | collective-permute-done | bytes 524320 | tf_op jit(solution)/shard_map/ppermute | solution.py:525
  160.5 6.8 %all-to-all-start.3 = ((f32[32,8,128]{2,1,0:T(8,128)}), f32[32,8,128]{2,1,0:T(8,128)}, u32[]{:S(2)}, u32[]{:S(2)}) async-start(f32[32,8,128]{2,1,0:T(8,128)} %copy-done.17), calls=%async_computation.3 | async-start | bytes 262144 | tf_op jit(solution)/shard_map/all_to_all | solution.py:49
  167.4 13.5 %collective-permute-start.6 = (bf16[64,4096]{1,0:T(8,128)(2,1)}, bf16[64,4096]{1,0:T(8,128)(2,1)}, u32[]{:S(2)}, u32[]{:S(2)}) collective-permute-start(bf16[64,4096]{1,0:T(8,128)(2,1)} %get-tuple-element.51), channel_id=1, source_target_pairs={{0,6},{1,7},{2,0},{3,1},{4,2},{5,3},{6,4},{7,5},{8,14},{9,15},{10,... | collective-permute-start | bytes 1572872 | tf_op jit(solution)/shard_map/ppermute | solution.py:525
  185.1 9.9 %all-to-all-start.4 = ((f32[8,32,512]{2,1,0:T(8,128)}), f32[8,32,512]{2,1,0:T(8,128)S(1)}, u32[]{:S(2)}, u32[]{:S(2)}) async-start(f32[8,32,512]{2,1,0:T(8,128)} %copy-done.15), calls=%async_computation.4 | async-start | bytes 1048576 | tf_op jit(solution)/shard_map/all_to_all | solution.py:49
  195.2 11.1 %collective-permute-done.7.rest_7_ = bf16[64,4096]{1,0:T(8,128)(2,1)} collective-permute-done((bf16[64,4096]{1,0:T(8,128)(2,1)}, bf16[64,4096]{1,0:T(8,128)(2,1)}, u32[]{:S(2)}, u32[]{:S(2)}) %collective-permute-start.7) | collective-permute-done | bytes 524320 | tf_op jit(solution)/shard_map/ppermute | solution.py:525
  206.3 7.5 %all-to-all-done.4.grads = f32[8,32,512]{2,1,0:T(8,128)S(1)} async-done(((f32[8,32,512]{2,1,0:T(8,128)}), f32[8,32,512]{2,1,0:T(8,128)S(1)}, u32[]{:S(2)}, u32[]{:S(2)}) %all-to-all-start.4) | async-done | bytes 524320 | tf_op jit(solution)/shard_map/all_to_all | solution.py:49
  213.8 1.9 copy-done.2
  217.5 4.3 %shard_map.107 = (f32[8,4096]{1,0:T(8,128)S(1)}, f32[192,1]{1,0:T(8,128)S(1)}, bf16[192,128]{1,0:T(8,128)(2,1)S(1)}, f32[4,4096]{1,0:T(4,128)S(1)}) custom-call(f32[8,32,512]{2,1,0:T(8,128)S(1)} %all-to-all-done.4.grads, f32[1,4096]{1,0:T(1,128)S(1)} %bitcast.21, f32[192,4096]{1,0:T(8,128)S(1)} %copy-done.2, bf16[512,4096]{1,0:T(8,128)(2,1)} %bitcast.1.rec, ...), custom_call_target="tpu_custom_call" | custom-call | tf_op jit(solution)/shard_map/pallas_call | solution.py:577
  225.7 21.3 %all_to_all.35 = f32[128,1,256]{2,1,0:T(1,128)S(1)} all-to-all(f32[128,1,256]{2,1,0:T(1,128)S(1)} %reshape.171), channel_id=1, replica_groups=mesh['u'=16,'c'=2,'expert'=8] {'u','expert'}, dimensions={0} | all-to-all | bytes 262144 | tf_op jit(solution)/shard_map/all_to_all | solution.py:49
  247.9 7.5 %all-to-all-start.6 = ((f32[128,1,256]{2,1,0:T(1,128)}), f32[128,1,256]{2,1,0:T(1,128)}, u32[]{:S(2)}, u32[]{:S(2)}) async-start(f32[128,1,256]{2,1,0:T(1,128)} %broadcast_in_dim.84), calls=%async_computation.6 | async-start | bytes 262144 | tf_op jit(solution)/shard_map/all_to_all | solution.py:49
  259.4 7.9 %shard_map.109 = bf16[8,64,4096]{2,1,0:T(8,128)(2,1)} custom-call(s32[1]{0:T(128)} %bitcast.4.place, f32[8,32,512]{2,1,0:T(8,128)S(1)} %all-to-all-done.4.grads, f32[1,4096]{1,0:T(1,128)S(1)} %bitcast.22, f32[8,64,8]{2,1,0:T(8,128)S(1)} %pad.14.notes, bf16[64,4096]{1,0:T(8,128)(2,1)S(1)} %copy-done.8, bf16[64,4096]{1,0:T(8,128)(2,1)S(1)} %copy-done.10, ...), custom_call_target="tpu_custom_call" | custom-call | flops 25165824 | bytes 9437184 | tf_op jit(solution)/shard_map/pallas_call | solution.py:478
  267.4 3.9 %shard_map.108 = bf16[192,4096]{1,0:T(8,128)(2,1)} custom-call(f32[192,4096]{1,0:T(8,128)S(1)} %copy-done.3, f32[4,4096]{1,0:T(4,128)S(1)} %get-tuple-element.55.weighted, f32[192,1]{1,0:T(8,128)S(1)} %copy-done.7, f32[192,1]{1,0:T(8,128)S(1)} %copy-done.23, bf16[192,128]{1,0:T(8,128)(2,1)S(1)} %copy-done.25, bf16[128,4096]{1,0:T(8,128)(2,1)S(1)} %pad.13.router), custom_call_target="tpu_custom_call" | custom-call | flops 201326592 | bytes 5242880 | tf_op jit(solution)/shard_map/pallas_call | solution.py:428
  (110 shorter events, 30.2 us)
Async XLA Ops:
  0.7 56.3 %all-to-all-start = ((bf16[8,64,4096]{2,1,0:T(8,128)(2,1)}), bf16[8,64,4096]{2,1,0:T(8,128)(2,1)}, u32[]{:S(2)}, u32[]{:S(2)}) async-start(bf16[8,64,4096]{2,1,0:T(8,128)(2,1)} %bitcast.23), calls=%async_computation | async-start | bytes 8388608 | tf_op jit(solution)/shard_map/all_to_all | solution.py:49
  8.3 48.7 %copy-start.16 = (f32[4096]{0:T(1024)S(1)}, f32[4096]{0:T(1024)}, u32[]{:S(2)}) copy-start(f32[4096]{0:T(1024)} %param.12) | copy-start | bytes 49156
  57.0 23.1 %copy-start.28 = (s32[2]{0:T(128)S(1)}, s32[2]{0:T(128)}, u32[]{:S(2)}) copy-start(s32[2]{0:T(128)} %param.9) | copy-start | bytes 28
  66.0 34.6 %copy-start.5 = (f32[192,1]{1,0:T(8,128)}, f32[192,1]{1,0:T(8,128)S(1)}, u32[]{:S(2)}) copy-start(f32[192,1]{1,0:T(8,128)S(1)} %get-tuple-element.40.inverse) | copy-start | bytes 2308
  66.0 31.9 %all-to-all-start.1 = ((bf16[128,4,512]{2,1,0:T(4,128)(2,1)}), bf16[128,4,512]{2,1,0:T(4,128)(2,1)S(1)}, u32[]{:S(2)}, u32[]{:S(2)}) async-start(bf16[128,4,512]{2,1,0:T(4,128)(2,1)} %get-tuple-element.37), calls=%async_computation.1 | async-start | bytes 1048576 | tf_op jit(solution)/shard_map/all_to_all | solution.py:49
  97.9 3.8 %collective-permute-start = (bf16[128,4,512]{2,1,0:T(4,128)(2,1)S(1)}, bf16[128,4,512]{2,1,0:T(4,128)(2,1)S(1)}, u32[]{:S(2)}, u32[]{:S(2)}) collective-permute-start(bf16[128,4,512]{2,1,0:T(4,128)(2,1)S(1)} %all-to-all-done.1), channel_id=1, source_target_pairs={{0,8},{8,0},{1,9},{9,1},{2,10},{10,2},{3,11},{11,3},{4,12},{12,4},... | collective-permute-start | bytes 1572872 | tf_op jit(solution)/shard_map/ppermute | solution.py:45
  103.4 55.5 %all-to-all-start.2 = ((f32[8,40,512]{2,1,0:T(8,128)}), f32[8,40,512]{2,1,0:T(8,128)S(1)}, u32[]{:S(2)}, u32[]{:S(2)}) async-start(f32[8,40,512]{2,1,0:T(8,128)} %copy-done.4), calls=%async_computation.2 | async-start | bytes 1310720 | tf_op jit(solution)/shard_map/all_to_all | solution.py:49
  107.1 31.9 %collective-permute-start.1 = (bf16[64,4096]{1,0:T(8,128)(2,1)}, bf16[64,4096]{1,0:T(8,128)(2,1)S(1)}, u32[]{:S(2)}, u32[]{:S(2)}) collective-permute-start(bf16[64,4096]{1,0:T(8,128)(2,1)} %get-tuple-element.41), channel_id=1, source_target_pairs={{0,1},{1,2},{2,3},{3,4},{4,5},{5,6},{6,7},{7,0},{8,9},{9,10},{10,1... | collective-permute-start | bytes 1572872 | tf_op jit(solution)/shard_map/ppermute | solution.py:525
  108.6 48.7 %collective-permute-start.2 = (bf16[64,4096]{1,0:T(8,128)(2,1)}, bf16[64,4096]{1,0:T(8,128)(2,1)S(1)}, u32[]{:S(2)}, u32[]{:S(2)}) collective-permute-start(bf16[64,4096]{1,0:T(8,128)(2,1)} %get-tuple-element.42), channel_id=1, source_target_pairs={{0,2},{1,3},{2,4},{3,5},{4,6},{5,7},{6,0},{7,1},{8,10},{9,11},{10,... | collective-permute-start | bytes 1572872 | tf_op jit(solution)/shard_map/ppermute | solution.py:525
  111.0 47.1 %collective-permute-start.3 = (bf16[64,4096]{1,0:T(8,128)(2,1)}, bf16[64,4096]{1,0:T(8,128)(2,1)S(1)}, u32[]{:S(2)}, u32[]{:S(2)}) collective-permute-start(bf16[64,4096]{1,0:T(8,128)(2,1)} %get-tuple-element.43), channel_id=1, source_target_pairs={{0,3},{1,4},{2,5},{3,6},{4,7},{5,0},{6,1},{7,2},{8,11},{9,12},{10,... | collective-permute-start | bytes 1572872 | tf_op jit(solution)/shard_map/ppermute | solution.py:525
  114.6 67.0 %collective-permute-start.4 = (bf16[64,4096]{1,0:T(8,128)(2,1)}, bf16[64,4096]{1,0:T(8,128)(2,1)}, u32[]{:S(2)}, u32[]{:S(2)}) collective-permute-start(bf16[64,4096]{1,0:T(8,128)(2,1)} %get-tuple-element.46), channel_id=1, source_target_pairs={{0,4},{1,5},{2,6},{3,7},{4,0},{5,1},{6,2},{7,3},{8,12},{9,13},{10,... | collective-permute-start | bytes 1572872 | tf_op jit(solution)/shard_map/ppermute | solution.py:525
  114.9 66.7 %collective-permute-start.5 = (bf16[64,4096]{1,0:T(8,128)(2,1)}, bf16[64,4096]{1,0:T(8,128)(2,1)}, u32[]{:S(2)}, u32[]{:S(2)}) collective-permute-start(bf16[64,4096]{1,0:T(8,128)(2,1)} %get-tuple-element.47), channel_id=1, source_target_pairs={{0,5},{1,6},{2,7},{3,0},{4,1},{5,2},{6,3},{7,4},{8,13},{9,14},{10,... | collective-permute-start | bytes 1572872 | tf_op jit(solution)/shard_map/ppermute | solution.py:525
  160.5 21.1 %all-to-all-start.3 = ((f32[32,8,128]{2,1,0:T(8,128)}), f32[32,8,128]{2,1,0:T(8,128)}, u32[]{:S(2)}, u32[]{:S(2)}) async-start(f32[32,8,128]{2,1,0:T(8,128)} %copy-done.17), calls=%async_computation.3 | async-start | bytes 262144 | tf_op jit(solution)/shard_map/all_to_all | solution.py:49
  167.4 27.8 %collective-permute-start.6 = (bf16[64,4096]{1,0:T(8,128)(2,1)}, bf16[64,4096]{1,0:T(8,128)(2,1)}, u32[]{:S(2)}, u32[]{:S(2)}) collective-permute-start(bf16[64,4096]{1,0:T(8,128)(2,1)} %get-tuple-element.51), channel_id=1, source_target_pairs={{0,6},{1,7},{2,0},{3,1},{4,2},{5,3},{6,4},{7,5},{8,14},{9,15},{10,... | collective-permute-start | bytes 1572872 | tf_op jit(solution)/shard_map/ppermute | solution.py:525
  180.9 25.4 %collective-permute-start.7 = (bf16[64,4096]{1,0:T(8,128)(2,1)}, bf16[64,4096]{1,0:T(8,128)(2,1)}, u32[]{:S(2)}, u32[]{:S(2)}) collective-permute-start(bf16[64,4096]{1,0:T(8,128)(2,1)} %get-tuple-element.52), channel_id=1, source_target_pairs={{0,7},{1,0},{2,1},{3,2},{4,3},{5,4},{6,5},{7,6},{8,15},{9,8},{10,9... | collective-permute-start | bytes 1572872 | tf_op jit(solution)/shard_map/ppermute | solution.py:525
  185.1 28.7 %all-to-all-start.4 = ((f32[8,32,512]{2,1,0:T(8,128)}), f32[8,32,512]{2,1,0:T(8,128)S(1)}, u32[]{:S(2)}, u32[]{:S(2)}) async-start(f32[8,32,512]{2,1,0:T(8,128)} %copy-done.15), calls=%async_computation.4 | async-start | bytes 1048576 | tf_op jit(solution)/shard_map/all_to_all | solution.py:49
  223.1 2.4 collective-permute-start.8
  225.5 31.8 %copy-start.8 = (bf16[64,4096]{1,0:T(8,128)(2,1)S(1)}, bf16[64,4096]{1,0:T(8,128)(2,1)}, u32[]{:S(2)}) copy-start(bf16[64,4096]{1,0:T(8,128)(2,1)} %get-tuple-element.58.rest_0_) | copy-start | bytes 1572868
  225.5 31.8 %copy-start.10 = (bf16[64,4096]{1,0:T(8,128)(2,1)S(1)}, bf16[64,4096]{1,0:T(8,128)(2,1)}, u32[]{:S(2)}) copy-start(bf16[64,4096]{1,0:T(8,128)(2,1)} %copy-done.9) | copy-start | bytes 1572868
  247.9 23.4 %all-to-all-start.6 = ((f32[128,1,256]{2,1,0:T(1,128)}), f32[128,1,256]{2,1,0:T(1,128)}, u32[]{:S(2)}, u32[]{:S(2)}) async-start(f32[128,1,256]{2,1,0:T(1,128)} %broadcast_in_dim.84), calls=%async_computation.6 | async-start | bytes 262144 | tf_op jit(solution)/shard_map/all_to_all | solution.py:49
  259.4 7.9 %copy-start.3 = (f32[192,4096]{1,0:T(8,128)S(1)}, f32[192,4096]{1,0:T(8,128)}, u32[]{:S(2)}) copy-start(f32[192,4096]{1,0:T(8,128)} %get-tuple-element.36.x.summed) | copy-start | bytes 9437188
  259.4 7.9 %copy-start.7 = (f32[192,1]{1,0:T(8,128)S(1)}, f32[192,1]{1,0:T(8,128)}, u32[]{:S(2)}) copy-start(f32[192,1]{1,0:T(8,128)} %copy-done.5) | copy-start | bytes 2308
  259.4 7.9 %copy-start.23 = (f32[192,1]{1,0:T(8,128)S(1)}, f32[192,1]{1,0:T(8,128)}, u32[]{:S(2)}) copy-start(f32[192,1]{1,0:T(8,128)} %copy-done.22) | copy-start | bytes 2308
  259.4 7.9 %copy-start.25 = (bf16[192,128]{1,0:T(8,128)(2,1)S(1)}, bf16[192,128]{1,0:T(8,128)(2,1)}, u32[]{:S(2)}) copy-start(bf16[192,128]{1,0:T(8,128)(2,1)} %copy-done.24) | copy-start | bytes 147460
  (20 other events, 39.1 us)

commit v4 on v3

--- a/solution.py
+++ b/solution.py
@@ -20,6 +20,7 @@
 SMEM = pl.BlockSpec(memory_space=pltpu.SMEM)
 HBM = pl.BlockSpec(memory_space=pltpu.HBM)
 NT = (((1,), (1,)), ((), ()))
+TURNS = ((4, 1, 7), (3, 5), (2, 6))
 
 
 def iota(shape, dim):
@@ -39,6 +40,21 @@
     for k in range(1, x.shape[1] // 128):
         total = total + x[:, 128 * k : 128 * (k + 1)]
     return total
+
+
+def in_hbm(*arrays):
+    return [pltpu.with_memory_space_constraint(x, pltpu.HBM) for x in arrays]
+
+
+def copy_all(copies):
+    for copy in copies:
+        copy.start()
+    for copy in copies:
+        copy.wait()
+
+
+def to_each(source, target, sems):
+    copy_all([pltpu.make_async_copy(source, target.at[i], sems.at[i]) for i in range(target.shape[0])])
 
 
 def swap_core(x):
@@ -149,7 +165,7 @@
     )(tokens, received, slot, gates, gain)
 
 
-def pack_kernel(steps, place, x, rec, slot, turned, overlap, *rest):
+def pack_kernel(steps, place, x, rec, slot, turned, facts, overlap, *rest):
     *outs, dots, packed, sems = rest
     step = pl.program_id(0)
     rows, part = x.shape
@@ -185,15 +201,17 @@
 
     @pl.when(step == steps - 1)
     def _():
-        overlap[...] = jnp.concatenate(
-            [jnp.sum(dots[k], axis=1, keepdims=True) for k in range(2)], axis=1
-        )
+        lane = iota((rows, 128), 1)
+        known = facts[...]
+        for k in range(2):
+            known = jnp.where(lane == k, jnp.sum(dots[k], axis=1, keepdims=True), known)
+        overlap[...] = known
         for e in range(steps):
             for r in range(len(outs)):
                 leave(e, r).wait()
 
 
-def pack(place, summed, received, slot, experts, capacity):
+def pack(place, summed, received, slot, facts, experts, capacity):
     rows, width = summed.shape
     slots = received.shape[0]
     part = width // experts
@@ -207,9 +225,10 @@
             pl.BlockSpec((slots, part), lambda i: (0, i)),
             whole((rows, 2)),
             whole((2, rows)),
-        ],
-        out_specs=[whole((rows, 2))] + [HBM] * experts,
-        out_shape=[jax.ShapeDtypeStruct((rows, 2), F32)]
+            whole((rows, 128)),
+        ],
+        out_specs=[whole((rows, 128))] + [HBM] * experts,
+        out_shape=[jax.ShapeDtypeStruct((rows, 128), F32)]
         + [pltpu.HBM((capacity, width), BF16)] * experts,
         scratch_shapes=[
             pltpu.VMEM((2, rows, 128), F32),
@@ -218,7 +237,7 @@
         ],
         compiler_params=params(12),
         cost_estimate=cost(6 * rows * slots * width, 11 << 20),
-    )(place, summed, received, slot, slot.T)
+    )(place, *in_hbm(summed, received), slot, slot.T, facts)
 
 
 def lanes_of(shape, dim):
@@ -236,7 +255,7 @@
     return (source == b).astype(BF16)
 
 
-def scores_kernel(near, far, notes, offered):
+def scores_kernel(near, far, notes, offered, whole, sems):
     experts, total, columns = offered.shape
     group = experts * PAIR_DEV
     wide = 2 * group
@@ -245,19 +264,16 @@
         jnp.dot(picker(group, kind), own, preferred_element_type=F32).astype(BF16) for kind in (0, 1)
     ]
     at_record = lanes_of((group, columns), 1)[2]
-    blocks = []
-    for side in (near, far):
+    for k, side in enumerate((near, far)):
         every = side[...]
         by_query = lax.dot_general(queries, every, NT, preferred_element_type=F32)
         by_record = lax.dot_general(records, every, NT, preferred_element_type=F32)
-        blocks.append(jnp.where(at_record, by_query, by_record))
-    blocks.append(notes[...])
-    for e in range(experts):
-        for k, block in enumerate(blocks):
-            offered[e, group * k : group * k + block.shape[0], :] = block
-
-
-def totals_kernel(scale, devices, gathered, offered, kept):
+        whole[group * k : group * (k + 1)] = jnp.where(at_record, by_query, by_record)
+    whole[2 * group :] = notes[...]
+    to_each(whole, offered, sems)
+
+
+def totals_kernel(scale, gathered, offered, kept_out, kept, spread, kept_sem, sem):
     place, core = lax.axis_index("u"), lax.axis_index("c")
     experts, total, columns = gathered.shape
     group = experts * PAIR_DEV
@@ -294,6 +310,8 @@
         chosen = chosen + jnp.sum(jnp.where(hit, side, 0.0), axis=1, keepdims=True)
     kept[2 * group : 3 * group, :128] = jnp.broadcast_to(log_total, (group, 128))
     kept[2 * group : 3 * group, 128:256] = jnp.broadcast_to(positive, (group, 128))
+    saved = pltpu.make_async_copy(kept, kept_out, kept_sem)
+    saved.start()
     row_loss = log_total - chosen
 
     total_lane = jnp.sum(jnp.where(here, log_total, 0.0), axis=0, keepdims=True)
@@ -305,8 +323,10 @@
     ]
     pieces = [a + b for a, b in zip(pieces, loss_pieces)] + pieces[columns // 128 :]
     message = jnp.concatenate(pieces, axis=0)
-    for d in range(devices):
-        offered[d] = message
+    for d in range(spread.shape[0]):
+        spread[d] = message
+    copy_all([pltpu.make_async_copy(spread, offered, sem)])
+    saved.wait()
 
 
 def column_names(lane, kind, group, core):
@@ -315,7 +335,7 @@
     return block * group + (lax.rem(lane, wide) // ROWS_DEV) * PAIR_DEV + lax.rem(kind, PAIR_DEV)
 
 
-def gradient_kernel(scale, factor, heard, kept, near, far, offered, loss):
+def gradient_kernel(scale, factor, heard, kept, near, far, offered, loss, whole, sems):
     place, core = lax.axis_index("u"), lax.axis_index("c")
     experts, wide, columns = offered.shape
     group = wide // 2
@@ -348,9 +368,8 @@
             picker(group, 1, True), by_record, preferred_element_type=F32
         )
         result = result + jnp.dot(rows.astype(BF16), side[...], preferred_element_type=F32)
-    result = result * scale
-    for e in range(experts):
-        offered[e] = result
+    whole[...] = result * scale
+    to_each(whole, offered, sems)
     loss[...] = jnp.sum(losses, axis=1, keepdims=True)
 
 
@@ -367,88 +386,143 @@
     return high, mid, low
 
 
-def router_kernel(grads, gain, summed, rec, tok, slot, routes, gate, inverse, overlap, part_out, shrink_out, choice_out, weighted_out):
+def router_kernel(
+    grads, gain, summed_in, rec_in, tok_in, facts_in, part_out, state_out, weighted_out,
+    summed, rec, tok, facts, state, weighted, sems, facts_sem, out_sems
+):
     experts, _, part = grads.shape
-    rows = summed.shape[0]
-    slots = rec.shape[0]
+    rows = summed.shape[1]
+    slots = rec.shape[1]
     count = rows // SEQ
-    acc = [jnp.zeros((SEQ, 128), F32) for _ in range(count)]
+
+    def load(e):
+        cols = pl.ds(e * part, part)
+        pairs = ((summed_in, summed), (rec_in, rec), (tok_in, tok))
+        return [
+            pltpu.make_async_copy(a.at[:, cols], b.at[e], sems.at[k, e]) for k, (a, b) in enumerate(pairs)
+        ]
+
+    known = pltpu.make_async_copy(facts_in, facts, facts_sem)
+    loads = [load(e) for e in range(experts)]
+    for k in (1, 0):
+        for e in range(experts):
+            loads[e][k].start()
+    known.start()
+    for e in range(experts):
+        loads[e][2].start()
+
+    w = []
+    for e in range(experts):
+        cols = slice(part * e, part * (e + 1))
+        w.append(rows_of(grads, e, lax.axis_index("expert")) * (gain[:, cols] / SEQ))
+        weighted[:, cols] = w[e]
     on_slots = jnp.zeros((16, slots), F32)
     for e in range(experts):
-        cols = slice(part * e, part * (e + 1))
-        w = rows_of(grads, e, lax.axis_index("expert")) * (gain[:, cols] / SEQ)
-        weighted_out[:, cols] = w
-        lhs = jnp.concatenate(list(split_bf16(w)) + [jnp.zeros((count, part), BF16)], axis=0)
-        on_slots = on_slots + lax.dot_general(lhs, rec[:, cols], NT, preferred_element_type=F32)
+        lhs = jnp.concatenate(list(split_bf16(w[e])) + [jnp.zeros((count, part), BF16)], axis=0)
+        loads[e][1].wait()
+        on_slots = on_slots + lax.dot_general(lhs, rec[e], NT, preferred_element_type=F32)
+    acc = [jnp.zeros((SEQ, 128), F32) for _ in range(count)]
+    for e in range(experts):
+        loads[e][0].wait()
         for q in range(count):
-            acc[q] = acc[q] + fold(summed[SEQ * q : SEQ * (q + 1), cols] * w[q : q + 1, :])
+            acc[q] = acc[q] + fold(summed[e, SEQ * q : SEQ * (q + 1), :] * w[e][q : q + 1, :])
+    known.wait()
     on_slots = on_slots[0:count] + on_slots[count : 2 * count] + on_slots[2 * count : 3 * count]
     ids = iota((SEQ, slots), 1)
     lanes = iota((SEQ, 128), 1)
     choices = []
     for q in range(count):
         at = slice(SEQ * q, SEQ * (q + 1))
-        inv = inverse[at]
+        fact = facts[at, :]
+        inv = fact[:, 2:3]
         shrink = inv * inv * inv * (jnp.sum(acc[q], axis=1, keepdims=True) / (experts * part))
-        shrink_out[at] = shrink
         row = on_slots[q : q + 1, :]
         grad_gate = []
         for k in range(2):
-            along = jnp.sum(jnp.where(slot[at, k : k + 1] == ids, row, 0.0), axis=1, keepdims=True)
-            grad_gate.append(inv * along - shrink * overlap[at, k : k + 1])
-        gates = [gate[at, k : k + 1] for k in range(2)]
+            spot = fact[:, 5 + k : 6 + k].astype(I32)
+            along = jnp.sum(jnp.where(spot == ids, row, 0.0), axis=1, keepdims=True)
+            grad_gate.append(inv * along - shrink * fact[:, k : k + 1])
+        gates = [fact[:, 3 + k : 4 + k] for k in range(2)]
         mean = gates[0] * grad_gate[0] + gates[1] * grad_gate[1]
         choice = jnp.zeros((SEQ, 128), F32)
         for k in range(2):
             chosen = gates[k] * (grad_gate[k] - mean)
-            choice = choice + jnp.where(routes[at, k : k + 1] == lanes, chosen, 0.0)
+            route = fact[:, 7 + k : 8 + k].astype(I32)
+            choice = choice + jnp.where(route == lanes, chosen, 0.0)
         choices.append(choice)
-    choice = jnp.concatenate(choices, axis=0)
-    choice_out[...] = choice.astype(BF16)
-    lhs = jnp.transpose(choice)[:experts].astype(BF16)
-    for k in range(experts):
-        cols = slice(part * k, part * (k + 1))
-        part_out[:, cols] = jnp.dot(lhs, tok[:, cols], preferred_element_type=F32)
-
-
-def token_kernel(summed, weighted, inverse, shrink, choice, router, out):
+        choice = jnp.where(lanes == experts, inv, choice)
+        state[at] = jnp.where(lanes == experts + 1, shrink, choice)
+    saved = [
+        pltpu.make_async_copy(state, state_out, out_sems.at[0]),
+        pltpu.make_async_copy(weighted, weighted_out, out_sems.at[1]),
+    ]
+    for copy in saved:
+        copy.start()
+    lhs = jnp.transpose(jnp.concatenate(choices, axis=0))[:experts].astype(BF16)
+    tiles = part // 128
+    for e in range(experts):
+        loads[e][2].wait()
+        block = jnp.dot(lhs, tok[e], preferred_element_type=F32)
+        for k in range(tiles):
+            at = experts * (tiles * e + k)
+            part_out[at : at + experts, :] = block[:, 128 * k : 128 * (k + 1)]
+    for copy in saved:
+        copy.wait()
+
+
+def token_kernel(experts, summed, weighted, state, router, out):
     rows = summed.shape[0]
-    through = jnp.dot(choice[...], router[...], preferred_element_type=F32)
+    known = state[...]
+    choice = jnp.where(iota(known.shape, 1) < experts, known, 0.0).astype(BF16)
+    through = jnp.dot(choice, router[...], preferred_element_type=F32)
     for q in range(rows // SEQ):
         at = slice(SEQ * q, SEQ * (q + 1))
-        x = inverse[at] * weighted[q : q + 1, :] - shrink[at] * summed[at]
+        inverse, shrink = known[at, experts : experts + 1], known[at, experts + 1 : experts + 2]
+        x = inverse * weighted[q : q + 1, :] - shrink * summed[at]
         out[at] = (x + through[SEQ * q : SEQ * (q + 1)]).astype(BF16)
 
 
-def token_rows(summed, weighted, inverse, shrink, choice, router, parts):
+def token_rows(summed, weighted, state, router, experts):
     rows, width = summed.shape
-    part = width // parts
-    whole = lambda shape: pl.BlockSpec(shape, lambda i: (0, 0))
+    part = width // experts
     split = lambda count: pl.BlockSpec((count, part), lambda i: (0, i))
     return pl.pallas_call(
-        token_kernel,
-        grid=(parts,),
-        in_specs=[split(rows), split(weighted.shape[0]), whole((rows, 1)), whole((rows, 1)), whole((rows, 128)), split(128)],
+        functools.partial(token_kernel, experts),
+        grid=(experts,),
+        in_specs=[
+            split(rows),
+            split(weighted.shape[0]),
+            pl.BlockSpec((rows, 128), lambda i: (0, 0)),
+            split(128),
+        ],
         out_specs=split(rows),
         out_shape=jax.ShapeDtypeStruct((rows, width), BF16),
         compiler_params=params(10),
         cost_estimate=cost(2 * rows * 128 * width, 5 << 20),
-    )(summed, weighted, inverse, shrink, choice, router)
+    )(*in_hbm(summed, weighted, state), router)
 
 
 def expert_kernel(place, grads, gain, notes, *rest):
-    experts = len(rest) - 1
-    backs, out = rest[:experts], rest[experts]
+    *sources, out, backs, sems = rest
+    experts = len(sources)
     _, _, part = grads.shape
     step = pl.program_id(0)
     source = lax.rem(place[0] + experts - step, experts)
     gate, inv, seq = notes[0, :, 0:1], notes[0, :, 1:2], notes[0, :, 2:3]
     capacity = gate.shape[0]
+    loads = [pltpu.make_async_copy(sources[r], backs.at[r], sems.at[r]) for r in range(experts)]
+
+    @pl.when(step == 0)
+    def _():
+        for load in loads:
+            load.start()
+
     for r in range(experts):
 
         @pl.when(step == r)
         def _():
-            back = backs[r]
+            loads[r].wait()
+            back = backs.at[r]
             acc = jnp.zeros((capacity, 128), F32)
             rows = []
             for e in range(experts):
@@ -485,13 +559,17 @@
                 whole((1, width)),
                 pl.BlockSpec((1, capacity, notes.shape[2]), source),
             ]
-            + [whole((capacity, width))] * experts,
+            + [HBM] * experts,
             out_specs=pl.BlockSpec((1, capacity, width), source),
+            scratch_shapes=[
+                pltpu.VMEM((experts, capacity, width), BF16),
+                pltpu.SemaphoreType.DMA((experts,)),
+            ],
         ),
         out_shape=jax.ShapeDtypeStruct((experts, capacity, width), BF16),
-        compiler_params=params(24),
+        compiler_params=params(16),
         cost_estimate=cost(12 * experts * capacity * width, 9 << 20),
-    )(place, grads, gain, notes, *backs)
+    )(place, grads, gain, notes, *in_hbm(*backs))
 
 
 def shards(tokens, routes, positives, expert_out, router, norm_gain, loss_scale):
@@ -520,11 +598,24 @@
 
     summed, offered, inverse = forward(tokens, received, slot, gates, gain, experts, outer)
     near = exchange(offered, ("u", "expert"))
-    overlap, *outgoing = pack(mine_at, summed, received, slot, experts, capacity)
-    backs = [outgoing[0]] + [
-        lax.ppermute(outgoing[r], "expert", [(i, (i + r) % experts) for i in range(experts)])
-        for r in range(1, experts)
-    ]
+    facts = jnp.concatenate(
+        [jnp.zeros((rows, 2), F32), inverse, gates, slot.astype(F32), routes.astype(F32)], axis=1
+    )
+    facts = jnp.pad(facts, ((0, 0), (0, 128 - facts.shape[1])))
+    facts, *backs = pack(mine_at, summed, received, slot, facts, experts, capacity)
+
+    def move(after, turns):
+        after, *ready = lax.optimization_barrier((after, *[backs[r] for r in turns]))
+        for r, x in zip(turns, ready):
+            backs[r] = lax.ppermute(x, "expert", [(i, (i + r) % experts) for i in range(experts)])
+        return after
+
+    def landed(value, turns):
+        value, *done = lax.optimization_barrier((value, *[backs[r] for r in turns]))
+        for r, x in zip(turns, done):
+            backs[r] = x
+        return value
+
     slot_ids = jnp.arange(slots, dtype=I32)[None, :]
     picks = [slot[:, k : k + 1] == slot_ids for k in range(2)]
     gate_slot = jnp.sum(
@@ -537,66 +628,82 @@
     notes = jnp.stack([gate_slot, inverse_slot, sequence_slot, spread_positive])
     notes = jnp.pad(notes, ((0, 4), (0, 0)))
 
-    near, overlap = lax.optimization_barrier((near, overlap))
+    near, facts = lax.optimization_barrier((near, facts))
     far = swap_core(near)
     near, far = near.reshape(columns, part), far.reshape(columns, part)
     offered = pl.pallas_call(
         scores_kernel,
         in_specs=[VMEM] * 3,
-        out_specs=VMEM,
-        out_shape=jax.ShapeDtypeStruct((experts, 2 * group + 8, columns), F32),
+        out_specs=HBM,
+        out_shape=pltpu.HBM((experts, 2 * group + 8, columns), F32),
+        scratch_shapes=[pltpu.VMEM((2 * group + 8, columns), F32), pltpu.SemaphoreType.DMA((experts,))],
         compiler_params=params(2),
     )(near, far, notes)
+    offered = move(offered, TURNS[0])
     gathered = exchange(offered, "expert")
-    gathered, *backs[1:4] = lax.optimization_barrier((gathered, *backs[1:4]))
+    devices = outer * CORES
     offered, kept = pl.pallas_call(
-        functools.partial(totals_kernel, scale, outer * CORES),
+        functools.partial(totals_kernel, scale),
         in_specs=[VMEM],
-        out_specs=[VMEM] * 2,
-        out_shape=[
-            jax.ShapeDtypeStruct((outer * CORES, 8, 128), F32),
-            jax.ShapeDtypeStruct((3 * group, columns), F32),
+        out_specs=[HBM] * 2,
+        out_shape=[pltpu.HBM((devices, 8, 128), F32), pltpu.HBM((3 * group, columns), F32)],
+        scratch_shapes=[
+            pltpu.VMEM((3 * group, columns), F32),
+            pltpu.VMEM((devices, 8, 128), F32),
+            pltpu.SemaphoreType.DMA(()),
+            pltpu.SemaphoreType.DMA(()),
         ],
         compiler_params=params(2),
     )(gathered)
+    offered = move(offered, TURNS[1])
     heard = exchange(offered, ("u", "c"))
-    heard, *backs[4:6] = lax.optimization_barrier((heard, *backs[4:6]))
+    heard = landed(heard, TURNS[0])
     offered, loss = pl.pallas_call(
         functools.partial(gradient_kernel, scale),
         in_specs=[SMEM] + [VMEM] * 4,
-        out_specs=[VMEM, VMEM],
-        out_shape=[
-            jax.ShapeDtypeStruct((experts, 2 * group, part), F32),
-            jax.ShapeDtypeStruct((1, 1), F32),
-        ],
+        out_specs=[HBM, VMEM],
+        out_shape=[pltpu.HBM((experts, 2 * group, part), F32), jax.ShapeDtypeStruct((1, 1), F32)],
+        scratch_shapes=[pltpu.VMEM((2 * group, part), F32), pltpu.SemaphoreType.DMA((experts,))],
         compiler_params=params(2),
     )((loss_scale / pairs)[None], heard, kept, near, far)
+    offered = move(offered, TURNS[2])
     grads = exchange(offered, "expert")
-    grads, *backs[6:8] = lax.optimization_barrier((grads, *backs[6:8]))
-
-    router_part, shrink, choice, weighted = pl.pallas_call(
+    grads = landed(grads, TURNS[1])
+
+    router_part, state, weighted = pl.pallas_call(
         router_kernel,
-        in_specs=[VMEM] * 10,
-        out_specs=[VMEM] * 4,
+        in_specs=[VMEM] * 2 + [HBM] * 4,
+        out_specs=[VMEM, HBM, HBM],
         out_shape=[
-            jax.ShapeDtypeStruct((experts, width), F32),
-            jax.ShapeDtypeStruct((rows, 1), F32),
-            jax.ShapeDtypeStruct((rows, 128), BF16),
-            jax.ShapeDtypeStruct((rows // SEQ, width), F32),
-        ],
-        compiler_params=params(6),
-    )(grads, gain, summed, received, tokens, slot, routes, gates, inverse, overlap)
+            jax.ShapeDtypeStruct((width * experts // 128, 128), F32),
+            pltpu.HBM((rows, 128), F32),
+            pltpu.HBM((rows // SEQ, width), F32),
+        ],
+        scratch_shapes=[
+            pltpu.VMEM((experts, rows, part), F32),
+            pltpu.VMEM((experts, slots, part), BF16),
+            pltpu.VMEM((experts, rows, part), BF16),
+            pltpu.VMEM((rows, 128), F32),
+            pltpu.VMEM((rows, 128), F32),
+            pltpu.VMEM((rows // SEQ, width), F32),
+            pltpu.SemaphoreType.DMA((3, experts)),
+            pltpu.SemaphoreType.DMA(()),
+            pltpu.SemaphoreType.DMA((2,)),
+        ],
+        compiler_params=params(16),
+    )(grads, gain, *in_hbm(summed, received, tokens, facts))
     router_part = router_part + swap_core(router_part)
-    router_part = exchange(router_part.reshape(wide, 1, -1), ("u", "expert"))
-    router_sum = jnp.sum(router_part, axis=0)
-    router_all = exchange(jnp.broadcast_to(router_sum[None], (wide,) + router_sum.shape), ("u", "expert"))
-    router_grad = router_all.reshape(experts, width).T
-
-    turned = jnp.pad(router.T, ((0, 128 - experts), (0, 0)))
-    token_grad = token_rows(summed, weighted, inverse, shrink, choice, turned, experts)
+    router_part = exchange(router_part.reshape(wide, -1, 128), ("u", "expert"))
     held = lax.dynamic_slice_in_dim(gathered[:, 2 * group : 2 * group + 3], mine * capacity, capacity, axis=2)
     held = jnp.pad(jnp.transpose(held, (0, 2, 1)), ((0, 0), (0, 0), (0, 5)))
     expert_grad = expert_rows(mine_at, grads, gain, held, backs)
+    router_part, expert_grad = lax.optimization_barrier((router_part, expert_grad))
+    router_sum = jnp.sum(router_part, axis=0)
+    turned = jnp.pad(router.T, ((0, 128 - experts), (0, 0)))
+    token_grad = token_rows(summed, weighted, state, turned, experts)
+    router_all = exchange(jnp.broadcast_to(router_sum[None], (wide,) + router_sum.shape), ("u", "expert"))
+    router_all, token_grad = lax.optimization_barrier((router_all, token_grad))
+    router_grad = router_all.reshape(-1, experts, 128).transpose(1, 0, 2).reshape(experts, width).T
     return token_grad, expert_grad.reshape(1, 1, experts, capacity, width), router_grad, loss[0, 0] / pairs
 
 

time: 276 us -> 239 us (0.87)
  waiting for transfers between devices: 110 us -> 78.4 us
  starting transfers between devices: 77.3 us -> 101 us
  blocking collectives: 21.3 us -> 0 us
  local copies, waits for them, and re-layouts: 20.4 us -> 6.14 us
  Pallas kernels: 38.1 us -> 44.9 us
    ppermute x7, waiting for transfers between devices: 50.1 us -> 13.1 us  [move(): lax.ppermute(x, 'expert', [(i, (i + r) % experts) for i in range(experts)])]
    all_to_all x6 -> x7, starting transfers between devices: 49.7 us -> 76.9 us  [exchange(): return lax.all_to_all(x, axes, split_axis=0, concat_axis=0, tiled=True)]
    all_to_all x1 -> x0, blocking collectives: 21.3 us -> none  [exchange(): return lax.all_to_all(x, axes, split_axis=0, concat_axis=0, tiled=True)]
    unnamed x60 -> x24, local copies, waits for them, and re-layouts: 16.1 us -> 3.26 us
    pallas_call x4, Pallas kernels: 9.24 us -> 16 us  [the longest x1 6.97 us: shards(): pl.pallas_call(router_kernel, in_specs=[VMEM] * 2 + [HBM] * 4, out_specs=...]
    ppermute x7, starting transfers between devices: 23.9 us -> 17.4 us  [move(): lax.ppermute(x, 'expert', [(i, (i + r) % experts) for i in range(experts)])]
    all_to_all x6 -> x7, waiting for transfers between devices: 58 us -> 63.7 us  [exchange(): return lax.all_to_all(x, axes, split_axis=0, concat_axis=0, tiled=True)]
    ppermute x2, starting transfers between devices: 3.73 us -> 7.14 us  [swap_core(): return lax.ppermute(x, 'c', [(0, 1), (1, 0)])]
  transfers between devices with their start and end apart: 15 -> 16, of which waited for: 8 -> 9; matrix products, arithmetic and copies ran while one was open for 2% -> 2% of each run, Pallas kernels for 9% -> 14%
where the time goes in v4:
time: 239 us; the launch traced here: 238 us
  starting transfers between devices  101 us (42%)
  waiting for transfers between devices  78.4 us (33%)
  Pallas kernels  44.9 us (19%)
  local copies, waits for them, and re-layouts  6.14 us (3%)
  between operations  3.46 us (1%)
  other arithmetic  2.83 us (1%)
    all_to_all x7, starting transfers between devices, exchange(): return lax.all_to_all(x, axes, split_axis=0, concat_axis=0, tiled=True)  76.9 us
    all_to_all x7, waiting for transfers between devices, exchange(): return lax.all_to_all(x, axes, split_axis=0, concat_axis=0, tiled=True)  63.7 us
    ppermute x7, starting transfers between devices, move(): lax.ppermute(x, 'expert', [(i, (i + r) % experts) for i in range(experts)])  17.4 us
    ppermute x7, waiting for transfers between devices, move(): lax.ppermute(x, 'expert', [(i, (i + r) % experts) for i in range(experts)])  13.1 us
    pallas_call x1, Pallas kernels, pack(): pl.pallas_call(functools.partial(pack_kernel, experts), grid=(experts,),...  10.7 us
    pallas_call x1, Pallas kernels, forward(): pl.pallas_call(functools.partial(forward_kernel, experts, outer), grid=(e...  8.95 us
    pallas_call x1, Pallas kernels, expert_rows(): pl.pallas_call(expert_kernel, grid_spec=pltpu.PrefetchScalarGridSpec(num_...  7.22 us
    ppermute x2, starting transfers between devices, swap_core(): return lax.ppermute(x, 'c', [(0, 1), (1, 0)])  7.14 us
  transfers between devices with their start and end apart: 16, of which 9 were waited for; matrix products, arithmetic and copies ran while one was open for 2% of the time, Pallas kernels for 14%

profile of v4, /device:TPU:1, one launch (start us, length us, event | category | flops | bytes accessed | tf_op | source)
XLA Modules:
  0.0 237.8 jit_solution(5897734821991412257)
XLA Ops:
  0.7 7.6 %all-to-all-start = ((bf16[8,64,4096]{2,1,0:T(8,128)(2,1)}), bf16[8,64,4096]{2,1,0:T(8,128)(2,1)}, u32[]{:S(2)}, u32[]{:S(2)}) async-start(bf16[8,64,4096]{2,1,0:T(8,128)(2,1)} %bitcast.30), calls=%async_computation | async-start | bytes 8388608 | tf_op jit(solution)/shard_map/all_to_all | solution.py:65
  9.7 47.3 %all-to-all-done = bf16[8,64,4096]{2,1,0:T(8,128)(2,1)} async-done(((bf16[8,64,4096]{2,1,0:T(8,128)(2,1)}), bf16[8,64,4096]{2,1,0:T(8,128)(2,1)}, u32[]{:S(2)}, u32[]{:S(2)}) %all-to-all-start) | async-done | bytes 4194336 | tf_op jit(solution)/shard_map/all_to_all | solution.py:65
  57.0 9.0 %shard_map.102 = (f32[192,4096]{1,0:T(8,128)}, bf16[128,4,512]{2,1,0:T(4,128)(2,1)}, f32[192,1]{1,0:T(8,128)S(1)}) custom-call(bf16[192,4096]{1,0:T(8,128)(2,1)S(1)} %copy-done, bf16[512,4096]{1,0:T(8,128)(2,1)} %bitcast.2.rec.rec_in, s32[192,2]{1,0:T(8,128)S(1)} %get-tuple-element.98.slot, f32[192,2]{1,0:T(8,128)S(1)} %exponential_divide_fusion.gate, ...), custom_call_target="tpu_custom_call" | custom-call | flops 1610612736 | bytes 10485760 | tf_op jit(solution)/shard_map/pallas_call | solution.py:140
  66.0 14.1 %all-to-all-start.1 = ((bf16[128,4,512]{2,1,0:T(4,128)(2,1)}), bf16[128,4,512]{2,1,0:T(4,128)(2,1)S(1)}, u32[]{:S(2)}, u32[]{:S(2)}) async-start(bf16[128,4,512]{2,1,0:T(4,128)(2,1)} %get-tuple-element.46), calls=%async_computation.1 | async-start | bytes 1048576 | tf_op jit(solution)/shard_map/all_to_all | solution.py:65
  82.4 10.7 %shard_map.103 = (f32[192,128]{1,0:T(8,128)S(1)}, bf16[64,4096]{1,0:T(8,128)(2,1)}, bf16[64,4096]{1,0:T(8,128)(2,1)}, bf16[64,4096]{1,0:T(8,128)(2,1)}, bf16[64,...) custom-call(s32[1]{0:T(128)} %bitcast.4.place, ...), custom_call_target="tpu_custom_call" | custom-call | flops 2415919104 | bytes 11534336 | tf_op jit(solution)/shard_map/pallas_call | solution.py:219
  93.7 4.1 %all-to-all-done.1 = bf16[128,4,512]{2,1,0:T(4,128)(2,1)S(1)} async-done(((bf16[128,4,512]{2,1,0:T(4,128)(2,1)}), bf16[128,4,512]{2,1,0:T(4,128)(2,1)S(1)}, u32[]{:S(2)}, u32[]{:S(2)}) %all-to-all-start.1) | async-done | bytes 524320 | tf_op jit(solution)/shard_map/all_to_all | solution.py:65
  103.5 3.7 %all-to-all-start.2 = ((f32[8,40,512]{2,1,0:T(8,128)}), f32[8,40,512]{2,1,0:T(8,128)S(1)}, u32[]{:S(2)}, u32[]{:S(2)}) async-start(f32[8,40,512]{2,1,0:T(8,128)} %shard_map.104), calls=%async_computation.2 | async-start | bytes 1310720 | tf_op jit(solution)/shard_map/all_to_all | solution.py:65
  107.2 3.0 %collective-permute-start.1 = (bf16[64,4096]{1,0:T(8,128)(2,1)}, bf16[64,4096]{1,0:T(8,128)(2,1)S(1)}, u32[]{:S(2)}, u32[]{:S(2)}) collective-permute-start(bf16[64,4096]{1,0:T(8,128)(2,1)} %get-tuple-element.59), channel_id=1, source_target_pairs={{0,4},{1,5},{2,6},{3,7},{4,0},{5,1},{6,2},{7,3},{8,12},{9,13},{10,... | collective-permute-start | bytes 1572872 | tf_op jit(solution)/shard_map/ppermute | solution.py:610
  111.3 3.9 %collective-permute-start.3 = (bf16[64,4096]{1,0:T(8,128)(2,1)}, bf16[64,4096]{1,0:T(8,128)(2,1)S(1)}, u32[]{:S(2)}, u32[]{:S(2)}) collective-permute-start(bf16[64,4096]{1,0:T(8,128)(2,1)} %get-tuple-element.61), channel_id=1, source_target_pairs={{0,7},{1,0},{2,1},{3,2},{4,3},{5,4},{6,5},{7,6},{8,15},{9,8},{10,9... | collective-permute-start | bytes 1572872 | tf_op jit(solution)/shard_map/ppermute | solution.py:610
  115.2 2.6 %all-to-all-done.2.gathered = f32[8,40,512]{2,1,0:T(8,128)S(1)} async-done(((f32[8,40,512]{2,1,0:T(8,128)}), f32[8,40,512]{2,1,0:T(8,128)S(1)}, u32[]{:S(2)}, u32[]{:S(2)}) %all-to-all-start.2) | async-done | bytes 655392 | tf_op jit(solution)/shard_map/all_to_all | solution.py:65
  118.8 6.8 %all-to-all-start.3 = ((f32[32,8,128]{2,1,0:T(8,128)}), f32[32,8,128]{2,1,0:T(8,128)S(1)}, u32[]{:S(2)}, u32[]{:S(2)}) async-start(f32[32,8,128]{2,1,0:T(8,128)} %get-tuple-element.58), calls=%async_computation.3 | async-start | bytes 262144 | tf_op jit(solution)/shard_map/all_to_all | solution.py:65
  130.2 13.1 %collective-permute-done.2.rest_1_ = bf16[64,4096]{1,0:T(8,128)(2,1)S(1)} collective-permute-done((bf16[64,4096]{1,0:T(8,128)(2,1)}, bf16[64,4096]{1,0:T(8,128)(2,1)S(1)}, u32[]{:S(2)}, u32[]{:S(2)}) %collective-permute-start.2) | collective-permute-done | bytes 524320 | tf_op jit(solution)/shard_map/ppermute | solution.py:610
  146.3 4.4 %all-to-all-start.4 = ((f32[8,32,512]{2,1,0:T(8,128)}), f32[8,32,512]{2,1,0:T(8,128)S(1)}, u32[]{:S(2)}, u32[]{:S(2)}) async-start(f32[8,32,512]{2,1,0:T(8,128)} %get-tuple-element.67), calls=%async_computation.4 | async-start | bytes 1048576 | tf_op jit(solution)/shard_map/all_to_all | solution.py:65
  150.7 3.0 %collective-permute-start.7 = (bf16[64,4096]{1,0:T(8,128)(2,1)}, bf16[64,4096]{1,0:T(8,128)(2,1)S(1)}, u32[]{:S(2)}, u32[]{:S(2)}) collective-permute-start(bf16[64,4096]{1,0:T(8,128)(2,1)} %get-tuple-element.75), channel_id=1, source_target_pairs={{0,2},{1,3},{2,4},{3,5},{4,6},{5,7},{6,0},{7,1},{8,10},{9,11},{10,... | collective-permute-start | bytes 1572872 | tf_op jit(solution)/shard_map/ppermute | solution.py:610
  153.6 2.4 %collective-permute-start.8 = (bf16[64,4096]{1,0:T(8,128)(2,1)}, bf16[64,4096]{1,0:T(8,128)(2,1)}, u32[]{:S(2)}, u32[]{:S(2)}) collective-permute-start(bf16[64,4096]{1,0:T(8,128)(2,1)} %get-tuple-element.79), channel_id=1, source_target_pairs={{0,6},{1,7},{2,0},{3,1},{4,2},{5,3},{6,4},{7,5},{8,14},{9,15},{10,... | collective-permute-start | bytes 1572872 | tf_op jit(solution)/shard_map/ppermute | solution.py:610
  156.1 3.4 %all-to-all-done.4.grads = f32[8,32,512]{2,1,0:T(8,128)S(1)} async-done(((f32[8,32,512]{2,1,0:T(8,128)}), f32[8,32,512]{2,1,0:T(8,128)S(1)}, u32[]{:S(2)}, u32[]{:S(2)}) %all-to-all-start.4) | async-done | bytes 524320 | tf_op jit(solution)/shard_map/all_to_all | solution.py:65
  159.5 7.0 %shard_map.107 = (f32[256,128]{1,0:T(8,128)S(1)}, f32[192,128]{1,0:T(8,128)}, f32[4,4096]{1,0:T(4,128)}) custom-call(f32[8,32,512]{2,1,0:T(8,128)S(1)} %all-to-all-done.4.grads, f32[1,4096]{1,0:T(1,128)S(1)} %bitcast.28, f32[192,4096]{1,0:T(8,128)} %get-tuple-element.47.x.summed_in.summed, bf16[512,4096]{1,0:T(8,128)(2,1)} %bitcast.2.rec.rec_in, ...), custom_call_target="tpu_custom_call" | custom-call | tf_op jit(solution)/shard_map/pallas_call | solution.py:673
  166.5 4.8 %collective-permute-start.6 = (f32[256,128]{1,0:T(8,128)S(1)}, f32[256,128]{1,0:T(8,128)S(1)}, u32[]{:S(2)}, u32[]{:S(2)}) collective-permute-start(f32[256,128]{1,0:T(8,128)S(1)} %get-tuple-element.72), channel_id=1, source_target_pairs={{0,8},{8,0},{1,9},{9,1},{2,10},{10,2},{3,11},{11,3},{4,12},{12,4},... | collective-permute-start | bytes 393224 | tf_op jit(solution)/shard_map/ppermute | solution.py:61
  173.0 29.8 %all-to-all-start.5 = ((f32[128,2,128]{2,1,0:T(2,128)}), f32[128,2,128]{2,1,0:T(2,128)S(1)}, u32[]{:S(2)}, u32[]{:S(2)}) async-start(f32[128,2,128]{2,1,0:T(2,128)} %bitcast.11), calls=%async_computation.5 | async-start | bytes 262144 | tf_op jit(solution)/shard_map/all_to_all | solution.py:65
  203.9 7.2 %shard_map.108 = bf16[8,64,4096]{2,1,0:T(8,128)(2,1)} custom-call(s32[1]{0:T(128)} %bitcast.4.place, f32[8,32,512]{2,1,0:T(8,128)S(1)} %all-to-all-done.4.grads, f32[1,4096]{1,0:T(1,128)S(1)} %bitcast.29, f32[8,64,8]{2,1,0:T(8,128)S(1)} %pad.18.notes, bf16[64,4096]{1,0:T(8,128)(2,1)} %get-tuple-element.73.rest_0_, bf16[64,4096]{1,0:T(8,128)(2,1)} %copy-done.5, ...), custom_call_target="tpu_custom_call" | custom-call | flops 25165824 | bytes 9437184 | tf_op jit(solution)/shard_map/pallas_call | solution.py:552
  211.2 2.5 %all-to-all-done.5 = f32[128,2,128]{2,1,0:T(2,128)S(1)} async-done(((f32[128,2,128]{2,1,0:T(2,128)}), f32[128,2,128]{2,1,0:T(2,128)S(1)}, u32[]{:S(2)}, u32[]{:S(2)}) %all-to-all-start.5) | async-done | bytes 131104 | tf_op jit(solution)/shard_map/all_to_all | solution.py:65
  214.5 10.6 %all-to-all-start.6 = ((f32[128,2,128]{2,1,0:T(2,128)}), f32[128,2,128]{2,1,0:T(2,128)S(1)}, u32[]{:S(2)}, u32[]{:S(2)}) async-start(f32[128,2,128]{2,1,0:T(2,128)} %broadcast_in_dim.88), calls=%async_computation.6 | async-start | bytes 262144 | tf_op jit(solution)/shard_map/all_to_all | solution.py:65
  225.9 6.5 %shard_map.109 = bf16[192,4096]{1,0:T(8,128)(2,1)} custom-call(f32[192,4096]{1,0:T(8,128)} %get-tuple-element.47.x.summed_in.summed, f32[4,4096]{1,0:T(4,128)} %get-tuple-element.82.weighted, f32[192,128]{1,0:T(8,128)} %get-tuple-element.83.state, bf16[128,4096]{1,0:T(8,128)(2,1)S(1)} %pad.19.router), custom_call_target="tpu_custom_call" | custom-call | flops 201326592 | bytes 5242880 | tf_op jit(solution)/shard_map/pallas_call | solution.py:489
  232.3 3.7 %all-to-all-done.6 = f32[128,2,128]{2,1,0:T(2,128)S(1)} async-done(((f32[128,2,128]{2,1,0:T(2,128)}), f32[128,2,128]{2,1,0:T(2,128)S(1)}, u32[]{:S(2)}, u32[]{:S(2)}) %all-to-all-start.6) | async-done | bytes 131104 | tf_op jit(solution)/shard_map/all_to_all | solution.py:65
  (76 shorter events, 23.2 us)
Async XLA Ops:
  0.6 7.7 %copy-start.9 = (s32[192,2]{0,1:T(2,128)S(1)}, s32[192,2]{0,1:T(2,128)}, u32[]{:S(2)}) copy-start(s32[192,2]{0,1:T(2,128)} %param.8) | copy-start | bytes 4612
  0.6 7.8 %copy-start = (bf16[192,4096]{1,0:T(8,128)(2,1)S(1)}, bf16[192,4096]{1,0:T(8,128)(2,1)}, u32[]{:S(2)}) copy-start(bf16[192,4096]{1,0:T(8,128)(2,1)} %tok_in.1) | copy-start | bytes 4718596
  0.7 7.8 %copy-start.8 = (bf16[4096,8]{0,1:T(8,128)(2,1)S(1)}, bf16[4096,8]{0,1:T(8,128)(2,1)}, u32[]{:S(2)}) copy-start(bf16[4096,8]{0,1:T(8,128)(2,1)} %param.11) | copy-start | bytes 196612
  0.7 56.3 %all-to-all-start = ((bf16[8,64,4096]{2,1,0:T(8,128)(2,1)}), bf16[8,64,4096]{2,1,0:T(8,128)(2,1)}, u32[]{:S(2)}, u32[]{:S(2)}) async-start(bf16[8,64,4096]{2,1,0:T(8,128)(2,1)} %bitcast.30), calls=%async_computation | async-start | bytes 8388608 | tf_op jit(solution)/shard_map/all_to_all | solution.py:65
  8.3 48.7 %copy-start.1 = (f32[4096]{0:T(1024)S(1)}, f32[4096]{0:T(1024)}, u32[]{:S(2)}) copy-start(f32[4096]{0:T(1024)} %param.12) | copy-start | bytes 49156
  57.0 23.2 %copy-start.10 = (s32[2]{0:T(128)S(1)}, s32[2]{0:T(128)}, u32[]{:S(2)}) copy-start(s32[2]{0:T(128)} %param.9) | copy-start | bytes 28
  66.0 31.9 %all-to-all-start.1 = ((bf16[128,4,512]{2,1,0:T(4,128)(2,1)}), bf16[128,4,512]{2,1,0:T(4,128)(2,1)S(1)}, u32[]{:S(2)}, u32[]{:S(2)}) async-start(bf16[128,4,512]{2,1,0:T(4,128)(2,1)} %get-tuple-element.46), calls=%async_computation.1 | async-start | bytes 1048576 | tf_op jit(solution)/shard_map/all_to_all | solution.py:65
  97.9 3.8 %collective-permute-start = (bf16[128,4,512]{2,1,0:T(4,128)(2,1)S(1)}, bf16[128,4,512]{2,1,0:T(4,128)(2,1)S(1)}, u32[]{:S(2)}, u32[]{:S(2)}) collective-permute-start(bf16[128,4,512]{2,1,0:T(4,128)(2,1)S(1)} %all-to-all-done.1), channel_id=1, source_target_pairs={{0,8},{8,0},{1,9},{9,1},{2,10},{10,2},{3,11},{11,3},{4,12},{12,4},... | collective-permute-start | bytes 1572872 | tf_op jit(solution)/shard_map/ppermute | solution.py:61
  103.5 14.4 %all-to-all-start.2 = ((f32[8,40,512]{2,1,0:T(8,128)}), f32[8,40,512]{2,1,0:T(8,128)S(1)}, u32[]{:S(2)}, u32[]{:S(2)}) async-start(f32[8,40,512]{2,1,0:T(8,128)} %shard_map.104), calls=%async_computation.2 | async-start | bytes 1310720 | tf_op jit(solution)/shard_map/all_to_all | solution.py:65
  107.2 23.0 %collective-permute-start.1 = (bf16[64,4096]{1,0:T(8,128)(2,1)}, bf16[64,4096]{1,0:T(8,128)(2,1)S(1)}, u32[]{:S(2)}, u32[]{:S(2)}) collective-permute-start(bf16[64,4096]{1,0:T(8,128)(2,1)} %get-tuple-element.59), channel_id=1, source_target_pairs={{0,4},{1,5},{2,6},{3,7},{4,0},{5,1},{6,2},{7,3},{8,12},{9,13},{10,... | collective-permute-start | bytes 1572872 | tf_op jit(solution)/shard_map/ppermute | solution.py:610
  110.1 33.2 %collective-permute-start.2 = (bf16[64,4096]{1,0:T(8,128)(2,1)}, bf16[64,4096]{1,0:T(8,128)(2,1)S(1)}, u32[]{:S(2)}, u32[]{:S(2)}) collective-permute-start(bf16[64,4096]{1,0:T(8,128)(2,1)} %get-tuple-element.60), channel_id=1, source_target_pairs={{0,1},{1,2},{2,3},{3,4},{4,5},{5,6},{6,7},{7,0},{8,9},{9,10},{10,1... | collective-permute-start | bytes 1572872 | tf_op jit(solution)/shard_map/ppermute | solution.py:610
  111.3 32.0 %collective-permute-start.3 = (bf16[64,4096]{1,0:T(8,128)(2,1)}, bf16[64,4096]{1,0:T(8,128)(2,1)S(1)}, u32[]{:S(2)}, u32[]{:S(2)}) collective-permute-start(bf16[64,4096]{1,0:T(8,128)(2,1)} %get-tuple-element.61), channel_id=1, source_target_pairs={{0,7},{1,0},{2,1},{3,2},{4,3},{5,4},{6,5},{7,6},{8,15},{9,8},{10,9... | collective-permute-start | bytes 1572872 | tf_op jit(solution)/shard_map/ppermute | solution.py:610
  118.8 24.5 %all-to-all-start.3 = ((f32[32,8,128]{2,1,0:T(8,128)}), f32[32,8,128]{2,1,0:T(8,128)S(1)}, u32[]{:S(2)}, u32[]{:S(2)}) async-start(f32[32,8,128]{2,1,0:T(8,128)} %get-tuple-element.58), calls=%async_computation.3 | async-start | bytes 262144 | tf_op jit(solution)/shard_map/all_to_all | solution.py:65
  125.6 30.5 %collective-permute-start.4 = (bf16[64,4096]{1,0:T(8,128)(2,1)}, bf16[64,4096]{1,0:T(8,128)(2,1)}, u32[]{:S(2)}, u32[]{:S(2)}) collective-permute-start(bf16[64,4096]{1,0:T(8,128)(2,1)} %get-tuple-element.68), channel_id=1, source_target_pairs={{0,3},{1,4},{2,5},{3,6},{4,7},{5,0},{6,1},{7,2},{8,11},{9,12},{10,... | collective-permute-start | bytes 1572872 | tf_op jit(solution)/shard_map/ppermute | solution.py:610
  127.7 28.4 %collective-permute-start.5 = (bf16[64,4096]{1,0:T(8,128)(2,1)}, bf16[64,4096]{1,0:T(8,128)(2,1)}, u32[]{:S(2)}, u32[]{:S(2)}) collective-permute-start(bf16[64,4096]{1,0:T(8,128)(2,1)} %get-tuple-element.69), channel_id=1, source_target_pairs={{0,5},{1,6},{2,7},{3,0},{4,1},{5,2},{6,3},{7,4},{8,13},{9,14},{10,... | collective-permute-start | bytes 1572872 | tf_op jit(solution)/shard_map/ppermute | solution.py:610
  130.2 36.3 %copy-start.4 = (bf16[64,4096]{1,0:T(8,128)(2,1)}, bf16[64,4096]{1,0:T(8,128)(2,1)S(1)}, u32[]{:S(2)}) copy-start(bf16[64,4096]{1,0:T(8,128)(2,1)S(1)} %collective-permute-done.1.rest_4_) | copy-start | bytes 1572868
  143.3 23.2 %copy-start.5 = (bf16[64,4096]{1,0:T(8,128)(2,1)}, bf16[64,4096]{1,0:T(8,128)(2,1)S(1)}, u32[]{:S(2)}) copy-start(bf16[64,4096]{1,0:T(8,128)(2,1)S(1)} %collective-permute-done.2.rest_1_) | copy-start | bytes 1572868
  143.3 23.2 %copy-start.6 = (bf16[64,4096]{1,0:T(8,128)(2,1)}, bf16[64,4096]{1,0:T(8,128)(2,1)S(1)}, u32[]{:S(2)}) copy-start(bf16[64,4096]{1,0:T(8,128)(2,1)S(1)} %collective-permute-done.3.rest_7_) | copy-start | bytes 1572868
  146.3 13.2 %all-to-all-start.4 = ((f32[8,32,512]{2,1,0:T(8,128)}), f32[8,32,512]{2,1,0:T(8,128)S(1)}, u32[]{:S(2)}, u32[]{:S(2)}) async-start(f32[8,32,512]{2,1,0:T(8,128)} %get-tuple-element.67), calls=%async_computation.4 | async-start | bytes 1048576 | tf_op jit(solution)/shard_map/all_to_all | solution.py:65
  150.7 52.5 %collective-permute-start.7 = (bf16[64,4096]{1,0:T(8,128)(2,1)}, bf16[64,4096]{1,0:T(8,128)(2,1)S(1)}, u32[]{:S(2)}, u32[]{:S(2)}) collective-permute-start(bf16[64,4096]{1,0:T(8,128)(2,1)} %get-tuple-element.75), channel_id=1, source_target_pairs={{0,2},{1,3},{2,4},{3,5},{4,6},{5,7},{6,0},{7,1},{8,10},{9,11},{10,... | collective-permute-start | bytes 1572872 | tf_op jit(solution)/shard_map/ppermute | solution.py:610
  153.6 49.5 %collective-permute-start.8 = (bf16[64,4096]{1,0:T(8,128)(2,1)}, bf16[64,4096]{1,0:T(8,128)(2,1)}, u32[]{:S(2)}, u32[]{:S(2)}) collective-permute-start(bf16[64,4096]{1,0:T(8,128)(2,1)} %get-tuple-element.79), channel_id=1, source_target_pairs={{0,6},{1,7},{2,0},{3,1},{4,2},{5,3},{6,4},{7,5},{8,14},{9,15},{10,... | collective-permute-start | bytes 1572872 | tf_op jit(solution)/shard_map/ppermute | solution.py:610
  166.5 5.8 %collective-permute-start.6 = (f32[256,128]{1,0:T(8,128)S(1)}, f32[256,128]{1,0:T(8,128)S(1)}, u32[]{:S(2)}, u32[]{:S(2)}) collective-permute-start(f32[256,128]{1,0:T(8,128)S(1)} %get-tuple-element.72), channel_id=1, source_target_pairs={{0,8},{8,0},{1,9},{9,1},{2,10},{10,2},{3,11},{11,3},{4,12},{12,4},... | collective-permute-start | bytes 393224 | tf_op jit(solution)/shard_map/ppermute | solution.py:61
  173.0 40.7 %all-to-all-start.5 = ((f32[128,2,128]{2,1,0:T(2,128)}), f32[128,2,128]{2,1,0:T(2,128)S(1)}, u32[]{:S(2)}, u32[]{:S(2)}) async-start(f32[128,2,128]{2,1,0:T(2,128)} %bitcast.11), calls=%async_computation.5 | async-start | bytes 262144 | tf_op jit(solution)/shard_map/all_to_all | solution.py:65
  214.5 21.5 %all-to-all-start.6 = ((f32[128,2,128]{2,1,0:T(2,128)}), f32[128,2,128]{2,1,0:T(2,128)S(1)}, u32[]{:S(2)}, u32[]{:S(2)}) async-start(f32[128,2,128]{2,1,0:T(2,128)} %broadcast_in_dim.88), calls=%async_computation.6 | async-start | bytes 262144 | tf_op jit(solution)/shard_map/all_to_all | solution.py:65
  (3 other events, 2.4 us)

commit v5 on v4

--- a/solution.py
+++ b/solution.py
@@ -20,7 +20,7 @@
 SMEM = pl.BlockSpec(memory_space=pltpu.SMEM)
 HBM = pl.BlockSpec(memory_space=pltpu.HBM)
 NT = (((1,), (1,)), ((), ()))
-TURNS = ((4, 1, 7), (3, 5), (2, 6))
+TURNS = ((1, 7), (4, 3), (5, 2, 6))
 
 
 def iota(shape, dim):
@@ -63,6 +63,10 @@
 
 def exchange(x, axes):
     return lax.all_to_all(x, axes, split_axis=0, concat_axis=0, tiled=True)
+
+
+def spread(x, axes, size):
+    return exchange(jnp.broadcast_to(x[None], (size,) + x.shape), axes)
 
 
 def routing(tokens, routes, router, experts, capacity):
@@ -165,24 +169,66 @@
     )(tokens, received, slot, gates, gain)
 
 
-def pack_kernel(steps, place, x, rec, slot, turned, facts, overlap, *rest):
-    *outs, dots, packed, sems = rest
+def pack_kernel(turns, place, x, turned, *rest):
+    *outs, packed, sems = rest
+    step, steps = pl.program_id(0), packed.shape[0]
+    rows, part = x.shape
+    capacity = outs[0].shape[0]
+    slots = steps * capacity
+
+    def leave(e, i):
+        start = pl.multiple_of(e * part, part)
+        return pltpu.make_async_copy(
+            packed.at[e, pl.ds(i * capacity, capacity)], outs[i].at[:, pl.ds(start, part)], sems.at[e, i]
+        )
+
+    first = jnp.concatenate([iota((capacity, rows), 0) + r * capacity for r in turns], axis=0)
+    target = lax.rem(first + place[0] * capacity, slots)
+    spot = ((turned[0:1, :] == target) | (turned[1:2, :] == target)).astype(BF16)
+    for k in range(part // 256):
+        cols = slice(256 * k, 256 * (k + 1))
+        packed[step, :, cols] = jnp.dot(
+            spot, x[:, cols].astype(BF16), preferred_element_type=F32
+        ).astype(BF16)
+    for i in range(len(outs)):
+        leave(step, i).start()
+
+    @pl.when(step == steps - 1)
+    def _():
+        for e in range(steps):
+            for i in range(len(outs)):
+                leave(e, i).wait()
+
+
+def pack(place, summed, turned, turns, experts, capacity):
+    rows, width = summed.shape
+    part = width // experts
+    return pl.pallas_call(
+        functools.partial(pack_kernel, turns),
+        grid=(experts,),
+        in_specs=[
+            SMEM,
+            pl.BlockSpec((rows, part), lambda i: (0, i)),
+            pl.BlockSpec((2, rows), lambda i: (0, 0)),
+        ],
+        out_specs=[HBM] * len(turns),
+        out_shape=[pltpu.HBM((capacity, width), BF16)] * len(turns),
+        scratch_shapes=[
+            pltpu.VMEM((experts, len(turns) * capacity, part), BF16),
+            pltpu.SemaphoreType.DMA((experts, len(turns))),
+        ],
+        compiler_params=params(12),
+        cost_estimate=cost(2 * rows * len(turns) * capacity * width, 5 << 20),
+    )(place, *in_hbm(summed), turned)
+
+
+def overlap_kernel(steps, x, rec, slot, facts, out, dots):
     step = pl.program_id(0)
     rows, part = x.shape
-
-    def leave(e, r):
-        start = pl.multiple_of(e * part, part)
-        return pltpu.make_async_copy(
-            packed.at[e, pl.ds(r * capacity, capacity)], outs[r].at[:, pl.ds(start, part)], sems.at[e, r]
-        )
-
     slots = rec.shape[0]
-    capacity = slots // len(outs)
     ids = iota((rows, slots), 1)
     first = (slot[:, 0:1] == ids).astype(BF16)
     second = (slot[:, 1:2] == ids).astype(BF16)
-    target = lax.rem(iota((slots, rows), 0) + place[0] * capacity, slots)
-    spot = ((turned[0:1, :] == target) | (turned[1:2, :] == target)).astype(BF16)
 
     @pl.when(step == 0)
     def _():
@@ -190,14 +236,9 @@
 
     for k in range(part // 256):
         cols = slice(256 * k, 256 * (k + 1))
-        value = x[:, cols]
-        block = rec[:, cols]
+        value, block = x[:, cols], rec[:, cols]
         dots[0] += fold(value * jnp.dot(first, block, preferred_element_type=F32))
         dots[1] += fold(value * jnp.dot(second, block, preferred_element_type=F32))
-        moved = jnp.dot(spot, value.astype(BF16), preferred_element_type=F32).astype(BF16)
-        packed[step, :, cols] = moved
-    for r in range(len(outs)):
-        leave(step, r).start()
 
     @pl.when(step == steps - 1)
     def _():
@@ -205,39 +246,29 @@
         known = facts[...]
         for k in range(2):
             known = jnp.where(lane == k, jnp.sum(dots[k], axis=1, keepdims=True), known)
-        overlap[...] = known
-        for e in range(steps):
-            for r in range(len(outs)):
-                leave(e, r).wait()
-
-
-def pack(place, summed, received, slot, facts, experts, capacity):
+        out[...] = known
+
+
+def overlaps(summed, received, slot, facts, experts):
     rows, width = summed.shape
     slots = received.shape[0]
     part = width // experts
-    whole = lambda shape: pl.BlockSpec(shape, lambda i: (0,) * len(shape))
+    whole = lambda shape: pl.BlockSpec(shape, lambda i: (0, 0))
     return pl.pallas_call(
-        functools.partial(pack_kernel, experts),
+        functools.partial(overlap_kernel, experts),
         grid=(experts,),
         in_specs=[
-            SMEM,
             pl.BlockSpec((rows, part), lambda i: (0, i)),
             pl.BlockSpec((slots, part), lambda i: (0, i)),
             whole((rows, 2)),
-            whole((2, rows)),
             whole((rows, 128)),
         ],
-        out_specs=[whole((rows, 128))] + [HBM] * experts,
-        out_shape=[jax.ShapeDtypeStruct((rows, 128), F32)]
-        + [pltpu.HBM((capacity, width), BF16)] * experts,
-        scratch_shapes=[
-            pltpu.VMEM((2, rows, 128), F32),
-            pltpu.VMEM((experts, slots, part), BF16),
-            pltpu.SemaphoreType.DMA((experts, experts)),
-        ],
+        out_specs=whole((rows, 128)),
+        out_shape=jax.ShapeDtypeStruct((rows, 128), F32),
+        scratch_shapes=[pltpu.VMEM((2, rows, 128), F32)],
         compiler_params=params(12),
-        cost_estimate=cost(6 * rows * slots * width, 11 << 20),
-    )(place, *in_hbm(summed, received), slot, slot.T, facts)
+        cost_estimate=cost(4 * rows * slots * width, 7 << 20),
+    )(*in_hbm(summed, received), slot, facts)
 
 
 def lanes_of(shape, dim):
@@ -368,14 +399,17 @@
             picker(group, 1, True), by_record, preferred_element_type=F32
         )
         result = result + jnp.dot(rows.astype(BF16), side[...], preferred_element_type=F32)
-    whole[...] = result * scale
+    whole[...] = (result * scale).astype(BF16)
     to_each(whole, offered, sems)
     loss[...] = jnp.sum(losses, axis=1, keepdims=True)
 
 
 def rows_of(grads, e, index):
-    tile = grads[e, pl.ds(pl.multiple_of((index // 2) * 8, 8), 8), :]
-    return jnp.where(lax.rem(index, 2) == 0, tile[:ROWS_DEV], tile[ROWS_DEV:])
+    tile = grads[e, pl.ds(pl.multiple_of((index // 4) * 16, 16), 16), :].astype(F32)
+    piece = lax.rem(index, 4)
+    quarters = [tile[ROWS_DEV * k : ROWS_DEV * (k + 1)] for k in range(4)]
+    half = jnp.where(piece < 2, quarters[0], quarters[2]), jnp.where(piece < 2, quarters[1], quarters[3])
+    return jnp.where(lax.rem(piece, 2) == 0, half[0], half[1])
 
 
 def split_bf16(x):
@@ -602,13 +636,15 @@
         [jnp.zeros((rows, 2), F32), inverse, gates, slot.astype(F32), routes.astype(F32)], axis=1
     )
     facts = jnp.pad(facts, ((0, 0), (0, 128 - facts.shape[1])))
-    facts, *backs = pack(mine_at, summed, received, slot, facts, experts, capacity)
+    backs = list(pack(mine_at, summed, slot.T, tuple(range(experts)), experts, capacity))
 
     def move(after, turns):
         after, *ready = lax.optimization_barrier((after, *[backs[r] for r in turns]))
         for r, x in zip(turns, ready):
             backs[r] = lax.ppermute(x, "expert", [(i, (i + r) % experts) for i in range(experts)])
         return after
+
+    move(slot, TURNS[0])
 
     def landed(value, turns):
         value, *done = lax.optimization_barrier((value, *[backs[r] for r in turns]))
@@ -628,7 +664,7 @@
     notes = jnp.stack([gate_slot, inverse_slot, sequence_slot, spread_positive])
     notes = jnp.pad(notes, ((0, 4), (0, 0)))
 
-    near, facts = lax.optimization_barrier((near, facts))
+    near, *backs = lax.optimization_barrier((near, *backs))
     far = swap_core(near)
     near, far = near.reshape(columns, part), far.reshape(columns, part)
     offered = pl.pallas_call(
@@ -639,7 +675,7 @@
         scratch_shapes=[pltpu.VMEM((2 * group + 8, columns), F32), pltpu.SemaphoreType.DMA((experts,))],
         compiler_params=params(2),
     )(near, far, notes)
-    offered = move(offered, TURNS[0])
+    offered = move(offered, TURNS[1] + TURNS[2])
     gathered = exchange(offered, "expert")
     devices = outer * CORES
     offered, kept = pl.pallas_call(
@@ -655,20 +691,21 @@
         ],
         compiler_params=params(2),
     )(gathered)
-    offered = move(offered, TURNS[1])
     heard = exchange(offered, ("u", "c"))
-    heard = landed(heard, TURNS[0])
+    heard = landed(heard, TURNS[1])
+    offered, facts = lax.optimization_barrier((offered, facts))
+    facts = overlaps(summed, received, slot, facts, experts)
+    heard, facts = lax.optimization_barrier((heard, facts))
     offered, loss = pl.pallas_call(
         functools.partial(gradient_kernel, scale),
         in_specs=[SMEM] + [VMEM] * 4,
         out_specs=[HBM, VMEM],
-        out_shape=[pltpu.HBM((experts, 2 * group, part), F32), jax.ShapeDtypeStruct((1, 1), F32)],
-        scratch_shapes=[pltpu.VMEM((2 * group, part), F32), pltpu.SemaphoreType.DMA((experts,))],
+        out_shape=[pltpu.HBM((experts, 2 * group, part), BF16), jax.ShapeDtypeStruct((1, 1), F32)],
+        scratch_shapes=[pltpu.VMEM((2 * group, part), BF16), pltpu.SemaphoreType.DMA((experts,))],
         compiler_params=params(2),
     )((loss_scale / pairs)[None], heard, kept, near, far)
-    offered = move(offered, TURNS[2])
     grads = exchange(offered, "expert")
-    grads = landed(grads, TURNS[1])
+    grads = landed(grads, TURNS[2])
 
     router_part, state, weighted = pl.pallas_call(
         router_kernel,
@@ -692,16 +729,17 @@
         ],
         compiler_params=params(16),
     )(grads, gain, *in_hbm(summed, received, tokens, facts))
-    router_part = router_part + swap_core(router_part)
-    router_part = exchange(router_part.reshape(wide, -1, 128), ("u", "expert"))
+    router_part = exchange(router_part.reshape(outer, -1, 128), "u")
+    router_part = jnp.sum(router_part, axis=0)
+    router_part = spread(router_part, ("c", "expert"), CORES * experts)
     held = lax.dynamic_slice_in_dim(gathered[:, 2 * group : 2 * group + 3], mine * capacity, capacity, axis=2)
     held = jnp.pad(jnp.transpose(held, (0, 2, 1)), ((0, 0), (0, 0), (0, 5)))
     expert_grad = expert_rows(mine_at, grads, gain, held, backs)
+    turned = jnp.pad(router.T, ((0, 128 - experts), (0, 0)))
     router_part, expert_grad = lax.optimization_barrier((router_part, expert_grad))
-    router_sum = jnp.sum(router_part, axis=0)
-    turned = jnp.pad(router.T, ((0, 128 - experts), (0, 0)))
+    router_part = jnp.sum(router_part, axis=0)
     token_grad = token_rows(summed, weighted, state, turned, experts)
-    router_all = exchange(jnp.broadcast_to(router_sum[None], (wide,) + router_sum.shape), ("u", "expert"))
+    router_all = spread(router_part, "u", outer)
     router_all, token_grad = lax.optimization_barrier((router_all, token_grad))
     router_grad = router_all.reshape(-1, experts, 128).transpose(1, 0, 2).reshape(experts, width).T
     return token_grad, expert_grad.reshape(1, 1, experts, capacity, width), router_grad, loss[0, 0] / pairs

time: 239 us -> 248 us (1.038)
  starting transfers between devices: 101 us -> 84.8 us
  blocking collectives: 0 us -> 13.7 us
  waiting for transfers between devices: 78.4 us -> 84.7 us
  Pallas kernels: 44.9 us -> 49.5 us
    all_to_all x0 -> x1, blocking collectives: none -> 13.7 us  [exchange(): return lax.all_to_all(x, axes, split_axis=0, concat_axis=0, tiled=True)]
    all_to_all x7, starting transfers between devices: 76.9 us -> 66 us  [exchange(): return lax.all_to_all(x, axes, split_axis=0, concat_axis=0, tiled=True)]
    all_to_all x7, waiting for transfers between devices: 63.7 us -> 71.2 us  [exchange(): return lax.all_to_all(x, axes, split_axis=0, concat_axis=0, tiled=True)]
    ppermute x2 -> x1, starting transfers between devices: 7.14 us -> 1.38 us  [swap_core(): return lax.ppermute(x, 'c', [(0, 1), (1, 0)])]
    pallas_call x1 -> x2, Pallas kernels: 10.7 us -> 15.3 us  [the longest x1 7.7 us: overlaps(): pl.pallas_call(functools.partial(overlap_kernel, experts), grid=(experts,...]
  transfers between devices with their start and end apart: 16 -> 15, of which waited for: 9 -> 8; matrix products, arithmetic and copies ran while one was open for 2% -> 3% of each run, Pallas kernels for 14% -> 13%
where the time goes in v5:
time: 248 us; the launch traced here: 246 us
  starting transfers between devices  84.8 us (34%)
  waiting for transfers between devices  84.7 us (34%)
  Pallas kernels  49.5 us (20%)
  blocking collectives  13.7 us (6%)
  local copies, waits for them, and re-layouts  7.56 us (3%)
  between operations  3.44 us (1%)
    all_to_all x7, waiting for transfers between devices, exchange(): return lax.all_to_all(x, axes, split_axis=0, concat_axis=0, tiled=True)  71.2 us
    all_to_all x7, starting transfers between devices, exchange(): return lax.all_to_all(x, axes, split_axis=0, concat_axis=0, tiled=True)  66 us
    ppermute x7, starting transfers between devices, move(): lax.ppermute(x, 'expert', [(i, (i + r) % experts) for i in range(experts)])  17.4 us
    all_to_all x1, blocking collectives, exchange(): return lax.all_to_all(x, axes, split_axis=0, concat_axis=0, tiled=True)  13.7 us
    ppermute x7, waiting for transfers between devices, move(): lax.ppermute(x, 'expert', [(i, (i + r) % experts) for i in range(experts)])  12.8 us
    pallas_call x1, Pallas kernels, forward(): pl.pallas_call(functools.partial(forward_kernel, experts, outer), grid=(e...  8.96 us
    pallas_call x1, Pallas kernels, overlaps(): pl.pallas_call(functools.partial(overlap_kernel, experts), grid=(experts,...  7.7 us
    pallas_call x1, Pallas kernels, pack(): pl.pallas_call(functools.partial(pack_kernel, turns), grid=(experts,), in...  7.65 us
  transfers between devices with their start and end apart: 15, of which 8 were waited for; matrix products, arithmetic and copies ran while one was open for 3% of the time, Pallas kernels for 13%

profile of v5, /device:TPU:1, one launch (start us, length us, event | category | flops | bytes accessed | tf_op | source)
XLA Modules:
  0.0 246.5 jit_solution(10713853660937072021)
XLA Ops:
  0.7 7.6 %all-to-all-start = ((bf16[8,64,4096]{2,1,0:T(8,128)(2,1)}), bf16[8,64,4096]{2,1,0:T(8,128)(2,1)}, u32[]{:S(2)}, u32[]{:S(2)}) async-start(bf16[8,64,4096]{2,1,0:T(8,128)(2,1)} %bitcast.31), calls=%async_computation | async-start | bytes 8388608 | tf_op jit(solution)/shard_map/all_to_all | solution.py:65
  9.7 47.3 %all-to-all-done = bf16[8,64,4096]{2,1,0:T(8,128)(2,1)} async-done(((bf16[8,64,4096]{2,1,0:T(8,128)(2,1)}), bf16[8,64,4096]{2,1,0:T(8,128)(2,1)}, u32[]{:S(2)}, u32[]{:S(2)}) %all-to-all-start) | async-done | bytes 4194336 | tf_op jit(solution)/shard_map/all_to_all | solution.py:65
  57.0 9.0 %shard_map.102 = (f32[192,4096]{1,0:T(8,128)}, bf16[128,4,512]{2,1,0:T(4,128)(2,1)}, f32[192,1]{1,0:T(8,128)S(1)}) custom-call(bf16[192,4096]{1,0:T(8,128)(2,1)S(1)} %copy-done, bf16[512,4096]{1,0:T(8,128)(2,1)} %bitcast.2.rec.rec_in, s32[192,2]{1,0:T(8,128)S(1)} %get-tuple-element.112.slot, f32[192,2]{1,0:T(8,128)S(1)} %exponential_divide_fusion.gate, ...), custom_call_target="tpu_custom_call" | custom-call | flops 1610612736 | bytes 10485760 | tf_op jit(solution)/shard_map/pallas_call | solution.py:144
  66.0 14.1 %all-to-all-start.1 = ((bf16[128,4,512]{2,1,0:T(4,128)(2,1)}), bf16[128,4,512]{2,1,0:T(4,128)(2,1)S(1)}, u32[]{:S(2)}, u32[]{:S(2)}) async-start(bf16[128,4,512]{2,1,0:T(4,128)(2,1)} %get-tuple-element.53), calls=%async_computation.1 | async-start | bytes 1048576 | tf_op jit(solution)/shard_map/all_to_all | solution.py:65
  80.1 7.6 %shard_map.103 = (bf16[64,4096]{1,0:T(8,128)(2,1)}, bf16[64,4096]{1,0:T(8,128)(2,1)}, bf16[64,4096]{1,0:T(8,128)(2,1)}, bf16[64,4096]{1,0:T(8,128)(2,1)}, bf16[6...) custom-call(s32[1]{0:T(128)} %bitcast.4.place, ...), custom_call_target="tpu_custom_call" | custom-call | flops 805306368 | bytes 5242880 | tf_op jit(solution)/shard_map/pallas_call | solution.py:206
  88.4 4.5 %collective-permute-start.1 = (bf16[64,4096]{1,0:T(8,128)(2,1)}, bf16[64,4096]{1,0:T(8,128)(2,1)S(1)}, u32[]{:S(2)}, u32[]{:S(2)}) collective-permute-start(bf16[64,4096]{1,0:T(8,128)(2,1)} %get-tuple-element.64), channel_id=1, source_target_pairs={{0,7},{1,0},{2,1},{3,2},{4,3},{5,4},{6,5},{7,6},{8,15},{9,8},{10,9... | collective-permute-start | bytes 1572872 | tf_op jit(solution)/shard_map/ppermute | solution.py:644
  94.8 11.7 %collective-permute-done.rest_1_ = bf16[64,4096]{1,0:T(8,128)(2,1)S(1)} collective-permute-done((bf16[64,4096]{1,0:T(8,128)(2,1)}, bf16[64,4096]{1,0:T(8,128)(2,1)S(1)}, u32[]{:S(2)}, u32[]{:S(2)}) %collective-permute-start) | collective-permute-done | bytes 524320 | tf_op jit(solution)/shard_map/ppermute | solution.py:644
  112.4 4.7 %all-to-all-start.2 = ((f32[8,40,512]{2,1,0:T(8,128)}), f32[8,40,512]{2,1,0:T(8,128)S(1)}, u32[]{:S(2)}, u32[]{:S(2)}) async-start(f32[8,40,512]{2,1,0:T(8,128)} %shard_map.104), calls=%async_computation.2 | async-start | bytes 1310720 | tf_op jit(solution)/shard_map/all_to_all | solution.py:65
  117.2 3.0 %collective-permute-start.3 = (bf16[64,4096]{1,0:T(8,128)(2,1)}, bf16[64,4096]{1,0:T(8,128)(2,1)S(1)}, u32[]{:S(2)}, u32[]{:S(2)}) collective-permute-start(bf16[64,4096]{1,0:T(8,128)(2,1)} %get-tuple-element.74), channel_id=1, source_target_pairs={{0,4},{1,5},{2,6},{3,7},{4,0},{5,1},{6,2},{7,3},{8,12},{9,13},{10,... | collective-permute-start | bytes 1572872 | tf_op jit(solution)/shard_map/ppermute | solution.py:644
  120.1 2.4 collective-permute-start.4
  124.0 2.7 %collective-permute-start.6 = (bf16[64,4096]{1,0:T(8,128)(2,1)}, bf16[64,4096]{1,0:T(8,128)(2,1)}, u32[]{:S(2)}, u32[]{:S(2)}) collective-permute-start(bf16[64,4096]{1,0:T(8,128)(2,1)} %get-tuple-element.82), channel_id=1, source_target_pairs={{0,2},{1,3},{2,4},{3,5},{4,6},{5,7},{6,0},{7,1},{8,10},{9,11},{10,... | collective-permute-start | bytes 1572872 | tf_op jit(solution)/shard_map/ppermute | solution.py:644
  126.7 2.7 %collective-permute-start.7 = (bf16[64,4096]{1,0:T(8,128)(2,1)}, bf16[64,4096]{1,0:T(8,128)(2,1)}, u32[]{:S(2)}, u32[]{:S(2)}) collective-permute-start(bf16[64,4096]{1,0:T(8,128)(2,1)} %get-tuple-element.83), channel_id=1, source_target_pairs={{0,6},{1,7},{2,0},{3,1},{4,2},{5,3},{6,4},{7,5},{8,14},{9,15},{10,... | collective-permute-start | bytes 1572872 | tf_op jit(solution)/shard_map/ppermute | solution.py:644
  130.4 9.7 %all-to-all-start.3 = ((f32[32,8,128]{2,1,0:T(8,128)}), f32[32,8,128]{2,1,0:T(8,128)S(1)}, u32[]{:S(2)}, u32[]{:S(2)}) async-start(f32[32,8,128]{2,1,0:T(8,128)} %get-tuple-element.73), calls=%async_computation.3 | async-start | bytes 262144 | tf_op jit(solution)/shard_map/all_to_all | solution.py:65
  142.6 7.7 %shard_map.106.facts_in = f32[192,128]{1,0:T(8,128)S(1)} custom-call(f32[192,4096]{1,0:T(8,128)} %get-tuple-element.54.x.summed_in.summed, bf16[512,4096]{1,0:T(8,128)(2,1)} %bitcast.2.rec.rec_in, s32[192,2]{1,0:T(8,128)S(1)} %get-tuple-element.112.slot, f32[192,128]{1,0:T(8,128)S(1)} %pad.17.facts), custom_call_target="tpu_custom_call" | custom-call | flops 1610612736 | bytes 7340032 | tf_op jit(solution)/shard_map/pallas_call | solution.py:257
  152.1 15.8 %all-to-all-done.3.heard = f32[32,8,128]{2,1,0:T(8,128)S(1)} async-done(((f32[32,8,128]{2,1,0:T(8,128)}), f32[32,8,128]{2,1,0:T(8,128)S(1)}, u32[]{:S(2)}, u32[]{:S(2)}) %all-to-all-start.3) | async-done | bytes 131104 | tf_op jit(solution)/shard_map/all_to_all | solution.py:65
  167.9 1.8 shard_map.107
  169.7 19.5 %all-to-all-start.4 = ((bf16[8,32,512]{2,1,0:T(8,128)(2,1)}), bf16[8,32,512]{2,1,0:T(8,128)(2,1)S(1)}, u32[]{:S(2)}, u32[]{:S(2)}) async-start(bf16[8,32,512]{2,1,0:T(8,128)(2,1)} %get-tuple-element.80), calls=%async_computation.4 | async-start | bytes 524288 | tf_op jit(solution)/shard_map/all_to_all | solution.py:65
  189.2 7.6 %all-to-all-done.4.grads = bf16[8,32,512]{2,1,0:T(8,128)(2,1)S(1)} async-done(((bf16[8,32,512]{2,1,0:T(8,128)(2,1)}), bf16[8,32,512]{2,1,0:T(8,128)(2,1)S(1)}, u32[]{:S(2)}, u32[]{:S(2)}) %all-to-all-start.4) | async-done | bytes 262176 | tf_op jit(solution)/shard_map/all_to_all | solution.py:65
  196.8 7.0 %shard_map.108 = (f32[256,128]{1,0:T(8,128)S(1)}, f32[192,128]{1,0:T(8,128)}, f32[4,4096]{1,0:T(4,128)}) custom-call(bf16[8,32,512]{2,1,0:T(8,128)(2,1)S(1)} %all-to-all-done.4.grads, f32[1,4096]{1,0:T(1,128)S(1)} %bitcast.28, f32[192,4096]{1,0:T(8,128)} %get-tuple-element.54.x.summed_in.summed, bf16[512,4096]{1,0:T(8,128)(2,1)} %bitcast.2.rec.rec_in, ...), custom_call_target="tpu_custom_call" | custom-call | tf_op jit(solution)/shard_map/pallas_call | solution.py:710
  203.8 13.7 %all_to_all.40 = f32[16,16,128]{2,1,0:T(8,128)S(1)} all-to-all(f32[16,16,128]{2,1,0:T(8,128)S(1)} %bitcast.30), channel_id=1, replica_groups=mesh['u'=16,'c'=2,'expert'=8] {'u'}, dimensions={0} | all-to-all | bytes 262144 | tf_op jit(solution)/shard_map/all_to_all | solution.py:65
  218.2 6.9 %all-to-all-start.6 = ((f32[16,16,128]{2,1,0:T(8,128)}), f32[16,16,128]{2,1,0:T(8,128)S(1)}, u32[]{:S(2)}, u32[]{:S(2)}) async-start(f32[16,16,128]{2,1,0:T(8,128)} %broadcast_in_dim.94), calls=%async_computation.6 | async-start | bytes 262144 | tf_op jit(solution)/shard_map/all_to_all | solution.py:65
  225.4 7.3 %shard_map.109 = bf16[8,64,4096]{2,1,0:T(8,128)(2,1)} custom-call(s32[1]{0:T(128)} %bitcast.4.place, bf16[8,32,512]{2,1,0:T(8,128)(2,1)S(1)} %all-to-all-done.4.grads, f32[1,4096]{1,0:T(1,128)S(1)} %bitcast.29, f32[8,64,8]{2,1,0:T(8,128)S(1)} %pad.18.notes, bf16[64,4096]{1,0:T(8,128)(2,1)} %get-tuple-element.87.rest_0_, bf16[64,4096]{1,0:T(8,128)(2,1)} %copy-done.4, ...), custom_call_target="tpu_custom_call" | custom-call | flops 25165824 | bytes 9437184 | tf_op jit(solution)/shard_map/pallas_call | solution.py:586
  233.7 3.5 %all-to-all-start.7 = ((f32[16,16,128]{2,1,0:T(8,128)}), f32[16,16,128]{2,1,0:T(8,128)S(1)}, u32[]{:S(2)}, u32[]{:S(2)}) async-start(f32[16,16,128]{2,1,0:T(8,128)} %broadcast_in_dim.95), calls=%async_computation.7 | async-start | bytes 262144 | tf_op jit(solution)/shard_map/all_to_all | solution.py:65
  237.9 6.5 %shard_map.110 = bf16[192,4096]{1,0:T(8,128)(2,1)} custom-call(f32[192,4096]{1,0:T(8,128)} %get-tuple-element.54.x.summed_in.summed, f32[4,4096]{1,0:T(4,128)} %get-tuple-element.96.weighted, f32[192,128]{1,0:T(8,128)} %get-tuple-element.97.state, bf16[128,4096]{1,0:T(8,128)(2,1)S(1)} %pad.19.router), custom_call_target="tpu_custom_call" | custom-call | flops 201326592 | bytes 5242880 | tf_op jit(solution)/shard_map/pallas_call | solution.py:523
  (77 shorter events, 18.8 us)
Async XLA Ops:
  0.6 7.7 %copy-start.9 = (s32[192,2]{0,1:T(2,128)S(1)}, s32[192,2]{0,1:T(2,128)}, u32[]{:S(2)}) copy-start(s32[192,2]{0,1:T(2,128)} %param.8) | copy-start | bytes 4612
  0.6 7.8 %copy-start = (bf16[192,4096]{1,0:T(8,128)(2,1)S(1)}, bf16[192,4096]{1,0:T(8,128)(2,1)}, u32[]{:S(2)}) copy-start(bf16[192,4096]{1,0:T(8,128)(2,1)} %tok_in.1) | copy-start | bytes 4718596
  0.7 7.8 %copy-start.8 = (bf16[4096,8]{0,1:T(8,128)(2,1)S(1)}, bf16[4096,8]{0,1:T(8,128)(2,1)}, u32[]{:S(2)}) copy-start(bf16[4096,8]{0,1:T(8,128)(2,1)} %param.11) | copy-start | bytes 196612
  0.7 56.3 %all-to-all-start = ((bf16[8,64,4096]{2,1,0:T(8,128)(2,1)}), bf16[8,64,4096]{2,1,0:T(8,128)(2,1)}, u32[]{:S(2)}, u32[]{:S(2)}) async-start(bf16[8,64,4096]{2,1,0:T(8,128)(2,1)} %bitcast.31), calls=%async_computation | async-start | bytes 8388608 | tf_op jit(solution)/shard_map/all_to_all | solution.py:65
  8.3 48.7 %copy-start.2 = (f32[4096]{0:T(1024)S(1)}, f32[4096]{0:T(1024)}, u32[]{:S(2)}) copy-start(f32[4096]{0:T(1024)} %param.12) | copy-start | bytes 49156
  66.0 40.6 %all-to-all-start.1 = ((bf16[128,4,512]{2,1,0:T(4,128)(2,1)}), bf16[128,4,512]{2,1,0:T(4,128)(2,1)S(1)}, u32[]{:S(2)}, u32[]{:S(2)}) async-start(bf16[128,4,512]{2,1,0:T(4,128)(2,1)} %get-tuple-element.53), calls=%async_computation.1 | async-start | bytes 1048576 | tf_op jit(solution)/shard_map/all_to_all | solution.py:65
  80.1 12.8 %copy-start.10 = (s32[2]{0:T(128)S(1)}, s32[2]{0:T(128)}, u32[]{:S(2)}) copy-start(s32[2]{0:T(128)} %param.9) | copy-start | bytes 28
  87.8 18.8 %collective-permute-start = (bf16[64,4096]{1,0:T(8,128)(2,1)}, bf16[64,4096]{1,0:T(8,128)(2,1)S(1)}, u32[]{:S(2)}, u32[]{:S(2)}) collective-permute-start(bf16[64,4096]{1,0:T(8,128)(2,1)} %get-tuple-element.58), channel_id=1, source_target_pairs={{0,1},{1,2},{2,3},{3,4},{4,5},{5,6},{6,7},{7,0},{8,9},{9,10},{10,1... | collective-permute-start | bytes 1572872 | tf_op jit(solution)/shard_map/ppermute | solution.py:644
  88.4 18.1 %collective-permute-start.1 = (bf16[64,4096]{1,0:T(8,128)(2,1)}, bf16[64,4096]{1,0:T(8,128)(2,1)S(1)}, u32[]{:S(2)}, u32[]{:S(2)}) collective-permute-start(bf16[64,4096]{1,0:T(8,128)(2,1)} %get-tuple-element.64), channel_id=1, source_target_pairs={{0,7},{1,0},{2,1},{3,2},{4,3},{5,4},{6,5},{7,6},{8,15},{9,8},{10,9... | collective-permute-start | bytes 1572872 | tf_op jit(solution)/shard_map/ppermute | solution.py:644
  106.6 5.9 %copy-start.5 = (bf16[64,4096]{1,0:T(8,128)(2,1)}, bf16[64,4096]{1,0:T(8,128)(2,1)S(1)}, u32[]{:S(2)}) copy-start(bf16[64,4096]{1,0:T(8,128)(2,1)S(1)} %collective-permute-done.1.rest_7_) | copy-start | bytes 1572868
  106.6 3.1 %collective-permute-start.2 = (bf16[128,4,512]{2,1,0:T(4,128)(2,1)S(1)}, bf16[128,4,512]{2,1,0:T(4,128)(2,1)}, u32[]{:S(2)}, u32[]{:S(2)}) collective-permute-start(bf16[128,4,512]{2,1,0:T(4,128)(2,1)S(1)} %all-to-all-done.1), channel_id=1, source_target_pairs={{0,8},{8,0},{1,9},{9,1},{2,10},{10,2},{3,11},{11,3},{4,12},{12,4},... | collective-permute-start | bytes 1572872 | tf_op jit(solution)/shard_map/ppermute | solution.py:61
  112.4 16.9 %all-to-all-start.2 = ((f32[8,40,512]{2,1,0:T(8,128)}), f32[8,40,512]{2,1,0:T(8,128)S(1)}, u32[]{:S(2)}, u32[]{:S(2)}) async-start(f32[8,40,512]{2,1,0:T(8,128)} %shard_map.104), calls=%async_computation.2 | async-start | bytes 1310720 | tf_op jit(solution)/shard_map/all_to_all | solution.py:65
  117.2 33.8 %collective-permute-start.3 = (bf16[64,4096]{1,0:T(8,128)(2,1)}, bf16[64,4096]{1,0:T(8,128)(2,1)S(1)}, u32[]{:S(2)}, u32[]{:S(2)}) collective-permute-start(bf16[64,4096]{1,0:T(8,128)(2,1)} %get-tuple-element.74), channel_id=1, source_target_pairs={{0,4},{1,5},{2,6},{3,7},{4,0},{5,1},{6,2},{7,3},{8,12},{9,13},{10,... | collective-permute-start | bytes 1572872 | tf_op jit(solution)/shard_map/ppermute | solution.py:644
  120.1 31.9 %collective-permute-start.4 = (bf16[64,4096]{1,0:T(8,128)(2,1)}, bf16[64,4096]{1,0:T(8,128)(2,1)S(1)}, u32[]{:S(2)}, u32[]{:S(2)}) collective-permute-start(bf16[64,4096]{1,0:T(8,128)(2,1)} %get-tuple-element.75), channel_id=1, source_target_pairs={{0,3},{1,4},{2,5},{3,6},{4,7},{5,0},{6,1},{7,2},{8,11},{9,12},{10,... | collective-permute-start | bytes 1572872 | tf_op jit(solution)/shard_map/ppermute | solution.py:644
  122.5 66.7 %collective-permute-start.5 = (bf16[64,4096]{1,0:T(8,128)(2,1)}, bf16[64,4096]{1,0:T(8,128)(2,1)}, u32[]{:S(2)}, u32[]{:S(2)}) collective-permute-start(bf16[64,4096]{1,0:T(8,128)(2,1)} %get-tuple-element.81), channel_id=1, source_target_pairs={{0,5},{1,6},{2,7},{3,0},{4,1},{5,2},{6,3},{7,4},{8,13},{9,14},{10,... | collective-permute-start | bytes 1572872 | tf_op jit(solution)/shard_map/ppermute | solution.py:644
  124.0 65.2 %collective-permute-start.6 = (bf16[64,4096]{1,0:T(8,128)(2,1)}, bf16[64,4096]{1,0:T(8,128)(2,1)}, u32[]{:S(2)}, u32[]{:S(2)}) collective-permute-start(bf16[64,4096]{1,0:T(8,128)(2,1)} %get-tuple-element.82), channel_id=1, source_target_pairs={{0,2},{1,3},{2,4},{3,5},{4,6},{5,7},{6,0},{7,1},{8,10},{9,11},{10,... | collective-permute-start | bytes 1572872 | tf_op jit(solution)/shard_map/ppermute | solution.py:644
  126.7 62.5 %collective-permute-start.7 = (bf16[64,4096]{1,0:T(8,128)(2,1)}, bf16[64,4096]{1,0:T(8,128)(2,1)}, u32[]{:S(2)}, u32[]{:S(2)}) collective-permute-start(bf16[64,4096]{1,0:T(8,128)(2,1)} %get-tuple-element.83), channel_id=1, source_target_pairs={{0,6},{1,7},{2,0},{3,1},{4,2},{5,3},{6,4},{7,5},{8,14},{9,15},{10,... | collective-permute-start | bytes 1572872 | tf_op jit(solution)/shard_map/ppermute | solution.py:644
  130.4 37.5 %all-to-all-start.3 = ((f32[32,8,128]{2,1,0:T(8,128)}), f32[32,8,128]{2,1,0:T(8,128)S(1)}, u32[]{:S(2)}, u32[]{:S(2)}) async-start(f32[32,8,128]{2,1,0:T(8,128)} %get-tuple-element.73), calls=%async_computation.3 | async-start | bytes 262144 | tf_op jit(solution)/shard_map/all_to_all | solution.py:65
  142.6 25.3 %copy-start.3 = (f32[48,512]{1,0:T(8,128)S(1)}, f32[48,512]{1,0:T(8,128)}, u32[]{:S(2)}) copy-start(f32[48,512]{1,0:T(8,128)} %get-tuple-element.79.kept) | copy-start | bytes 294916
  151.0 52.8 %copy-start.6 = (bf16[64,4096]{1,0:T(8,128)(2,1)}, bf16[64,4096]{1,0:T(8,128)(2,1)S(1)}, u32[]{:S(2)}) copy-start(bf16[64,4096]{1,0:T(8,128)(2,1)S(1)} %collective-permute-done.3.rest_4_) | copy-start | bytes 1572868
  152.1 51.7 %copy-start.7 = (bf16[64,4096]{1,0:T(8,128)(2,1)}, bf16[64,4096]{1,0:T(8,128)(2,1)S(1)}, u32[]{:S(2)}) copy-start(bf16[64,4096]{1,0:T(8,128)(2,1)S(1)} %collective-permute-done.4.rest_3_) | copy-start | bytes 1572868
  169.7 27.0 %all-to-all-start.4 = ((bf16[8,32,512]{2,1,0:T(8,128)(2,1)}), bf16[8,32,512]{2,1,0:T(8,128)(2,1)S(1)}, u32[]{:S(2)}, u32[]{:S(2)}) async-start(bf16[8,32,512]{2,1,0:T(8,128)(2,1)} %get-tuple-element.80), calls=%async_computation.4 | async-start | bytes 524288 | tf_op jit(solution)/shard_map/all_to_all | solution.py:65
  218.2 14.8 %all-to-all-start.6 = ((f32[16,16,128]{2,1,0:T(8,128)}), f32[16,16,128]{2,1,0:T(8,128)S(1)}, u32[]{:S(2)}, u32[]{:S(2)}) async-start(f32[16,16,128]{2,1,0:T(8,128)} %broadcast_in_dim.94), calls=%async_computation.6 | async-start | bytes 262144 | tf_op jit(solution)/shard_map/all_to_all | solution.py:65
  233.7 11.0 %all-to-all-start.7 = ((f32[16,16,128]{2,1,0:T(8,128)}), f32[16,16,128]{2,1,0:T(8,128)S(1)}, u32[]{:S(2)}, u32[]{:S(2)}) async-start(f32[16,16,128]{2,1,0:T(8,128)} %broadcast_in_dim.95), calls=%async_computation.7 | async-start | bytes 262144 | tf_op jit(solution)/shard_map/all_to_all | solution.py:65
  (2 other events, 6.5 us)

commit v6 on v5

--- a/solution.py
+++ b/solution.py
@@ -20,7 +20,7 @@
 SMEM = pl.BlockSpec(memory_space=pltpu.SMEM)
 HBM = pl.BlockSpec(memory_space=pltpu.HBM)
 NT = (((1,), (1,)), ((), ()))
-TURNS = ((1, 7), (4, 3), (5, 2, 6))
+TURNS = ((1, 7), (4, 3), (5,), (2, 6))
 
 
 def iota(shape, dim):
@@ -84,36 +84,30 @@
     return gates, routes * capacity + rank
 
 
+def one_hots(slot, slots):
+    ids = iota((slot.shape[0], slots), 1)
+    return jnp.concatenate([(slot[:, k : k + 1] == ids).astype(BF16) for k in range(2)], axis=0)
+
+
 def forward_kernel(
-    steps, outer, tok, rec, slot, gate, gain, summed, offered, inverse, held, square, sliced, row_sem, slice_sem
+    steps, tok, rec, slot, gate, gain, summed, sliced_out, inverse, held, square, picks, sliced, row_sem, slice_sem
 ):
     step = pl.program_id(0)
-    part = tok.shape[1]
+    rows, part = tok.shape
 
     def keep(e):
         start = pl.multiple_of(e * part, part)
         return pltpu.make_async_copy(held.at[e], summed.at[:, pl.ds(start, part)], row_sem.at[e])
 
-    def offer(u):
-        return pltpu.make_async_copy(sliced, offered.at[pl.ds(u * steps, steps)], slice_sem.at[u])
-
-    rows, slots = tok.shape[0], rec.shape[0]
-    ids = iota((rows, slots), 1)
-    first = (slot[:, 0:1] == ids).astype(BF16)
-    second = (slot[:, 1:2] == ids).astype(BF16)
-
     @pl.when(step == 0)
     def _():
         square[...] = jnp.zeros_like(square)
+        picks[...] = one_hots(slot, rec.shape[0])
 
     for k in range(part // 256):
         cols = slice(256 * k, 256 * (k + 1))
-        block = rec[:, cols]
-        x = (
-            tok[:, cols].astype(F32)
-            + gate[:, 0:1] * jnp.dot(first, block, preferred_element_type=F32)
-            + gate[:, 1:2] * jnp.dot(second, block, preferred_element_type=F32)
-        )
+        both = jnp.dot(picks[...], rec[:, cols], preferred_element_type=F32)
+        x = tok[:, cols].astype(F32) + gate[:, 0:1] * both[:rows] + gate[:, 1:2] * both[rows:]
         held[step, :, cols] = x
         square[...] += fold(x * x)
     keep(step).start()
@@ -128,21 +122,20 @@
             x = held[e] * scale
             x = jnp.sum(x.reshape(count, SEQ, part), axis=1) / SEQ
             sliced[e] = (x * gain[:, part * e : part * (e + 1)]).astype(BF16)
-        for u in range(outer):
-            offer(u).start()
+        offer = pltpu.make_async_copy(sliced, sliced_out, slice_sem)
+        offer.start()
         for e in range(steps):
             keep(e).wait()
-        for u in range(outer):
-            offer(u).wait()
-
-
-def forward(tokens, received, slot, gates, gain, experts, outer):
+        offer.wait()
+
+
+def forward(tokens, received, slot, gates, gain, experts):
     rows, width = tokens.shape
     slots = received.shape[0]
     part = width // experts
     whole = lambda shape: pl.BlockSpec(shape, lambda i: (0,) * len(shape))
     return pl.pallas_call(
-        functools.partial(forward_kernel, experts, outer),
+        functools.partial(forward_kernel, experts),
         grid=(experts,),
         in_specs=[
             pl.BlockSpec((rows, part), lambda i: (0, i)),
@@ -154,27 +147,28 @@
         out_specs=[HBM, HBM, whole((rows, 1))],
         out_shape=[
             pltpu.HBM((rows, width), F32),
-            pltpu.HBM((outer * experts, rows // SEQ, part), BF16),
+            pltpu.HBM((experts, rows // SEQ, part), BF16),
             jax.ShapeDtypeStruct((rows, 1), F32),
         ],
         scratch_shapes=[
             pltpu.VMEM((experts, rows, part), F32),
             pltpu.VMEM((rows, 128), F32),
+            pltpu.VMEM((2 * rows, slots), BF16),
             pltpu.VMEM((experts, rows // SEQ, part), BF16),
             pltpu.SemaphoreType.DMA((experts,)),
-            pltpu.SemaphoreType.DMA((outer,)),
+            pltpu.SemaphoreType.DMA(()),
         ],
         compiler_params=params(14),
         cost_estimate=cost(4 * rows * slots * width, 10 << 20),
     )(tokens, received, slot, gates, gain)
 
 
-def pack_kernel(turns, place, x, turned, *rest):
-    *outs, packed, sems = rest
+def pack_kernel(place, x, turned, *rest):
+    *outs, spot, packed, sems = rest
     step, steps = pl.program_id(0), packed.shape[0]
     rows, part = x.shape
     capacity = outs[0].shape[0]
-    slots = steps * capacity
+    slots = spot.shape[0]
 
     def leave(e, i):
         start = pl.multiple_of(e * part, part)
@@ -182,13 +176,15 @@
             packed.at[e, pl.ds(i * capacity, capacity)], outs[i].at[:, pl.ds(start, part)], sems.at[e, i]
         )
 
-    first = jnp.concatenate([iota((capacity, rows), 0) + r * capacity for r in turns], axis=0)
-    target = lax.rem(first + place[0] * capacity, slots)
-    spot = ((turned[0:1, :] == target) | (turned[1:2, :] == target)).astype(BF16)
-    for k in range(part // 256):
-        cols = slice(256 * k, 256 * (k + 1))
+    @pl.when(step == 0)
+    def _():
+        target = lax.rem(iota((slots, rows), 0) + place[0] * capacity, slots)
+        spot[...] = ((turned[0:1, :] == target) | (turned[1:2, :] == target)).astype(BF16)
+
+    for k in range(part // 512):
+        cols = slice(512 * k, 512 * (k + 1))
         packed[step, :, cols] = jnp.dot(
-            spot, x[:, cols].astype(BF16), preferred_element_type=F32
+            spot[...], x[:, cols].astype(BF16), preferred_element_type=F32
         ).astype(BF16)
     for i in range(len(outs)):
         leave(step, i).start()
@@ -200,52 +196,55 @@
                 leave(e, i).wait()
 
 
-def pack(place, summed, turned, turns, experts, capacity):
+def pack(place, summed, turned, experts, capacity):
     rows, width = summed.shape
-    part = width // experts
+    steps = experts // 2
+    part = width // steps
+    slots = experts * capacity
     return pl.pallas_call(
-        functools.partial(pack_kernel, turns),
-        grid=(experts,),
+        pack_kernel,
+        grid=(steps,),
         in_specs=[
             SMEM,
             pl.BlockSpec((rows, part), lambda i: (0, i)),
             pl.BlockSpec((2, rows), lambda i: (0, 0)),
         ],
-        out_specs=[HBM] * len(turns),
-        out_shape=[pltpu.HBM((capacity, width), BF16)] * len(turns),
+        out_specs=[HBM] * experts,
+        out_shape=[pltpu.HBM((capacity, width), BF16)] * experts,
         scratch_shapes=[
-            pltpu.VMEM((experts, len(turns) * capacity, part), BF16),
-            pltpu.SemaphoreType.DMA((experts, len(turns))),
-        ],
-        compiler_params=params(12),
-        cost_estimate=cost(2 * rows * len(turns) * capacity * width, 5 << 20),
+            pltpu.VMEM((slots, rows), BF16),
+            pltpu.VMEM((steps, slots, part), BF16),
+            pltpu.SemaphoreType.DMA((steps, experts)),
+        ],
+        compiler_params=params(14),
+        cost_estimate=cost(2 * rows * slots * width, 7 << 20),
     )(place, *in_hbm(summed), turned)
 
 
-def overlap_kernel(steps, x, rec, slot, facts, out, dots):
+def overlap_kernel(steps, x, rec, slot, facts, out, fetched, picks, dots):
     step = pl.program_id(0)
     rows, part = x.shape
-    slots = rec.shape[0]
-    ids = iota((rows, slots), 1)
-    first = (slot[:, 0:1] == ids).astype(BF16)
-    second = (slot[:, 1:2] == ids).astype(BF16)
 
     @pl.when(step == 0)
     def _():
         dots[...] = jnp.zeros_like(dots)
+        picks[...] = one_hots(slot, rec.shape[0])
 
     for k in range(part // 256):
         cols = slice(256 * k, 256 * (k + 1))
-        value, block = x[:, cols], rec[:, cols]
-        dots[0] += fold(value * jnp.dot(first, block, preferred_element_type=F32))
-        dots[1] += fold(value * jnp.dot(second, block, preferred_element_type=F32))
+        both = jnp.dot(picks[...], rec[:, cols], preferred_element_type=F32)
+        fetched[:, cols] = both.astype(BF16)
+        value = x[:, cols]
+        dots[:rows] += fold(value * both[:rows])
+        dots[rows:] += fold(value * both[rows:])
 
     @pl.when(step == steps - 1)
     def _():
         lane = iota((rows, 128), 1)
         known = facts[...]
         for k in range(2):
-            known = jnp.where(lane == k, jnp.sum(dots[k], axis=1, keepdims=True), known)
+            total = jnp.sum(dots[rows * k : rows * (k + 1)], axis=1, keepdims=True)
+            known = jnp.where(lane == k, total, known)
         out[...] = known
 
 
@@ -263,11 +262,11 @@
             whole((rows, 2)),
             whole((rows, 128)),
         ],
-        out_specs=whole((rows, 128)),
-        out_shape=jax.ShapeDtypeStruct((rows, 128), F32),
-        scratch_shapes=[pltpu.VMEM((2, rows, 128), F32)],
+        out_specs=[whole((rows, 128)), pl.BlockSpec((2 * rows, part), lambda i: (0, i))],
+        out_shape=[pltpu.HBM((rows, 128), F32), pltpu.HBM((2 * rows, width), BF16)],
+        scratch_shapes=[pltpu.VMEM((2 * rows, slots), BF16), pltpu.VMEM((2 * rows, 128), F32)],
         compiler_params=params(12),
-        cost_estimate=cost(4 * rows * slots * width, 7 << 20),
+        cost_estimate=cost(4 * rows * slots * width, 10 << 20),
     )(*in_hbm(summed, received), slot, facts)
 
 
@@ -286,13 +285,11 @@
     return (source == b).astype(BF16)
 
 
-def scores_kernel(near, far, notes, offered, whole, sems):
+def scores_kernel(own, near, far, notes, offered, whole, sems):
     experts, total, columns = offered.shape
     group = experts * PAIR_DEV
-    wide = 2 * group
-    own = near[pl.ds(pl.multiple_of(lax.axis_index("u") * wide, wide), wide), :]
     queries, records = [
-        jnp.dot(picker(group, kind), own, preferred_element_type=F32).astype(BF16) for kind in (0, 1)
+        jnp.dot(picker(group, kind), own[...], preferred_element_type=F32).astype(BF16) for kind in (0, 1)
     ]
     at_record = lanes_of((group, columns), 1)[2]
     for k, side in enumerate((near, far)):
@@ -412,76 +409,62 @@
     return jnp.where(lax.rem(piece, 2) == 0, half[0], half[1])
 
 
-def split_bf16(x):
-    high = x.astype(BF16)
-    rest = x - high.astype(F32)
-    mid = rest.astype(BF16)
-    low = (rest - mid.astype(F32)).astype(BF16)
-    return high, mid, low
-
-
 def router_kernel(
-    grads, gain, summed_in, rec_in, tok_in, facts_in, part_out, state_out, weighted_out,
-    summed, rec, tok, facts, state, weighted, sems, facts_sem, out_sems
+    grads, gain, summed_in, fetched_in, tok_in, facts_in, part_out, state_out, weighted_out,
+    summed, fetched, tok, facts, state, weighted, acc, sems, facts_sem, out_sems
 ):
     experts, _, part = grads.shape
     rows = summed.shape[1]
-    slots = rec.shape[1]
     count = rows // SEQ
+    sources = ((summed_in, summed), (fetched_in, fetched), (tok_in, tok))
 
     def load(e):
         cols = pl.ds(e * part, part)
-        pairs = ((summed_in, summed), (rec_in, rec), (tok_in, tok))
         return [
-            pltpu.make_async_copy(a.at[:, cols], b.at[e], sems.at[k, e]) for k, (a, b) in enumerate(pairs)
+            pltpu.make_async_copy(a.at[:, cols], b.at[e], sems.at[k, e]) for k, (a, b) in enumerate(sources)
         ]
 
     known = pltpu.make_async_copy(facts_in, facts, facts_sem)
     loads = [load(e) for e in range(experts)]
-    for k in (1, 0):
-        for e in range(experts):
-            loads[e][k].start()
+    for e in range(experts):
+        loads[e][0].start()
+        loads[e][1].start()
     known.start()
     for e in range(experts):
         loads[e][2].start()
 
-    w = []
     for e in range(experts):
         cols = slice(part * e, part * (e + 1))
-        w.append(rows_of(grads, e, lax.axis_index("expert")) * (gain[:, cols] / SEQ))
-        weighted[:, cols] = w[e]
-    on_slots = jnp.zeros((16, slots), F32)
-    for e in range(experts):
-        lhs = jnp.concatenate(list(split_bf16(w[e])) + [jnp.zeros((count, part), BF16)], axis=0)
+        w = rows_of(grads, e, lax.axis_index("expert")) * (gain[:, cols] / SEQ)
+        weighted[:, cols] = w
+        loads[e][0].wait()
         loads[e][1].wait()
-        on_slots = on_slots + lax.dot_general(lhs, rec[e], NT, preferred_element_type=F32)
-    acc = [jnp.zeros((SEQ, 128), F32) for _ in range(count)]
-    for e in range(experts):
-        loads[e][0].wait()
         for q in range(count):
-            acc[q] = acc[q] + fold(summed[e, SEQ * q : SEQ * (q + 1), :] * w[e][q : q + 1, :])
+            row = w[q : q + 1, :]
+            at = [slice(rows * k + SEQ * q, rows * k + SEQ * (q + 1)) for k in range(2)]
+            terms = [summed[e, at[0], :], fetched[e, at[0], :].astype(F32), fetched[e, at[1], :].astype(F32)]
+            for k, term in enumerate(terms):
+                total = fold(term * row)
+                spot = slice(SEQ * q, SEQ * (q + 1))
+                acc[k, spot] = total if e == 0 else acc[k, spot] + total
     known.wait()
-    on_slots = on_slots[0:count] + on_slots[count : 2 * count] + on_slots[2 * count : 3 * count]
-    ids = iota((SEQ, slots), 1)
     lanes = iota((SEQ, 128), 1)
     choices = []
     for q in range(count):
         at = slice(SEQ * q, SEQ * (q + 1))
         fact = facts[at, :]
         inv = fact[:, 2:3]
-        shrink = inv * inv * inv * (jnp.sum(acc[q], axis=1, keepdims=True) / (experts * part))
-        row = on_slots[q : q + 1, :]
+        shrink = inv * inv * inv * (jnp.sum(acc[0, at], axis=1, keepdims=True) / (experts * part))
         grad_gate = []
         for k in range(2):
-            spot = fact[:, 5 + k : 6 + k].astype(I32)
-            along = jnp.sum(jnp.where(spot == ids, row, 0.0), axis=1, keepdims=True)
+            along = jnp.sum(acc[1 + k, at], axis=1, keepdims=True)
             grad_gate.append(inv * along - shrink * fact[:, k : k + 1])
         gates = [fact[:, 3 + k : 4 + k] for k in range(2)]
         mean = gates[0] * grad_gate[0] + gates[1] * grad_gate[1]
         choice = jnp.zeros((SEQ, 128), F32)
         for k in range(2):
             chosen = gates[k] * (grad_gate[k] - mean)
-            route = fact[:, 7 + k : 8 + k].astype(I32)
+            route = fact[:, 5 + k : 6 + k].astype(I32)
             choice = choice + jnp.where(route == lanes, chosen, 0.0)
         choices.append(choice)
         choice = jnp.where(lanes == experts, inv, choice)
@@ -613,7 +596,6 @@
     outer = lax.axis_size("u")
     mine = lax.axis_index("expert").astype(I32)
     mine_at = mine[None]
-    wide = outer * experts
     part = width // experts
     group = PAIR_DEV * experts
     pairs = group * outer * CORES
@@ -630,13 +612,13 @@
         0,
     ).astype(F32)
 
-    summed, offered, inverse = forward(tokens, received, slot, gates, gain, experts, outer)
-    near = exchange(offered, ("u", "expert"))
+    summed, sliced, inverse = forward(tokens, received, slot, gates, gain, experts)
+    own = exchange(sliced, "expert").reshape(2 * group, part)
     facts = jnp.concatenate(
-        [jnp.zeros((rows, 2), F32), inverse, gates, slot.astype(F32), routes.astype(F32)], axis=1
+        [jnp.zeros((rows, 2), F32), inverse, gates, routes.astype(F32)], axis=1
     )
     facts = jnp.pad(facts, ((0, 0), (0, 128 - facts.shape[1])))
-    backs = list(pack(mine_at, summed, slot.T, tuple(range(experts)), experts, capacity))
+    backs = list(pack(mine_at, summed, slot.T, experts, capacity))
 
     def move(after, turns):
         after, *ready = lax.optimization_barrier((after, *[backs[r] for r in turns]))
@@ -644,7 +626,6 @@
             backs[r] = lax.ppermute(x, "expert", [(i, (i + r) % experts) for i in range(experts)])
         return after
 
-    move(slot, TURNS[0])
 
     def landed(value, turns):
         value, *done = lax.optimization_barrier((value, *[backs[r] for r in turns]))
@@ -664,18 +645,21 @@
     notes = jnp.stack([gate_slot, inverse_slot, sequence_slot, spread_positive])
     notes = jnp.pad(notes, ((0, 4), (0, 0)))
 
-    near, *backs = lax.optimization_barrier((near, *backs))
+    own, *backs = lax.optimization_barrier((own, *backs))
+    own = move(own, TURNS[0])
+    near = spread(own, "u", outer)
     far = swap_core(near)
     near, far = near.reshape(columns, part), far.reshape(columns, part)
     offered = pl.pallas_call(
         scores_kernel,
-        in_specs=[VMEM] * 3,
+        in_specs=[VMEM] * 4,
         out_specs=HBM,
         out_shape=pltpu.HBM((experts, 2 * group + 8, columns), F32),
         scratch_shapes=[pltpu.VMEM((2 * group + 8, columns), F32), pltpu.SemaphoreType.DMA((experts,))],
         compiler_params=params(2),
-    )(near, far, notes)
-    offered = move(offered, TURNS[1] + TURNS[2])
+    )(own, near, far, notes)
+    offered = landed(offered, TURNS[0])
+    offered = move(offered, TURNS[1])
     gathered = exchange(offered, "expert")
     devices = outer * CORES
     offered, kept = pl.pallas_call(
@@ -691,10 +675,10 @@
         ],
         compiler_params=params(2),
     )(gathered)
+    offered = move(offered, TURNS[2])
     heard = exchange(offered, ("u", "c"))
     heard = landed(heard, TURNS[1])
-    offered, facts = lax.optimization_barrier((offered, facts))
-    facts = overlaps(summed, received, slot, facts, experts)
+    facts, fetched = overlaps(summed, received, slot, facts, experts)
     heard, facts = lax.optimization_barrier((heard, facts))
     offered, loss = pl.pallas_call(
         functools.partial(gradient_kernel, scale),
@@ -704,6 +688,7 @@
         scratch_shapes=[pltpu.VMEM((2 * group, part), BF16), pltpu.SemaphoreType.DMA((experts,))],
         compiler_params=params(2),
     )((loss_scale / pairs)[None], heard, kept, near, far)
+    offered = move(offered, TURNS[3])
     grads = exchange(offered, "expert")
     grads = landed(grads, TURNS[2])
 
@@ -718,17 +703,18 @@
         ],
         scratch_shapes=[
             pltpu.VMEM((experts, rows, part), F32),
-            pltpu.VMEM((experts, slots, part), BF16),
+            pltpu.VMEM((experts, 2 * rows, part), BF16),
             pltpu.VMEM((experts, rows, part), BF16),
             pltpu.VMEM((rows, 128), F32),
             pltpu.VMEM((rows, 128), F32),
             pltpu.VMEM((rows // SEQ, width), F32),
+            pltpu.VMEM((3, rows, 128), F32),
             pltpu.SemaphoreType.DMA((3, experts)),
             pltpu.SemaphoreType.DMA(()),
             pltpu.SemaphoreType.DMA((2,)),
         ],
         compiler_params=params(16),
-    )(grads, gain, *in_hbm(summed, received, tokens, facts))
+    )(grads, gain, *in_hbm(summed, fetched, tokens, facts))
     router_part = exchange(router_part.reshape(outer, -1, 128), "u")
     router_part = jnp.sum(router_part, axis=0)
     router_part = spread(router_part, ("c", "expert"), CORES * experts)

time: 248 us -> 236 us (0.952)
  waiting for transfers between devices: 84.7 us -> 64.1 us
  starting transfers between devices: 84.8 us -> 97.9 us
  Pallas kernels: 49.5 us -> 46.6 us
    all_to_all x7 -> x8, waiting for transfers between devices: 71.2 us -> 59.5 us  [exchange(): return lax.all_to_all(x, axes, split_axis=0, concat_axis=0, tiled=True)]
    all_to_all x7 -> x8, starting transfers between devices: 66 us -> 77.2 us  [exchange(): return lax.all_to_all(x, axes, split_axis=0, concat_axis=0, tiled=True)]
    ppermute x7, waiting for transfers between devices: 12.8 us -> 3.83 us  [move(): lax.ppermute(x, 'expert', [(i, (i + r) % experts) for i in range(experts)])]
    pallas_call x3, Pallas kernels: 18.2 us -> 15.4 us  [the longest x1 8.12 us: forward(): pl.pallas_call(functools.partial(forward_kernel, experts), grid=(experts,...]
  transfers between devices with their start and end apart: 15 -> 16, of which waited for: 8 -> 9; matrix products, arithmetic and copies ran while one was open for 3% -> 2% of each run, Pallas kernels for 13% -> 16%
where the time goes in v6:
time: 236 us; the launch traced here: 234 us
  starting transfers between devices  97.9 us (41%)
  waiting for transfers between devices  64.1 us (27%)
  Pallas kernels  46.6 us (20%)
  blocking collectives  12.7 us (5%)
  local copies, waits for them, and re-layouts  6.34 us (3%)
  between operations  3.49 us (1%)
    all_to_all x8, starting transfers between devices, exchange(): return lax.all_to_all(x, axes, split_axis=0, concat_axis=0, tiled=True)  77.2 us
    all_to_all x8, waiting for transfers between devices, exchange(): return lax.all_to_all(x, axes, split_axis=0, concat_axis=0, tiled=True)  59.5 us
    ppermute x7, starting transfers between devices, move(): lax.ppermute(x, 'expert', [(i, (i + r) % experts) for i in range(experts)])  17.4 us
    all_to_all x1, blocking collectives, exchange(): return lax.all_to_all(x, axes, split_axis=0, concat_axis=0, tiled=True)  12.7 us
    pallas_call x1, Pallas kernels, overlaps(): pl.pallas_call(functools.partial(overlap_kernel, experts), grid=(experts,...  8.46 us
    pallas_call x1, Pallas kernels, forward(): pl.pallas_call(functools.partial(forward_kernel, experts), grid=(experts,...  8.12 us
    pallas_call x1, Pallas kernels, expert_rows(): pl.pallas_call(expert_kernel, grid_spec=pltpu.PrefetchScalarGridSpec(num_...  7.25 us
    pallas_call x1, Pallas kernels, token_rows(): pl.pallas_call(functools.partial(token_kernel, experts), grid=(experts,),...  6.47 us
  transfers between devices with their start and end apart: 16, of which 9 were waited for; matrix products, arithmetic and copies ran while one was open for 2% of the time, Pallas kernels for 16%

profile of v6, /device:TPU:1, one launch (start us, length us, event | category | flops | bytes accessed | tf_op | source)
XLA Modules:
  0.0 234.0 jit_solution(7735481242562635342)
XLA Ops:
  0.7 7.6 %all-to-all-start = ((bf16[8,64,4096]{2,1,0:T(8,128)(2,1)}), bf16[8,64,4096]{2,1,0:T(8,128)(2,1)}, u32[]{:S(2)}, u32[]{:S(2)}) async-start(bf16[8,64,4096]{2,1,0:T(8,128)(2,1)} %bitcast.37), calls=%async_computation | async-start | bytes 8388608 | tf_op jit(solution)/shard_map/all_to_all | solution.py:65
  9.8 47.2 %all-to-all-done = bf16[8,64,4096]{2,1,0:T(8,128)(2,1)} async-done(((bf16[8,64,4096]{2,1,0:T(8,128)(2,1)}), bf16[8,64,4096]{2,1,0:T(8,128)(2,1)}, u32[]{:S(2)}, u32[]{:S(2)}) %all-to-all-start) | async-done | bytes 4194336 | tf_op jit(solution)/shard_map/all_to_all | solution.py:65
  57.0 8.1 %shard_map.102 = (f32[192,4096]{1,0:T(8,128)}, bf16[8,4,512]{2,1,0:T(4,128)(2,1)}, f32[192,1]{1,0:T(8,128)S(1)}) custom-call(bf16[192,4096]{1,0:T(8,128)(2,1)S(1)} %copy-done, bf16[512,4096]{1,0:T(8,128)(2,1)} %bitcast.2.rec, s32[192,2]{1,0:T(8,128)S(1)} %add.58.slot, f32[192,2]{1,0:T(8,128)S(1)} %exponential_divide_fusion.gate, f32[1,4096]{1,0:T(1,128)S(1)} %bitcast.33), custom_call_target="tpu_custom_call" | custom-call | flops 1610612736 | bytes 10485760 | tf_op jit(solution)/shard_map/pallas_call | solution.py:137
  65.2 5.2 %all-to-all-start.1 = ((bf16[8,4,512]{2,1,0:T(4,128)(2,1)}), bf16[8,4,512]{2,1,0:T(4,128)(2,1)S(1)}, u32[]{:S(2)}, u32[]{:S(2)}) async-start(bf16[8,4,512]{2,1,0:T(4,128)(2,1)} %get-tuple-element.58), calls=%async_computation.1 | async-start | bytes 65536 | tf_op jit(solution)/shard_map/all_to_all | solution.py:65
  70.4 5.7 %shard_map.103 = (bf16[64,4096]{1,0:T(8,128)(2,1)}, bf16[64,4096]{1,0:T(8,128)(2,1)}, bf16[64,4096]{1,0:T(8,128)(2,1)}, bf16[64,4096]{1,0:T(8,128)(2,1)}, bf16[6...) custom-call(s32[1]{0:T(128)} %bitcast.4.place, ...), custom_call_target="tpu_custom_call" | custom-call | flops 805306368 | bytes 7340032 | tf_op jit(solution)/shard_map/pallas_call | solution.py:204
  77.9 8.3 %all-to-all-start.2 = ((bf16[16,32,512]{2,1,0:T(8,128)(2,1)}), bf16[16,32,512]{2,1,0:T(8,128)(2,1)S(1)}, u32[]{:S(2)}, u32[]{:S(2)}) async-start(bf16[16,32,512]{2,1,0:T(8,128)(2,1)} %broadcast_in_dim.89), calls=%async_computation.2 | async-start | bytes 1048576 | tf_op jit(solution)/shard_map/all_to_all | solution.py:65
  88.7 4.6 %collective-permute-start.2 = (bf16[64,4096]{1,0:T(8,128)(2,1)}, bf16[64,4096]{1,0:T(8,128)(2,1)S(1)}, u32[]{:S(2)}, u32[]{:S(2)}) collective-permute-start(bf16[64,4096]{1,0:T(8,128)(2,1)} %get-tuple-element.74), channel_id=1, source_target_pairs={{0,7},{1,0},{2,1},{3,2},{4,3},{5,4},{6,5},{7,6},{8,15},{9,8},{10,9... | collective-permute-start | bytes 1572872 | tf_op jit(solution)/shard_map/ppermute | solution.py:626
  93.3 5.7 %all-to-all-done.2 = bf16[16,32,512]{2,1,0:T(8,128)(2,1)S(1)} async-done(((bf16[16,32,512]{2,1,0:T(8,128)(2,1)}), bf16[16,32,512]{2,1,0:T(8,128)(2,1)S(1)}, u32[]{:S(2)}, u32[]{:S(2)}) %all-to-all-start.2) | async-done | bytes 524320 | tf_op jit(solution)/shard_map/all_to_all | solution.py:65
  99.0 3.3 %collective-permute-start = (bf16[16,32,512]{2,1,0:T(8,128)(2,1)S(1)}, bf16[16,32,512]{2,1,0:T(8,128)(2,1)S(1)}, u32[]{:S(2)}, u32[]{:S(2)}) collective-permute-start(bf16[16,32,512]{2,1,0:T(8,128)(2,1)S(1)} %all-to-all-done.2), channel_id=1, source_target_pairs={{0,8},{8,0},{1,9},{9,1},{2,10},{10,2},{3,11},{11,3},{4,12},{12,4},... | collective-permute-start | bytes 1572872 | tf_op jit(solution)/shard_map/ppermute | solution.py:61
  105.4 3.4 %collective-permute-done.1.rest_1_ = bf16[64,4096]{1,0:T(8,128)(2,1)S(1)} collective-permute-done((bf16[64,4096]{1,0:T(8,128)(2,1)}, bf16[64,4096]{1,0:T(8,128)(2,1)S(1)}, u32[]{:S(2)}, u32[]{:S(2)}) %collective-permute-start.1) | collective-permute-done | bytes 524320 | tf_op jit(solution)/shard_map/ppermute | solution.py:626
  108.8 4.5 %all-to-all-start.3 = ((f32[8,40,512]{2,1,0:T(8,128)}), f32[8,40,512]{2,1,0:T(8,128)S(1)}, u32[]{:S(2)}, u32[]{:S(2)}) async-start(f32[8,40,512]{2,1,0:T(8,128)} %shard_map.104), calls=%async_computation.3 | async-start | bytes 1310720 | tf_op jit(solution)/shard_map/all_to_all | solution.py:65
  113.3 3.0 %collective-permute-start.3 = (bf16[64,4096]{1,0:T(8,128)(2,1)}, bf16[64,4096]{1,0:T(8,128)(2,1)}, u32[]{:S(2)}, u32[]{:S(2)}) collective-permute-start(bf16[64,4096]{1,0:T(8,128)(2,1)} %get-tuple-element.82), channel_id=1, source_target_pairs={{0,4},{1,5},{2,6},{3,7},{4,0},{5,1},{6,2},{7,3},{8,12},{9,13},{10,... | collective-permute-start | bytes 1572872 | tf_op jit(solution)/shard_map/ppermute | solution.py:626
  119.5 3.2 %all-to-all-done.3.gathered = f32[8,40,512]{2,1,0:T(8,128)S(1)} async-done(((f32[8,40,512]{2,1,0:T(8,128)}), f32[8,40,512]{2,1,0:T(8,128)S(1)}, u32[]{:S(2)}, u32[]{:S(2)}) %all-to-all-start.3) | async-done | bytes 655392 | tf_op jit(solution)/shard_map/all_to_all | solution.py:65
  123.7 12.5 %all-to-all-start.4 = ((f32[32,8,128]{2,1,0:T(8,128)}), f32[32,8,128]{2,1,0:T(8,128)S(1)}, u32[]{:S(2)}, u32[]{:S(2)}) async-start(f32[32,8,128]{2,1,0:T(8,128)} %get-tuple-element.81), calls=%async_computation.4 | async-start | bytes 262144 | tf_op jit(solution)/shard_map/all_to_all | solution.py:65
  137.8 8.5 %shard_map.106 = (f32[192,128]{1,0:T(8,128)}, bf16[384,4096]{1,0:T(8,128)(2,1)}) custom-call(f32[192,4096]{1,0:T(8,128)} %get-tuple-element.59.x.summed_in.summed, bf16[512,4096]{1,0:T(8,128)(2,1)} %bitcast.2.rec, s32[192,2]{1,0:T(8,128)S(1)} %add.58.slot, f32[192,128]{1,0:T(8,128)S(1)} %pad.17.facts), custom_call_target="tpu_custom_call" | custom-call | flops 1610612736 | bytes 10485760 | tf_op jit(solution)/shard_map/pallas_call | solution.py:256
  148.6 10.4 %all-to-all-start.5 = ((bf16[8,32,512]{2,1,0:T(8,128)(2,1)}), bf16[8,32,512]{2,1,0:T(8,128)(2,1)S(1)}, u32[]{:S(2)}, u32[]{:S(2)}) async-start(bf16[8,32,512]{2,1,0:T(8,128)(2,1)} %get-tuple-element.91), calls=%async_computation.5 | async-start | bytes 524288 | tf_op jit(solution)/shard_map/all_to_all | solution.py:65
  159.0 3.0 %collective-permute-start.6 = (bf16[64,4096]{1,0:T(8,128)(2,1)}, bf16[64,4096]{1,0:T(8,128)(2,1)S(1)}, u32[]{:S(2)}, u32[]{:S(2)}) collective-permute-start(bf16[64,4096]{1,0:T(8,128)(2,1)} %get-tuple-element.99), channel_id=1, source_target_pairs={{0,2},{1,3},{2,4},{3,5},{4,6},{5,7},{6,0},{7,1},{8,10},{9,11},{10,... | collective-permute-start | bytes 1572872 | tf_op jit(solution)/shard_map/ppermute | solution.py:626
  162.0 2.4 %collective-permute-start.7 = (bf16[64,4096]{1,0:T(8,128)(2,1)}, bf16[64,4096]{1,0:T(8,128)(2,1)S(1)}, u32[]{:S(2)}, u32[]{:S(2)}) collective-permute-start(bf16[64,4096]{1,0:T(8,128)(2,1)} %get-tuple-element.103), channel_id=1, source_target_pairs={{0,6},{1,7},{2,0},{3,1},{4,2},{5,3},{6,4},{7,5},{8,14},{9,15},{10,... | collective-permute-start | bytes 1572872 | tf_op jit(solution)/shard_map/ppermute | solution.py:626
  166.6 6.2 %shard_map.108 = (f32[256,128]{1,0:T(8,128)S(1)}, f32[192,128]{1,0:T(8,128)}, f32[4,4096]{1,0:T(4,128)}) custom-call(bf16[8,32,512]{2,1,0:T(8,128)(2,1)S(1)} %all-to-all-done.5.grads, f32[1,4096]{1,0:T(1,128)S(1)} %bitcast.34, f32[192,4096]{1,0:T(8,128)} %get-tuple-element.59.x.summed_in.summed, bf16[384,4096]{1,0:T(8,128)(2,1)} %get-tuple-element.94.fetched_in, ...), custom_call_target="tpu_custom_call" | custom-call | tf_op jit(solution)/shard_map/pallas_call | solution.py:695
  172.8 12.7 %all_to_all.45 = f32[16,16,128]{2,1,0:T(8,128)S(1)} all-to-all(f32[16,16,128]{2,1,0:T(8,128)S(1)} %bitcast.36), channel_id=1, replica_groups=mesh['u'=16,'c'=2,'expert'=8] {'u'}, dimensions={0} | all-to-all | bytes 262144 | tf_op jit(solution)/shard_map/all_to_all | solution.py:65
  186.2 25.2 %all-to-all-start.7 = ((f32[16,16,128]{2,1,0:T(8,128)}), f32[16,16,128]{2,1,0:T(8,128)S(1)}, u32[]{:S(2)}, u32[]{:S(2)}) async-start(f32[16,16,128]{2,1,0:T(8,128)} %broadcast_in_dim.101), calls=%async_computation.7 | async-start | bytes 262144 | tf_op jit(solution)/shard_map/all_to_all | solution.py:65
  213.2 7.3 %shard_map.109 = bf16[8,64,4096]{2,1,0:T(8,128)(2,1)} custom-call(s32[1]{0:T(128)} %bitcast.4.place, bf16[8,32,512]{2,1,0:T(8,128)(2,1)S(1)} %all-to-all-done.5.grads, f32[1,4096]{1,0:T(1,128)S(1)} %bitcast.35, f32[8,64,8]{2,1,0:T(8,128)S(1)} %pad.18.notes, bf16[64,4096]{1,0:T(8,128)(2,1)} %get-tuple-element.97.rest_0_, bf16[64,4096]{1,0:T(8,128)(2,1)} %copy-done.3, ...), custom_call_target="tpu_custom_call" | custom-call | flops 25165824 | bytes 9437184 | tf_op jit(solution)/shard_map/pallas_call | solution.py:569
  221.2 3.5 %all-to-all-start.8 = ((f32[16,16,128]{2,1,0:T(8,128)}), f32[16,16,128]{2,1,0:T(8,128)S(1)}, u32[]{:S(2)}, u32[]{:S(2)}) async-start(f32[16,16,128]{2,1,0:T(8,128)} %broadcast_in_dim.102), calls=%async_computation.8 | async-start | bytes 262144 | tf_op jit(solution)/shard_map/all_to_all | solution.py:65
  225.5 6.5 %shard_map.110 = bf16[192,4096]{1,0:T(8,128)(2,1)} custom-call(f32[192,4096]{1,0:T(8,128)} %get-tuple-element.59.x.summed_in.summed, f32[4,4096]{1,0:T(4,128)} %get-tuple-element.106.weighted, f32[192,128]{1,0:T(8,128)} %get-tuple-element.107.state, bf16[128,4096]{1,0:T(8,128)(2,1)S(1)} %pad.19.router), custom_call_target="tpu_custom_call" | custom-call | flops 201326592 | bytes 5242880 | tf_op jit(solution)/shard_map/pallas_call | solution.py:506
  (78 shorter events, 22.8 us)
Async XLA Ops:
  0.6 7.7 %copy-start.8 = (s32[192,2]{0,1:T(2,128)S(1)}, s32[192,2]{0,1:T(2,128)}, u32[]{:S(2)}) copy-start(s32[192,2]{0,1:T(2,128)} %param.8) | copy-start | bytes 4612
  0.6 7.8 %copy-start = (bf16[192,4096]{1,0:T(8,128)(2,1)S(1)}, bf16[192,4096]{1,0:T(8,128)(2,1)}, u32[]{:S(2)}) copy-start(bf16[192,4096]{1,0:T(8,128)(2,1)} %tok_in.1) | copy-start | bytes 4718596
  0.7 7.8 %copy-start.7 = (bf16[4096,8]{0,1:T(8,128)(2,1)S(1)}, bf16[4096,8]{0,1:T(8,128)(2,1)}, u32[]{:S(2)}) copy-start(bf16[4096,8]{0,1:T(8,128)(2,1)} %param.11) | copy-start | bytes 196612
  0.7 56.4 %copy-start.1 = (f32[4096]{0:T(1024)S(1)}, f32[4096]{0:T(1024)}, u32[]{:S(2)}) copy-start(f32[4096]{0:T(1024)} %param.12) | copy-start | bytes 49156
  0.7 56.3 %all-to-all-start = ((bf16[8,64,4096]{2,1,0:T(8,128)(2,1)}), bf16[8,64,4096]{2,1,0:T(8,128)(2,1)}, u32[]{:S(2)}, u32[]{:S(2)}) async-start(bf16[8,64,4096]{2,1,0:T(8,128)(2,1)} %bitcast.37), calls=%async_computation | async-start | bytes 8388608 | tf_op jit(solution)/shard_map/all_to_all | solution.py:65
  65.2 21.0 %copy-start.9 = (s32[2]{0:T(128)S(1)}, s32[2]{0:T(128)}, u32[]{:S(2)}) copy-start(s32[2]{0:T(128)} %param.9) | copy-start | bytes 28
  65.2 11.8 %all-to-all-start.1 = ((bf16[8,4,512]{2,1,0:T(4,128)(2,1)}), bf16[8,4,512]{2,1,0:T(4,128)(2,1)S(1)}, u32[]{:S(2)}, u32[]{:S(2)}) async-start(bf16[8,4,512]{2,1,0:T(4,128)(2,1)} %get-tuple-element.58), calls=%async_computation.1 | async-start | bytes 65536 | tf_op jit(solution)/shard_map/all_to_all | solution.py:65
  77.9 21.1 %all-to-all-start.2 = ((bf16[16,32,512]{2,1,0:T(8,128)(2,1)}), bf16[16,32,512]{2,1,0:T(8,128)(2,1)S(1)}, u32[]{:S(2)}, u32[]{:S(2)}) async-start(bf16[16,32,512]{2,1,0:T(8,128)(2,1)} %broadcast_in_dim.89), calls=%async_computation.2 | async-start | bytes 1048576 | tf_op jit(solution)/shard_map/all_to_all | solution.py:65
  88.1 20.7 %collective-permute-start.1 = (bf16[64,4096]{1,0:T(8,128)(2,1)}, bf16[64,4096]{1,0:T(8,128)(2,1)S(1)}, u32[]{:S(2)}, u32[]{:S(2)}) collective-permute-start(bf16[64,4096]{1,0:T(8,128)(2,1)} %get-tuple-element.73), channel_id=1, source_target_pairs={{0,1},{1,2},{2,3},{3,4},{4,5},{5,6},{6,7},{7,0},{8,9},{9,10},{10,1... | collective-permute-start | bytes 1572872 | tf_op jit(solution)/shard_map/ppermute | solution.py:626
  88.7 20.1 %collective-permute-start.2 = (bf16[64,4096]{1,0:T(8,128)(2,1)}, bf16[64,4096]{1,0:T(8,128)(2,1)S(1)}, u32[]{:S(2)}, u32[]{:S(2)}) collective-permute-start(bf16[64,4096]{1,0:T(8,128)(2,1)} %get-tuple-element.74), channel_id=1, source_target_pairs={{0,7},{1,0},{2,1},{3,2},{4,3},{5,4},{6,5},{7,6},{8,15},{9,8},{10,9... | collective-permute-start | bytes 1572872 | tf_op jit(solution)/shard_map/ppermute | solution.py:626
  99.0 4.8 %collective-permute-start = (bf16[16,32,512]{2,1,0:T(8,128)(2,1)S(1)}, bf16[16,32,512]{2,1,0:T(8,128)(2,1)S(1)}, u32[]{:S(2)}, u32[]{:S(2)}) collective-permute-start(bf16[16,32,512]{2,1,0:T(8,128)(2,1)S(1)} %all-to-all-done.2), channel_id=1, source_target_pairs={{0,8},{8,0},{1,9},{9,1},{2,10},{10,2},{3,11},{11,3},{4,12},{12,4},... | collective-permute-start | bytes 1572872 | tf_op jit(solution)/shard_map/ppermute | solution.py:61
  108.8 37.5 %copy-start.3 = (bf16[64,4096]{1,0:T(8,128)(2,1)}, bf16[64,4096]{1,0:T(8,128)(2,1)S(1)}, u32[]{:S(2)}) copy-start(bf16[64,4096]{1,0:T(8,128)(2,1)S(1)} %collective-permute-done.1.rest_1_) | copy-start | bytes 1572868
  108.8 37.5 %copy-start.4 = (bf16[64,4096]{1,0:T(8,128)(2,1)}, bf16[64,4096]{1,0:T(8,128)(2,1)S(1)}, u32[]{:S(2)}) copy-start(bf16[64,4096]{1,0:T(8,128)(2,1)S(1)} %collective-permute-done.2.rest_7_) | copy-start | bytes 1572868
  108.8 13.9 %all-to-all-start.3 = ((f32[8,40,512]{2,1,0:T(8,128)}), f32[8,40,512]{2,1,0:T(8,128)S(1)}, u32[]{:S(2)}, u32[]{:S(2)}) async-start(f32[8,40,512]{2,1,0:T(8,128)} %shard_map.104), calls=%async_computation.3 | async-start | bytes 1310720 | tf_op jit(solution)/shard_map/all_to_all | solution.py:65
  113.3 33.0 %collective-permute-start.3 = (bf16[64,4096]{1,0:T(8,128)(2,1)}, bf16[64,4096]{1,0:T(8,128)(2,1)}, u32[]{:S(2)}, u32[]{:S(2)}) collective-permute-start(bf16[64,4096]{1,0:T(8,128)(2,1)} %get-tuple-element.82), channel_id=1, source_target_pairs={{0,4},{1,5},{2,6},{3,7},{4,0},{5,1},{6,2},{7,3},{8,12},{9,13},{10,... | collective-permute-start | bytes 1572872 | tf_op jit(solution)/shard_map/ppermute | solution.py:626
  116.3 30.4 %collective-permute-start.4 = (bf16[64,4096]{1,0:T(8,128)(2,1)}, bf16[64,4096]{1,0:T(8,128)(2,1)}, u32[]{:S(2)}, u32[]{:S(2)}) collective-permute-start(bf16[64,4096]{1,0:T(8,128)(2,1)} %get-tuple-element.83), channel_id=1, source_target_pairs={{0,3},{1,4},{2,5},{3,6},{4,7},{5,0},{6,1},{7,2},{8,11},{9,12},{10,... | collective-permute-start | bytes 1572872 | tf_op jit(solution)/shard_map/ppermute | solution.py:626
  123.7 23.0 %all-to-all-start.4 = ((f32[32,8,128]{2,1,0:T(8,128)}), f32[32,8,128]{2,1,0:T(8,128)S(1)}, u32[]{:S(2)}, u32[]{:S(2)}) async-start(f32[32,8,128]{2,1,0:T(8,128)} %get-tuple-element.81), calls=%async_computation.4 | async-start | bytes 262144 | tf_op jit(solution)/shard_map/all_to_all | solution.py:65
  136.1 30.5 %collective-permute-start.5 = (bf16[64,4096]{1,0:T(8,128)(2,1)}, bf16[64,4096]{1,0:T(8,128)(2,1)}, u32[]{:S(2)}, u32[]{:S(2)}) collective-permute-start(bf16[64,4096]{1,0:T(8,128)(2,1)} %get-tuple-element.92), channel_id=1, source_target_pairs={{0,5},{1,6},{2,7},{3,0},{4,1},{5,2},{6,3},{7,4},{8,13},{9,14},{10,... | collective-permute-start | bytes 1572872 | tf_op jit(solution)/shard_map/ppermute | solution.py:626
  137.8 8.9 %copy-start.2 = (f32[48,512]{1,0:T(8,128)S(1)}, f32[48,512]{1,0:T(8,128)}, u32[]{:S(2)}) copy-start(f32[48,512]{1,0:T(8,128)} %get-tuple-element.87.kept) | copy-start | bytes 294916
  148.6 18.0 %all-to-all-start.5 = ((bf16[8,32,512]{2,1,0:T(8,128)(2,1)}), bf16[8,32,512]{2,1,0:T(8,128)(2,1)S(1)}, u32[]{:S(2)}, u32[]{:S(2)}) async-start(bf16[8,32,512]{2,1,0:T(8,128)(2,1)} %get-tuple-element.91), calls=%async_computation.5 | async-start | bytes 524288 | tf_op jit(solution)/shard_map/all_to_all | solution.py:65
  159.0 52.7 %collective-permute-start.6 = (bf16[64,4096]{1,0:T(8,128)(2,1)}, bf16[64,4096]{1,0:T(8,128)(2,1)S(1)}, u32[]{:S(2)}, u32[]{:S(2)}) collective-permute-start(bf16[64,4096]{1,0:T(8,128)(2,1)} %get-tuple-element.99), channel_id=1, source_target_pairs={{0,2},{1,3},{2,4},{3,5},{4,6},{5,7},{6,0},{7,1},{8,10},{9,11},{10,... | collective-permute-start | bytes 1572872 | tf_op jit(solution)/shard_map/ppermute | solution.py:626
  162.0 49.7 %collective-permute-start.7 = (bf16[64,4096]{1,0:T(8,128)(2,1)}, bf16[64,4096]{1,0:T(8,128)(2,1)S(1)}, u32[]{:S(2)}, u32[]{:S(2)}) collective-permute-start(bf16[64,4096]{1,0:T(8,128)(2,1)} %get-tuple-element.103), channel_id=1, source_target_pairs={{0,6},{1,7},{2,0},{3,1},{4,2},{5,3},{6,4},{7,5},{8,14},{9,15},{10,... | collective-permute-start | bytes 1572872 | tf_op jit(solution)/shard_map/ppermute | solution.py:626
  186.2 34.3 %all-to-all-start.7 = ((f32[16,16,128]{2,1,0:T(8,128)}), f32[16,16,128]{2,1,0:T(8,128)S(1)}, u32[]{:S(2)}, u32[]{:S(2)}) async-start(f32[16,16,128]{2,1,0:T(8,128)} %broadcast_in_dim.101), calls=%async_computation.7 | async-start | bytes 262144 | tf_op jit(solution)/shard_map/all_to_all | solution.py:65
  221.2 11.0 %all-to-all-start.8 = ((f32[16,16,128]{2,1,0:T(8,128)}), f32[16,16,128]{2,1,0:T(8,128)S(1)}, u32[]{:S(2)}, u32[]{:S(2)}) async-start(f32[16,16,128]{2,1,0:T(8,128)} %broadcast_in_dim.102), calls=%async_computation.8 | async-start | bytes 262144 | tf_op jit(solution)/shard_map/all_to_all | solution.py:65
  (2 other events, 1.6 us)

commit v7 on v6

--- a/solution.py
+++ b/solution.py
@@ -20,7 +20,8 @@
 SMEM = pl.BlockSpec(memory_space=pltpu.SMEM)
 HBM = pl.BlockSpec(memory_space=pltpu.HBM)
 NT = (((1,), (1,)), ((), ()))
-TURNS = ((1, 7), (4, 3), (5,), (2, 6))
+TURNS = ((4, 1, 7), (3, 5), (2, 6))
+SHARED = 6
 
 
 def iota(shape, dim):
@@ -90,7 +91,8 @@
 
 
 def forward_kernel(
-    steps, tok, rec, slot, gate, gain, summed, sliced_out, inverse, held, square, picks, sliced, row_sem, slice_sem
+    steps, tok, rec, slot, gate, gain, summed, sliced_out, rows_out, inverse,
+    held, square, picks, sliced, rounded, row_sem, slice_sem, rounded_sem
 ):
     step = pl.program_id(0)
     rows, part = tok.shape
@@ -98,6 +100,12 @@
     def keep(e):
         start = pl.multiple_of(e * part, part)
         return pltpu.make_async_copy(held.at[e], summed.at[:, pl.ds(start, part)], row_sem.at[e])
+
+    shared = rounded.shape[0]
+
+    def share(e):
+        start = pl.multiple_of(e * part, part)
+        return pltpu.make_async_copy(rounded.at[e], rows_out.at[:, pl.ds(start, part)], rounded_sem.at[e])
 
     @pl.when(step == 0)
     def _():
@@ -111,6 +119,11 @@
         held[step, :, cols] = x
         square[...] += fold(x * x)
     keep(step).start()
+
+    @pl.when(step < shared)
+    def _():
+        rounded[step] = held[step].astype(BF16)
+        share(step).start()
 
     @pl.when(step == steps - 1)
     def _():
@@ -126,6 +139,8 @@
         offer.start()
         for e in range(steps):
             keep(e).wait()
+        for e in range(shared):
+            share(e).wait()
         offer.wait()
 
 
@@ -144,10 +159,11 @@
             whole((rows, 2)),
             whole((1, width)),
         ],
-        out_specs=[HBM, HBM, whole((rows, 1))],
+        out_specs=[HBM, HBM, HBM, whole((rows, 1))],
         out_shape=[
             pltpu.HBM((rows, width), F32),
             pltpu.HBM((experts, rows // SEQ, part), BF16),
+            pltpu.HBM((rows, SHARED * part), BF16),
             jax.ShapeDtypeStruct((rows, 1), F32),
         ],
         scratch_shapes=[
@@ -155,10 +171,12 @@
             pltpu.VMEM((rows, 128), F32),
             pltpu.VMEM((2 * rows, slots), BF16),
             pltpu.VMEM((experts, rows // SEQ, part), BF16),
+            pltpu.VMEM((SHARED, rows, part), BF16),
             pltpu.SemaphoreType.DMA((experts,)),
             pltpu.SemaphoreType.DMA(()),
-        ],
-        compiler_params=params(14),
+            pltpu.SemaphoreType.DMA((SHARED,)),
+        ],
+        compiler_params=params(16),
         cost_estimate=cost(4 * rows * slots * width, 10 << 20),
     )(tokens, received, slot, gates, gain)
 
@@ -198,26 +216,26 @@
 
 def pack(place, summed, turned, experts, capacity):
     rows, width = summed.shape
-    steps = experts // 2
-    part = width // steps
+    part = width // experts
+    steps = experts - SHARED
     slots = experts * capacity
     return pl.pallas_call(
         pack_kernel,
         grid=(steps,),
         in_specs=[
             SMEM,
-            pl.BlockSpec((rows, part), lambda i: (0, i)),
+            pl.BlockSpec((rows, part), lambda i: (0, i + SHARED)),
             pl.BlockSpec((2, rows), lambda i: (0, 0)),
         ],
         out_specs=[HBM] * experts,
-        out_shape=[pltpu.HBM((capacity, width), BF16)] * experts,
+        out_shape=[pltpu.HBM((capacity, steps * part), BF16)] * experts,
         scratch_shapes=[
             pltpu.VMEM((slots, rows), BF16),
             pltpu.VMEM((steps, slots, part), BF16),
             pltpu.SemaphoreType.DMA((steps, experts)),
         ],
         compiler_params=params(14),
-        cost_estimate=cost(2 * rows * slots * width, 7 << 20),
+        cost_estimate=cost(2 * rows * slots * steps * part, 2 << 20),
     )(place, *in_hbm(summed), turned)
 
 
@@ -519,51 +537,69 @@
     )(*in_hbm(summed, weighted, state), router)
 
 
-def expert_kernel(place, grads, gain, notes, *rest):
-    *sources, out, backs, sems = rest
+def expert_kernel(place, grads, gain, notes, shared_in, *rest):
+    *sources, out, backs, shared, row, sems, shared_sems = rest
     experts = len(sources)
     _, _, part = grads.shape
     step = pl.program_id(0)
-    source = lax.rem(place[0] + experts - step, experts)
-    gate, inv, seq = notes[0, :, 0:1], notes[0, :, 1:2], notes[0, :, 2:3]
-    capacity = gate.shape[0]
-    loads = [pltpu.make_async_copy(sources[r], backs.at[r], sems.at[r]) for r in range(experts)]
+    rows = shared.shape[1]
+    capacity = row.shape[0]
+    split = shared.shape[2] // part
+    gate, inv, token = notes[0, :, 0:1], notes[0, :, 1:2], notes[0, :, 2:3]
+
+    def origin(r):
+        return lax.rem(place[0] + experts - r, experts)
+
+    def load(r):
+        start = pl.multiple_of(origin(r) * rows, rows)
+        return [
+            pltpu.make_async_copy(shared_in.at[pl.ds(start, rows)], shared.at[r], shared_sems.at[r]),
+            pltpu.make_async_copy(sources[r], backs.at[r], sems.at[r]),
+        ]
 
     @pl.when(step == 0)
     def _():
-        for load in loads:
-            load.start()
+        for r in range(experts):
+            for copy in load(r):
+                copy.start()
 
     for r in range(experts):
 
         @pl.when(step == r)
         def _():
-            loads[r].wait()
-            back = backs.at[r]
-            acc = jnp.zeros((capacity, 128), F32)
-            rows = []
-            for e in range(experts):
-                cols = slice(part * e, part * (e + 1))
-                w = rows_of(grads, e, source) * (gain[:, cols] / SEQ)
-                x = jnp.broadcast_to(w[0:1], (capacity, part))
-                for s in range(1, ROWS_DEV):
-                    x = jnp.where(seq == s, w[s : s + 1], x)
-                rows.append(w)
-                acc = acc + fold(x * back[:, cols].astype(F32))
-            shrink = inv * inv * inv * (jnp.sum(acc, axis=1, keepdims=True) / (experts * part))
-            for e in range(experts):
-                cols = slice(part * e, part * (e + 1))
-                w = rows[e]
-                x = jnp.broadcast_to(w[0:1], (capacity, part))
-                for s in range(1, ROWS_DEV):
-                    x = jnp.where(seq == s, w[s : s + 1], x)
-                x = gate * (inv * x - shrink * back[:, cols].astype(F32))
-                out[0, :, cols] = x.astype(BF16)
-
-
-def expert_rows(place, grads, gain, notes, backs):
+            for copy in load(r):
+                copy.wait()
+
+    pick = (token.astype(I32) == iota((capacity, rows), 1)).astype(BF16)
+    acc = jnp.zeros((capacity, 128), F32)
+
+    def gradient_rows(e):
+        cols = slice(part * e, part * (e + 1))
+        w = rows_of(grads, e, origin(step)) * (gain[:, cols] / SEQ)
+        x = jnp.broadcast_to(w[0:1], (capacity, part))
+        for s in range(1, ROWS_DEV):
+            x = jnp.where(token >= s * SEQ, w[s : s + 1], x)
+        return x
+
+    for e in range(experts):
+        cols = slice(part * e, part * (e + 1))
+        if e < split:
+            back = jnp.dot(pick, shared[step, :, cols], preferred_element_type=F32)
+        else:
+            back = backs[step, :, part * (e - split) : part * (e - split + 1)].astype(F32)
+        row[:, cols] = back
+        acc = acc + fold(gradient_rows(e) * back)
+    shrink = inv * inv * inv * (jnp.sum(acc, axis=1, keepdims=True) / (experts * part))
+    keep, drop = gate * inv, gate * shrink
+    for e in range(experts):
+        cols = slice(part * e, part * (e + 1))
+        out[0, :, cols] = (keep * gradient_rows(e) - drop * row[:, cols]).astype(BF16)
+
+
+def expert_rows(place, grads, gain, notes, shared, backs):
     experts, capacity = notes.shape[:2]
     width = gain.shape[1]
+    rows = shared.shape[0] // experts
     whole = lambda shape: pl.BlockSpec(shape, lambda i, p: (0,) * len(shape))
     source = lambda i, p: (lax.rem(p[0] + experts - i, experts), 0, 0)
     return pl.pallas_call(
@@ -576,17 +612,20 @@
                 whole((1, width)),
                 pl.BlockSpec((1, capacity, notes.shape[2]), source),
             ]
-            + [HBM] * experts,
+            + [HBM] * (experts + 1),
             out_specs=pl.BlockSpec((1, capacity, width), source),
             scratch_shapes=[
-                pltpu.VMEM((experts, capacity, width), BF16),
+                pltpu.VMEM((experts,) + backs[0].shape, BF16),
+                pltpu.VMEM((experts, rows, shared.shape[1]), BF16),
+                pltpu.VMEM((capacity, width), F32),
+                pltpu.SemaphoreType.DMA((experts,)),
                 pltpu.SemaphoreType.DMA((experts,)),
             ],
         ),
         out_shape=jax.ShapeDtypeStruct((experts, capacity, width), BF16),
-        compiler_params=params(16),
-        cost_estimate=cost(12 * experts * capacity * width, 9 << 20),
-    )(place, grads, gain, notes, *in_hbm(*backs))
+        compiler_params=params(24),
+        cost_estimate=cost(12 * experts * capacity * width, 15 << 20),
+    )(place, grads, gain, notes, *in_hbm(shared, *backs))
 
 
 def shards(tokens, routes, positives, expert_out, router, norm_gain, loss_scale):
@@ -612,7 +651,8 @@
         0,
     ).astype(F32)
 
-    summed, sliced, inverse = forward(tokens, received, slot, gates, gain, experts)
+    summed, sliced, rounded, inverse = forward(tokens, received, slot, gates, gain, experts)
+    shared = lax.all_gather(rounded, "expert", axis=0, tiled=True)
     own = exchange(sliced, "expert").reshape(2 * group, part)
     facts = jnp.concatenate(
         [jnp.zeros((rows, 2), F32), inverse, gates, routes.astype(F32)], axis=1
@@ -640,14 +680,15 @@
     )
     taken = picks[0] | picks[1]
     inverse_slot = jnp.sum(jnp.where(taken, inverse, 0.0), axis=0)
-    sequence = (jnp.arange(rows, dtype=I32) // SEQ).astype(F32)
-    sequence_slot = jnp.sum(jnp.where(taken, sequence[:, None], 0.0), axis=0)
-    notes = jnp.stack([gate_slot, inverse_slot, sequence_slot, spread_positive])
+    order = jnp.arange(rows, dtype=I32).astype(F32)
+    token_slot = jnp.sum(jnp.where(taken, order[:, None], 0.0), axis=0)
+    notes = jnp.stack([gate_slot, inverse_slot, token_slot, spread_positive])
     notes = jnp.pad(notes, ((0, 4), (0, 0)))
 
     own, *backs = lax.optimization_barrier((own, *backs))
-    own = move(own, TURNS[0])
     near = spread(own, "u", outer)
+    facts, fetched = overlaps(summed, received, slot, facts, experts)
+    near, facts, fetched = lax.optimization_barrier((near, facts, fetched))
     far = swap_core(near)
     near, far = near.reshape(columns, part), far.reshape(columns, part)
     offered = pl.pallas_call(
@@ -658,9 +699,9 @@
         scratch_shapes=[pltpu.VMEM((2 * group + 8, columns), F32), pltpu.SemaphoreType.DMA((experts,))],
         compiler_params=params(2),
     )(own, near, far, notes)
-    offered = landed(offered, TURNS[0])
-    offered = move(offered, TURNS[1])
+    offered = move(offered, TURNS[0])
     gathered = exchange(offered, "expert")
+    gathered = landed(gathered, TURNS[0])
     devices = outer * CORES
     offered, kept = pl.pallas_call(
         functools.partial(totals_kernel, scale),
@@ -675,11 +716,9 @@
         ],
         compiler_params=params(2),
     )(gathered)
-    offered = move(offered, TURNS[2])
+    offered = move(offered, TURNS[1])
     heard = exchange(offered, ("u", "c"))
     heard = landed(heard, TURNS[1])
-    facts, fetched = overlaps(summed, received, slot, facts, experts)
-    heard, facts = lax.optimization_barrier((heard, facts))
     offered, loss = pl.pallas_call(
         functools.partial(gradient_kernel, scale),
         in_specs=[SMEM] + [VMEM] * 4,
@@ -688,7 +727,7 @@
         scratch_shapes=[pltpu.VMEM((2 * group, part), BF16), pltpu.SemaphoreType.DMA((experts,))],
         compiler_params=params(2),
     )((loss_scale / pairs)[None], heard, kept, near, far)
-    offered = move(offered, TURNS[3])
+    offered = move(offered, TURNS[2])
     grads = exchange(offered, "expert")
     grads = landed(grads, TURNS[2])
 
@@ -720,13 +759,13 @@
     router_part = spread(router_part, ("c", "expert"), CORES * experts)
     held = lax.dynamic_slice_in_dim(gathered[:, 2 * group : 2 * group + 3], mine * capacity, capacity, axis=2)
     held = jnp.pad(jnp.transpose(held, (0, 2, 1)), ((0, 0), (0, 0), (0, 5)))
-    expert_grad = expert_rows(mine_at, grads, gain, held, backs)
     turned = jnp.pad(router.T, ((0, 128 - experts), (0, 0)))
-    router_part, expert_grad = lax.optimization_barrier((router_part, expert_grad))
+    token_grad = token_rows(summed, weighted, state, turned, experts)
+    router_part, token_grad = lax.optimization_barrier((router_part, token_grad))
     router_part = jnp.sum(router_part, axis=0)
-    token_grad = token_rows(summed, weighted, state, turned, experts)
     router_all = spread(router_part, "u", outer)
-    router_all, token_grad = lax.optimization_barrier((router_all, token_grad))
+    expert_grad = expert_rows(mine_at, grads, gain, held, shared, backs)
+    router_all, expert_grad = lax.optimization_barrier((router_all, expert_grad))
     router_grad = router_all.reshape(-1, experts, 128).transpose(1, 0, 2).reshape(experts, width).T
     return token_grad, expert_grad.reshape(1, 1, experts, capacity, width), router_grad, loss[0, 0] / pairs
 

time: 236 us -> 244 us (1.034)
  starting transfers between devices: 97.9 us -> 72.4 us
  waiting for transfers between devices: 64.1 us -> 83.4 us
  between operations: 3.49 us -> 17 us
    all_to_all x8, starting transfers between devices: 77.2 us -> 51.5 us  [exchange(): return lax.all_to_all(x, axes, split_axis=0, concat_axis=0, tiled=True)]
    ppermute x7, waiting for transfers between devices: 3.83 us -> 28.1 us  [move(): lax.ppermute(x, 'expert', [(i, (i + r) % experts) for i in range(experts)])]
    all_to_all x8, waiting for transfers between devices: 59.5 us -> 54.5 us  [exchange(): return lax.all_to_all(x, axes, split_axis=0, concat_axis=0, tiled=True)]
    pallas_call x1, Pallas kernels: 7.25 us -> 10.5 us  [expert_rows(): pl.pallas_call(expert_kernel, grid_spec=pltpu.PrefetchScalarGridSpec(num_...]
    pallas_call x1, Pallas kernels: 5.66 us -> 2.68 us  [pack(): pl.pallas_call(pack_kernel, grid=(steps,), in_specs=[SMEM, pl.BlockSpec((...]
  transfers between devices with their start and end apart: 16 -> 17, of which waited for: 9 -> 9; matrix products, arithmetic and copies ran while one was open for 2% -> 3% of each run, Pallas kernels for 16% -> 16%
where the time goes in v7:
time: 244 us; the launch traced here: 242 us
  waiting for transfers between devices  83.4 us (34%)
  starting transfers between devices  72.4 us (30%)
  Pallas kernels  47.3 us (19%)
  between operations  17 us (7%)
  blocking collectives  13.7 us (6%)
  local copies, waits for them, and re-layouts  5.82 us (2%)
    all_to_all x8, waiting for transfers between devices, exchange(): return lax.all_to_all(x, axes, split_axis=0, concat_axis=0, tiled=True)  54.5 us
    all_to_all x8, starting transfers between devices, exchange(): return lax.all_to_all(x, axes, split_axis=0, concat_axis=0, tiled=True)  51.5 us
    ppermute x7, waiting for transfers between devices, move(): lax.ppermute(x, 'expert', [(i, (i + r) % experts) for i in range(experts)])  28.1 us
    ppermute x7, starting transfers between devices, move(): lax.ppermute(x, 'expert', [(i, (i + r) % experts) for i in range(experts)])  17.6 us
    all_to_all x1, blocking collectives, exchange(): return lax.all_to_all(x, axes, split_axis=0, concat_axis=0, tiled=True)  13.7 us
    pallas_call x1, Pallas kernels, expert_rows(): pl.pallas_call(expert_kernel, grid_spec=pltpu.PrefetchScalarGridSpec(num_...  10.5 us
    pallas_call x1, Pallas kernels, overlaps(): pl.pallas_call(functools.partial(overlap_kernel, experts), grid=(experts,...  8.49 us
    pallas_call x1, Pallas kernels, forward(): pl.pallas_call(functools.partial(forward_kernel, experts), grid=(experts,...  8.4 us
  transfers between devices with their start and end apart: 17, of which 9 were waited for; matrix products, arithmetic and copies ran while one was open for 3% of the time, Pallas kernels for 16%

profile of v7, /device:TPU:1, one launch (start us, length us, event | category | flops | bytes accessed | tf_op | source)
XLA Modules:
  0.0 242.3 jit_solution(11845510556527398539)
XLA Ops:
  7.2 7.6 %all-to-all-start = ((bf16[8,64,4096]{2,1,0:T(8,128)(2,1)}), bf16[8,64,4096]{2,1,0:T(8,128)(2,1)}, u32[]{:S(2)}, u32[]{:S(2)}) async-start(bf16[8,64,4096]{2,1,0:T(8,128)(2,1)} %bitcast.37), calls=%async_computation | async-start | bytes 8388608 | tf_op jit(solution)/shard_map/all_to_all | solution.py:66
  16.3 47.2 %all-to-all-done = bf16[8,64,4096]{2,1,0:T(8,128)(2,1)} async-done(((bf16[8,64,4096]{2,1,0:T(8,128)(2,1)}), bf16[8,64,4096]{2,1,0:T(8,128)(2,1)}, u32[]{:S(2)}, u32[]{:S(2)}) %all-to-all-start) | async-done | bytes 4194336 | tf_op jit(solution)/shard_map/all_to_all | solution.py:66
  63.6 8.4 %shard_map.102 = (f32[192,4096]{1,0:T(8,128)}, bf16[8,4,512]{2,1,0:T(4,128)(2,1)}, bf16[192,3072]{1,0:T(8,128)(2,1)}, f32[192,1]{1,0:T(8,128)S(1)}) custom-call(bf16[192,4096]{1,0:T(8,128)(2,1)S(1)} %copy-done, bf16[512,4096]{1,0:T(8,128)(2,1)} %bitcast.2.rec, s32[192,2]{1,0:T(8,128)S(1)} %add.53.slot, f32[192,2]{1,0:T(8,128)S(1)} %exponential_divide_fusion.gate, ...), custom_call_target="tpu_custom_call" | custom-call | flops 1610612736 | bytes 10485760 | tf_op jit(solution)/shard_map/pallas_call | solution.py:152
  72.0 5.2 %all-to-all-start.1 = ((bf16[8,4,512]{2,1,0:T(4,128)(2,1)}), bf16[8,4,512]{2,1,0:T(4,128)(2,1)S(1)}, u32[]{:S(2)}, u32[]{:S(2)}) async-start(bf16[8,4,512]{2,1,0:T(4,128)(2,1)} %get-tuple-element.61), calls=%async_computation.1 | async-start | bytes 65536 | tf_op jit(solution)/shard_map/all_to_all | solution.py:66
  80.0 3.8 %all-to-all-done.1 = bf16[8,4,512]{2,1,0:T(4,128)(2,1)S(1)} async-done(((bf16[8,4,512]{2,1,0:T(4,128)(2,1)}), bf16[8,4,512]{2,1,0:T(4,128)(2,1)S(1)}, u32[]{:S(2)}, u32[]{:S(2)}) %all-to-all-start.1) | async-done | bytes 32800 | tf_op jit(solution)/shard_map/all_to_all | solution.py:66
  84.7 8.3 %all-to-all-start.2 = ((bf16[16,32,512]{2,1,0:T(8,128)(2,1)}), bf16[16,32,512]{2,1,0:T(8,128)(2,1)S(1)}, u32[]{:S(2)}, u32[]{:S(2)}) async-start(bf16[16,32,512]{2,1,0:T(8,128)(2,1)} %broadcast_in_dim.89), calls=%async_computation.2 | async-start | bytes 1048576 | tf_op jit(solution)/shard_map/all_to_all | solution.py:66
  95.2 8.5 %shard_map.104 = (f32[192,128]{1,0:T(8,128)}, bf16[384,4096]{1,0:T(8,128)(2,1)}) custom-call(f32[192,4096]{1,0:T(8,128)} %get-tuple-element.62.x.summed_in.summed, bf16[512,4096]{1,0:T(8,128)(2,1)} %bitcast.2.rec, s32[192,2]{1,0:T(8,128)S(1)} %add.53.slot, f32[192,128]{1,0:T(8,128)S(1)} %pad.16.facts), custom_call_target="tpu_custom_call" | custom-call | flops 1610612736 | bytes 10485760 | tf_op jit(solution)/shard_map/pallas_call | solution.py:274
  105.8 3.3 %collective-permute-start = (bf16[16,32,512]{2,1,0:T(8,128)(2,1)S(1)}, bf16[16,32,512]{2,1,0:T(8,128)(2,1)S(1)}, u32[]{:S(2)}, u32[]{:S(2)}) collective-permute-start(bf16[16,32,512]{2,1,0:T(8,128)(2,1)S(1)} %all-to-all-done.2), channel_id=1, source_target_pairs={{0,8},{8,0},{1,9},{9,1},{2,10},{10,2},{3,11},{11,3},{4,12},{12,4},... | collective-permute-start | bytes 1572872 | tf_op jit(solution)/shard_map/ppermute | solution.py:62
  112.2 3.6 %all-to-all-start.3 = ((f32[8,40,512]{2,1,0:T(8,128)}), f32[8,40,512]{2,1,0:T(8,128)S(1)}, u32[]{:S(2)}, u32[]{:S(2)}) async-start(f32[8,40,512]{2,1,0:T(8,128)} %shard_map.105), calls=%async_computation.3 | async-start | bytes 1310720 | tf_op jit(solution)/shard_map/all_to_all | solution.py:66
  119.9 3.9 %collective-permute-start.3 = (bf16[64,1024]{1,0:T(8,128)(2,1)S(1)}, bf16[64,1024]{1,0:T(8,128)(2,1)S(1)}, u32[]{:S(2)}, u32[]{:S(2)}) collective-permute-start(bf16[64,1024]{1,0:T(8,128)(2,1)S(1)} %copy-done.17), channel_id=1, source_target_pairs={{0,7},{1,0},{2,1},{3,2},{4,3},{5,4},{6,5},{7,6},{8,15},{9,8},{10,9... | collective-permute-start | bytes 393224 | tf_op jit(solution)/shard_map/ppermute | solution.py:666
  123.8 5.1 %collective-permute-done.1.rest_4_ = bf16[64,1024]{1,0:T(8,128)(2,1)S(1)} collective-permute-done((bf16[64,1024]{1,0:T(8,128)(2,1)S(1)}, bf16[64,1024]{1,0:T(8,128)(2,1)S(1)}, u32[]{:S(2)}, u32[]{:S(2)}) %collective-permute-start.1) | collective-permute-done | bytes 131104 | tf_op jit(solution)/shard_map/ppermute | solution.py:666
  128.9 4.9 %collective-permute-done.2.rest_1_ = bf16[64,1024]{1,0:T(8,128)(2,1)S(1)} collective-permute-done((bf16[64,1024]{1,0:T(8,128)(2,1)S(1)}, bf16[64,1024]{1,0:T(8,128)(2,1)S(1)}, u32[]{:S(2)}, u32[]{:S(2)}) %collective-permute-start.2) | collective-permute-done | bytes 131104 | tf_op jit(solution)/shard_map/ppermute | solution.py:666
  134.8 6.8 %all-to-all-start.4 = ((f32[32,8,128]{2,1,0:T(8,128)}), f32[32,8,128]{2,1,0:T(8,128)S(1)}, u32[]{:S(2)}, u32[]{:S(2)}) async-start(f32[32,8,128]{2,1,0:T(8,128)} %get-tuple-element.87), calls=%async_computation.4 | async-start | bytes 262144 | tf_op jit(solution)/shard_map/all_to_all | solution.py:66
  141.9 3.6 %collective-permute-start.5 = (bf16[64,1024]{1,0:T(8,128)(2,1)S(1)}, bf16[64,1024]{1,0:T(8,128)(2,1)S(1)}, u32[]{:S(2)}, u32[]{:S(2)}) collective-permute-start(bf16[64,1024]{1,0:T(8,128)(2,1)S(1)} %copy-done.15), channel_id=1, source_target_pairs={{0,5},{1,6},{2,7},{3,0},{4,1},{5,2},{6,3},{7,4},{8,13},{9,14},{10,... | collective-permute-start | bytes 393224 | tf_op jit(solution)/shard_map/ppermute | solution.py:666
  146.2 6.3 %collective-permute-done.4.rest_3_ = bf16[64,1024]{1,0:T(8,128)(2,1)S(1)} collective-permute-done((bf16[64,1024]{1,0:T(8,128)(2,1)S(1)}, bf16[64,1024]{1,0:T(8,128)(2,1)S(1)}, u32[]{:S(2)}, u32[]{:S(2)}) %collective-permute-start.4) | collective-permute-done | bytes 131104 | tf_op jit(solution)/shard_map/ppermute | solution.py:666
  155.4 9.3 %all-to-all-start.5 = ((bf16[8,32,512]{2,1,0:T(8,128)(2,1)}), bf16[8,32,512]{2,1,0:T(8,128)(2,1)S(1)}, u32[]{:S(2)}, u32[]{:S(2)}) async-start(bf16[8,32,512]{2,1,0:T(8,128)(2,1)} %get-tuple-element.95), calls=%async_computation.5 | async-start | bytes 524288 | tf_op jit(solution)/shard_map/all_to_all | solution.py:66
  164.8 3.0 %collective-permute-start.6 = (bf16[64,1024]{1,0:T(8,128)(2,1)S(1)}, bf16[64,1024]{1,0:T(8,128)(2,1)S(1)}, u32[]{:S(2)}, u32[]{:S(2)}) collective-permute-start(bf16[64,1024]{1,0:T(8,128)(2,1)S(1)} %copy-done.14), channel_id=1, source_target_pairs={{0,2},{1,3},{2,4},{3,5},{4,6},{5,7},{6,0},{7,1},{8,10},{9,11},{10,... | collective-permute-start | bytes 393224 | tf_op jit(solution)/shard_map/ppermute | solution.py:666
  170.4 11.8 %collective-permute-done.6.rest_2_ = bf16[64,1024]{1,0:T(8,128)(2,1)S(1)} collective-permute-done((bf16[64,1024]{1,0:T(8,128)(2,1)S(1)}, bf16[64,1024]{1,0:T(8,128)(2,1)S(1)}, u32[]{:S(2)}, u32[]{:S(2)}) %collective-permute-start.6) | collective-permute-done | bytes 131104 | tf_op jit(solution)/shard_map/ppermute | solution.py:666
  182.3 6.2 %shard_map.108 = (f32[256,128]{1,0:T(8,128)S(1)}, f32[192,128]{1,0:T(8,128)}, f32[4,4096]{1,0:T(4,128)}) custom-call(bf16[8,32,512]{2,1,0:T(8,128)(2,1)S(1)} %all-to-all-done.5.grads, f32[1,4096]{1,0:T(1,128)S(1)} %bitcast.34, f32[192,4096]{1,0:T(8,128)} %get-tuple-element.62.x.summed_in.summed, bf16[384,4096]{1,0:T(8,128)(2,1)} %get-tuple-element.99.fetched_in, ...), custom_call_target="tpu_custom_call" | custom-call | tf_op jit(solution)/shard_map/pallas_call | solution.py:734
  188.6 13.7 %all_to_all.45 = f32[16,16,128]{2,1,0:T(8,128)S(1)} all-to-all(f32[16,16,128]{2,1,0:T(8,128)S(1)} %bitcast.36), channel_id=1, replica_groups=mesh['u'=16,'c'=2,'expert'=8] {'u'}, dimensions={0} | all-to-all | bytes 262144 | tf_op jit(solution)/shard_map/all_to_all | solution.py:66
  202.9 7.2 %all-to-all-start.7 = ((f32[16,16,128]{2,1,0:T(8,128)}), f32[16,16,128]{2,1,0:T(8,128)S(1)}, u32[]{:S(2)}, u32[]{:S(2)}) async-start(f32[16,16,128]{2,1,0:T(8,128)} %broadcast_in_dim.101), calls=%async_computation.7 | async-start | bytes 262144 | tf_op jit(solution)/shard_map/all_to_all | solution.py:66
  210.2 6.5 %shard_map.109 = bf16[192,4096]{1,0:T(8,128)(2,1)} custom-call(f32[192,4096]{1,0:T(8,128)} %get-tuple-element.62.x.summed_in.summed, f32[4,4096]{1,0:T(4,128)} %get-tuple-element.102.weighted, f32[192,128]{1,0:T(8,128)} %get-tuple-element.103.state, bf16[128,4096]{1,0:T(8,128)(2,1)S(1)} %pad.18.router), custom_call_target="tpu_custom_call" | custom-call | flops 201326592 | bytes 5242880 | tf_op jit(solution)/shard_map/pallas_call | solution.py:524
  218.7 3.5 %all-to-all-start.8 = ((f32[16,16,128]{2,1,0:T(8,128)}), f32[16,16,128]{2,1,0:T(8,128)S(1)}, u32[]{:S(2)}, u32[]{:S(2)}) async-start(f32[16,16,128]{2,1,0:T(8,128)} %broadcast_in_dim.102), calls=%async_computation.8 | async-start | bytes 262144 | tf_op jit(solution)/shard_map/all_to_all | solution.py:66
  223.2 10.5 %shard_map.110 = bf16[8,64,4096]{2,1,0:T(8,128)(2,1)} custom-call(s32[1]{0:T(128)} %bitcast.4.place, bf16[8,32,512]{2,1,0:T(8,128)(2,1)S(1)} %all-to-all-done.5.grads, f32[1,4096]{1,0:T(1,128)S(1)} %bitcast.35, f32[8,64,8]{2,1,0:T(8,128)S(1)} %pad.19.notes, bf16[1536,3072]{1,0:T(8,128)(2,1)} %all-gather.2.cloned.1.call-done.shared_in, ...), custom_call_target="tpu_custom_call" | custom-call | flops 25165824 | bytes 15728640 | tf_op jit(solution)/shard_map/pallas_call | solution.py:605
  (101 shorter events, 27.2 us)
Async XLA Ops:
  7.2 56.4 %copy-start.1 = (f32[4096]{0:T(1024)S(1)}, f32[4096]{0:T(1024)}, u32[]{:S(2)}) copy-start(f32[4096]{0:T(1024)} %param.12) | copy-start | bytes 49156
  7.2 56.3 %all-to-all-start = ((bf16[8,64,4096]{2,1,0:T(8,128)(2,1)}), bf16[8,64,4096]{2,1,0:T(8,128)(2,1)}, u32[]{:S(2)}, u32[]{:S(2)}) async-start(bf16[8,64,4096]{2,1,0:T(8,128)(2,1)} %bitcast.37), calls=%async_computation | async-start | bytes 8388608 | tf_op jit(solution)/shard_map/all_to_all | solution.py:66
  14.8 208.4 %all-gather.2.cloned.1.call-start = ((), (), s32[]{:S(2)}) async-start(), calls=%async_computation.9 | async-start | bytes 10616832 | tf_op jit(solution)/shard_map/all_gather | solution.py:655
  72.0 11.8 %all-to-all-start.1 = ((bf16[8,4,512]{2,1,0:T(4,128)(2,1)}), bf16[8,4,512]{2,1,0:T(4,128)(2,1)S(1)}, u32[]{:S(2)}, u32[]{:S(2)}) async-start(bf16[8,4,512]{2,1,0:T(4,128)(2,1)} %get-tuple-element.61), calls=%async_computation.1 | async-start | bytes 65536 | tf_op jit(solution)/shard_map/all_to_all | solution.py:66
  84.7 21.1 %all-to-all-start.2 = ((bf16[16,32,512]{2,1,0:T(8,128)(2,1)}), bf16[16,32,512]{2,1,0:T(8,128)(2,1)S(1)}, u32[]{:S(2)}, u32[]{:S(2)}) async-start(bf16[16,32,512]{2,1,0:T(8,128)(2,1)} %broadcast_in_dim.89), calls=%async_computation.2 | async-start | bytes 1048576 | tf_op jit(solution)/shard_map/all_to_all | solution.py:66
  103.8 38.2 %copy-start.15 = (bf16[64,1024]{1,0:T(8,128)(2,1)S(1)}, bf16[64,1024]{1,0:T(8,128)(2,1)}, u32[]{:S(2)}) copy-start(bf16[64,1024]{1,0:T(8,128)(2,1)} %get-tuple-element.89) | copy-start | bytes 393220
  105.8 4.8 %collective-permute-start = (bf16[16,32,512]{2,1,0:T(8,128)(2,1)S(1)}, bf16[16,32,512]{2,1,0:T(8,128)(2,1)S(1)}, u32[]{:S(2)}, u32[]{:S(2)}) collective-permute-start(bf16[16,32,512]{2,1,0:T(8,128)(2,1)S(1)} %all-to-all-done.2), channel_id=1, source_target_pairs={{0,8},{8,0},{1,9},{9,1},{2,10},{10,2},{3,11},{11,3},{4,12},{12,4},... | collective-permute-start | bytes 1572872 | tf_op jit(solution)/shard_map/ppermute | solution.py:62
  109.1 55.7 %copy-start.14 = (bf16[64,1024]{1,0:T(8,128)(2,1)S(1)}, bf16[64,1024]{1,0:T(8,128)(2,1)}, u32[]{:S(2)}) copy-start(bf16[64,1024]{1,0:T(8,128)(2,1)} %get-tuple-element.96) | copy-start | bytes 393220
  109.1 58.6 %copy-start.13 = (bf16[64,1024]{1,0:T(8,128)(2,1)S(1)}, bf16[64,1024]{1,0:T(8,128)(2,1)}, u32[]{:S(2)}) copy-start(bf16[64,1024]{1,0:T(8,128)(2,1)} %get-tuple-element.97) | copy-start | bytes 393220
  112.2 21.6 %all-to-all-start.3 = ((f32[8,40,512]{2,1,0:T(8,128)}), f32[8,40,512]{2,1,0:T(8,128)S(1)}, u32[]{:S(2)}, u32[]{:S(2)}) async-start(f32[8,40,512]{2,1,0:T(8,128)} %shard_map.105), calls=%async_computation.3 | async-start | bytes 1310720 | tf_op jit(solution)/shard_map/all_to_all | solution.py:66
  115.8 13.1 %collective-permute-start.1 = (bf16[64,1024]{1,0:T(8,128)(2,1)S(1)}, bf16[64,1024]{1,0:T(8,128)(2,1)S(1)}, u32[]{:S(2)}, u32[]{:S(2)}) collective-permute-start(bf16[64,1024]{1,0:T(8,128)(2,1)S(1)} %copy-done.19), channel_id=1, source_target_pairs={{0,4},{1,5},{2,6},{3,7},{4,0},{5,1},{6,2},{7,3},{8,12},{9,13},{10,... | collective-permute-start | bytes 393224 | tf_op jit(solution)/shard_map/ppermute | solution.py:666
  118.7 15.1 %collective-permute-start.2 = (bf16[64,1024]{1,0:T(8,128)(2,1)S(1)}, bf16[64,1024]{1,0:T(8,128)(2,1)S(1)}, u32[]{:S(2)}, u32[]{:S(2)}) collective-permute-start(bf16[64,1024]{1,0:T(8,128)(2,1)S(1)} %copy-done.18), channel_id=1, source_target_pairs={{0,1},{1,2},{2,3},{3,4},{4,5},{5,6},{6,7},{7,0},{8,9},{9,10},{10,1... | collective-permute-start | bytes 393224 | tf_op jit(solution)/shard_map/ppermute | solution.py:666
  119.9 13.9 %collective-permute-start.3 = (bf16[64,1024]{1,0:T(8,128)(2,1)S(1)}, bf16[64,1024]{1,0:T(8,128)(2,1)S(1)}, u32[]{:S(2)}, u32[]{:S(2)}) collective-permute-start(bf16[64,1024]{1,0:T(8,128)(2,1)S(1)} %copy-done.17), channel_id=1, source_target_pairs={{0,7},{1,0},{2,1},{3,2},{4,3},{5,4},{6,5},{7,6},{8,15},{9,8},{10,9... | collective-permute-start | bytes 393224 | tf_op jit(solution)/shard_map/ppermute | solution.py:666
  128.9 59.6 %copy-start.4 = (bf16[64,1024]{1,0:T(8,128)(2,1)}, bf16[64,1024]{1,0:T(8,128)(2,1)S(1)}, u32[]{:S(2)}) copy-start(bf16[64,1024]{1,0:T(8,128)(2,1)S(1)} %collective-permute-done.1.rest_4_) | copy-start | bytes 393220
  133.8 54.7 %copy-start.5 = (bf16[64,1024]{1,0:T(8,128)(2,1)}, bf16[64,1024]{1,0:T(8,128)(2,1)S(1)}, u32[]{:S(2)}) copy-start(bf16[64,1024]{1,0:T(8,128)(2,1)S(1)} %collective-permute-done.2.rest_1_) | copy-start | bytes 393220
  133.8 54.7 %copy-start.6 = (bf16[64,1024]{1,0:T(8,128)(2,1)}, bf16[64,1024]{1,0:T(8,128)(2,1)S(1)}, u32[]{:S(2)}) copy-start(bf16[64,1024]{1,0:T(8,128)(2,1)S(1)} %collective-permute-done.3.rest_7_) | copy-start | bytes 393220
  134.8 17.7 %all-to-all-start.4 = ((f32[32,8,128]{2,1,0:T(8,128)}), f32[32,8,128]{2,1,0:T(8,128)S(1)}, u32[]{:S(2)}, u32[]{:S(2)}) async-start(f32[32,8,128]{2,1,0:T(8,128)} %get-tuple-element.87), calls=%async_computation.4 | async-start | bytes 262144 | tf_op jit(solution)/shard_map/all_to_all | solution.py:66
  141.6 10.9 %collective-permute-start.4 = (bf16[64,1024]{1,0:T(8,128)(2,1)S(1)}, bf16[64,1024]{1,0:T(8,128)(2,1)S(1)}, u32[]{:S(2)}, u32[]{:S(2)}) collective-permute-start(bf16[64,1024]{1,0:T(8,128)(2,1)S(1)} %copy-done.16), channel_id=1, source_target_pairs={{0,3},{1,4},{2,5},{3,6},{4,7},{5,0},{6,1},{7,2},{8,11},{9,12},{10,... | collective-permute-start | bytes 393224 | tf_op jit(solution)/shard_map/ppermute | solution.py:666
  141.9 10.5 %collective-permute-start.5 = (bf16[64,1024]{1,0:T(8,128)(2,1)S(1)}, bf16[64,1024]{1,0:T(8,128)(2,1)S(1)}, u32[]{:S(2)}, u32[]{:S(2)}) collective-permute-start(bf16[64,1024]{1,0:T(8,128)(2,1)S(1)} %copy-done.15), channel_id=1, source_target_pairs={{0,5},{1,6},{2,7},{3,0},{4,1},{5,2},{6,3},{7,4},{8,13},{9,14},{10,... | collective-permute-start | bytes 393224 | tf_op jit(solution)/shard_map/ppermute | solution.py:666
  155.4 26.8 %all-to-all-start.5 = ((bf16[8,32,512]{2,1,0:T(8,128)(2,1)}), bf16[8,32,512]{2,1,0:T(8,128)(2,1)S(1)}, u32[]{:S(2)}, u32[]{:S(2)}) async-start(bf16[8,32,512]{2,1,0:T(8,128)(2,1)} %get-tuple-element.95), calls=%async_computation.5 | async-start | bytes 524288 | tf_op jit(solution)/shard_map/all_to_all | solution.py:66
  164.8 17.5 %collective-permute-start.6 = (bf16[64,1024]{1,0:T(8,128)(2,1)S(1)}, bf16[64,1024]{1,0:T(8,128)(2,1)S(1)}, u32[]{:S(2)}, u32[]{:S(2)}) collective-permute-start(bf16[64,1024]{1,0:T(8,128)(2,1)S(1)} %copy-done.14), channel_id=1, source_target_pairs={{0,2},{1,3},{2,4},{3,5},{4,6},{5,7},{6,0},{7,1},{8,10},{9,11},{10,... | collective-permute-start | bytes 393224 | tf_op jit(solution)/shard_map/ppermute | solution.py:666
  167.7 14.5 %collective-permute-start.7 = (bf16[64,1024]{1,0:T(8,128)(2,1)S(1)}, bf16[64,1024]{1,0:T(8,128)(2,1)S(1)}, u32[]{:S(2)}, u32[]{:S(2)}) collective-permute-start(bf16[64,1024]{1,0:T(8,128)(2,1)S(1)} %copy-done.13), channel_id=1, source_target_pairs={{0,6},{1,7},{2,0},{3,1},{4,2},{5,3},{6,4},{7,5},{8,14},{9,15},{10,... | collective-permute-start | bytes 393224 | tf_op jit(solution)/shard_map/ppermute | solution.py:666
  202.9 15.1 %all-to-all-start.7 = ((f32[16,16,128]{2,1,0:T(8,128)}), f32[16,16,128]{2,1,0:T(8,128)S(1)}, u32[]{:S(2)}, u32[]{:S(2)}) async-start(f32[16,16,128]{2,1,0:T(8,128)} %broadcast_in_dim.101), calls=%async_computation.7 | async-start | bytes 262144 | tf_op jit(solution)/shard_map/all_to_all | solution.py:66
  218.7 15.0 %all-to-all-start.8 = ((f32[16,16,128]{2,1,0:T(8,128)}), f32[16,16,128]{2,1,0:T(8,128)S(1)}, u32[]{:S(2)}, u32[]{:S(2)}) async-start(f32[16,16,128]{2,1,0:T(8,128)} %broadcast_in_dim.102), calls=%async_computation.8 | async-start | bytes 262144 | tf_op jit(solution)/shard_map/all_to_all | solution.py:66
  (13 other events, 211.7 us)
Sparse Core Ops, SparseCore 0:
  72.1 150.7 all-gather.1

commit v8 on v6

--- a/solution.py
+++ b/solution.py
@@ -20,7 +20,7 @@
 SMEM = pl.BlockSpec(memory_space=pltpu.SMEM)
 HBM = pl.BlockSpec(memory_space=pltpu.HBM)
 NT = (((1,), (1,)), ((), ()))
-TURNS = ((1, 7), (4, 3), (5,), (2, 6))
+TURNS = ((4, 1, 7), (3, 5), (2, 6))
 
 
 def iota(shape, dim):
@@ -646,8 +646,9 @@
     notes = jnp.pad(notes, ((0, 4), (0, 0)))
 
     own, *backs = lax.optimization_barrier((own, *backs))
-    own = move(own, TURNS[0])
     near = spread(own, "u", outer)
+    facts, fetched = overlaps(summed, received, slot, facts, experts)
+    near, facts, fetched = lax.optimization_barrier((near, facts, fetched))
     far = swap_core(near)
     near, far = near.reshape(columns, part), far.reshape(columns, part)
     offered = pl.pallas_call(
@@ -658,8 +659,7 @@
         scratch_shapes=[pltpu.VMEM((2 * group + 8, columns), F32), pltpu.SemaphoreType.DMA((experts,))],
         compiler_params=params(2),
     )(own, near, far, notes)
-    offered = landed(offered, TURNS[0])
-    offered = move(offered, TURNS[1])
+    offered = move(offered, TURNS[0])
     gathered = exchange(offered, "expert")
     devices = outer * CORES
     offered, kept = pl.pallas_call(
@@ -675,11 +675,9 @@
         ],
         compiler_params=params(2),
     )(gathered)
-    offered = move(offered, TURNS[2])
+    offered = move(offered, TURNS[1])
     heard = exchange(offered, ("u", "c"))
-    heard = landed(heard, TURNS[1])
-    facts, fetched = overlaps(summed, received, slot, facts, experts)
-    heard, facts = lax.optimization_barrier((heard, facts))
+    heard = landed(heard, TURNS[0][:1])
     offered, loss = pl.pallas_call(
         functools.partial(gradient_kernel, scale),
         in_specs=[SMEM] + [VMEM] * 4,
@@ -688,9 +686,9 @@
         scratch_shapes=[pltpu.VMEM((2 * group, part), BF16), pltpu.SemaphoreType.DMA((experts,))],
         compiler_params=params(2),
     )((loss_scale / pairs)[None], heard, kept, near, far)
-    offered = move(offered, TURNS[3])
+    offered = move(offered, TURNS[2])
     grads = exchange(offered, "expert")
-    grads = landed(grads, TURNS[2])
+    grads = landed(grads, TURNS[0][1:])
 
     router_part, state, weighted = pl.pallas_call(
         router_kernel,
@@ -716,17 +714,18 @@
         compiler_params=params(16),
     )(grads, gain, *in_hbm(summed, fetched, tokens, facts))
     router_part = exchange(router_part.reshape(outer, -1, 128), "u")
+    router_part = landed(router_part, TURNS[1])
     router_part = jnp.sum(router_part, axis=0)
     router_part = spread(router_part, ("c", "expert"), CORES * experts)
     held = lax.dynamic_slice_in_dim(gathered[:, 2 * group : 2 * group + 3], mine * capacity, capacity, axis=2)
     held = jnp.pad(jnp.transpose(held, (0, 2, 1)), ((0, 0), (0, 0), (0, 5)))
+    turned = jnp.pad(router.T, ((0, 128 - experts), (0, 0)))
+    token_grad = token_rows(summed, weighted, state, turned, experts)
+    router_part, token_grad = lax.optimization_barrier((router_part, token_grad))
+    router_part = jnp.sum(router_part, axis=0)
+    router_all = spread(router_part, "u", outer)
     expert_grad = expert_rows(mine_at, grads, gain, held, backs)
-    turned = jnp.pad(router.T, ((0, 128 - experts), (0, 0)))
-    router_part, expert_grad = lax.optimization_barrier((router_part, expert_grad))
-    router_part = jnp.sum(router_part, axis=0)
-    token_grad = token_rows(summed, weighted, state, turned, experts)
-    router_all = spread(router_part, "u", outer)
-    router_all, token_grad = lax.optimization_barrier((router_all, token_grad))
+    router_all, expert_grad = lax.optimization_barrier((router_all, expert_grad))
     router_grad = router_all.reshape(-1, experts, 128).transpose(1, 0, 2).reshape(experts, width).T
     return token_grad, expert_grad.reshape(1, 1, experts, capacity, width), router_grad, loss[0, 0] / pairs
 

time: 236 us -> 227 us (0.962)
  waiting for transfers between devices: 64.1 us -> 80.5 us
  starting transfers between devices: 97.9 us -> 84 us
  blocking collectives: 12.7 us -> 0 us
    all_to_all x8 -> x9, waiting for transfers between devices: 59.5 us -> 79.8 us  [exchange(): return lax.all_to_all(x, axes, split_axis=0, concat_axis=0, tiled=True)]
    all_to_all x8 -> x9, starting transfers between devices: 77.2 us -> 63.3 us  [exchange(): return lax.all_to_all(x, axes, split_axis=0, concat_axis=0, tiled=True)]
    all_to_all x1 -> x0, blocking collectives: 12.7 us -> none  [exchange(): return lax.all_to_all(x, axes, split_axis=0, concat_axis=0, tiled=True)]
    ppermute x7, waiting for transfers between devices: 3.83 us -> 0.02 us  [move(): lax.ppermute(x, 'expert', [(i, (i + r) % experts) for i in range(experts)])]
  transfers between devices with their start and end apart: 16 -> 17, of which waited for: 9 -> 9; matrix products, arithmetic and copies ran while one was open for 2% -> 3% of each run, Pallas kernels for 16% -> 17%
where the time goes in v8:
time: 227 us; the launch traced here: 225 us
  starting transfers between devices  84 us (37%)
  waiting for transfers between devices  80.5 us (35%)
  Pallas kernels  47.4 us (21%)
  local copies, waits for them, and re-layouts  7.25 us (3%)
  between operations  3.49 us (2%)
    all_to_all x9, waiting for transfers between devices, exchange(): return lax.all_to_all(x, axes, split_axis=0, concat_axis=0, tiled=True)  79.8 us
    all_to_all x9, starting transfers between devices, exchange(): return lax.all_to_all(x, axes, split_axis=0, concat_axis=0, tiled=True)  63.3 us
    ppermute x7, starting transfers between devices, move(): lax.ppermute(x, 'expert', [(i, (i + r) % experts) for i in range(experts)])  17.4 us
    pallas_call x1, Pallas kernels, overlaps(): pl.pallas_call(functools.partial(overlap_kernel, experts), grid=(experts,...  8.56 us
    pallas_call x1, Pallas kernels, forward(): pl.pallas_call(functools.partial(forward_kernel, experts), grid=(experts,...  8.12 us
    pallas_call x1, Pallas kernels, expert_rows(): pl.pallas_call(expert_kernel, grid_spec=pltpu.PrefetchScalarGridSpec(num_...  7.25 us
    pallas_call x1, Pallas kernels, shards(): pl.pallas_call(router_kernel, in_specs=[VMEM] * 2 + [HBM] * 4, out_specs=...  6.8 us
    pallas_call x1, Pallas kernels, token_rows(): pl.pallas_call(functools.partial(token_kernel, experts), grid=(experts,),...  6.47 us
  transfers between devices with their start and end apart: 17, of which 9 were waited for; matrix products, arithmetic and copies ran while one was open for 3% of the time, Pallas kernels for 17%

profile of v8, /device:TPU:1, one launch (start us, length us, event | category | flops | bytes accessed | tf_op | source)
XLA Modules:
  0.0 225.5 jit_solution(5519371799062852671)
XLA Ops:
  0.7 7.6 %all-to-all-start = ((bf16[8,64,4096]{2,1,0:T(8,128)(2,1)}), bf16[8,64,4096]{2,1,0:T(8,128)(2,1)}, u32[]{:S(2)}, u32[]{:S(2)}) async-start(bf16[8,64,4096]{2,1,0:T(8,128)(2,1)} %bitcast.36), calls=%async_computation | async-start | bytes 8388608 | tf_op jit(solution)/shard_map/all_to_all | solution.py:65
  9.8 47.2 %all-to-all-done = bf16[8,64,4096]{2,1,0:T(8,128)(2,1)} async-done(((bf16[8,64,4096]{2,1,0:T(8,128)(2,1)}), bf16[8,64,4096]{2,1,0:T(8,128)(2,1)}, u32[]{:S(2)}, u32[]{:S(2)}) %all-to-all-start) | async-done | bytes 4194336 | tf_op jit(solution)/shard_map/all_to_all | solution.py:65
  57.0 8.1 %shard_map.102 = (f32[192,4096]{1,0:T(8,128)}, bf16[8,4,512]{2,1,0:T(4,128)(2,1)}, f32[192,1]{1,0:T(8,128)S(1)}) custom-call(bf16[192,4096]{1,0:T(8,128)(2,1)S(1)} %copy-done, bf16[512,4096]{1,0:T(8,128)(2,1)} %bitcast.2.rec, s32[192,2]{1,0:T(8,128)S(1)} %add.58.slot, f32[192,2]{1,0:T(8,128)S(1)} %exponential_divide_fusion.gate, f32[1,4096]{1,0:T(1,128)S(1)} %bitcast.33), custom_call_target="tpu_custom_call" | custom-call | flops 1610612736 | bytes 10485760 | tf_op jit(solution)/shard_map/pallas_call | solution.py:137
  65.2 5.2 %all-to-all-start.1 = ((bf16[8,4,512]{2,1,0:T(4,128)(2,1)}), bf16[8,4,512]{2,1,0:T(4,128)(2,1)S(1)}, u32[]{:S(2)}, u32[]{:S(2)}) async-start(bf16[8,4,512]{2,1,0:T(4,128)(2,1)} %get-tuple-element.58), calls=%async_computation.1 | async-start | bytes 65536 | tf_op jit(solution)/shard_map/all_to_all | solution.py:65
  70.4 5.7 %shard_map.103 = (bf16[64,4096]{1,0:T(8,128)(2,1)}, bf16[64,4096]{1,0:T(8,128)(2,1)}, bf16[64,4096]{1,0:T(8,128)(2,1)}, bf16[64,4096]{1,0:T(8,128)(2,1)}, bf16[6...) custom-call(s32[1]{0:T(128)} %bitcast.4.place, ...), custom_call_target="tpu_custom_call" | custom-call | flops 805306368 | bytes 7340032 | tf_op jit(solution)/shard_map/pallas_call | solution.py:204
  77.9 8.3 %all-to-all-start.2 = ((bf16[16,32,512]{2,1,0:T(8,128)(2,1)}), bf16[16,32,512]{2,1,0:T(8,128)(2,1)S(1)}, u32[]{:S(2)}, u32[]{:S(2)}) async-start(bf16[16,32,512]{2,1,0:T(8,128)(2,1)} %broadcast_in_dim.89), calls=%async_computation.2 | async-start | bytes 1048576 | tf_op jit(solution)/shard_map/all_to_all | solution.py:65
  88.4 8.6 %shard_map.104 = (f32[192,128]{1,0:T(8,128)}, bf16[384,4096]{1,0:T(8,128)(2,1)}) custom-call(f32[192,4096]{1,0:T(8,128)} %get-tuple-element.59.x.summed_in.summed, bf16[512,4096]{1,0:T(8,128)(2,1)} %bitcast.2.rec, s32[192,2]{1,0:T(8,128)S(1)} %add.58.slot, f32[192,128]{1,0:T(8,128)S(1)} %pad.16.facts), custom_call_target="tpu_custom_call" | custom-call | flops 1610612736 | bytes 10485760 | tf_op jit(solution)/shard_map/pallas_call | solution.py:256
  99.0 3.3 %collective-permute-start = (bf16[16,32,512]{2,1,0:T(8,128)(2,1)S(1)}, bf16[16,32,512]{2,1,0:T(8,128)(2,1)S(1)}, u32[]{:S(2)}, u32[]{:S(2)}) collective-permute-start(bf16[16,32,512]{2,1,0:T(8,128)(2,1)S(1)} %all-to-all-done.2), channel_id=1, source_target_pairs={{0,8},{8,0},{1,9},{9,1},{2,10},{10,2},{3,11},{11,3},{4,12},{12,4},... | collective-permute-start | bytes 1572872 | tf_op jit(solution)/shard_map/ppermute | solution.py:61
  105.4 6.4 %all-to-all-start.3 = ((f32[8,40,512]{2,1,0:T(8,128)}), f32[8,40,512]{2,1,0:T(8,128)S(1)}, u32[]{:S(2)}, u32[]{:S(2)}) async-start(f32[8,40,512]{2,1,0:T(8,128)} %shard_map.105), calls=%async_computation.3 | async-start | bytes 1310720 | tf_op jit(solution)/shard_map/all_to_all | solution.py:65
  111.8 3.0 %collective-permute-start.1 = (bf16[64,4096]{1,0:T(8,128)(2,1)}, bf16[64,4096]{1,0:T(8,128)(2,1)S(1)}, u32[]{:S(2)}, u32[]{:S(2)}) collective-permute-start(bf16[64,4096]{1,0:T(8,128)(2,1)} %get-tuple-element.81), channel_id=1, source_target_pairs={{0,4},{1,5},{2,6},{3,7},{4,0},{5,1},{6,2},{7,3},{8,12},{9,13},{10,... | collective-permute-start | bytes 1572872 | tf_op jit(solution)/shard_map/ppermute | solution.py:626
  116.0 3.9 %collective-permute-start.3 = (bf16[64,4096]{1,0:T(8,128)(2,1)}, bf16[64,4096]{1,0:T(8,128)(2,1)S(1)}, u32[]{:S(2)}, u32[]{:S(2)}) collective-permute-start(bf16[64,4096]{1,0:T(8,128)(2,1)} %get-tuple-element.89), channel_id=1, source_target_pairs={{0,7},{1,0},{2,1},{3,2},{4,3},{5,4},{6,5},{7,6},{8,15},{9,8},{10,9... | collective-permute-start | bytes 1572872 | tf_op jit(solution)/shard_map/ppermute | solution.py:626
  119.8 2.6 %all-to-all-done.3.gathered = f32[8,40,512]{2,1,0:T(8,128)S(1)} async-done(((f32[8,40,512]{2,1,0:T(8,128)}), f32[8,40,512]{2,1,0:T(8,128)S(1)}, u32[]{:S(2)}, u32[]{:S(2)}) %all-to-all-start.3) | async-done | bytes 655392 | tf_op jit(solution)/shard_map/all_to_all | solution.py:65
  123.4 7.4 %all-to-all-start.4 = ((f32[32,8,128]{2,1,0:T(8,128)}), f32[32,8,128]{2,1,0:T(8,128)S(1)}, u32[]{:S(2)}, u32[]{:S(2)}) async-start(f32[32,8,128]{2,1,0:T(8,128)} %get-tuple-element.80), calls=%async_computation.4 | async-start | bytes 262144 | tf_op jit(solution)/shard_map/all_to_all | solution.py:65
  135.5 9.7 %all-to-all-done.4.heard = f32[32,8,128]{2,1,0:T(8,128)S(1)} async-done(((f32[32,8,128]{2,1,0:T(8,128)}), f32[32,8,128]{2,1,0:T(8,128)S(1)}, u32[]{:S(2)}, u32[]{:S(2)}) %all-to-all-start.4) | async-done | bytes 131104 | tf_op jit(solution)/shard_map/all_to_all | solution.py:65
  148.0 7.3 %all-to-all-start.5 = ((bf16[8,32,512]{2,1,0:T(8,128)(2,1)}), bf16[8,32,512]{2,1,0:T(8,128)(2,1)S(1)}, u32[]{:S(2)}, u32[]{:S(2)}) async-start(bf16[8,32,512]{2,1,0:T(8,128)(2,1)} %get-tuple-element.87), calls=%async_computation.5 | async-start | bytes 524288 | tf_op jit(solution)/shard_map/all_to_all | solution.py:65
  155.3 7.5 %all-to-all-done.5.grads = bf16[8,32,512]{2,1,0:T(8,128)(2,1)S(1)} async-done(((bf16[8,32,512]{2,1,0:T(8,128)(2,1)}), bf16[8,32,512]{2,1,0:T(8,128)(2,1)S(1)}, u32[]{:S(2)}, u32[]{:S(2)}) %all-to-all-start.5) | async-done | bytes 262176 | tf_op jit(solution)/shard_map/all_to_all | solution.py:65
  162.8 6.8 %shard_map.108 = (f32[256,128]{1,0:T(8,128)}, f32[192,128]{1,0:T(8,128)}, f32[4,4096]{1,0:T(4,128)}) custom-call(bf16[8,32,512]{2,1,0:T(8,128)(2,1)S(1)} %all-to-all-done.5.grads, f32[1,4096]{1,0:T(1,128)S(1)} %bitcast.34, f32[192,4096]{1,0:T(8,128)} %get-tuple-element.59.x.summed_in.summed, bf16[384,4096]{1,0:T(8,128)(2,1)} %get-tuple-element.91.fetched_in, ...), custom_call_target="tpu_custom_call" | custom-call | tf_op jit(solution)/shard_map/pallas_call | solution.py:693
  169.7 6.0 %all-to-all-start.6 = ((f32[16,16,128]{2,1,0:T(8,128)}), f32[16,16,128]{2,1,0:T(8,128)S(1)}, u32[]{:S(2)}, u32[]{:S(2)}) async-start(f32[16,16,128]{2,1,0:T(8,128)} %bitcast.13), calls=%async_computation.6 | async-start | bytes 262144 | tf_op jit(solution)/shard_map/all_to_all | solution.py:65
  177.5 3.6 %collective-permute-start.7 = (bf16[64,4096]{1,0:T(8,128)(2,1)}, bf16[64,4096]{1,0:T(8,128)(2,1)S(1)}, u32[]{:S(2)}, u32[]{:S(2)}) collective-permute-start(bf16[64,4096]{1,0:T(8,128)(2,1)} %get-tuple-element.107), channel_id=1, source_target_pairs={{0,6},{1,7},{2,0},{3,1},{4,2},{5,3},{6,4},{7,5},{8,14},{9,15},{10,... | collective-permute-start | bytes 1572872 | tf_op jit(solution)/shard_map/ppermute | solution.py:626
  183.8 7.5 %all-to-all-start.7 = ((f32[16,16,128]{2,1,0:T(8,128)}), f32[16,16,128]{2,1,0:T(8,128)S(1)}, u32[]{:S(2)}, u32[]{:S(2)}) async-start(f32[16,16,128]{2,1,0:T(8,128)} %broadcast_in_dim.101), calls=%async_computation.7 | async-start | bytes 262144 | tf_op jit(solution)/shard_map/all_to_all | solution.py:65
  191.4 6.5 %shard_map.109 = bf16[192,4096]{1,0:T(8,128)(2,1)} custom-call(f32[192,4096]{1,0:T(8,128)} %get-tuple-element.59.x.summed_in.summed, f32[4,4096]{1,0:T(4,128)} %get-tuple-element.97.weighted, f32[192,128]{1,0:T(8,128)} %get-tuple-element.98.state, bf16[128,4096]{1,0:T(8,128)(2,1)S(1)} %pad.18.router), custom_call_target="tpu_custom_call" | custom-call | flops 201326592 | bytes 5242880 | tf_op jit(solution)/shard_map/pallas_call | solution.py:506
  197.9 7.9 %all-to-all-done.7 = f32[16,16,128]{2,1,0:T(8,128)S(1)} async-done(((f32[16,16,128]{2,1,0:T(8,128)}), f32[16,16,128]{2,1,0:T(8,128)S(1)}, u32[]{:S(2)}, u32[]{:S(2)}) %all-to-all-start.7) | async-done | bytes 131104 | tf_op jit(solution)/shard_map/all_to_all | solution.py:65
  206.4 7.5 %all-to-all-start.8 = ((f32[16,16,128]{2,1,0:T(8,128)}), f32[16,16,128]{2,1,0:T(8,128)S(1)}, u32[]{:S(2)}, u32[]{:S(2)}) async-start(f32[16,16,128]{2,1,0:T(8,128)} %broadcast_in_dim.102), calls=%async_computation.8 | async-start | bytes 262144 | tf_op jit(solution)/shard_map/all_to_all | solution.py:65
  216.4 7.3 %shard_map.110 = bf16[8,64,4096]{2,1,0:T(8,128)(2,1)} custom-call(s32[1]{0:T(128)} %bitcast.4.place, bf16[8,32,512]{2,1,0:T(8,128)(2,1)S(1)} %all-to-all-done.5.grads, f32[1,4096]{1,0:T(1,128)S(1)} %bitcast.35, f32[8,64,8]{2,1,0:T(8,128)S(1)} %pad.19.notes, bf16[64,4096]{1,0:T(8,128)(2,1)} %get-tuple-element.101.rest_0_, bf16[64,4096]{1,0:T(8,128)(2,1)} %copy-done.4, ...), custom_call_target="tpu_custom_call" | custom-call | flops 25165824 | bytes 9437184 | tf_op jit(solution)/shard_map/pallas_call | solution.py:569
  (81 shorter events, 27.2 us)
Async XLA Ops:
  0.6 7.8 %copy-start = (bf16[192,4096]{1,0:T(8,128)(2,1)S(1)}, bf16[192,4096]{1,0:T(8,128)(2,1)}, u32[]{:S(2)}) copy-start(bf16[192,4096]{1,0:T(8,128)(2,1)} %tok_in.1) | copy-start | bytes 4718596
  0.7 7.8 %copy-start.8 = (bf16[4096,8]{0,1:T(8,128)(2,1)S(1)}, bf16[4096,8]{0,1:T(8,128)(2,1)}, u32[]{:S(2)}) copy-start(bf16[4096,8]{0,1:T(8,128)(2,1)} %param.11) | copy-start | bytes 196612
  0.7 56.4 %copy-start.1 = (f32[4096]{0:T(1024)S(1)}, f32[4096]{0:T(1024)}, u32[]{:S(2)}) copy-start(f32[4096]{0:T(1024)} %param.12) | copy-start | bytes 49156
  0.7 56.3 %all-to-all-start = ((bf16[8,64,4096]{2,1,0:T(8,128)(2,1)}), bf16[8,64,4096]{2,1,0:T(8,128)(2,1)}, u32[]{:S(2)}, u32[]{:S(2)}) async-start(bf16[8,64,4096]{2,1,0:T(8,128)(2,1)} %bitcast.36), calls=%async_computation | async-start | bytes 8388608 | tf_op jit(solution)/shard_map/all_to_all | solution.py:65
  65.2 21.2 %copy-start.10 = (s32[2]{0:T(128)S(1)}, s32[2]{0:T(128)}, u32[]{:S(2)}) copy-start(s32[2]{0:T(128)} %param.9) | copy-start | bytes 28
  65.2 11.8 %all-to-all-start.1 = ((bf16[8,4,512]{2,1,0:T(4,128)(2,1)}), bf16[8,4,512]{2,1,0:T(4,128)(2,1)S(1)}, u32[]{:S(2)}, u32[]{:S(2)}) async-start(bf16[8,4,512]{2,1,0:T(4,128)(2,1)} %get-tuple-element.58), calls=%async_computation.1 | async-start | bytes 65536 | tf_op jit(solution)/shard_map/all_to_all | solution.py:65
  77.9 21.1 %all-to-all-start.2 = ((bf16[16,32,512]{2,1,0:T(8,128)(2,1)}), bf16[16,32,512]{2,1,0:T(8,128)(2,1)S(1)}, u32[]{:S(2)}, u32[]{:S(2)}) async-start(bf16[16,32,512]{2,1,0:T(8,128)(2,1)} %broadcast_in_dim.89), calls=%async_computation.2 | async-start | bytes 1048576 | tf_op jit(solution)/shard_map/all_to_all | solution.py:65
  99.0 4.8 %collective-permute-start = (bf16[16,32,512]{2,1,0:T(8,128)(2,1)S(1)}, bf16[16,32,512]{2,1,0:T(8,128)(2,1)S(1)}, u32[]{:S(2)}, u32[]{:S(2)}) collective-permute-start(bf16[16,32,512]{2,1,0:T(8,128)(2,1)S(1)} %all-to-all-done.2), channel_id=1, source_target_pairs={{0,8},{8,0},{1,9},{9,1},{2,10},{10,2},{3,11},{11,3},{4,12},{12,4},... | collective-permute-start | bytes 1572872 | tf_op jit(solution)/shard_map/ppermute | solution.py:61
  105.4 17.1 %all-to-all-start.3 = ((f32[8,40,512]{2,1,0:T(8,128)}), f32[8,40,512]{2,1,0:T(8,128)S(1)}, u32[]{:S(2)}, u32[]{:S(2)}) async-start(f32[8,40,512]{2,1,0:T(8,128)} %shard_map.105), calls=%async_computation.3 | async-start | bytes 1310720 | tf_op jit(solution)/shard_map/all_to_all | solution.py:65
  111.8 23.7 %collective-permute-start.1 = (bf16[64,4096]{1,0:T(8,128)(2,1)}, bf16[64,4096]{1,0:T(8,128)(2,1)S(1)}, u32[]{:S(2)}, u32[]{:S(2)}) collective-permute-start(bf16[64,4096]{1,0:T(8,128)(2,1)} %get-tuple-element.81), channel_id=1, source_target_pairs={{0,4},{1,5},{2,6},{3,7},{4,0},{5,1},{6,2},{7,3},{8,12},{9,13},{10,... | collective-permute-start | bytes 1572872 | tf_op jit(solution)/shard_map/ppermute | solution.py:626
  114.8 40.5 %collective-permute-start.2 = (bf16[64,4096]{1,0:T(8,128)(2,1)}, bf16[64,4096]{1,0:T(8,128)(2,1)S(1)}, u32[]{:S(2)}, u32[]{:S(2)}) collective-permute-start(bf16[64,4096]{1,0:T(8,128)(2,1)} %get-tuple-element.88), channel_id=1, source_target_pairs={{0,1},{1,2},{2,3},{3,4},{4,5},{5,6},{6,7},{7,0},{8,9},{9,10},{10,1... | collective-permute-start | bytes 1572872 | tf_op jit(solution)/shard_map/ppermute | solution.py:626
  116.0 39.3 %collective-permute-start.3 = (bf16[64,4096]{1,0:T(8,128)(2,1)}, bf16[64,4096]{1,0:T(8,128)(2,1)S(1)}, u32[]{:S(2)}, u32[]{:S(2)}) collective-permute-start(bf16[64,4096]{1,0:T(8,128)(2,1)} %get-tuple-element.89), channel_id=1, source_target_pairs={{0,7},{1,0},{2,1},{3,2},{4,3},{5,4},{6,5},{7,6},{8,15},{9,8},{10,9... | collective-permute-start | bytes 1572872 | tf_op jit(solution)/shard_map/ppermute | solution.py:626
  123.4 21.7 %all-to-all-start.4 = ((f32[32,8,128]{2,1,0:T(8,128)}), f32[32,8,128]{2,1,0:T(8,128)S(1)}, u32[]{:S(2)}, u32[]{:S(2)}) async-start(f32[32,8,128]{2,1,0:T(8,128)} %get-tuple-element.80), calls=%async_computation.4 | async-start | bytes 262144 | tf_op jit(solution)/shard_map/all_to_all | solution.py:65
  130.9 50.2 %collective-permute-start.4 = (bf16[64,4096]{1,0:T(8,128)(2,1)}, bf16[64,4096]{1,0:T(8,128)(2,1)}, u32[]{:S(2)}, u32[]{:S(2)}) collective-permute-start(bf16[64,4096]{1,0:T(8,128)(2,1)} %get-tuple-element.94), channel_id=1, source_target_pairs={{0,3},{1,4},{2,5},{3,6},{4,7},{5,0},{6,1},{7,2},{8,11},{9,12},{10,... | collective-permute-start | bytes 1572872 | tf_op jit(solution)/shard_map/ppermute | solution.py:626
  133.0 48.1 %collective-permute-start.5 = (bf16[64,4096]{1,0:T(8,128)(2,1)}, bf16[64,4096]{1,0:T(8,128)(2,1)}, u32[]{:S(2)}, u32[]{:S(2)}) collective-permute-start(bf16[64,4096]{1,0:T(8,128)(2,1)} %get-tuple-element.95), channel_id=1, source_target_pairs={{0,5},{1,6},{2,7},{3,0},{4,1},{5,2},{6,3},{7,4},{8,13},{9,14},{10,... | collective-permute-start | bytes 1572872 | tf_op jit(solution)/shard_map/ppermute | solution.py:626
  135.5 34.1 %copy-start.3 = (bf16[64,4096]{1,0:T(8,128)(2,1)}, bf16[64,4096]{1,0:T(8,128)(2,1)S(1)}, u32[]{:S(2)}) copy-start(bf16[64,4096]{1,0:T(8,128)(2,1)S(1)} %collective-permute-done.1.rest_4_) | copy-start | bytes 1572868
  148.0 14.9 %all-to-all-start.5 = ((bf16[8,32,512]{2,1,0:T(8,128)(2,1)}), bf16[8,32,512]{2,1,0:T(8,128)(2,1)S(1)}, u32[]{:S(2)}, u32[]{:S(2)}) async-start(bf16[8,32,512]{2,1,0:T(8,128)(2,1)} %get-tuple-element.87), calls=%async_computation.5 | async-start | bytes 524288 | tf_op jit(solution)/shard_map/all_to_all | solution.py:65
  155.3 14.4 %copy-start.4 = (bf16[64,4096]{1,0:T(8,128)(2,1)}, bf16[64,4096]{1,0:T(8,128)(2,1)S(1)}, u32[]{:S(2)}) copy-start(bf16[64,4096]{1,0:T(8,128)(2,1)S(1)} %collective-permute-done.2.rest_1_) | copy-start | bytes 1572868
  155.3 14.4 %copy-start.5 = (bf16[64,4096]{1,0:T(8,128)(2,1)}, bf16[64,4096]{1,0:T(8,128)(2,1)S(1)}, u32[]{:S(2)}) copy-start(bf16[64,4096]{1,0:T(8,128)(2,1)S(1)} %collective-permute-done.3.rest_7_) | copy-start | bytes 1572868
  169.7 13.4 %all-to-all-start.6 = ((f32[16,16,128]{2,1,0:T(8,128)}), f32[16,16,128]{2,1,0:T(8,128)S(1)}, u32[]{:S(2)}, u32[]{:S(2)}) async-start(f32[16,16,128]{2,1,0:T(8,128)} %bitcast.13), calls=%async_computation.6 | async-start | bytes 262144 | tf_op jit(solution)/shard_map/all_to_all | solution.py:65
  175.6 39.2 %collective-permute-start.6 = (bf16[64,4096]{1,0:T(8,128)(2,1)}, bf16[64,4096]{1,0:T(8,128)(2,1)S(1)}, u32[]{:S(2)}, u32[]{:S(2)}) collective-permute-start(bf16[64,4096]{1,0:T(8,128)(2,1)} %get-tuple-element.103), channel_id=1, source_target_pairs={{0,2},{1,3},{2,4},{3,5},{4,6},{5,7},{6,0},{7,1},{8,10},{9,11},{10,... | collective-permute-start | bytes 1572872 | tf_op jit(solution)/shard_map/ppermute | solution.py:626
  177.5 37.4 %collective-permute-start.7 = (bf16[64,4096]{1,0:T(8,128)(2,1)}, bf16[64,4096]{1,0:T(8,128)(2,1)S(1)}, u32[]{:S(2)}, u32[]{:S(2)}) collective-permute-start(bf16[64,4096]{1,0:T(8,128)(2,1)} %get-tuple-element.107), channel_id=1, source_target_pairs={{0,6},{1,7},{2,0},{3,1},{4,2},{5,3},{6,4},{7,5},{8,14},{9,15},{10,... | collective-permute-start | bytes 1572872 | tf_op jit(solution)/shard_map/ppermute | solution.py:626
  183.8 22.0 %all-to-all-start.7 = ((f32[16,16,128]{2,1,0:T(8,128)}), f32[16,16,128]{2,1,0:T(8,128)S(1)}, u32[]{:S(2)}, u32[]{:S(2)}) async-start(f32[16,16,128]{2,1,0:T(8,128)} %broadcast_in_dim.101), calls=%async_computation.7 | async-start | bytes 262144 | tf_op jit(solution)/shard_map/all_to_all | solution.py:65
  206.4 17.3 %all-to-all-start.8 = ((f32[16,16,128]{2,1,0:T(8,128)}), f32[16,16,128]{2,1,0:T(8,128)S(1)}, u32[]{:S(2)}, u32[]{:S(2)}) async-start(f32[16,16,128]{2,1,0:T(8,128)} %broadcast_in_dim.102), calls=%async_computation.8 | async-start | bytes 262144 | tf_op jit(solution)/shard_map/all_to_all | solution.py:65
  (4 other events, 10.2 us)

commit v9 on v8

--- a/solution.py
+++ b/solution.py
@@ -714,18 +714,18 @@
         compiler_params=params(16),
     )(grads, gain, *in_hbm(summed, fetched, tokens, facts))
     router_part = exchange(router_part.reshape(outer, -1, 128), "u")
+    turned = jnp.pad(router.T, ((0, 128 - experts), (0, 0)))
+    token_grad = token_rows(summed, weighted, state, turned, experts)
+    router_part, token_grad = lax.optimization_barrier((router_part, token_grad))
     router_part = landed(router_part, TURNS[1])
     router_part = jnp.sum(router_part, axis=0)
     router_part = spread(router_part, ("c", "expert"), CORES * experts)
     held = lax.dynamic_slice_in_dim(gathered[:, 2 * group : 2 * group + 3], mine * capacity, capacity, axis=2)
     held = jnp.pad(jnp.transpose(held, (0, 2, 1)), ((0, 0), (0, 0), (0, 5)))
-    turned = jnp.pad(router.T, ((0, 128 - experts), (0, 0)))
-    token_grad = token_rows(summed, weighted, state, turned, experts)
-    router_part, token_grad = lax.optimization_barrier((router_part, token_grad))
+    expert_grad = expert_rows(mine_at, grads, gain, held, backs)
+    router_part, expert_grad = lax.optimization_barrier((router_part, expert_grad))
     router_part = jnp.sum(router_part, axis=0)
     router_all = spread(router_part, "u", outer)
-    expert_grad = expert_rows(mine_at, grads, gain, held, backs)
-    router_all, expert_grad = lax.optimization_barrier((router_all, expert_grad))
     router_grad = router_all.reshape(-1, experts, 128).transpose(1, 0, 2).reshape(experts, width).T
     return token_grad, expert_grad.reshape(1, 1, experts, capacity, width), router_grad, loss[0, 0] / pairs
 

time: 227 us -> 240 us (1.057)
  starting transfers between devices: 84 us -> 104 us
  waiting for transfers between devices: 80.5 us -> 72.9 us
    all_to_all x9, starting transfers between devices: 63.3 us -> 83.2 us  [exchange(): return lax.all_to_all(x, axes, split_axis=0, concat_axis=0, tiled=True)]
    all_to_all x9, waiting for transfers between devices: 79.8 us -> 72.1 us  [exchange(): return lax.all_to_all(x, axes, split_axis=0, concat_axis=0, tiled=True)]
  transfers between devices with their start and end apart: 17 -> 17, of which waited for: 9 -> 9; matrix products, arithmetic and copies ran while one was open for 3% -> 2% of each run, Pallas kernels for 17% -> 16%
where the time goes in v9:
time: 240 us; the launch traced here: 237 us
  starting transfers between devices  104 us (43%)
  waiting for transfers between devices  72.9 us (30%)
  Pallas kernels  47.4 us (20%)
  local copies, waits for them, and re-layouts  6.44 us (3%)
  between operations  3.45 us (1%)
    all_to_all x9, starting transfers between devices, exchange(): return lax.all_to_all(x, axes, split_axis=0, concat_axis=0, tiled=True)  83.2 us
    all_to_all x9, waiting for transfers between devices, exchange(): return lax.all_to_all(x, axes, split_axis=0, concat_axis=0, tiled=True)  72.1 us
    ppermute x7, starting transfers between devices, move(): lax.ppermute(x, 'expert', [(i, (i + r) % experts) for i in range(experts)])  17.6 us
    pallas_call x1, Pallas kernels, overlaps(): pl.pallas_call(functools.partial(overlap_kernel, experts), grid=(experts,...  8.56 us
    pallas_call x1, Pallas kernels, forward(): pl.pallas_call(functools.partial(forward_kernel, experts), grid=(experts,...  8.12 us
    pallas_call x1, Pallas kernels, expert_rows(): pl.pallas_call(expert_kernel, grid_spec=pltpu.PrefetchScalarGridSpec(num_...  7.25 us
    pallas_call x1, Pallas kernels, shards(): pl.pallas_call(router_kernel, in_specs=[VMEM] * 2 + [HBM] * 4, out_specs=...  6.8 us
    pallas_call x1, Pallas kernels, token_rows(): pl.pallas_call(functools.partial(token_kernel, experts), grid=(experts,),...  6.47 us
  transfers between devices with their start and end apart: 17, of which 9 were waited for; matrix products, arithmetic and copies ran while one was open for 2% of the time, Pallas kernels for 16%

profile of v9, /device:TPU:1, one launch (start us, length us, event | category | flops | bytes accessed | tf_op | source)
XLA Modules:
  0.0 237.1 jit_solution(16902767838040361693)
XLA Ops:
  0.7 7.6 %all-to-all-start = ((bf16[8,64,4096]{2,1,0:T(8,128)(2,1)}), bf16[8,64,4096]{2,1,0:T(8,128)(2,1)}, u32[]{:S(2)}, u32[]{:S(2)}) async-start(bf16[8,64,4096]{2,1,0:T(8,128)(2,1)} %bitcast.36), calls=%async_computation | async-start | bytes 8388608 | tf_op jit(solution)/shard_map/all_to_all | solution.py:65
  9.8 47.2 %all-to-all-done = bf16[8,64,4096]{2,1,0:T(8,128)(2,1)} async-done(((bf16[8,64,4096]{2,1,0:T(8,128)(2,1)}), bf16[8,64,4096]{2,1,0:T(8,128)(2,1)}, u32[]{:S(2)}, u32[]{:S(2)}) %all-to-all-start) | async-done | bytes 4194336 | tf_op jit(solution)/shard_map/all_to_all | solution.py:65
  57.0 8.1 %shard_map.102 = (f32[192,4096]{1,0:T(8,128)}, bf16[8,4,512]{2,1,0:T(4,128)(2,1)}, f32[192,1]{1,0:T(8,128)S(1)}) custom-call(bf16[192,4096]{1,0:T(8,128)(2,1)S(1)} %copy-done, bf16[512,4096]{1,0:T(8,128)(2,1)} %bitcast.2.rec, s32[192,2]{1,0:T(8,128)S(1)} %add.58.slot, f32[192,2]{1,0:T(8,128)S(1)} %exponential_divide_fusion.gate, f32[1,4096]{1,0:T(1,128)S(1)} %bitcast.33), custom_call_target="tpu_custom_call" | custom-call | flops 1610612736 | bytes 10485760 | tf_op jit(solution)/shard_map/pallas_call | solution.py:137
  65.2 5.2 %all-to-all-start.1 = ((bf16[8,4,512]{2,1,0:T(4,128)(2,1)}), bf16[8,4,512]{2,1,0:T(4,128)(2,1)S(1)}, u32[]{:S(2)}, u32[]{:S(2)}) async-start(bf16[8,4,512]{2,1,0:T(4,128)(2,1)} %get-tuple-element.58), calls=%async_computation.1 | async-start | bytes 65536 | tf_op jit(solution)/shard_map/all_to_all | solution.py:65
  70.4 5.7 %shard_map.103 = (bf16[64,4096]{1,0:T(8,128)(2,1)}, bf16[64,4096]{1,0:T(8,128)(2,1)}, bf16[64,4096]{1,0:T(8,128)(2,1)}, bf16[64,4096]{1,0:T(8,128)(2,1)}, bf16[6...) custom-call(s32[1]{0:T(128)} %bitcast.4.place, ...), custom_call_target="tpu_custom_call" | custom-call | flops 805306368 | bytes 7340032 | tf_op jit(solution)/shard_map/pallas_call | solution.py:204
  77.9 8.3 %all-to-all-start.2 = ((bf16[16,32,512]{2,1,0:T(8,128)(2,1)}), bf16[16,32,512]{2,1,0:T(8,128)(2,1)S(1)}, u32[]{:S(2)}, u32[]{:S(2)}) async-start(bf16[16,32,512]{2,1,0:T(8,128)(2,1)} %broadcast_in_dim.89), calls=%async_computation.2 | async-start | bytes 1048576 | tf_op jit(solution)/shard_map/all_to_all | solution.py:65
  88.4 8.6 %shard_map.104 = (f32[192,128]{1,0:T(8,128)}, bf16[384,4096]{1,0:T(8,128)(2,1)}) custom-call(f32[192,4096]{1,0:T(8,128)} %get-tuple-element.59.x.summed_in.summed, bf16[512,4096]{1,0:T(8,128)(2,1)} %bitcast.2.rec, s32[192,2]{1,0:T(8,128)S(1)} %add.58.slot, f32[192,128]{1,0:T(8,128)S(1)} %pad.16.facts), custom_call_target="tpu_custom_call" | custom-call | flops 1610612736 | bytes 10485760 | tf_op jit(solution)/shard_map/pallas_call | solution.py:256
  99.0 3.3 %collective-permute-start = (bf16[16,32,512]{2,1,0:T(8,128)(2,1)S(1)}, bf16[16,32,512]{2,1,0:T(8,128)(2,1)S(1)}, u32[]{:S(2)}, u32[]{:S(2)}) collective-permute-start(bf16[16,32,512]{2,1,0:T(8,128)(2,1)S(1)} %all-to-all-done.2), channel_id=1, source_target_pairs={{0,8},{8,0},{1,9},{9,1},{2,10},{10,2},{3,11},{11,3},{4,12},{12,4},... | collective-permute-start | bytes 1572872 | tf_op jit(solution)/shard_map/ppermute | solution.py:61
  105.4 6.4 %all-to-all-start.3 = ((f32[8,40,512]{2,1,0:T(8,128)}), f32[8,40,512]{2,1,0:T(8,128)S(1)}, u32[]{:S(2)}, u32[]{:S(2)}) async-start(f32[8,40,512]{2,1,0:T(8,128)} %shard_map.105), calls=%async_computation.3 | async-start | bytes 1310720 | tf_op jit(solution)/shard_map/all_to_all | solution.py:65
  111.8 3.0 %collective-permute-start.1 = (bf16[64,4096]{1,0:T(8,128)(2,1)}, bf16[64,4096]{1,0:T(8,128)(2,1)S(1)}, u32[]{:S(2)}, u32[]{:S(2)}) collective-permute-start(bf16[64,4096]{1,0:T(8,128)(2,1)} %get-tuple-element.81), channel_id=1, source_target_pairs={{0,4},{1,5},{2,6},{3,7},{4,0},{5,1},{6,2},{7,3},{8,12},{9,13},{10,... | collective-permute-start | bytes 1572872 | tf_op jit(solution)/shard_map/ppermute | solution.py:626
  116.0 3.9 %collective-permute-start.3 = (bf16[64,4096]{1,0:T(8,128)(2,1)}, bf16[64,4096]{1,0:T(8,128)(2,1)S(1)}, u32[]{:S(2)}, u32[]{:S(2)}) collective-permute-start(bf16[64,4096]{1,0:T(8,128)(2,1)} %get-tuple-element.89), channel_id=1, source_target_pairs={{0,7},{1,0},{2,1},{3,2},{4,3},{5,4},{6,5},{7,6},{8,15},{9,8},{10,9... | collective-permute-start | bytes 1572872 | tf_op jit(solution)/shard_map/ppermute | solution.py:626
  119.9 2.6 %all-to-all-done.3.gathered = f32[8,40,512]{2,1,0:T(8,128)S(1)} async-done(((f32[8,40,512]{2,1,0:T(8,128)}), f32[8,40,512]{2,1,0:T(8,128)S(1)}, u32[]{:S(2)}, u32[]{:S(2)}) %all-to-all-start.3) | async-done | bytes 655392 | tf_op jit(solution)/shard_map/all_to_all | solution.py:65
  123.5 7.4 %all-to-all-start.4 = ((f32[32,8,128]{2,1,0:T(8,128)}), f32[32,8,128]{2,1,0:T(8,128)S(1)}, u32[]{:S(2)}, u32[]{:S(2)}) async-start(f32[32,8,128]{2,1,0:T(8,128)} %get-tuple-element.80), calls=%async_computation.4 | async-start | bytes 262144 | tf_op jit(solution)/shard_map/all_to_all | solution.py:65
  135.5 9.7 %all-to-all-done.4.heard = f32[32,8,128]{2,1,0:T(8,128)S(1)} async-done(((f32[32,8,128]{2,1,0:T(8,128)}), f32[32,8,128]{2,1,0:T(8,128)S(1)}, u32[]{:S(2)}, u32[]{:S(2)}) %all-to-all-start.4) | async-done | bytes 131104 | tf_op jit(solution)/shard_map/all_to_all | solution.py:65
  148.0 7.3 %all-to-all-start.5 = ((bf16[8,32,512]{2,1,0:T(8,128)(2,1)}), bf16[8,32,512]{2,1,0:T(8,128)(2,1)S(1)}, u32[]{:S(2)}, u32[]{:S(2)}) async-start(bf16[8,32,512]{2,1,0:T(8,128)(2,1)} %get-tuple-element.87), calls=%async_computation.5 | async-start | bytes 524288 | tf_op jit(solution)/shard_map/all_to_all | solution.py:65
  155.3 3.0 %collective-permute-start.6 = (bf16[64,4096]{1,0:T(8,128)(2,1)}, bf16[64,4096]{1,0:T(8,128)(2,1)S(1)}, u32[]{:S(2)}, u32[]{:S(2)}) collective-permute-start(bf16[64,4096]{1,0:T(8,128)(2,1)} %get-tuple-element.103), channel_id=1, source_target_pairs={{0,2},{1,3},{2,4},{3,5},{4,6},{5,7},{6,0},{7,1},{8,10},{9,11},{10,... | collective-permute-start | bytes 1572872 | tf_op jit(solution)/shard_map/ppermute | solution.py:626
  158.3 2.7 %collective-permute-start.7 = (bf16[64,4096]{1,0:T(8,128)(2,1)}, bf16[64,4096]{1,0:T(8,128)(2,1)}, u32[]{:S(2)}, u32[]{:S(2)}) collective-permute-start(bf16[64,4096]{1,0:T(8,128)(2,1)} %get-tuple-element.107), channel_id=1, source_target_pairs={{0,6},{1,7},{2,0},{3,1},{4,2},{5,3},{6,4},{7,5},{8,14},{9,15},{10,... | collective-permute-start | bytes 1572872 | tf_op jit(solution)/shard_map/ppermute | solution.py:626
  162.9 6.8 %shard_map.108 = (f32[256,128]{1,0:T(8,128)}, f32[192,128]{1,0:T(8,128)}, f32[4,4096]{1,0:T(4,128)}) custom-call(bf16[8,32,512]{2,1,0:T(8,128)(2,1)S(1)} %all-to-all-done.5.grads, f32[1,4096]{1,0:T(1,128)S(1)} %bitcast.34, f32[192,4096]{1,0:T(8,128)} %get-tuple-element.59.x.summed_in.summed, bf16[384,4096]{1,0:T(8,128)(2,1)} %get-tuple-element.91.fetched_in, ...), custom_call_target="tpu_custom_call" | custom-call | tf_op jit(solution)/shard_map/pallas_call | solution.py:693
  169.7 5.9 %all-to-all-start.6 = ((f32[16,16,128]{2,1,0:T(8,128)}), f32[16,16,128]{2,1,0:T(8,128)S(1)}, u32[]{:S(2)}, u32[]{:S(2)}) async-start(f32[16,16,128]{2,1,0:T(8,128)} %bitcast.13), calls=%async_computation.6 | async-start | bytes 262144 | tf_op jit(solution)/shard_map/all_to_all | solution.py:65
  175.8 6.5 %shard_map.109 = bf16[192,4096]{1,0:T(8,128)(2,1)} custom-call(f32[192,4096]{1,0:T(8,128)} %get-tuple-element.59.x.summed_in.summed, f32[4,4096]{1,0:T(4,128)} %get-tuple-element.94.weighted, f32[192,128]{1,0:T(8,128)} %get-tuple-element.95.state, bf16[128,4096]{1,0:T(8,128)(2,1)S(1)} %pad.18.router), custom_call_target="tpu_custom_call" | custom-call | flops 201326592 | bytes 5242880 | tf_op jit(solution)/shard_map/pallas_call | solution.py:506
  183.8 29.9 %all-to-all-start.7 = ((f32[16,16,128]{2,1,0:T(8,128)}), f32[16,16,128]{2,1,0:T(8,128)S(1)}, u32[]{:S(2)}, u32[]{:S(2)}) async-start(f32[16,16,128]{2,1,0:T(8,128)} %broadcast_in_dim.101), calls=%async_computation.7 | async-start | bytes 262144 | tf_op jit(solution)/shard_map/all_to_all | solution.py:65
  214.8 7.3 %shard_map.110 = bf16[8,64,4096]{2,1,0:T(8,128)(2,1)} custom-call(s32[1]{0:T(128)} %bitcast.4.place, bf16[8,32,512]{2,1,0:T(8,128)(2,1)S(1)} %all-to-all-done.5.grads, f32[1,4096]{1,0:T(1,128)S(1)} %bitcast.35, f32[8,64,8]{2,1,0:T(8,128)S(1)} %pad.19.notes, bf16[64,4096]{1,0:T(8,128)(2,1)} %get-tuple-element.101.rest_0_, bf16[64,4096]{1,0:T(8,128)(2,1)} %copy-done.4, ...), custom_call_target="tpu_custom_call" | custom-call | flops 25165824 | bytes 9437184 | tf_op jit(solution)/shard_map/pallas_call | solution.py:569
  222.7 5.1 %all-to-all-start.8 = ((f32[16,16,128]{2,1,0:T(8,128)}), f32[16,16,128]{2,1,0:T(8,128)S(1)}, u32[]{:S(2)}, u32[]{:S(2)}) async-start(f32[16,16,128]{2,1,0:T(8,128)} %broadcast_in_dim.102), calls=%async_computation.8 | async-start | bytes 262144 | tf_op jit(solution)/shard_map/all_to_all | solution.py:65
  228.4 6.9 %all-to-all-done.8 = f32[16,16,128]{2,1,0:T(8,128)S(1)} async-done(((f32[16,16,128]{2,1,0:T(8,128)}), f32[16,16,128]{2,1,0:T(8,128)S(1)}, u32[]{:S(2)}, u32[]{:S(2)}) %all-to-all-start.8) | async-done | bytes 131104 | tf_op jit(solution)/shard_map/all_to_all | solution.py:65
  (79 shorter events, 25.4 us)
Async XLA Ops:
  0.6 7.8 %copy-start = (bf16[192,4096]{1,0:T(8,128)(2,1)S(1)}, bf16[192,4096]{1,0:T(8,128)(2,1)}, u32[]{:S(2)}) copy-start(bf16[192,4096]{1,0:T(8,128)(2,1)} %tok_in.1) | copy-start | bytes 4718596
  0.7 7.8 %copy-start.7 = (bf16[4096,8]{0,1:T(8,128)(2,1)S(1)}, bf16[4096,8]{0,1:T(8,128)(2,1)}, u32[]{:S(2)}) copy-start(bf16[4096,8]{0,1:T(8,128)(2,1)} %param.11) | copy-start | bytes 196612
  0.7 56.4 %copy-start.1 = (f32[4096]{0:T(1024)S(1)}, f32[4096]{0:T(1024)}, u32[]{:S(2)}) copy-start(f32[4096]{0:T(1024)} %param.12) | copy-start | bytes 49156
  0.7 56.3 %all-to-all-start = ((bf16[8,64,4096]{2,1,0:T(8,128)(2,1)}), bf16[8,64,4096]{2,1,0:T(8,128)(2,1)}, u32[]{:S(2)}, u32[]{:S(2)}) async-start(bf16[8,64,4096]{2,1,0:T(8,128)(2,1)} %bitcast.36), calls=%async_computation | async-start | bytes 8388608 | tf_op jit(solution)/shard_map/all_to_all | solution.py:65
  65.2 21.2 %copy-start.9 = (s32[2]{0:T(128)S(1)}, s32[2]{0:T(128)}, u32[]{:S(2)}) copy-start(s32[2]{0:T(128)} %param.9) | copy-start | bytes 28
  65.2 11.8 %all-to-all-start.1 = ((bf16[8,4,512]{2,1,0:T(4,128)(2,1)}), bf16[8,4,512]{2,1,0:T(4,128)(2,1)S(1)}, u32[]{:S(2)}, u32[]{:S(2)}) async-start(bf16[8,4,512]{2,1,0:T(4,128)(2,1)} %get-tuple-element.58), calls=%async_computation.1 | async-start | bytes 65536 | tf_op jit(solution)/shard_map/all_to_all | solution.py:65
  77.9 21.1 %all-to-all-start.2 = ((bf16[16,32,512]{2,1,0:T(8,128)(2,1)}), bf16[16,32,512]{2,1,0:T(8,128)(2,1)S(1)}, u32[]{:S(2)}, u32[]{:S(2)}) async-start(bf16[16,32,512]{2,1,0:T(8,128)(2,1)} %broadcast_in_dim.89), calls=%async_computation.2 | async-start | bytes 1048576 | tf_op jit(solution)/shard_map/all_to_all | solution.py:65
  99.0 4.8 %collective-permute-start = (bf16[16,32,512]{2,1,0:T(8,128)(2,1)S(1)}, bf16[16,32,512]{2,1,0:T(8,128)(2,1)S(1)}, u32[]{:S(2)}, u32[]{:S(2)}) collective-permute-start(bf16[16,32,512]{2,1,0:T(8,128)(2,1)S(1)} %all-to-all-done.2), channel_id=1, source_target_pairs={{0,8},{8,0},{1,9},{9,1},{2,10},{10,2},{3,11},{11,3},{4,12},{12,4},... | collective-permute-start | bytes 1572872 | tf_op jit(solution)/shard_map/ppermute | solution.py:61
  105.4 17.1 %all-to-all-start.3 = ((f32[8,40,512]{2,1,0:T(8,128)}), f32[8,40,512]{2,1,0:T(8,128)S(1)}, u32[]{:S(2)}, u32[]{:S(2)}) async-start(f32[8,40,512]{2,1,0:T(8,128)} %shard_map.105), calls=%async_computation.3 | async-start | bytes 1310720 | tf_op jit(solution)/shard_map/all_to_all | solution.py:65
  111.8 23.7 %collective-permute-start.1 = (bf16[64,4096]{1,0:T(8,128)(2,1)}, bf16[64,4096]{1,0:T(8,128)(2,1)S(1)}, u32[]{:S(2)}, u32[]{:S(2)}) collective-permute-start(bf16[64,4096]{1,0:T(8,128)(2,1)} %get-tuple-element.81), channel_id=1, source_target_pairs={{0,4},{1,5},{2,6},{3,7},{4,0},{5,1},{6,2},{7,3},{8,12},{9,13},{10,... | collective-permute-start | bytes 1572872 | tf_op jit(solution)/shard_map/ppermute | solution.py:626
  114.8 43.5 %collective-permute-start.2 = (bf16[64,4096]{1,0:T(8,128)(2,1)}, bf16[64,4096]{1,0:T(8,128)(2,1)S(1)}, u32[]{:S(2)}, u32[]{:S(2)}) collective-permute-start(bf16[64,4096]{1,0:T(8,128)(2,1)} %get-tuple-element.88), channel_id=1, source_target_pairs={{0,1},{1,2},{2,3},{3,4},{4,5},{5,6},{6,7},{7,0},{8,9},{9,10},{10,1... | collective-permute-start | bytes 1572872 | tf_op jit(solution)/shard_map/ppermute | solution.py:626
  116.0 45.0 %collective-permute-start.3 = (bf16[64,4096]{1,0:T(8,128)(2,1)}, bf16[64,4096]{1,0:T(8,128)(2,1)S(1)}, u32[]{:S(2)}, u32[]{:S(2)}) collective-permute-start(bf16[64,4096]{1,0:T(8,128)(2,1)} %get-tuple-element.89), channel_id=1, source_target_pairs={{0,7},{1,0},{2,1},{3,2},{4,3},{5,4},{6,5},{7,6},{8,15},{9,8},{10,9... | collective-permute-start | bytes 1572872 | tf_op jit(solution)/shard_map/ppermute | solution.py:626
  123.5 21.7 %all-to-all-start.4 = ((f32[32,8,128]{2,1,0:T(8,128)}), f32[32,8,128]{2,1,0:T(8,128)S(1)}, u32[]{:S(2)}, u32[]{:S(2)}) async-start(f32[32,8,128]{2,1,0:T(8,128)} %get-tuple-element.80), calls=%async_computation.4 | async-start | bytes 262144 | tf_op jit(solution)/shard_map/all_to_all | solution.py:65
  130.9 52.2 %collective-permute-start.4 = (bf16[64,4096]{1,0:T(8,128)(2,1)}, bf16[64,4096]{1,0:T(8,128)(2,1)}, u32[]{:S(2)}, u32[]{:S(2)}) collective-permute-start(bf16[64,4096]{1,0:T(8,128)(2,1)} %get-tuple-element.98), channel_id=1, source_target_pairs={{0,3},{1,4},{2,5},{3,6},{4,7},{5,0},{6,1},{7,2},{8,11},{9,12},{10,... | collective-permute-start | bytes 1572872 | tf_op jit(solution)/shard_map/ppermute | solution.py:626
  133.0 50.1 %collective-permute-start.5 = (bf16[64,4096]{1,0:T(8,128)(2,1)}, bf16[64,4096]{1,0:T(8,128)(2,1)}, u32[]{:S(2)}, u32[]{:S(2)}) collective-permute-start(bf16[64,4096]{1,0:T(8,128)(2,1)} %get-tuple-element.99), channel_id=1, source_target_pairs={{0,5},{1,6},{2,7},{3,0},{4,1},{5,2},{6,3},{7,4},{8,13},{9,14},{10,... | collective-permute-start | bytes 1572872 | tf_op jit(solution)/shard_map/ppermute | solution.py:626
  135.5 34.2 %copy-start.3 = (bf16[64,4096]{1,0:T(8,128)(2,1)}, bf16[64,4096]{1,0:T(8,128)(2,1)S(1)}, u32[]{:S(2)}) copy-start(bf16[64,4096]{1,0:T(8,128)(2,1)S(1)} %collective-permute-done.1.rest_4_) | copy-start | bytes 1572868
  148.0 14.9 %all-to-all-start.5 = ((bf16[8,32,512]{2,1,0:T(8,128)(2,1)}), bf16[8,32,512]{2,1,0:T(8,128)(2,1)S(1)}, u32[]{:S(2)}, u32[]{:S(2)}) async-start(bf16[8,32,512]{2,1,0:T(8,128)(2,1)} %get-tuple-element.87), calls=%async_computation.5 | async-start | bytes 524288 | tf_op jit(solution)/shard_map/all_to_all | solution.py:65
  155.3 58.7 %collective-permute-start.6 = (bf16[64,4096]{1,0:T(8,128)(2,1)}, bf16[64,4096]{1,0:T(8,128)(2,1)S(1)}, u32[]{:S(2)}, u32[]{:S(2)}) collective-permute-start(bf16[64,4096]{1,0:T(8,128)(2,1)} %get-tuple-element.103), channel_id=1, source_target_pairs={{0,2},{1,3},{2,4},{3,5},{4,6},{5,7},{6,0},{7,1},{8,10},{9,11},{10,... | collective-permute-start | bytes 1572872 | tf_op jit(solution)/shard_map/ppermute | solution.py:626
  158.3 11.5 %copy-start.4 = (bf16[64,4096]{1,0:T(8,128)(2,1)}, bf16[64,4096]{1,0:T(8,128)(2,1)S(1)}, u32[]{:S(2)}) copy-start(bf16[64,4096]{1,0:T(8,128)(2,1)S(1)} %collective-permute-done.2.rest_1_) | copy-start | bytes 1572868
  158.3 55.7 %collective-permute-start.7 = (bf16[64,4096]{1,0:T(8,128)(2,1)}, bf16[64,4096]{1,0:T(8,128)(2,1)}, u32[]{:S(2)}, u32[]{:S(2)}) collective-permute-start(bf16[64,4096]{1,0:T(8,128)(2,1)} %get-tuple-element.107), channel_id=1, source_target_pairs={{0,6},{1,7},{2,0},{3,1},{4,2},{5,3},{6,4},{7,5},{8,14},{9,15},{10,... | collective-permute-start | bytes 1572872 | tf_op jit(solution)/shard_map/ppermute | solution.py:626
  161.0 8.8 %copy-start.5 = (bf16[64,4096]{1,0:T(8,128)(2,1)}, bf16[64,4096]{1,0:T(8,128)(2,1)S(1)}, u32[]{:S(2)}) copy-start(bf16[64,4096]{1,0:T(8,128)(2,1)S(1)} %collective-permute-done.3.rest_7_) | copy-start | bytes 1572868
  169.7 13.3 %all-to-all-start.6 = ((f32[16,16,128]{2,1,0:T(8,128)}), f32[16,16,128]{2,1,0:T(8,128)S(1)}, u32[]{:S(2)}, u32[]{:S(2)}) async-start(f32[16,16,128]{2,1,0:T(8,128)} %bitcast.13), calls=%async_computation.6 | async-start | bytes 262144 | tf_op jit(solution)/shard_map/all_to_all | solution.py:65
  183.8 38.3 %all-to-all-start.7 = ((f32[16,16,128]{2,1,0:T(8,128)}), f32[16,16,128]{2,1,0:T(8,128)S(1)}, u32[]{:S(2)}, u32[]{:S(2)}) async-start(f32[16,16,128]{2,1,0:T(8,128)} %broadcast_in_dim.101), calls=%async_computation.7 | async-start | bytes 262144 | tf_op jit(solution)/shard_map/all_to_all | solution.py:65
  222.7 12.6 %all-to-all-start.8 = ((f32[16,16,128]{2,1,0:T(8,128)}), f32[16,16,128]{2,1,0:T(8,128)S(1)}, u32[]{:S(2)}, u32[]{:S(2)}) async-start(f32[16,16,128]{2,1,0:T(8,128)} %broadcast_in_dim.102), calls=%async_computation.8 | async-start | bytes 262144 | tf_op jit(solution)/shard_map/all_to_all | solution.py:65
  (3 other events, 9.3 us)

commit v10 on v8

--- a/solution.py
+++ b/solution.py
@@ -519,74 +519,72 @@
     )(*in_hbm(summed, weighted, state), router)
 
 
-def expert_kernel(place, grads, gain, notes, *rest):
-    *sources, out, backs, sems = rest
-    experts = len(sources)
-    _, _, part = grads.shape
+def expert_kernel(count, source, grads, gain, notes, *rest):
+    sources, (out, backs, sems) = rest[:count], rest[-3:]
+    experts, _, part = grads.shape
     step = pl.program_id(0)
-    source = lax.rem(place[0] + experts - step, experts)
     gate, inv, seq = notes[0, :, 0:1], notes[0, :, 1:2], notes[0, :, 2:3]
     capacity = gate.shape[0]
-    loads = [pltpu.make_async_copy(sources[r], backs.at[r], sems.at[r]) for r in range(experts)]
+    loads = [pltpu.make_async_copy(sources[r], backs.at[r], sems.at[r]) for r in range(count)]
 
     @pl.when(step == 0)
     def _():
         for load in loads:
             load.start()
 
-    for r in range(experts):
+    for r in range(count):
 
         @pl.when(step == r)
         def _():
             loads[r].wait()
-            back = backs.at[r]
-            acc = jnp.zeros((capacity, 128), F32)
-            rows = []
-            for e in range(experts):
-                cols = slice(part * e, part * (e + 1))
-                w = rows_of(grads, e, source) * (gain[:, cols] / SEQ)
-                x = jnp.broadcast_to(w[0:1], (capacity, part))
-                for s in range(1, ROWS_DEV):
-                    x = jnp.where(seq == s, w[s : s + 1], x)
-                rows.append(w)
-                acc = acc + fold(x * back[:, cols].astype(F32))
-            shrink = inv * inv * inv * (jnp.sum(acc, axis=1, keepdims=True) / (experts * part))
-            for e in range(experts):
-                cols = slice(part * e, part * (e + 1))
-                w = rows[e]
-                x = jnp.broadcast_to(w[0:1], (capacity, part))
-                for s in range(1, ROWS_DEV):
-                    x = jnp.where(seq == s, w[s : s + 1], x)
-                x = gate * (inv * x - shrink * back[:, cols].astype(F32))
-                out[0, :, cols] = x.astype(BF16)
-
-
-def expert_rows(place, grads, gain, notes, backs):
+
+    def gradient_rows(e):
+        w = rows_of(grads, e, source[step]) * (gain[:, part * e : part * (e + 1)] / SEQ)
+        x = jnp.broadcast_to(w[0:1], (capacity, part))
+        for s in range(1, ROWS_DEV):
+            x = jnp.where(seq == s, w[s : s + 1], x)
+        return x
+
+    acc = jnp.zeros((capacity, 128), F32)
+    for e in range(experts):
+        back = backs[step, :, part * e : part * (e + 1)].astype(F32)
+        acc = acc + fold(gradient_rows(e) * back)
+    shrink = inv * inv * inv * (jnp.sum(acc, axis=1, keepdims=True) / (experts * part))
+    keep, drop = gate * inv, gate * shrink
+    for e in range(experts):
+        cols = slice(part * e, part * (e + 1))
+        out[0, :, cols] = (keep * gradient_rows(e) - drop * backs[step, :, cols].astype(F32)).astype(BF16)
+
+
+def expert_rows(source, grads, gain, notes, backs, before=None):
     experts, capacity = notes.shape[:2]
     width = gain.shape[1]
+    count = len(backs)
     whole = lambda shape: pl.BlockSpec(shape, lambda i, p: (0,) * len(shape))
-    source = lambda i, p: (lax.rem(p[0] + experts - i, experts), 0, 0)
+    block = lambda i, p: (p[i], 0, 0)
+    kept = [] if before is None else [before]
     return pl.pallas_call(
-        expert_kernel,
+        functools.partial(expert_kernel, count),
         grid_spec=pltpu.PrefetchScalarGridSpec(
             num_scalar_prefetch=1,
-            grid=(experts,),
+            grid=(count,),
             in_specs=[
                 whole(grads.shape),
                 whole((1, width)),
-                pl.BlockSpec((1, capacity, notes.shape[2]), source),
+                pl.BlockSpec((1, capacity, notes.shape[2]), block),
             ]
-            + [HBM] * experts,
-            out_specs=pl.BlockSpec((1, capacity, width), source),
+            + [HBM] * (count + len(kept)),
+            out_specs=pl.BlockSpec((1, capacity, width), block),
             scratch_shapes=[
-                pltpu.VMEM((experts, capacity, width), BF16),
-                pltpu.SemaphoreType.DMA((experts,)),
+                pltpu.VMEM((count, capacity, width), BF16),
+                pltpu.SemaphoreType.DMA((count,)),
             ],
         ),
         out_shape=jax.ShapeDtypeStruct((experts, capacity, width), BF16),
+        input_output_aliases={4 + count: 0} if kept else {},
         compiler_params=params(16),
-        cost_estimate=cost(12 * experts * capacity * width, 9 << 20),
-    )(place, grads, gain, notes, *in_hbm(*backs))
+        cost_estimate=cost(12 * count * capacity * width, count << 20),
+    )(source, grads, gain, notes, *in_hbm(*backs), *kept)
 
 
 def shards(tokens, routes, positives, expert_out, router, norm_gain, loss_scale):
@@ -675,7 +673,6 @@
         ],
         compiler_params=params(2),
     )(gathered)
-    offered = move(offered, TURNS[1])
     heard = exchange(offered, ("u", "c"))
     heard = landed(heard, TURNS[0][:1])
     offered, loss = pl.pallas_call(
@@ -686,7 +683,7 @@
         scratch_shapes=[pltpu.VMEM((2 * group, part), BF16), pltpu.SemaphoreType.DMA((experts,))],
         compiler_params=params(2),
     )((loss_scale / pairs)[None], heard, kept, near, far)
-    offered = move(offered, TURNS[2])
+    offered = move(offered, TURNS[1])
     grads = exchange(offered, "expert")
     grads = landed(grads, TURNS[0][1:])
 
@@ -713,18 +710,21 @@
         ],
         compiler_params=params(16),
     )(grads, gain, *in_hbm(summed, fetched, tokens, facts))
+    router_part = move(router_part, TURNS[2])
     router_part = exchange(router_part.reshape(outer, -1, 128), "u")
-    router_part = landed(router_part, TURNS[1])
     router_part = jnp.sum(router_part, axis=0)
     router_part = spread(router_part, ("c", "expert"), CORES * experts)
     held = lax.dynamic_slice_in_dim(gathered[:, 2 * group : 2 * group + 3], mine * capacity, capacity, axis=2)
     held = jnp.pad(jnp.transpose(held, (0, 2, 1)), ((0, 0), (0, 0), (0, 5)))
     turned = jnp.pad(router.T, ((0, 128 - experts), (0, 0)))
     token_grad = token_rows(summed, weighted, state, turned, experts)
-    router_part, token_grad = lax.optimization_barrier((router_part, token_grad))
+    parts = [(0,) + TURNS[0] + TURNS[1], TURNS[2]]
+    places = [(mine + experts - jnp.array(turns, I32)) % experts for turns in parts]
+    expert_grad = expert_rows(places[0], grads, gain, held, [backs[r] for r in parts[0]])
+    router_part, token_grad, expert_grad = lax.optimization_barrier((router_part, token_grad, expert_grad))
     router_part = jnp.sum(router_part, axis=0)
     router_all = spread(router_part, "u", outer)
-    expert_grad = expert_rows(mine_at, grads, gain, held, backs)
+    expert_grad = expert_rows(places[1], grads, gain, held, [backs[r] for r in parts[1]], expert_grad)
     router_all, expert_grad = lax.optimization_barrier((router_all, expert_grad))
     router_grad = router_all.reshape(-1, experts, 128).transpose(1, 0, 2).reshape(experts, width).T
     return token_grad, expert_grad.reshape(1, 1, experts, capacity, width), router_grad, loss[0, 0] / pairs

time: 227 us -> 226 us (level)
  waiting for transfers between devices: 80.5 us -> 75.1 us
  Pallas kernels: 47.4 us -> 51 us
    all_to_all x9, waiting for transfers between devices: 79.8 us -> 72.5 us  [exchange(): return lax.all_to_all(x, axes, split_axis=0, concat_axis=0, tiled=True)]
    pallas_call x1 -> x2, Pallas kernels: 7.25 us -> 10.9 us  [expert_rows(): pl.pallas_call(functools.partial(expert_kernel, count), grid_spec=pltpu.P...]
  transfers between devices with their start and end apart: 17 -> 17, of which waited for: 9 -> 11; matrix products, arithmetic and copies ran while one was open for 3% -> 3% of each run, Pallas kernels for 17% -> 18%
where the time goes in v10:
time: 226 us; the launch traced here: 225 us
  starting transfers between devices  84.9 us (38%)
  waiting for transfers between devices  75.1 us (33%)
  Pallas kernels  51 us (23%)
  local copies, waits for them, and re-layouts  7.24 us (3%)
  between operations  3.48 us (2%)
    all_to_all x9, waiting for transfers between devices, exchange(): return lax.all_to_all(x, axes, split_axis=0, concat_axis=0, tiled=True)  72.5 us
    all_to_all x9, starting transfers between devices, exchange(): return lax.all_to_all(x, axes, split_axis=0, concat_axis=0, tiled=True)  64.1 us
    ppermute x7, starting transfers between devices, move(): lax.ppermute(x, 'expert', [(i, (i + r) % experts) for i in range(experts)])  17.4 us
    pallas_call x2, Pallas kernels, expert_rows(): pl.pallas_call(functools.partial(expert_kernel, count), grid_spec=pltpu.P...  10.9 us
    pallas_call x1, Pallas kernels, overlaps(): pl.pallas_call(functools.partial(overlap_kernel, experts), grid=(experts,...  8.59 us
    pallas_call x1, Pallas kernels, forward(): pl.pallas_call(functools.partial(forward_kernel, experts), grid=(experts,...  8.12 us
    pallas_call x1, Pallas kernels, shards(): pl.pallas_call(router_kernel, in_specs=[VMEM] * 2 + [HBM] * 4, out_specs=...  6.8 us
    pallas_call x1, Pallas kernels, token_rows(): pl.pallas_call(functools.partial(token_kernel, experts), grid=(experts,),...  6.47 us
  transfers between devices with their start and end apart: 17, of which 11 were waited for; matrix products, arithmetic and copies ran while one was open for 3% of the time, Pallas kernels for 18%

profile of v10, /device:TPU:1, one launch (start us, length us, event | category | flops | bytes accessed | tf_op | source)
XLA Modules:
  0.0 224.5 jit_solution(6299098277067387842)
XLA Ops:
  0.7 7.6 %all-to-all-start = ((bf16[8,64,4096]{2,1,0:T(8,128)(2,1)}), bf16[8,64,4096]{2,1,0:T(8,128)(2,1)}, u32[]{:S(2)}, u32[]{:S(2)}) async-start(bf16[8,64,4096]{2,1,0:T(8,128)(2,1)} %bitcast.38), calls=%async_computation | async-start | bytes 8388608 | tf_op jit(solution)/shard_map/all_to_all | solution.py:65
  9.8 47.2 %all-to-all-done = bf16[8,64,4096]{2,1,0:T(8,128)(2,1)} async-done(((bf16[8,64,4096]{2,1,0:T(8,128)(2,1)}), bf16[8,64,4096]{2,1,0:T(8,128)(2,1)}, u32[]{:S(2)}, u32[]{:S(2)}) %all-to-all-start) | async-done | bytes 4194336 | tf_op jit(solution)/shard_map/all_to_all | solution.py:65
  57.0 8.1 %shard_map.120 = (f32[192,4096]{1,0:T(8,128)}, bf16[8,4,512]{2,1,0:T(4,128)(2,1)}, f32[192,1]{1,0:T(8,128)S(1)}) custom-call(bf16[192,4096]{1,0:T(8,128)(2,1)S(1)} %copy-done, bf16[512,4096]{1,0:T(8,128)(2,1)} %bitcast.2.rec, s32[192,2]{1,0:T(8,128)S(1)} %add.74.slot, f32[192,2]{1,0:T(8,128)S(1)} %exponential_divide_fusion.gate, f32[1,4096]{1,0:T(1,128)S(1)} %bitcast.33), custom_call_target="tpu_custom_call" | custom-call | flops 1610612736 | bytes 10485760 | tf_op jit(solution)/shard_map/pallas_call | solution.py:137
  65.2 5.2 %all-to-all-start.1 = ((bf16[8,4,512]{2,1,0:T(4,128)(2,1)}), bf16[8,4,512]{2,1,0:T(4,128)(2,1)S(1)}, u32[]{:S(2)}, u32[]{:S(2)}) async-start(bf16[8,4,512]{2,1,0:T(4,128)(2,1)} %get-tuple-element.56), calls=%async_computation.1 | async-start | bytes 65536 | tf_op jit(solution)/shard_map/all_to_all | solution.py:65
  70.4 5.7 %shard_map.121 = (bf16[64,4096]{1,0:T(8,128)(2,1)}, bf16[64,4096]{1,0:T(8,128)(2,1)}, bf16[64,4096]{1,0:T(8,128)(2,1)}, bf16[64,4096]{1,0:T(8,128)(2,1)}, bf16[6...) custom-call(s32[1]{0:T(128)} %bitcast.4.place, ...), custom_call_target="tpu_custom_call" | custom-call | flops 805306368 | bytes 7340032 | tf_op jit(solution)/shard_map/pallas_call | solution.py:204
  77.9 8.3 %all-to-all-start.2 = ((bf16[16,32,512]{2,1,0:T(8,128)(2,1)}), bf16[16,32,512]{2,1,0:T(8,128)(2,1)S(1)}, u32[]{:S(2)}, u32[]{:S(2)}) async-start(bf16[16,32,512]{2,1,0:T(8,128)(2,1)} %broadcast_in_dim.89), calls=%async_computation.2 | async-start | bytes 1048576 | tf_op jit(solution)/shard_map/all_to_all | solution.py:65
  88.4 8.6 %shard_map.122 = (f32[192,128]{1,0:T(8,128)}, bf16[384,4096]{1,0:T(8,128)(2,1)}) custom-call(f32[192,4096]{1,0:T(8,128)} %get-tuple-element.57.x.summed_in.summed, bf16[512,4096]{1,0:T(8,128)(2,1)} %bitcast.2.rec, s32[192,2]{1,0:T(8,128)S(1)} %add.74.slot, f32[192,128]{1,0:T(8,128)S(1)} %pad.16.facts), custom_call_target="tpu_custom_call" | custom-call | flops 1610612736 | bytes 10485760 | tf_op jit(solution)/shard_map/pallas_call | solution.py:256
  99.0 3.3 %collective-permute-start = (bf16[16,32,512]{2,1,0:T(8,128)(2,1)S(1)}, bf16[16,32,512]{2,1,0:T(8,128)(2,1)S(1)}, u32[]{:S(2)}, u32[]{:S(2)}) collective-permute-start(bf16[16,32,512]{2,1,0:T(8,128)(2,1)S(1)} %all-to-all-done.2), channel_id=1, source_target_pairs={{0,8},{8,0},{1,9},{9,1},{2,10},{10,2},{3,11},{11,3},{4,12},{12,4},... | collective-permute-start | bytes 1572872 | tf_op jit(solution)/shard_map/ppermute | solution.py:61
  105.4 6.4 %all-to-all-start.3 = ((f32[8,40,512]{2,1,0:T(8,128)}), f32[8,40,512]{2,1,0:T(8,128)S(1)}, u32[]{:S(2)}, u32[]{:S(2)}) async-start(f32[8,40,512]{2,1,0:T(8,128)} %shard_map.123), calls=%async_computation.3 | async-start | bytes 1310720 | tf_op jit(solution)/shard_map/all_to_all | solution.py:65
  111.8 3.0 %collective-permute-start.1 = (bf16[64,4096]{1,0:T(8,128)(2,1)}, bf16[64,4096]{1,0:T(8,128)(2,1)S(1)}, u32[]{:S(2)}, u32[]{:S(2)}) collective-permute-start(bf16[64,4096]{1,0:T(8,128)(2,1)} %get-tuple-element.76), channel_id=1, source_target_pairs={{0,4},{1,5},{2,6},{3,7},{4,0},{5,1},{6,2},{7,3},{8,12},{9,13},{10,... | collective-permute-start | bytes 1572872 | tf_op jit(solution)/shard_map/ppermute | solution.py:624
  115.9 3.9 %collective-permute-start.3 = (bf16[64,4096]{1,0:T(8,128)(2,1)}, bf16[64,4096]{1,0:T(8,128)(2,1)S(1)}, u32[]{:S(2)}, u32[]{:S(2)}) collective-permute-start(bf16[64,4096]{1,0:T(8,128)(2,1)} %get-tuple-element.84), channel_id=1, source_target_pairs={{0,7},{1,0},{2,1},{3,2},{4,3},{5,4},{6,5},{7,6},{8,15},{9,8},{10,9... | collective-permute-start | bytes 1572872 | tf_op jit(solution)/shard_map/ppermute | solution.py:624
  123.4 7.4 %all-to-all-start.4 = ((f32[32,8,128]{2,1,0:T(8,128)}), f32[32,8,128]{2,1,0:T(8,128)S(1)}, u32[]{:S(2)}, u32[]{:S(2)}) async-start(f32[32,8,128]{2,1,0:T(8,128)} %get-tuple-element.75), calls=%async_computation.4 | async-start | bytes 262144 | tf_op jit(solution)/shard_map/all_to_all | solution.py:65
  133.3 11.0 %all-to-all-done.4.heard = f32[32,8,128]{2,1,0:T(8,128)S(1)} async-done(((f32[32,8,128]{2,1,0:T(8,128)}), f32[32,8,128]{2,1,0:T(8,128)S(1)}, u32[]{:S(2)}, u32[]{:S(2)}) %all-to-all-start.4) | async-done | bytes 131104 | tf_op jit(solution)/shard_map/all_to_all | solution.py:65
  147.1 6.7 %all-to-all-start.5 = ((bf16[8,32,512]{2,1,0:T(8,128)(2,1)}), bf16[8,32,512]{2,1,0:T(8,128)(2,1)S(1)}, u32[]{:S(2)}, u32[]{:S(2)}) async-start(bf16[8,32,512]{2,1,0:T(8,128)(2,1)} %get-tuple-element.82), calls=%async_computation.5 | async-start | bytes 524288 | tf_op jit(solution)/shard_map/all_to_all | solution.py:65
  153.8 2.7 %collective-permute-start.4 = (bf16[64,4096]{1,0:T(8,128)(2,1)}, bf16[64,4096]{1,0:T(8,128)(2,1)}, u32[]{:S(2)}, u32[]{:S(2)}) collective-permute-start(bf16[64,4096]{1,0:T(8,128)(2,1)} %get-tuple-element.98), channel_id=1, source_target_pairs={{0,3},{1,4},{2,5},{3,6},{4,7},{5,0},{6,1},{7,2},{8,11},{9,12},{10,... | collective-permute-start | bytes 1572872 | tf_op jit(solution)/shard_map/ppermute | solution.py:624
  157.7 3.6 %all-to-all-done.5.grads = bf16[8,32,512]{2,1,0:T(8,128)(2,1)S(1)} async-done(((bf16[8,32,512]{2,1,0:T(8,128)(2,1)}), bf16[8,32,512]{2,1,0:T(8,128)(2,1)S(1)}, u32[]{:S(2)}, u32[]{:S(2)}) %all-to-all-start.5) | async-done | bytes 262176 | tf_op jit(solution)/shard_map/all_to_all | solution.py:65
  161.3 6.8 %shard_map.126 = (f32[256,128]{1,0:T(8,128)}, f32[192,128]{1,0:T(8,128)}, f32[4,4096]{1,0:T(4,128)}) custom-call(bf16[8,32,512]{2,1,0:T(8,128)(2,1)S(1)} %all-to-all-done.5.grads, f32[1,4096]{1,0:T(1,128)S(1)} %bitcast.34, f32[192,4096]{1,0:T(8,128)} %get-tuple-element.57.x.summed_in.summed, bf16[384,4096]{1,0:T(8,128)(2,1)} %get-tuple-element.86.fetched_in, ...), custom_call_target="tpu_custom_call" | custom-call | tf_op jit(solution)/shard_map/pallas_call | solution.py:690
  168.2 4.3 %all-to-all-start.6 = ((f32[16,16,128]{2,1,0:T(8,128)}), f32[16,16,128]{2,1,0:T(8,128)S(1)}, u32[]{:S(2)}, u32[]{:S(2)}) async-start(f32[16,16,128]{2,1,0:T(8,128)} %bitcast.13), calls=%async_computation.6 | async-start | bytes 262144 | tf_op jit(solution)/shard_map/all_to_all | solution.py:65
  173.6 4.5 %collective-permute-start.7 = (bf16[64,4096]{1,0:T(8,128)(2,1)}, bf16[64,4096]{1,0:T(8,128)(2,1)S(1)}, u32[]{:S(2)}, u32[]{:S(2)}) collective-permute-start(bf16[64,4096]{1,0:T(8,128)(2,1)} %get-tuple-element.103), channel_id=1, source_target_pairs={{0,6},{1,7},{2,0},{3,1},{4,2},{5,3},{6,4},{7,5},{8,14},{9,15},{10,... | collective-permute-start | bytes 1572872 | tf_op jit(solution)/shard_map/ppermute | solution.py:624
  180.6 13.3 %all-to-all-start.7 = ((f32[16,16,128]{2,1,0:T(8,128)}), f32[16,16,128]{2,1,0:T(8,128)S(1)}, u32[]{:S(2)}, u32[]{:S(2)}) async-start(f32[16,16,128]{2,1,0:T(8,128)} %broadcast_in_dim.101), calls=%async_computation.7 | async-start | bytes 262144 | tf_op jit(solution)/shard_map/all_to_all | solution.py:65
  194.2 6.5 %shard_map.127 = bf16[192,4096]{1,0:T(8,128)(2,1)} custom-call(f32[192,4096]{1,0:T(8,128)} %get-tuple-element.57.x.summed_in.summed, f32[4,4096]{1,0:T(4,128)} %get-tuple-element.92.weighted, f32[192,128]{1,0:T(8,128)} %get-tuple-element.93.state, bf16[128,4096]{1,0:T(8,128)(2,1)S(1)} %pad.18.router), custom_call_target="tpu_custom_call" | custom-call | flops 201326592 | bytes 5242880 | tf_op jit(solution)/shard_map/pallas_call | solution.py:506
  200.6 7.0 %shard_map.128.rest_2_ = bf16[8,64,4096]{2,1,0:T(8,128)(2,1)} custom-call(s32[6]{0:T(128)S(1)} %and_select_fusion.4.source, bf16[8,32,512]{2,1,0:T(8,128)(2,1)S(1)} %all-to-all-done.5.grads, f32[1,4096]{1,0:T(1,128)S(1)} %bitcast.35, f32[8,64,8]{2,1,0:T(8,128)S(1)} %pad.19.notes, bf16[64,4096]{1,0:T(8,128)(2,1)} %get-tuple-element.94.rest_0_, ...), custom_call_target="tpu_custom_call" | custom-call | flops 18874368 | bytes 6291456 | tf_op jit(solution)/shard_map/pallas_call | solution.py:566
  210.4 4.9 %all-to-all-start.8 = ((f32[16,16,128]{2,1,0:T(8,128)}), f32[16,16,128]{2,1,0:T(8,128)S(1)}, u32[]{:S(2)}, u32[]{:S(2)}) async-start(f32[16,16,128]{2,1,0:T(8,128)} %broadcast_in_dim.102), calls=%async_computation.8 | async-start | bytes 262144 | tf_op jit(solution)/shard_map/all_to_all | solution.py:65
  217.6 3.9 %shard_map.129 = bf16[8,64,4096]{2,1,0:T(8,128)(2,1)} custom-call(s32[2]{0:T(128)S(1)} %and_select_fusion.3.source, bf16[8,32,512]{2,1,0:T(8,128)(2,1)S(1)} %all-to-all-done.5.grads, f32[1,4096]{1,0:T(1,128)S(1)} %bitcast.36, f32[8,64,8]{2,1,0:T(8,128)S(1)} %pad.19.notes, bf16[64,4096]{1,0:T(8,128)(2,1)} %copy-done.6, ...), custom_call_target="tpu_custom_call", output_to_operand_aliasing={{}: (6, {})} | custom-call | flops 6291456 | bytes 2097152 | tf_op jit(solution)/shard_map/pallas_call | solution.py:566
  (88 shorter events, 31.3 us)
Async XLA Ops:
  0.7 56.4 %copy-start.1 = (f32[4096]{0:T(1024)S(1)}, f32[4096]{0:T(1024)}, u32[]{:S(2)}) copy-start(f32[4096]{0:T(1024)} %param.14) | copy-start | bytes 49156
  0.7 56.3 %all-to-all-start = ((bf16[8,64,4096]{2,1,0:T(8,128)(2,1)}), bf16[8,64,4096]{2,1,0:T(8,128)(2,1)}, u32[]{:S(2)}, u32[]{:S(2)}) async-start(bf16[8,64,4096]{2,1,0:T(8,128)(2,1)} %bitcast.38), calls=%async_computation | async-start | bytes 8388608 | tf_op jit(solution)/shard_map/all_to_all | solution.py:65
  65.2 21.2 %copy-start.10 = (s32[2]{0:T(128)S(1)}, s32[2]{0:T(128)}, u32[]{:S(2)}) copy-start(s32[2]{0:T(128)} %param.11) | copy-start | bytes 28
  65.2 11.8 %all-to-all-start.1 = ((bf16[8,4,512]{2,1,0:T(4,128)(2,1)}), bf16[8,4,512]{2,1,0:T(4,128)(2,1)S(1)}, u32[]{:S(2)}, u32[]{:S(2)}) async-start(bf16[8,4,512]{2,1,0:T(4,128)(2,1)} %get-tuple-element.56), calls=%async_computation.1 | async-start | bytes 65536 | tf_op jit(solution)/shard_map/all_to_all | solution.py:65
  77.9 21.1 %all-to-all-start.2 = ((bf16[16,32,512]{2,1,0:T(8,128)(2,1)}), bf16[16,32,512]{2,1,0:T(8,128)(2,1)S(1)}, u32[]{:S(2)}, u32[]{:S(2)}) async-start(bf16[16,32,512]{2,1,0:T(8,128)(2,1)} %broadcast_in_dim.89), calls=%async_computation.2 | async-start | bytes 1048576 | tf_op jit(solution)/shard_map/all_to_all | solution.py:65
  99.0 4.8 %collective-permute-start = (bf16[16,32,512]{2,1,0:T(8,128)(2,1)S(1)}, bf16[16,32,512]{2,1,0:T(8,128)(2,1)S(1)}, u32[]{:S(2)}, u32[]{:S(2)}) collective-permute-start(bf16[16,32,512]{2,1,0:T(8,128)(2,1)S(1)} %all-to-all-done.2), channel_id=1, source_target_pairs={{0,8},{8,0},{1,9},{9,1},{2,10},{10,2},{3,11},{11,3},{4,12},{12,4},... | collective-permute-start | bytes 1572872 | tf_op jit(solution)/shard_map/ppermute | solution.py:61
  105.4 17.0 %all-to-all-start.3 = ((f32[8,40,512]{2,1,0:T(8,128)}), f32[8,40,512]{2,1,0:T(8,128)S(1)}, u32[]{:S(2)}, u32[]{:S(2)}) async-start(f32[8,40,512]{2,1,0:T(8,128)} %shard_map.123), calls=%async_computation.3 | async-start | bytes 1310720 | tf_op jit(solution)/shard_map/all_to_all | solution.py:65
  111.8 21.5 %collective-permute-start.1 = (bf16[64,4096]{1,0:T(8,128)(2,1)}, bf16[64,4096]{1,0:T(8,128)(2,1)S(1)}, u32[]{:S(2)}, u32[]{:S(2)}) collective-permute-start(bf16[64,4096]{1,0:T(8,128)(2,1)} %get-tuple-element.76), channel_id=1, source_target_pairs={{0,4},{1,5},{2,6},{3,7},{4,0},{5,1},{6,2},{7,3},{8,12},{9,13},{10,... | collective-permute-start | bytes 1572872 | tf_op jit(solution)/shard_map/ppermute | solution.py:624
  114.8 43.0 %collective-permute-start.2 = (bf16[64,4096]{1,0:T(8,128)(2,1)}, bf16[64,4096]{1,0:T(8,128)(2,1)S(1)}, u32[]{:S(2)}, u32[]{:S(2)}) collective-permute-start(bf16[64,4096]{1,0:T(8,128)(2,1)} %get-tuple-element.83), channel_id=1, source_target_pairs={{0,1},{1,2},{2,3},{3,4},{4,5},{5,6},{6,7},{7,0},{8,9},{9,10},{10,1... | collective-permute-start | bytes 1572872 | tf_op jit(solution)/shard_map/ppermute | solution.py:624
  115.9 41.8 %collective-permute-start.3 = (bf16[64,4096]{1,0:T(8,128)(2,1)}, bf16[64,4096]{1,0:T(8,128)(2,1)S(1)}, u32[]{:S(2)}, u32[]{:S(2)}) collective-permute-start(bf16[64,4096]{1,0:T(8,128)(2,1)} %get-tuple-element.84), channel_id=1, source_target_pairs={{0,7},{1,0},{2,1},{3,2},{4,3},{5,4},{6,5},{7,6},{8,15},{9,8},{10,9... | collective-permute-start | bytes 1572872 | tf_op jit(solution)/shard_map/ppermute | solution.py:624
  123.4 20.9 %all-to-all-start.4 = ((f32[32,8,128]{2,1,0:T(8,128)}), f32[32,8,128]{2,1,0:T(8,128)S(1)}, u32[]{:S(2)}, u32[]{:S(2)}) async-start(f32[32,8,128]{2,1,0:T(8,128)} %get-tuple-element.75), calls=%async_computation.4 | async-start | bytes 262144 | tf_op jit(solution)/shard_map/all_to_all | solution.py:65
  133.3 34.8 %copy-start.3 = (bf16[64,4096]{1,0:T(8,128)(2,1)}, bf16[64,4096]{1,0:T(8,128)(2,1)S(1)}, u32[]{:S(2)}) copy-start(bf16[64,4096]{1,0:T(8,128)(2,1)S(1)} %collective-permute-done.1.rest_1_) | copy-start | bytes 1572868
  147.1 14.3 %all-to-all-start.5 = ((bf16[8,32,512]{2,1,0:T(8,128)(2,1)}), bf16[8,32,512]{2,1,0:T(8,128)(2,1)S(1)}, u32[]{:S(2)}, u32[]{:S(2)}) async-start(bf16[8,32,512]{2,1,0:T(8,128)(2,1)} %get-tuple-element.82), calls=%async_computation.5 | async-start | bytes 524288 | tf_op jit(solution)/shard_map/all_to_all | solution.py:65
  153.8 24.3 %copy-start.12 = (s32[6]{0:T(128)S(1)}, s32[6]{0:T(128)}, u32[]{:S(2)}) copy-start(s32[6]{0:T(128)} %constant.122) | copy-start | bytes 76
  153.8 46.9 %collective-permute-start.4 = (bf16[64,4096]{1,0:T(8,128)(2,1)}, bf16[64,4096]{1,0:T(8,128)(2,1)}, u32[]{:S(2)}, u32[]{:S(2)}) collective-permute-start(bf16[64,4096]{1,0:T(8,128)(2,1)} %get-tuple-element.98), channel_id=1, source_target_pairs={{0,3},{1,4},{2,5},{3,6},{4,7},{5,0},{6,1},{7,2},{8,11},{9,12},{10,... | collective-permute-start | bytes 1572872 | tf_op jit(solution)/shard_map/ppermute | solution.py:624
  156.4 44.2 %collective-permute-start.5 = (bf16[64,4096]{1,0:T(8,128)(2,1)}, bf16[64,4096]{1,0:T(8,128)(2,1)}, u32[]{:S(2)}, u32[]{:S(2)}) collective-permute-start(bf16[64,4096]{1,0:T(8,128)(2,1)} %get-tuple-element.99), channel_id=1, source_target_pairs={{0,5},{1,6},{2,7},{3,0},{4,1},{5,2},{6,3},{7,4},{8,13},{9,14},{10,... | collective-permute-start | bytes 1572872 | tf_op jit(solution)/shard_map/ppermute | solution.py:624
  157.7 10.5 %copy-start.4 = (bf16[64,4096]{1,0:T(8,128)(2,1)}, bf16[64,4096]{1,0:T(8,128)(2,1)S(1)}, u32[]{:S(2)}) copy-start(bf16[64,4096]{1,0:T(8,128)(2,1)S(1)} %collective-permute-done.2.rest_2_) | copy-start | bytes 1572868
  157.7 10.5 %copy-start.5 = (bf16[64,4096]{1,0:T(8,128)(2,1)}, bf16[64,4096]{1,0:T(8,128)(2,1)S(1)}, u32[]{:S(2)}) copy-start(bf16[64,4096]{1,0:T(8,128)(2,1)S(1)} %collective-permute-done.3.rest_3_) | copy-start | bytes 1572868
  168.2 11.7 %all-to-all-start.6 = ((f32[16,16,128]{2,1,0:T(8,128)}), f32[16,16,128]{2,1,0:T(8,128)S(1)}, u32[]{:S(2)}, u32[]{:S(2)}) async-start(f32[16,16,128]{2,1,0:T(8,128)} %bitcast.13), calls=%async_computation.6 | async-start | bytes 262144 | tf_op jit(solution)/shard_map/all_to_all | solution.py:65
  172.6 43.3 %collective-permute-start.6 = (bf16[64,4096]{1,0:T(8,128)(2,1)}, bf16[64,4096]{1,0:T(8,128)(2,1)S(1)}, u32[]{:S(2)}, u32[]{:S(2)}) collective-permute-start(bf16[64,4096]{1,0:T(8,128)(2,1)} %get-tuple-element.102), channel_id=1, source_target_pairs={{0,2},{1,3},{2,4},{3,5},{4,6},{5,7},{6,0},{7,1},{8,10},{9,11},{10,... | collective-permute-start | bytes 1572872 | tf_op jit(solution)/shard_map/ppermute | solution.py:624
  173.6 42.4 %collective-permute-start.7 = (bf16[64,4096]{1,0:T(8,128)(2,1)}, bf16[64,4096]{1,0:T(8,128)(2,1)S(1)}, u32[]{:S(2)}, u32[]{:S(2)}) collective-permute-start(bf16[64,4096]{1,0:T(8,128)(2,1)} %get-tuple-element.103), channel_id=1, source_target_pairs={{0,6},{1,7},{2,0},{3,1},{4,2},{5,3},{6,4},{7,5},{8,14},{9,15},{10,... | collective-permute-start | bytes 1572872 | tf_op jit(solution)/shard_map/ppermute | solution.py:624
  180.6 29.1 %all-to-all-start.7 = ((f32[16,16,128]{2,1,0:T(8,128)}), f32[16,16,128]{2,1,0:T(8,128)S(1)}, u32[]{:S(2)}, u32[]{:S(2)}) async-start(f32[16,16,128]{2,1,0:T(8,128)} %broadcast_in_dim.101), calls=%async_computation.7 | async-start | bytes 262144 | tf_op jit(solution)/shard_map/all_to_all | solution.py:65
  200.6 14.7 %copy-start.11 = (s32[2]{0:T(128)S(1)}, s32[2]{0:T(128)}, u32[]{:S(2)}) copy-start(s32[2]{0:T(128)} %constant.123) | copy-start | bytes 28
  210.4 12.3 %all-to-all-start.8 = ((f32[16,16,128]{2,1,0:T(8,128)}), f32[16,16,128]{2,1,0:T(8,128)S(1)}, u32[]{:S(2)}, u32[]{:S(2)}) async-start(f32[16,16,128]{2,1,0:T(8,128)} %broadcast_in_dim.102), calls=%async_computation.8 | async-start | bytes 262144 | tf_op jit(solution)/shard_map/all_to_all | solution.py:65
  (6 other events, 25.8 us)

commit v11 on v10

--- a/solution.py
+++ b/solution.py
@@ -20,7 +20,8 @@
 SMEM = pl.BlockSpec(memory_space=pltpu.SMEM)
 HBM = pl.BlockSpec(memory_space=pltpu.HBM)
 NT = (((1,), (1,)), ((), ()))
-TURNS = ((4, 1, 7), (3, 5), (2, 6))
+TURNS = ((1, 3, 2), (5, 7), (4, 6))
+HALVES, RING = 2, 4
 
 
 def iota(shape, dim):
@@ -44,6 +45,10 @@
 
 def in_hbm(*arrays):
     return [pltpu.with_memory_space_constraint(x, pltpu.HBM) for x in arrays]
+
+
+def shifted(index, halves, along):
+    return lax.rem(index // RING + halves, HALVES) * RING + lax.rem(lax.rem(index, RING) + along, RING)
 
 
 def copy_all(copies):
@@ -178,7 +183,9 @@
 
     @pl.when(step == 0)
     def _():
-        target = lax.rem(iota((slots, rows), 0) + place[0] * capacity, slots)
+        row = iota((slots, 1), 0)
+        chunk = row // capacity
+        target = shifted(place[0], chunk // RING, lax.rem(chunk, RING)) * capacity + lax.rem(row, capacity)
         spot[...] = ((turned[0:1, :] == target) | (turned[1:2, :] == target)).astype(BF16)
 
     for k in range(part // 512):
@@ -621,7 +628,8 @@
     def move(after, turns):
         after, *ready = lax.optimization_barrier((after, *[backs[r] for r in turns]))
         for r, x in zip(turns, ready):
-            backs[r] = lax.ppermute(x, "expert", [(i, (i + r) % experts) for i in range(experts)])
+            pairs = [(i, (i // RING + r // RING) % HALVES * RING + (i + r) % RING) for i in range(experts)]
+            backs[r] = lax.ppermute(x, "expert", pairs)
         return after
 
 
@@ -719,7 +727,10 @@
     turned = jnp.pad(router.T, ((0, 128 - experts), (0, 0)))
     token_grad = token_rows(summed, weighted, state, turned, experts)
     parts = [(0,) + TURNS[0] + TURNS[1], TURNS[2]]
-    places = [(mine + experts - jnp.array(turns, I32)) % experts for turns in parts]
+    places = [
+        jnp.stack([shifted(mine, (HALVES - r // RING) % HALVES, (RING - r % RING) % RING) for r in turns])
+        for turns in parts
+    ]
     expert_grad = expert_rows(places[0], grads, gain, held, [backs[r] for r in parts[0]])
     router_part, token_grad, expert_grad = lax.optimization_barrier((router_part, token_grad, expert_grad))
     router_part = jnp.sum(router_part, axis=0)

time: 226 us -> 219 us (0.969)
  starting transfers between devices: 84.9 us -> 75.5 us
    all_to_all x9, starting transfers between devices: 64.1 us -> 58.6 us  [exchange(): return lax.all_to_all(x, axes, split_axis=0, concat_axis=0, tiled=True)]
    ppermute x7, starting transfers between devices: 17.4 us -> 13.6 us  [move(): backs[r] = lax.ppermute(x, 'expert', pairs)]
  transfers between devices with their start and end apart: 17 -> 17, of which waited for: 11 -> 11; matrix products, arithmetic and copies ran while one was open for 3% -> 3% of each run, Pallas kernels for 18% -> 19%
where the time goes in v11:
time: 219 us; the launch traced here: 217 us
  waiting for transfers between devices  77 us (35%)
  starting transfers between devices  75.5 us (34%)
  Pallas kernels  51.1 us (23%)
  local copies, waits for them, and re-layouts  7.3 us (3%)
  between operations  3.44 us (2%)
  other arithmetic  2.28 us (1%)
    all_to_all x9, waiting for transfers between devices, exchange(): return lax.all_to_all(x, axes, split_axis=0, concat_axis=0, tiled=True)  73.4 us
    all_to_all x9, starting transfers between devices, exchange(): return lax.all_to_all(x, axes, split_axis=0, concat_axis=0, tiled=True)  58.6 us
    ppermute x7, starting transfers between devices, move(): backs[r] = lax.ppermute(x, 'expert', pairs)  13.6 us
    pallas_call x2, Pallas kernels, expert_rows(): pl.pallas_call(functools.partial(expert_kernel, count), grid_spec=pltpu.P...  10.9 us
    pallas_call x1, Pallas kernels, overlaps(): pl.pallas_call(functools.partial(overlap_kernel, experts), grid=(experts,...  8.56 us
    pallas_call x1, Pallas kernels, forward(): pl.pallas_call(functools.partial(forward_kernel, experts), grid=(experts,...  8.12 us
    pallas_call x1, Pallas kernels, shards(): pl.pallas_call(router_kernel, in_specs=[VMEM] * 2 + [HBM] * 4, out_specs=...  6.8 us
    pallas_call x1, Pallas kernels, token_rows(): pl.pallas_call(functools.partial(token_kernel, experts), grid=(experts,),...  6.47 us
  transfers between devices with their start and end apart: 17, of which 11 were waited for; matrix products, arithmetic and copies ran while one was open for 3% of the time, Pallas kernels for 19%

profile of v11, /device:TPU:1, one launch (start us, length us, event | category | flops | bytes accessed | tf_op | source)
XLA Modules:
  0.0 217.3 jit_solution(7157586203655338869)
XLA Ops:
  0.7 7.6 %all-to-all-start = ((bf16[8,64,4096]{2,1,0:T(8,128)(2,1)}), bf16[8,64,4096]{2,1,0:T(8,128)(2,1)}, u32[]{:S(2)}, u32[]{:S(2)}) async-start(bf16[8,64,4096]{2,1,0:T(8,128)(2,1)} %bitcast.46), calls=%async_computation | async-start | bytes 8388608 | tf_op jit(solution)/shard_map/all_to_all | solution.py:70
  9.8 47.2 %all-to-all-done = bf16[8,64,4096]{2,1,0:T(8,128)(2,1)} async-done(((bf16[8,64,4096]{2,1,0:T(8,128)(2,1)}), bf16[8,64,4096]{2,1,0:T(8,128)(2,1)}, u32[]{:S(2)}, u32[]{:S(2)}) %all-to-all-start) | async-done | bytes 4194336 | tf_op jit(solution)/shard_map/all_to_all | solution.py:70
  57.0 8.1 %shard_map.102 = (f32[192,4096]{1,0:T(8,128)}, bf16[8,4,512]{2,1,0:T(4,128)(2,1)}, f32[192,1]{1,0:T(8,128)S(1)}) custom-call(bf16[192,4096]{1,0:T(8,128)(2,1)S(1)} %copy-done, bf16[512,4096]{1,0:T(8,128)(2,1)} %bitcast.2.rec, s32[192,2]{1,0:T(8,128)S(1)} %add.101.slot, f32[192,2]{1,0:T(8,128)S(1)} %exponential_divide_fusion.gate, f32[1,4096]{1,0:T(1,128)S(1)} %bitcast.41), custom_call_target="tpu_custom_call" | custom-call | flops 1610612736 | bytes 10485760 | tf_op jit(solution)/shard_map/pallas_call | solution.py:142
  65.2 5.2 %all-to-all-start.1 = ((bf16[8,4,512]{2,1,0:T(4,128)(2,1)}), bf16[8,4,512]{2,1,0:T(4,128)(2,1)S(1)}, u32[]{:S(2)}, u32[]{:S(2)}) async-start(bf16[8,4,512]{2,1,0:T(4,128)(2,1)} %get-tuple-element.56), calls=%async_computation.1 | async-start | bytes 65536 | tf_op jit(solution)/shard_map/all_to_all | solution.py:70
  70.4 5.8 %shard_map.103 = (bf16[64,4096]{1,0:T(8,128)(2,1)}, bf16[64,4096]{1,0:T(8,128)(2,1)}, bf16[64,4096]{1,0:T(8,128)(2,1)}, bf16[64,4096]{1,0:T(8,128)(2,1)}, bf16[6...) custom-call(s32[1]{0:T(128)} %bitcast.4.place, ...), custom_call_target="tpu_custom_call" | custom-call | flops 805306368 | bytes 7340032 | tf_op jit(solution)/shard_map/pallas_call | solution.py:211
  77.9 8.3 %all-to-all-start.2 = ((bf16[16,32,512]{2,1,0:T(8,128)(2,1)}), bf16[16,32,512]{2,1,0:T(8,128)(2,1)S(1)}, u32[]{:S(2)}, u32[]{:S(2)}) async-start(bf16[16,32,512]{2,1,0:T(8,128)(2,1)} %broadcast_in_dim.89), calls=%async_computation.2 | async-start | bytes 1048576 | tf_op jit(solution)/shard_map/all_to_all | solution.py:70
  88.4 8.6 %shard_map.104 = (f32[192,128]{1,0:T(8,128)}, bf16[384,4096]{1,0:T(8,128)(2,1)}) custom-call(f32[192,4096]{1,0:T(8,128)} %get-tuple-element.57.x.summed_in.summed, bf16[512,4096]{1,0:T(8,128)(2,1)} %bitcast.2.rec, s32[192,2]{1,0:T(8,128)S(1)} %add.101.slot, f32[192,128]{1,0:T(8,128)S(1)} %pad.16.facts), custom_call_target="tpu_custom_call" | custom-call | flops 1610612736 | bytes 10485760 | tf_op jit(solution)/shard_map/pallas_call | solution.py:263
  99.0 3.3 %collective-permute-start = (bf16[16,32,512]{2,1,0:T(8,128)(2,1)S(1)}, bf16[16,32,512]{2,1,0:T(8,128)(2,1)S(1)}, u32[]{:S(2)}, u32[]{:S(2)}) collective-permute-start(bf16[16,32,512]{2,1,0:T(8,128)(2,1)S(1)} %all-to-all-done.2), channel_id=1, source_target_pairs={{0,8},{8,0},{1,9},{9,1},{2,10},{10,2},{3,11},{11,3},{4,12},{12,4},... | collective-permute-start | bytes 1572872 | tf_op jit(solution)/shard_map/ppermute | solution.py:66
  105.4 6.5 %all-to-all-start.3 = ((f32[8,40,512]{2,1,0:T(8,128)}), f32[8,40,512]{2,1,0:T(8,128)S(1)}, u32[]{:S(2)}, u32[]{:S(2)}) async-start(f32[8,40,512]{2,1,0:T(8,128)} %shard_map.105), calls=%async_computation.3 | async-start | bytes 1310720 | tf_op jit(solution)/shard_map/all_to_all | solution.py:70
  116.4 6.2 %all-to-all-done.3.gathered = f32[8,40,512]{2,1,0:T(8,128)S(1)} async-done(((f32[8,40,512]{2,1,0:T(8,128)}), f32[8,40,512]{2,1,0:T(8,128)S(1)}, u32[]{:S(2)}, u32[]{:S(2)}) %all-to-all-start.3) | async-done | bytes 655392 | tf_op jit(solution)/shard_map/all_to_all | solution.py:70
  123.6 7.2 %all-to-all-start.4 = ((f32[32,8,128]{2,1,0:T(8,128)}), f32[32,8,128]{2,1,0:T(8,128)S(1)}, u32[]{:S(2)}, u32[]{:S(2)}) async-start(f32[32,8,128]{2,1,0:T(8,128)} %get-tuple-element.75), calls=%async_computation.4 | async-start | bytes 262144 | tf_op jit(solution)/shard_map/all_to_all | solution.py:70
  134.3 5.5 %all-to-all-done.4.heard = f32[32,8,128]{2,1,0:T(8,128)S(1)} async-done(((f32[32,8,128]{2,1,0:T(8,128)}), f32[32,8,128]{2,1,0:T(8,128)S(1)}, u32[]{:S(2)}, u32[]{:S(2)}) %all-to-all-start.4) | async-done | bytes 131104 | tf_op jit(solution)/shard_map/all_to_all | solution.py:70
  142.6 4.1 %all-to-all-start.5 = ((bf16[8,32,512]{2,1,0:T(8,128)(2,1)}), bf16[8,32,512]{2,1,0:T(8,128)(2,1)S(1)}, u32[]{:S(2)}, u32[]{:S(2)}) async-start(bf16[8,32,512]{2,1,0:T(8,128)(2,1)} %get-tuple-element.82), calls=%async_computation.5 | async-start | bytes 524288 | tf_op jit(solution)/shard_map/all_to_all | solution.py:70
  146.7 3.9 %collective-permute-start.4 = (bf16[64,4096]{1,0:T(8,128)(2,1)}, bf16[64,4096]{1,0:T(8,128)(2,1)}, u32[]{:S(2)}, u32[]{:S(2)}) collective-permute-start(bf16[64,4096]{1,0:T(8,128)(2,1)} %get-tuple-element.98), channel_id=1, source_target_pairs={{0,5},{1,6},{2,7},{3,4},{4,1},{5,2},{6,3},{7,0},{8,13},{9,14},{10,... | collective-permute-start | bytes 1572872 | tf_op jit(solution)/shard_map/ppermute | solution.py:632
  154.3 6.8 %shard_map.108 = (f32[256,128]{1,0:T(8,128)}, f32[192,128]{1,0:T(8,128)}, f32[4,4096]{1,0:T(4,128)}) custom-call(bf16[8,32,512]{2,1,0:T(8,128)(2,1)S(1)} %all-to-all-done.5.grads, f32[1,4096]{1,0:T(1,128)S(1)} %bitcast.42, f32[192,4096]{1,0:T(8,128)} %get-tuple-element.57.x.summed_in.summed, bf16[384,4096]{1,0:T(8,128)(2,1)} %get-tuple-element.86.fetched_in, ...), custom_call_target="tpu_custom_call" | custom-call | tf_op jit(solution)/shard_map/pallas_call | solution.py:698
  161.2 3.9 %all-to-all-start.6 = ((f32[16,16,128]{2,1,0:T(8,128)}), f32[16,16,128]{2,1,0:T(8,128)S(1)}, u32[]{:S(2)}, u32[]{:S(2)}) async-start(f32[16,16,128]{2,1,0:T(8,128)} %bitcast.13), calls=%async_computation.6 | async-start | bytes 262144 | tf_op jit(solution)/shard_map/all_to_all | solution.py:70
  165.6 3.5 %collective-permute-start.7 = (bf16[64,4096]{1,0:T(8,128)(2,1)}, bf16[64,4096]{1,0:T(8,128)(2,1)S(1)}, u32[]{:S(2)}, u32[]{:S(2)}) collective-permute-start(bf16[64,4096]{1,0:T(8,128)(2,1)} %get-tuple-element.103), channel_id=1, source_target_pairs={{0,6},{1,7},{2,4},{3,5},{4,2},{5,3},{6,0},{7,1},{8,14},{9,15},{10,... | collective-permute-start | bytes 1572872 | tf_op jit(solution)/shard_map/ppermute | solution.py:632
  169.3 3.3 %all-to-all-done.6 = f32[16,16,128]{2,1,0:T(8,128)S(1)} async-done(((f32[16,16,128]{2,1,0:T(8,128)}), f32[16,16,128]{2,1,0:T(8,128)S(1)}, u32[]{:S(2)}, u32[]{:S(2)}) %all-to-all-start.6) | async-done | bytes 131104 | tf_op jit(solution)/shard_map/all_to_all | solution.py:70
  173.3 12.2 %all-to-all-start.7 = ((f32[16,16,128]{2,1,0:T(8,128)}), f32[16,16,128]{2,1,0:T(8,128)S(1)}, u32[]{:S(2)}, u32[]{:S(2)}) async-start(f32[16,16,128]{2,1,0:T(8,128)} %broadcast_in_dim.101), calls=%async_computation.7 | async-start | bytes 262144 | tf_op jit(solution)/shard_map/all_to_all | solution.py:70
  185.8 6.5 %shard_map.109 = bf16[192,4096]{1,0:T(8,128)(2,1)} custom-call(f32[192,4096]{1,0:T(8,128)} %get-tuple-element.57.x.summed_in.summed, f32[4,4096]{1,0:T(4,128)} %get-tuple-element.92.weighted, f32[192,128]{1,0:T(8,128)} %get-tuple-element.93.state, bf16[128,4096]{1,0:T(8,128)(2,1)S(1)} %pad.18.router), custom_call_target="tpu_custom_call" | custom-call | flops 201326592 | bytes 5242880 | tf_op jit(solution)/shard_map/pallas_call | solution.py:513
  192.2 7.0 %shard_map.110.rest_2_ = bf16[8,64,4096]{2,1,0:T(8,128)(2,1)} custom-call(s32[6]{0:T(128)S(1)} %stack.53.source, bf16[8,32,512]{2,1,0:T(8,128)(2,1)S(1)} %all-to-all-done.5.grads, f32[1,4096]{1,0:T(1,128)S(1)} %bitcast.43, f32[8,64,8]{2,1,0:T(8,128)S(1)} %pad.19.notes, bf16[64,4096]{1,0:T(8,128)(2,1)} %get-tuple-element.94.rest_0_, ...), custom_call_target="tpu_custom_call" | custom-call | flops 18874368 | bytes 6291456 | tf_op jit(solution)/shard_map/pallas_call | solution.py:573
  199.2 4.6 %all-to-all-done.7 = f32[16,16,128]{2,1,0:T(8,128)S(1)} async-done(((f32[16,16,128]{2,1,0:T(8,128)}), f32[16,16,128]{2,1,0:T(8,128)S(1)}, u32[]{:S(2)}, u32[]{:S(2)}) %all-to-all-start.7) | async-done | bytes 131104 | tf_op jit(solution)/shard_map/all_to_all | solution.py:70
  204.5 3.5 %all-to-all-start.8 = ((f32[16,16,128]{2,1,0:T(8,128)}), f32[16,16,128]{2,1,0:T(8,128)S(1)}, u32[]{:S(2)}, u32[]{:S(2)}) async-start(f32[16,16,128]{2,1,0:T(8,128)} %broadcast_in_dim.102), calls=%async_computation.8 | async-start | bytes 262144 | tf_op jit(solution)/shard_map/all_to_all | solution.py:70
  210.3 3.9 %shard_map.111 = bf16[8,64,4096]{2,1,0:T(8,128)(2,1)} custom-call(s32[2]{0:T(128)S(1)} %pad_add_fusion.source, bf16[8,32,512]{2,1,0:T(8,128)(2,1)S(1)} %all-to-all-done.5.grads, f32[1,4096]{1,0:T(1,128)S(1)} %bitcast.44, f32[8,64,8]{2,1,0:T(8,128)S(1)} %pad.19.notes, bf16[64,4096]{1,0:T(8,128)(2,1)} %copy-done.5, ...), custom_call_target="tpu_custom_call", output_to_operand_aliasing={{}: (6, {})} | custom-call | flops 6291456 | bytes 2097152 | tf_op jit(solution)/shard_map/pallas_call | solution.py:573
  (82 shorter events, 31.1 us)
Async XLA Ops:
  0.6 7.7 %copy-start.8 = (s32[192,2]{0,1:T(2,128)S(1)}, s32[192,2]{0,1:T(2,128)}, u32[]{:S(2)}) copy-start(s32[192,2]{0,1:T(2,128)} %param.8) | copy-start | bytes 4612
  0.6 7.8 %copy-start = (bf16[192,4096]{1,0:T(8,128)(2,1)S(1)}, bf16[192,4096]{1,0:T(8,128)(2,1)}, u32[]{:S(2)}) copy-start(bf16[192,4096]{1,0:T(8,128)(2,1)} %tok_in.1) | copy-start | bytes 4718596
  0.7 7.8 %copy-start.7 = (bf16[4096,8]{0,1:T(8,128)(2,1)S(1)}, bf16[4096,8]{0,1:T(8,128)(2,1)}, u32[]{:S(2)}) copy-start(bf16[4096,8]{0,1:T(8,128)(2,1)} %param.11) | copy-start | bytes 196612
  0.7 56.4 %copy-start.1 = (f32[4096]{0:T(1024)S(1)}, f32[4096]{0:T(1024)}, u32[]{:S(2)}) copy-start(f32[4096]{0:T(1024)} %param.12) | copy-start | bytes 49156
  0.7 56.3 %all-to-all-start = ((bf16[8,64,4096]{2,1,0:T(8,128)(2,1)}), bf16[8,64,4096]{2,1,0:T(8,128)(2,1)}, u32[]{:S(2)}, u32[]{:S(2)}) async-start(bf16[8,64,4096]{2,1,0:T(8,128)(2,1)} %bitcast.46), calls=%async_computation | async-start | bytes 8388608 | tf_op jit(solution)/shard_map/all_to_all | solution.py:70
  65.2 21.2 %copy-start.9 = (s32[2]{0:T(128)S(1)}, s32[2]{0:T(128)}, u32[]{:S(2)}) copy-start(s32[2]{0:T(128)} %param.9) | copy-start | bytes 28
  65.2 11.8 %all-to-all-start.1 = ((bf16[8,4,512]{2,1,0:T(4,128)(2,1)}), bf16[8,4,512]{2,1,0:T(4,128)(2,1)S(1)}, u32[]{:S(2)}, u32[]{:S(2)}) async-start(bf16[8,4,512]{2,1,0:T(4,128)(2,1)} %get-tuple-element.56), calls=%async_computation.1 | async-start | bytes 65536 | tf_op jit(solution)/shard_map/all_to_all | solution.py:70
  77.9 21.1 %all-to-all-start.2 = ((bf16[16,32,512]{2,1,0:T(8,128)(2,1)}), bf16[16,32,512]{2,1,0:T(8,128)(2,1)S(1)}, u32[]{:S(2)}, u32[]{:S(2)}) async-start(bf16[16,32,512]{2,1,0:T(8,128)(2,1)} %broadcast_in_dim.89), calls=%async_computation.2 | async-start | bytes 1048576 | tf_op jit(solution)/shard_map/all_to_all | solution.py:70
  99.0 4.8 %collective-permute-start = (bf16[16,32,512]{2,1,0:T(8,128)(2,1)S(1)}, bf16[16,32,512]{2,1,0:T(8,128)(2,1)S(1)}, u32[]{:S(2)}, u32[]{:S(2)}) collective-permute-start(bf16[16,32,512]{2,1,0:T(8,128)(2,1)S(1)} %all-to-all-done.2), channel_id=1, source_target_pairs={{0,8},{8,0},{1,9},{9,1},{2,10},{10,2},{3,11},{11,3},{4,12},{12,4},... | collective-permute-start | bytes 1572872 | tf_op jit(solution)/shard_map/ppermute | solution.py:66
  105.4 17.2 %all-to-all-start.3 = ((f32[8,40,512]{2,1,0:T(8,128)}), f32[8,40,512]{2,1,0:T(8,128)S(1)}, u32[]{:S(2)}, u32[]{:S(2)}) async-start(f32[8,40,512]{2,1,0:T(8,128)} %shard_map.105), calls=%async_computation.3 | async-start | bytes 1310720 | tf_op jit(solution)/shard_map/all_to_all | solution.py:70
  111.9 22.4 %collective-permute-start.1 = (bf16[64,4096]{1,0:T(8,128)(2,1)}, bf16[64,4096]{1,0:T(8,128)(2,1)S(1)}, u32[]{:S(2)}, u32[]{:S(2)}) collective-permute-start(bf16[64,4096]{1,0:T(8,128)(2,1)} %get-tuple-element.76), channel_id=1, source_target_pairs={{0,1},{1,2},{2,3},{3,0},{4,5},{5,6},{6,7},{7,4},{8,9},{9,10},{10,1... | collective-permute-start | bytes 1572872 | tf_op jit(solution)/shard_map/ppermute | solution.py:632
  113.4 38.4 %collective-permute-start.2 = (bf16[64,4096]{1,0:T(8,128)(2,1)}, bf16[64,4096]{1,0:T(8,128)(2,1)S(1)}, u32[]{:S(2)}, u32[]{:S(2)}) collective-permute-start(bf16[64,4096]{1,0:T(8,128)(2,1)} %get-tuple-element.83), channel_id=1, source_target_pairs={{0,3},{1,0},{2,1},{3,2},{4,7},{5,4},{6,5},{7,6},{8,11},{9,8},{10,9... | collective-permute-start | bytes 1572872 | tf_op jit(solution)/shard_map/ppermute | solution.py:632
  114.6 37.2 %collective-permute-start.3 = (bf16[64,4096]{1,0:T(8,128)(2,1)}, bf16[64,4096]{1,0:T(8,128)(2,1)}, u32[]{:S(2)}, u32[]{:S(2)}) collective-permute-start(bf16[64,4096]{1,0:T(8,128)(2,1)} %get-tuple-element.84), channel_id=1, source_target_pairs={{0,2},{1,3},{2,0},{3,1},{4,6},{5,7},{6,4},{7,5},{8,10},{9,11},{10,... | collective-permute-start | bytes 1572872 | tf_op jit(solution)/shard_map/ppermute | solution.py:632
  123.6 16.3 %all-to-all-start.4 = ((f32[32,8,128]{2,1,0:T(8,128)}), f32[32,8,128]{2,1,0:T(8,128)S(1)}, u32[]{:S(2)}, u32[]{:S(2)}) async-start(f32[32,8,128]{2,1,0:T(8,128)} %get-tuple-element.75), calls=%async_computation.4 | async-start | bytes 262144 | tf_op jit(solution)/shard_map/all_to_all | solution.py:70
  134.3 26.8 %copy-start.3 = (bf16[64,4096]{1,0:T(8,128)(2,1)}, bf16[64,4096]{1,0:T(8,128)(2,1)S(1)}, u32[]{:S(2)}) copy-start(bf16[64,4096]{1,0:T(8,128)(2,1)S(1)} %collective-permute-done.1.rest_1_) | copy-start | bytes 1572868
  142.6 11.7 %all-to-all-start.5 = ((bf16[8,32,512]{2,1,0:T(8,128)(2,1)}), bf16[8,32,512]{2,1,0:T(8,128)(2,1)S(1)}, u32[]{:S(2)}, u32[]{:S(2)}) async-start(bf16[8,32,512]{2,1,0:T(8,128)(2,1)} %get-tuple-element.82), calls=%async_computation.5 | async-start | bytes 524288 | tf_op jit(solution)/shard_map/all_to_all | solution.py:70
  146.7 45.5 %collective-permute-start.4 = (bf16[64,4096]{1,0:T(8,128)(2,1)}, bf16[64,4096]{1,0:T(8,128)(2,1)}, u32[]{:S(2)}, u32[]{:S(2)}) collective-permute-start(bf16[64,4096]{1,0:T(8,128)(2,1)} %get-tuple-element.98), channel_id=1, source_target_pairs={{0,5},{1,6},{2,7},{3,4},{4,1},{5,2},{6,3},{7,0},{8,13},{9,14},{10,... | collective-permute-start | bytes 1572872 | tf_op jit(solution)/shard_map/ppermute | solution.py:632
  150.6 41.7 %collective-permute-start.5 = (bf16[64,4096]{1,0:T(8,128)(2,1)}, bf16[64,4096]{1,0:T(8,128)(2,1)}, u32[]{:S(2)}, u32[]{:S(2)}) collective-permute-start(bf16[64,4096]{1,0:T(8,128)(2,1)} %get-tuple-element.99), channel_id=1, source_target_pairs={{0,7},{1,4},{2,5},{3,6},{4,3},{5,0},{6,1},{7,2},{8,15},{9,12},{10,... | collective-permute-start | bytes 1572872 | tf_op jit(solution)/shard_map/ppermute | solution.py:632
  151.8 9.3 %copy-start.4 = (bf16[64,4096]{1,0:T(8,128)(2,1)}, bf16[64,4096]{1,0:T(8,128)(2,1)S(1)}, u32[]{:S(2)}) copy-start(bf16[64,4096]{1,0:T(8,128)(2,1)S(1)} %collective-permute-done.2.rest_2_) | copy-start | bytes 1572868
  161.2 11.4 %all-to-all-start.6 = ((f32[16,16,128]{2,1,0:T(8,128)}), f32[16,16,128]{2,1,0:T(8,128)S(1)}, u32[]{:S(2)}, u32[]{:S(2)}) async-start(f32[16,16,128]{2,1,0:T(8,128)} %bitcast.13), calls=%async_computation.6 | async-start | bytes 262144 | tf_op jit(solution)/shard_map/all_to_all | solution.py:70
  165.1 43.6 %collective-permute-start.6 = (bf16[64,4096]{1,0:T(8,128)(2,1)}, bf16[64,4096]{1,0:T(8,128)(2,1)S(1)}, u32[]{:S(2)}, u32[]{:S(2)}) collective-permute-start(bf16[64,4096]{1,0:T(8,128)(2,1)} %get-tuple-element.102), channel_id=1, source_target_pairs={{0,4},{1,5},{2,6},{3,7},{4,0},{5,1},{6,2},{7,3},{8,12},{9,13},{10,... | collective-permute-start | bytes 1572872 | tf_op jit(solution)/shard_map/ppermute | solution.py:632
  165.6 43.1 %collective-permute-start.7 = (bf16[64,4096]{1,0:T(8,128)(2,1)}, bf16[64,4096]{1,0:T(8,128)(2,1)S(1)}, u32[]{:S(2)}, u32[]{:S(2)}) collective-permute-start(bf16[64,4096]{1,0:T(8,128)(2,1)} %get-tuple-element.103), channel_id=1, source_target_pairs={{0,6},{1,7},{2,4},{3,5},{4,2},{5,3},{6,0},{7,1},{8,14},{9,15},{10,... | collective-permute-start | bytes 1572872 | tf_op jit(solution)/shard_map/ppermute | solution.py:632
  173.3 30.5 %all-to-all-start.7 = ((f32[16,16,128]{2,1,0:T(8,128)}), f32[16,16,128]{2,1,0:T(8,128)S(1)}, u32[]{:S(2)}, u32[]{:S(2)}) async-start(f32[16,16,128]{2,1,0:T(8,128)} %broadcast_in_dim.101), calls=%async_computation.7 | async-start | bytes 262144 | tf_op jit(solution)/shard_map/all_to_all | solution.py:70
  204.5 11.0 %all-to-all-start.8 = ((f32[16,16,128]{2,1,0:T(8,128)}), f32[16,16,128]{2,1,0:T(8,128)S(1)}, u32[]{:S(2)}, u32[]{:S(2)}) async-start(f32[16,16,128]{2,1,0:T(8,128)} %broadcast_in_dim.102), calls=%async_computation.8 | async-start | bytes 262144 | tf_op jit(solution)/shard_map/all_to_all | solution.py:70
  (3 other events, 2.5 us)

commit v12 on v11

--- a/solution.py
+++ b/solution.py
@@ -720,19 +720,20 @@
     )(grads, gain, *in_hbm(summed, fetched, tokens, facts))
     router_part = move(router_part, TURNS[2])
     router_part = exchange(router_part.reshape(outer, -1, 128), "u")
+    turned = jnp.pad(router.T, ((0, 128 - experts), (0, 0)))
+    token_grad = token_rows(summed, weighted, state, turned, experts)
+    router_part, token_grad = lax.optimization_barrier((router_part, token_grad))
     router_part = jnp.sum(router_part, axis=0)
     router_part = spread(router_part, ("c", "expert"), CORES * experts)
     held = lax.dynamic_slice_in_dim(gathered[:, 2 * group : 2 * group + 3], mine * capacity, capacity, axis=2)
     held = jnp.pad(jnp.transpose(held, (0, 2, 1)), ((0, 0), (0, 0), (0, 5)))
-    turned = jnp.pad(router.T, ((0, 128 - experts), (0, 0)))
-    token_grad = token_rows(summed, weighted, state, turned, experts)
     parts = [(0,) + TURNS[0] + TURNS[1], TURNS[2]]
     places = [
         jnp.stack([shifted(mine, (HALVES - r // RING) % HALVES, (RING - r % RING) % RING) for r in turns])
         for turns in parts
     ]
     expert_grad = expert_rows(places[0], grads, gain, held, [backs[r] for r in parts[0]])
-    router_part, token_grad, expert_grad = lax.optimization_barrier((router_part, token_grad, expert_grad))
+    router_part, expert_grad = lax.optimization_barrier((router_part, expert_grad))
     router_part = jnp.sum(router_part, axis=0)
     router_all = spread(router_part, "u", outer)
     expert_grad = expert_rows(places[1], grads, gain, held, [backs[r] for r in parts[1]], expert_grad)

time: 219 us -> 219 us (level)
  starting transfers between devices: 75.5 us -> 71.6 us
  waiting for transfers between devices: 77 us -> 80 us
    all_to_all x9, starting transfers between devices: 58.6 us -> 54.8 us  [exchange(): return lax.all_to_all(x, axes, split_axis=0, concat_axis=0, tiled=True)]
    all_to_all x9, waiting for transfers between devices: 73.4 us -> 76.4 us  [exchange(): return lax.all_to_all(x, axes, split_axis=0, concat_axis=0, tiled=True)]
  transfers between devices with their start and end apart: 17 -> 17, of which waited for: 11 -> 10; matrix products, arithmetic and copies ran while one was open for 3% -> 3% of each run, Pallas kernels for 19% -> 19%
where the time goes in v12:
time: 219 us; the launch traced here: 217 us
  waiting for transfers between devices  80 us (37%)
  starting transfers between devices  71.6 us (33%)
  Pallas kernels  51.1 us (23%)
  local copies, waits for them, and re-layouts  8.17 us (4%)
  between operations  3.48 us (2%)
  other arithmetic  2.28 us (1%)
    all_to_all x9, waiting for transfers between devices, exchange(): return lax.all_to_all(x, axes, split_axis=0, concat_axis=0, tiled=True)  76.4 us
    all_to_all x9, starting transfers between devices, exchange(): return lax.all_to_all(x, axes, split_axis=0, concat_axis=0, tiled=True)  54.8 us
    ppermute x7, starting transfers between devices, move(): backs[r] = lax.ppermute(x, 'expert', pairs)  13.6 us
    pallas_call x2, Pallas kernels, expert_rows(): pl.pallas_call(functools.partial(expert_kernel, count), grid_spec=pltpu.P...  10.9 us
    pallas_call x1, Pallas kernels, overlaps(): pl.pallas_call(functools.partial(overlap_kernel, experts), grid=(experts,...  8.56 us
    pallas_call x1, Pallas kernels, forward(): pl.pallas_call(functools.partial(forward_kernel, experts), grid=(experts,...  8.13 us
    pallas_call x1, Pallas kernels, shards(): pl.pallas_call(router_kernel, in_specs=[VMEM] * 2 + [HBM] * 4, out_specs=...  6.8 us
    pallas_call x1, Pallas kernels, token_rows(): pl.pallas_call(functools.partial(token_kernel, experts), grid=(experts,),...  6.46 us
  transfers between devices with their start and end apart: 17, of which 10 were waited for; matrix products, arithmetic and copies ran while one was open for 3% of the time, Pallas kernels for 19%

profile of v12, /device:TPU:1, one launch (start us, length us, event | category | flops | bytes accessed | tf_op | source)
XLA Modules:
  0.0 217.3 jit_solution(7783964542159211388)
XLA Ops:
  0.7 7.6 %all-to-all-start = ((bf16[8,64,4096]{2,1,0:T(8,128)(2,1)}), bf16[8,64,4096]{2,1,0:T(8,128)(2,1)}, u32[]{:S(2)}, u32[]{:S(2)}) async-start(bf16[8,64,4096]{2,1,0:T(8,128)(2,1)} %bitcast.46), calls=%async_computation | async-start | bytes 8388608 | tf_op jit(solution)/shard_map/all_to_all | solution.py:70
  9.8 47.2 %all-to-all-done = bf16[8,64,4096]{2,1,0:T(8,128)(2,1)} async-done(((bf16[8,64,4096]{2,1,0:T(8,128)(2,1)}), bf16[8,64,4096]{2,1,0:T(8,128)(2,1)}, u32[]{:S(2)}, u32[]{:S(2)}) %all-to-all-start) | async-done | bytes 4194336 | tf_op jit(solution)/shard_map/all_to_all | solution.py:70
  57.0 8.1 %shard_map.102 = (f32[192,4096]{1,0:T(8,128)}, bf16[8,4,512]{2,1,0:T(4,128)(2,1)}, f32[192,1]{1,0:T(8,128)S(1)}) custom-call(bf16[192,4096]{1,0:T(8,128)(2,1)S(1)} %copy-done, bf16[512,4096]{1,0:T(8,128)(2,1)} %bitcast.2.rec, s32[192,2]{1,0:T(8,128)S(1)} %add.101.slot, f32[192,2]{1,0:T(8,128)S(1)} %exponential_divide_fusion.gate, f32[1,4096]{1,0:T(1,128)S(1)} %bitcast.41), custom_call_target="tpu_custom_call" | custom-call | flops 1610612736 | bytes 10485760 | tf_op jit(solution)/shard_map/pallas_call | solution.py:142
  65.2 5.2 %all-to-all-start.1 = ((bf16[8,4,512]{2,1,0:T(4,128)(2,1)}), bf16[8,4,512]{2,1,0:T(4,128)(2,1)S(1)}, u32[]{:S(2)}, u32[]{:S(2)}) async-start(bf16[8,4,512]{2,1,0:T(4,128)(2,1)} %get-tuple-element.57), calls=%async_computation.1 | async-start | bytes 65536 | tf_op jit(solution)/shard_map/all_to_all | solution.py:70
  70.4 5.9 %shard_map.103 = (bf16[64,4096]{1,0:T(8,128)(2,1)}, bf16[64,4096]{1,0:T(8,128)(2,1)}, bf16[64,4096]{1,0:T(8,128)(2,1)}, bf16[64,4096]{1,0:T(8,128)(2,1)}, bf16[6...) custom-call(s32[1]{0:T(128)} %bitcast.4.place, ...), custom_call_target="tpu_custom_call" | custom-call | flops 805306368 | bytes 7340032 | tf_op jit(solution)/shard_map/pallas_call | solution.py:211
  77.9 8.3 %all-to-all-start.2 = ((bf16[16,32,512]{2,1,0:T(8,128)(2,1)}), bf16[16,32,512]{2,1,0:T(8,128)(2,1)S(1)}, u32[]{:S(2)}, u32[]{:S(2)}) async-start(bf16[16,32,512]{2,1,0:T(8,128)(2,1)} %broadcast_in_dim.89), calls=%async_computation.2 | async-start | bytes 1048576 | tf_op jit(solution)/shard_map/all_to_all | solution.py:70
  88.4 8.6 %shard_map.104 = (f32[192,128]{1,0:T(8,128)}, bf16[384,4096]{1,0:T(8,128)(2,1)}) custom-call(f32[192,4096]{1,0:T(8,128)} %get-tuple-element.58.x.summed_in.summed, bf16[512,4096]{1,0:T(8,128)(2,1)} %bitcast.2.rec, s32[192,2]{1,0:T(8,128)S(1)} %add.101.slot, f32[192,128]{1,0:T(8,128)S(1)} %pad.16.facts), custom_call_target="tpu_custom_call" | custom-call | flops 1610612736 | bytes 10485760 | tf_op jit(solution)/shard_map/pallas_call | solution.py:263
  99.0 3.3 %collective-permute-start = (bf16[16,32,512]{2,1,0:T(8,128)(2,1)S(1)}, bf16[16,32,512]{2,1,0:T(8,128)(2,1)S(1)}, u32[]{:S(2)}, u32[]{:S(2)}) collective-permute-start(bf16[16,32,512]{2,1,0:T(8,128)(2,1)S(1)} %all-to-all-done.2), channel_id=1, source_target_pairs={{0,8},{8,0},{1,9},{9,1},{2,10},{10,2},{3,11},{11,3},{4,12},{12,4},... | collective-permute-start | bytes 1572872 | tf_op jit(solution)/shard_map/ppermute | solution.py:66
  105.4 6.6 %all-to-all-start.3 = ((f32[8,40,512]{2,1,0:T(8,128)}), f32[8,40,512]{2,1,0:T(8,128)S(1)}, u32[]{:S(2)}, u32[]{:S(2)}) async-start(f32[8,40,512]{2,1,0:T(8,128)} %shard_map.105), calls=%async_computation.3 | async-start | bytes 1310720 | tf_op jit(solution)/shard_map/all_to_all | solution.py:70
  116.4 6.2 %all-to-all-done.3.gathered = f32[8,40,512]{2,1,0:T(8,128)S(1)} async-done(((f32[8,40,512]{2,1,0:T(8,128)}), f32[8,40,512]{2,1,0:T(8,128)S(1)}, u32[]{:S(2)}, u32[]{:S(2)}) %all-to-all-start.3) | async-done | bytes 655392 | tf_op jit(solution)/shard_map/all_to_all | solution.py:70
  123.6 7.2 %all-to-all-start.4 = ((f32[32,8,128]{2,1,0:T(8,128)}), f32[32,8,128]{2,1,0:T(8,128)S(1)}, u32[]{:S(2)}, u32[]{:S(2)}) async-start(f32[32,8,128]{2,1,0:T(8,128)} %get-tuple-element.76), calls=%async_computation.4 | async-start | bytes 262144 | tf_op jit(solution)/shard_map/all_to_all | solution.py:70
  131.5 2.9 %collective-permute-done.1.rest_1_ = bf16[64,4096]{1,0:T(8,128)(2,1)S(1)} collective-permute-done((bf16[64,4096]{1,0:T(8,128)(2,1)}, bf16[64,4096]{1,0:T(8,128)(2,1)S(1)}, u32[]{:S(2)}, u32[]{:S(2)}) %collective-permute-start.1) | collective-permute-done | bytes 524320 | tf_op jit(solution)/shard_map/ppermute | solution.py:632
  134.4 5.5 %all-to-all-done.4.heard = f32[32,8,128]{2,1,0:T(8,128)S(1)} async-done(((f32[32,8,128]{2,1,0:T(8,128)}), f32[32,8,128]{2,1,0:T(8,128)S(1)}, u32[]{:S(2)}, u32[]{:S(2)}) %all-to-all-start.4) | async-done | bytes 131104 | tf_op jit(solution)/shard_map/all_to_all | solution.py:70
  142.7 4.1 %all-to-all-start.5 = ((bf16[8,32,512]{2,1,0:T(8,128)(2,1)}), bf16[8,32,512]{2,1,0:T(8,128)(2,1)S(1)}, u32[]{:S(2)}, u32[]{:S(2)}) async-start(bf16[8,32,512]{2,1,0:T(8,128)(2,1)} %get-tuple-element.83), calls=%async_computation.5 | async-start | bytes 524288 | tf_op jit(solution)/shard_map/all_to_all | solution.py:70
  146.8 3.9 %collective-permute-start.4 = (bf16[64,4096]{1,0:T(8,128)(2,1)}, bf16[64,4096]{1,0:T(8,128)(2,1)}, u32[]{:S(2)}, u32[]{:S(2)}) collective-permute-start(bf16[64,4096]{1,0:T(8,128)(2,1)} %get-tuple-element.101), channel_id=1, source_target_pairs={{0,5},{1,6},{2,7},{3,4},{4,1},{5,2},{6,3},{7,0},{8,13},{9,14},{10,... | collective-permute-start | bytes 1572872 | tf_op jit(solution)/shard_map/ppermute | solution.py:632
  154.4 6.8 %shard_map.108 = (f32[256,128]{1,0:T(8,128)}, f32[192,128]{1,0:T(8,128)}, f32[4,4096]{1,0:T(4,128)}) custom-call(bf16[8,32,512]{2,1,0:T(8,128)(2,1)S(1)} %all-to-all-done.5.grads, f32[1,4096]{1,0:T(1,128)S(1)} %bitcast.42, f32[192,4096]{1,0:T(8,128)} %get-tuple-element.58.x.summed_in.summed, bf16[384,4096]{1,0:T(8,128)(2,1)} %get-tuple-element.87.fetched_in, ...), custom_call_target="tpu_custom_call" | custom-call | tf_op jit(solution)/shard_map/pallas_call | solution.py:698
  161.2 3.7 %all-to-all-start.6 = ((f32[16,16,128]{2,1,0:T(8,128)}), f32[16,16,128]{2,1,0:T(8,128)S(1)}, u32[]{:S(2)}, u32[]{:S(2)}) async-start(f32[16,16,128]{2,1,0:T(8,128)} %bitcast.13), calls=%async_computation.6 | async-start | bytes 262144 | tf_op jit(solution)/shard_map/all_to_all | solution.py:70
  165.9 3.1 %collective-permute-start.7 = (bf16[64,4096]{1,0:T(8,128)(2,1)}, bf16[64,4096]{1,0:T(8,128)(2,1)S(1)}, u32[]{:S(2)}, u32[]{:S(2)}) collective-permute-start(bf16[64,4096]{1,0:T(8,128)(2,1)} %get-tuple-element.105), channel_id=1, source_target_pairs={{0,6},{1,7},{2,4},{3,5},{4,2},{5,3},{6,0},{7,1},{8,14},{9,15},{10,... | collective-permute-start | bytes 1572872 | tf_op jit(solution)/shard_map/ppermute | solution.py:632
  169.9 6.5 %shard_map.109 = bf16[192,4096]{1,0:T(8,128)(2,1)} custom-call(f32[192,4096]{1,0:T(8,128)} %get-tuple-element.58.x.summed_in.summed, f32[4,4096]{1,0:T(4,128)} %get-tuple-element.93.weighted, f32[192,128]{1,0:T(8,128)} %get-tuple-element.94.state, bf16[128,4096]{1,0:T(8,128)(2,1)S(1)} %pad.18.router), custom_call_target="tpu_custom_call" | custom-call | flops 201326592 | bytes 5242880 | tf_op jit(solution)/shard_map/pallas_call | solution.py:513
  177.1 8.5 %all-to-all-start.7 = ((f32[16,16,128]{2,1,0:T(8,128)}), f32[16,16,128]{2,1,0:T(8,128)S(1)}, u32[]{:S(2)}, u32[]{:S(2)}) async-start(f32[16,16,128]{2,1,0:T(8,128)} %broadcast_in_dim.101), calls=%async_computation.7 | async-start | bytes 262144 | tf_op jit(solution)/shard_map/all_to_all | solution.py:70
  185.9 7.0 %shard_map.110.rest_2_ = bf16[8,64,4096]{2,1,0:T(8,128)(2,1)} custom-call(s32[6]{0:T(128)S(1)} %stack.53.source, bf16[8,32,512]{2,1,0:T(8,128)(2,1)S(1)} %all-to-all-done.5.grads, f32[1,4096]{1,0:T(1,128)S(1)} %bitcast.43, f32[8,64,8]{2,1,0:T(8,128)S(1)} %pad.19.notes, bf16[64,4096]{1,0:T(8,128)(2,1)} %get-tuple-element.97.rest_0_, ...), custom_call_target="tpu_custom_call" | custom-call | flops 18874368 | bytes 6291456 | tf_op jit(solution)/shard_map/pallas_call | solution.py:573
  192.9 10.9 %all-to-all-done.7 = f32[16,16,128]{2,1,0:T(8,128)S(1)} async-done(((f32[16,16,128]{2,1,0:T(8,128)}), f32[16,16,128]{2,1,0:T(8,128)S(1)}, u32[]{:S(2)}, u32[]{:S(2)}) %all-to-all-start.7) | async-done | bytes 131104 | tf_op jit(solution)/shard_map/all_to_all | solution.py:70
  204.5 3.5 %all-to-all-start.8 = ((f32[16,16,128]{2,1,0:T(8,128)}), f32[16,16,128]{2,1,0:T(8,128)S(1)}, u32[]{:S(2)}, u32[]{:S(2)}) async-start(f32[16,16,128]{2,1,0:T(8,128)} %broadcast_in_dim.102), calls=%async_computation.8 | async-start | bytes 262144 | tf_op jit(solution)/shard_map/all_to_all | solution.py:70
  210.4 3.9 %shard_map.111 = bf16[8,64,4096]{2,1,0:T(8,128)(2,1)} custom-call(s32[2]{0:T(128)S(1)} %pad_add_fusion.source, bf16[8,32,512]{2,1,0:T(8,128)(2,1)S(1)} %all-to-all-done.5.grads, f32[1,4096]{1,0:T(1,128)S(1)} %bitcast.44, f32[8,64,8]{2,1,0:T(8,128)S(1)} %pad.19.notes, bf16[64,4096]{1,0:T(8,128)(2,1)} %copy-done.6, ...), custom_call_target="tpu_custom_call", output_to_operand_aliasing={{}: (6, {})} | custom-call | flops 6291456 | bytes 2097152 | tf_op jit(solution)/shard_map/pallas_call | solution.py:573
  (84 shorter events, 29.4 us)
Async XLA Ops:
  0.6 7.8 %copy-start = (bf16[192,4096]{1,0:T(8,128)(2,1)S(1)}, bf16[192,4096]{1,0:T(8,128)(2,1)}, u32[]{:S(2)}) copy-start(bf16[192,4096]{1,0:T(8,128)(2,1)} %tok_in.1) | copy-start | bytes 4718596
  0.7 7.8 %copy-start.8 = (bf16[4096,8]{0,1:T(8,128)(2,1)S(1)}, bf16[4096,8]{0,1:T(8,128)(2,1)}, u32[]{:S(2)}) copy-start(bf16[4096,8]{0,1:T(8,128)(2,1)} %param.11) | copy-start | bytes 196612
  0.7 56.4 %copy-start.1 = (f32[4096]{0:T(1024)S(1)}, f32[4096]{0:T(1024)}, u32[]{:S(2)}) copy-start(f32[4096]{0:T(1024)} %param.12) | copy-start | bytes 49156
  0.7 56.3 %all-to-all-start = ((bf16[8,64,4096]{2,1,0:T(8,128)(2,1)}), bf16[8,64,4096]{2,1,0:T(8,128)(2,1)}, u32[]{:S(2)}, u32[]{:S(2)}) async-start(bf16[8,64,4096]{2,1,0:T(8,128)(2,1)} %bitcast.46), calls=%async_computation | async-start | bytes 8388608 | tf_op jit(solution)/shard_map/all_to_all | solution.py:70
  65.2 21.2 %copy-start.10 = (s32[2]{0:T(128)S(1)}, s32[2]{0:T(128)}, u32[]{:S(2)}) copy-start(s32[2]{0:T(128)} %param.9) | copy-start | bytes 28
  65.2 11.8 %all-to-all-start.1 = ((bf16[8,4,512]{2,1,0:T(4,128)(2,1)}), bf16[8,4,512]{2,1,0:T(4,128)(2,1)S(1)}, u32[]{:S(2)}, u32[]{:S(2)}) async-start(bf16[8,4,512]{2,1,0:T(4,128)(2,1)} %get-tuple-element.57), calls=%async_computation.1 | async-start | bytes 65536 | tf_op jit(solution)/shard_map/all_to_all | solution.py:70
  77.9 21.1 %all-to-all-start.2 = ((bf16[16,32,512]{2,1,0:T(8,128)(2,1)}), bf16[16,32,512]{2,1,0:T(8,128)(2,1)S(1)}, u32[]{:S(2)}, u32[]{:S(2)}) async-start(bf16[16,32,512]{2,1,0:T(8,128)(2,1)} %broadcast_in_dim.89), calls=%async_computation.2 | async-start | bytes 1048576 | tf_op jit(solution)/shard_map/all_to_all | solution.py:70
  99.0 4.8 %collective-permute-start = (bf16[16,32,512]{2,1,0:T(8,128)(2,1)S(1)}, bf16[16,32,512]{2,1,0:T(8,128)(2,1)S(1)}, u32[]{:S(2)}, u32[]{:S(2)}) collective-permute-start(bf16[16,32,512]{2,1,0:T(8,128)(2,1)S(1)} %all-to-all-done.2), channel_id=1, source_target_pairs={{0,8},{8,0},{1,9},{9,1},{2,10},{10,2},{3,11},{11,3},{4,12},{12,4},... | collective-permute-start | bytes 1572872 | tf_op jit(solution)/shard_map/ppermute | solution.py:66
  105.4 17.2 %all-to-all-start.3 = ((f32[8,40,512]{2,1,0:T(8,128)}), f32[8,40,512]{2,1,0:T(8,128)S(1)}, u32[]{:S(2)}, u32[]{:S(2)}) async-start(f32[8,40,512]{2,1,0:T(8,128)} %shard_map.105), calls=%async_computation.3 | async-start | bytes 1310720 | tf_op jit(solution)/shard_map/all_to_all | solution.py:70
  112.0 22.4 %collective-permute-start.1 = (bf16[64,4096]{1,0:T(8,128)(2,1)}, bf16[64,4096]{1,0:T(8,128)(2,1)S(1)}, u32[]{:S(2)}, u32[]{:S(2)}) collective-permute-start(bf16[64,4096]{1,0:T(8,128)(2,1)} %get-tuple-element.77), channel_id=1, source_target_pairs={{0,1},{1,2},{2,3},{3,0},{4,5},{5,6},{6,7},{7,4},{8,9},{9,10},{10,1... | collective-permute-start | bytes 1572872 | tf_op jit(solution)/shard_map/ppermute | solution.py:632
  113.4 38.5 %collective-permute-start.2 = (bf16[64,4096]{1,0:T(8,128)(2,1)}, bf16[64,4096]{1,0:T(8,128)(2,1)S(1)}, u32[]{:S(2)}, u32[]{:S(2)}) collective-permute-start(bf16[64,4096]{1,0:T(8,128)(2,1)} %get-tuple-element.84), channel_id=1, source_target_pairs={{0,3},{1,0},{2,1},{3,2},{4,7},{5,4},{6,5},{7,6},{8,11},{9,8},{10,9... | collective-permute-start | bytes 1572872 | tf_op jit(solution)/shard_map/ppermute | solution.py:632
  114.7 37.2 %collective-permute-start.3 = (bf16[64,4096]{1,0:T(8,128)(2,1)}, bf16[64,4096]{1,0:T(8,128)(2,1)S(1)}, u32[]{:S(2)}, u32[]{:S(2)}) collective-permute-start(bf16[64,4096]{1,0:T(8,128)(2,1)} %get-tuple-element.85), channel_id=1, source_target_pairs={{0,2},{1,3},{2,0},{3,1},{4,6},{5,7},{6,4},{7,5},{8,10},{9,11},{10,... | collective-permute-start | bytes 1572872 | tf_op jit(solution)/shard_map/ppermute | solution.py:632
  123.6 16.3 %all-to-all-start.4 = ((f32[32,8,128]{2,1,0:T(8,128)}), f32[32,8,128]{2,1,0:T(8,128)S(1)}, u32[]{:S(2)}, u32[]{:S(2)}) async-start(f32[32,8,128]{2,1,0:T(8,128)} %get-tuple-element.76), calls=%async_computation.4 | async-start | bytes 262144 | tf_op jit(solution)/shard_map/all_to_all | solution.py:70
  134.4 26.8 %copy-start.3 = (bf16[64,4096]{1,0:T(8,128)(2,1)}, bf16[64,4096]{1,0:T(8,128)(2,1)S(1)}, u32[]{:S(2)}) copy-start(bf16[64,4096]{1,0:T(8,128)(2,1)S(1)} %collective-permute-done.1.rest_1_) | copy-start | bytes 1572868
  142.7 11.7 %all-to-all-start.5 = ((bf16[8,32,512]{2,1,0:T(8,128)(2,1)}), bf16[8,32,512]{2,1,0:T(8,128)(2,1)S(1)}, u32[]{:S(2)}, u32[]{:S(2)}) async-start(bf16[8,32,512]{2,1,0:T(8,128)(2,1)} %get-tuple-element.83), calls=%async_computation.5 | async-start | bytes 524288 | tf_op jit(solution)/shard_map/all_to_all | solution.py:70
  146.8 39.2 %collective-permute-start.4 = (bf16[64,4096]{1,0:T(8,128)(2,1)}, bf16[64,4096]{1,0:T(8,128)(2,1)}, u32[]{:S(2)}, u32[]{:S(2)}) collective-permute-start(bf16[64,4096]{1,0:T(8,128)(2,1)} %get-tuple-element.101), channel_id=1, source_target_pairs={{0,5},{1,6},{2,7},{3,4},{4,1},{5,2},{6,3},{7,0},{8,13},{9,14},{10,... | collective-permute-start | bytes 1572872 | tf_op jit(solution)/shard_map/ppermute | solution.py:632
  150.6 35.3 %collective-permute-start.5 = (bf16[64,4096]{1,0:T(8,128)(2,1)}, bf16[64,4096]{1,0:T(8,128)(2,1)}, u32[]{:S(2)}, u32[]{:S(2)}) collective-permute-start(bf16[64,4096]{1,0:T(8,128)(2,1)} %get-tuple-element.102), channel_id=1, source_target_pairs={{0,7},{1,4},{2,5},{3,6},{4,3},{5,0},{6,1},{7,2},{8,15},{9,12},{10,... | collective-permute-start | bytes 1572872 | tf_op jit(solution)/shard_map/ppermute | solution.py:632
  151.9 9.3 %copy-start.4 = (bf16[64,4096]{1,0:T(8,128)(2,1)}, bf16[64,4096]{1,0:T(8,128)(2,1)S(1)}, u32[]{:S(2)}) copy-start(bf16[64,4096]{1,0:T(8,128)(2,1)S(1)} %collective-permute-done.2.rest_2_) | copy-start | bytes 1572868
  151.9 9.3 %copy-start.5 = (bf16[64,4096]{1,0:T(8,128)(2,1)}, bf16[64,4096]{1,0:T(8,128)(2,1)S(1)}, u32[]{:S(2)}) copy-start(bf16[64,4096]{1,0:T(8,128)(2,1)S(1)} %collective-permute-done.3.rest_3_) | copy-start | bytes 1572868
  161.2 15.1 %all-to-all-start.6 = ((f32[16,16,128]{2,1,0:T(8,128)}), f32[16,16,128]{2,1,0:T(8,128)S(1)}, u32[]{:S(2)}, u32[]{:S(2)}) async-start(f32[16,16,128]{2,1,0:T(8,128)} %bitcast.13), calls=%async_computation.6 | async-start | bytes 262144 | tf_op jit(solution)/shard_map/all_to_all | solution.py:70
  165.0 43.8 %collective-permute-start.6 = (bf16[64,4096]{1,0:T(8,128)(2,1)}, bf16[64,4096]{1,0:T(8,128)(2,1)S(1)}, u32[]{:S(2)}, u32[]{:S(2)}) collective-permute-start(bf16[64,4096]{1,0:T(8,128)(2,1)} %get-tuple-element.104), channel_id=1, source_target_pairs={{0,4},{1,5},{2,6},{3,7},{4,0},{5,1},{6,2},{7,3},{8,12},{9,13},{10,... | collective-permute-start | bytes 1572872 | tf_op jit(solution)/shard_map/ppermute | solution.py:632
  165.9 43.0 %collective-permute-start.7 = (bf16[64,4096]{1,0:T(8,128)(2,1)}, bf16[64,4096]{1,0:T(8,128)(2,1)S(1)}, u32[]{:S(2)}, u32[]{:S(2)}) collective-permute-start(bf16[64,4096]{1,0:T(8,128)(2,1)} %get-tuple-element.105), channel_id=1, source_target_pairs={{0,6},{1,7},{2,4},{3,5},{4,2},{5,3},{6,0},{7,1},{8,14},{9,15},{10,... | collective-permute-start | bytes 1572872 | tf_op jit(solution)/shard_map/ppermute | solution.py:632
  177.1 26.8 %all-to-all-start.7 = ((f32[16,16,128]{2,1,0:T(8,128)}), f32[16,16,128]{2,1,0:T(8,128)S(1)}, u32[]{:S(2)}, u32[]{:S(2)}) async-start(f32[16,16,128]{2,1,0:T(8,128)} %broadcast_in_dim.101), calls=%async_computation.7 | async-start | bytes 262144 | tf_op jit(solution)/shard_map/all_to_all | solution.py:70
  204.5 11.0 %all-to-all-start.8 = ((f32[16,16,128]{2,1,0:T(8,128)}), f32[16,16,128]{2,1,0:T(8,128)S(1)}, u32[]{:S(2)}, u32[]{:S(2)}) async-start(f32[16,16,128]{2,1,0:T(8,128)} %broadcast_in_dim.102), calls=%async_computation.8 | async-start | bytes 262144 | tf_op jit(solution)/shard_map/all_to_all | solution.py:70
  (4 other events, 10.2 us)

commit v13 on v12

--- a/solution.py
+++ b/solution.py
@@ -20,7 +20,7 @@
 SMEM = pl.BlockSpec(memory_space=pltpu.SMEM)
 HBM = pl.BlockSpec(memory_space=pltpu.HBM)
 NT = (((1,), (1,)), ((), ()))
-TURNS = ((1, 3, 2), (5, 7), (4, 6))
+TURNS = ((4, 1, 3, 2), (5, 7), (6,))
 HALVES, RING = 2, 4
 
 

time: 219 us -> 213 us (0.973)
  waiting for transfers between devices: 80 us -> 68.6 us
  starting transfers between devices: 71.6 us -> 77.2 us
    all_to_all x9, waiting for transfers between devices: 76.4 us -> 66.1 us  [exchange(): return lax.all_to_all(x, axes, split_axis=0, concat_axis=0, tiled=True)]
    all_to_all x9, starting transfers between devices: 54.8 us -> 59.6 us  [exchange(): return lax.all_to_all(x, axes, split_axis=0, concat_axis=0, tiled=True)]
  transfers between devices with their start and end apart: 17 -> 17, of which waited for: 10 -> 9; matrix products, arithmetic and copies ran while one was open for 3% -> 3% of each run, Pallas kernels for 19% -> 19%
where the time goes in v13:
time: 213 us; the launch traced here: 210 us
  starting transfers between devices  77.2 us (36%)
  waiting for transfers between devices  68.6 us (32%)
  Pallas kernels  50.5 us (24%)
  local copies, waits for them, and re-layouts  7.33 us (3%)
  between operations  3.48 us (2%)
  other arithmetic  2.2 us (1%)
    all_to_all x9, waiting for transfers between devices, exchange(): return lax.all_to_all(x, axes, split_axis=0, concat_axis=0, tiled=True)  66.1 us
    all_to_all x9, starting transfers between devices, exchange(): return lax.all_to_all(x, axes, split_axis=0, concat_axis=0, tiled=True)  59.6 us
    ppermute x7, starting transfers between devices, move(): backs[r] = lax.ppermute(x, 'expert', pairs)  14.3 us
    pallas_call x2, Pallas kernels, expert_rows(): pl.pallas_call(functools.partial(expert_kernel, count), grid_spec=pltpu.P...  10.3 us
    pallas_call x1, Pallas kernels, overlaps(): pl.pallas_call(functools.partial(overlap_kernel, experts), grid=(experts,...  8.56 us
    pallas_call x1, Pallas kernels, forward(): pl.pallas_call(functools.partial(forward_kernel, experts), grid=(experts,...  8.12 us
    pallas_call x1, Pallas kernels, shards(): pl.pallas_call(router_kernel, in_specs=[VMEM] * 2 + [HBM] * 4, out_specs=...  6.8 us
    pallas_call x1, Pallas kernels, token_rows(): pl.pallas_call(functools.partial(token_kernel, experts), grid=(experts,),...  6.47 us
  transfers between devices with their start and end apart: 17, of which 9 were waited for; matrix products, arithmetic and copies ran while one was open for 3% of the time, Pallas kernels for 19%

profile of v13, /device:TPU:1, one launch (start us, length us, event | category | flops | bytes accessed | tf_op | source)
XLA Modules:
  0.0 210.0 jit_solution(1267075445139718429)
XLA Ops:
  0.7 7.6 %all-to-all-start = ((bf16[8,64,4096]{2,1,0:T(8,128)(2,1)}), bf16[8,64,4096]{2,1,0:T(8,128)(2,1)}, u32[]{:S(2)}, u32[]{:S(2)}) async-start(bf16[8,64,4096]{2,1,0:T(8,128)(2,1)} %bitcast.46), calls=%async_computation | async-start | bytes 8388608 | tf_op jit(solution)/shard_map/all_to_all | solution.py:70
  9.8 47.2 %all-to-all-done = bf16[8,64,4096]{2,1,0:T(8,128)(2,1)} async-done(((bf16[8,64,4096]{2,1,0:T(8,128)(2,1)}), bf16[8,64,4096]{2,1,0:T(8,128)(2,1)}, u32[]{:S(2)}, u32[]{:S(2)}) %all-to-all-start) | async-done | bytes 4194336 | tf_op jit(solution)/shard_map/all_to_all | solution.py:70
  57.0 8.1 %shard_map.102 = (f32[192,4096]{1,0:T(8,128)}, bf16[8,4,512]{2,1,0:T(4,128)(2,1)}, f32[192,1]{1,0:T(8,128)S(1)}) custom-call(bf16[192,4096]{1,0:T(8,128)(2,1)S(1)} %copy-done, bf16[512,4096]{1,0:T(8,128)(2,1)} %bitcast.2.rec, s32[192,2]{1,0:T(8,128)S(1)} %add.101.slot, f32[192,2]{1,0:T(8,128)S(1)} %exponential_divide_fusion.gate, f32[1,4096]{1,0:T(1,128)S(1)} %bitcast.41), custom_call_target="tpu_custom_call" | custom-call | flops 1610612736 | bytes 10485760 | tf_op jit(solution)/shard_map/pallas_call | solution.py:142
  65.2 5.2 %all-to-all-start.1 = ((bf16[8,4,512]{2,1,0:T(4,128)(2,1)}), bf16[8,4,512]{2,1,0:T(4,128)(2,1)S(1)}, u32[]{:S(2)}, u32[]{:S(2)}) async-start(bf16[8,4,512]{2,1,0:T(4,128)(2,1)} %get-tuple-element.58), calls=%async_computation.1 | async-start | bytes 65536 | tf_op jit(solution)/shard_map/all_to_all | solution.py:70
  70.4 5.8 %shard_map.103 = (bf16[64,4096]{1,0:T(8,128)(2,1)}, bf16[64,4096]{1,0:T(8,128)(2,1)}, bf16[64,4096]{1,0:T(8,128)(2,1)}, bf16[64,4096]{1,0:T(8,128)(2,1)}, bf16[6...) custom-call(s32[1]{0:T(128)} %bitcast.4.place, ...), custom_call_target="tpu_custom_call" | custom-call | flops 805306368 | bytes 7340032 | tf_op jit(solution)/shard_map/pallas_call | solution.py:211
  77.9 8.3 %all-to-all-start.2 = ((bf16[16,32,512]{2,1,0:T(8,128)(2,1)}), bf16[16,32,512]{2,1,0:T(8,128)(2,1)S(1)}, u32[]{:S(2)}, u32[]{:S(2)}) async-start(bf16[16,32,512]{2,1,0:T(8,128)(2,1)} %broadcast_in_dim.89), calls=%async_computation.2 | async-start | bytes 1048576 | tf_op jit(solution)/shard_map/all_to_all | solution.py:70
  88.4 8.6 %shard_map.104 = (f32[192,128]{1,0:T(8,128)}, bf16[384,4096]{1,0:T(8,128)(2,1)}) custom-call(f32[192,4096]{1,0:T(8,128)} %get-tuple-element.59.x.summed_in.summed, bf16[512,4096]{1,0:T(8,128)(2,1)} %bitcast.2.rec, s32[192,2]{1,0:T(8,128)S(1)} %add.101.slot, f32[192,128]{1,0:T(8,128)S(1)} %pad.16.facts), custom_call_target="tpu_custom_call" | custom-call | flops 1610612736 | bytes 10485760 | tf_op jit(solution)/shard_map/pallas_call | solution.py:263
  99.0 3.3 %collective-permute-start = (bf16[16,32,512]{2,1,0:T(8,128)(2,1)S(1)}, bf16[16,32,512]{2,1,0:T(8,128)(2,1)S(1)}, u32[]{:S(2)}, u32[]{:S(2)}) collective-permute-start(bf16[16,32,512]{2,1,0:T(8,128)(2,1)S(1)} %all-to-all-done.2), channel_id=1, source_target_pairs={{0,8},{8,0},{1,9},{9,1},{2,10},{10,2},{3,11},{11,3},{4,12},{12,4},... | collective-permute-start | bytes 1572872 | tf_op jit(solution)/shard_map/ppermute | solution.py:66
  105.4 6.5 %all-to-all-start.3 = ((f32[8,40,512]{2,1,0:T(8,128)}), f32[8,40,512]{2,1,0:T(8,128)S(1)}, u32[]{:S(2)}, u32[]{:S(2)}) async-start(f32[8,40,512]{2,1,0:T(8,128)} %shard_map.105), calls=%async_computation.3 | async-start | bytes 1310720 | tf_op jit(solution)/shard_map/all_to_all | solution.py:70
  111.9 3.0 %collective-permute-start.1 = (bf16[64,4096]{1,0:T(8,128)(2,1)}, bf16[64,4096]{1,0:T(8,128)(2,1)S(1)}, u32[]{:S(2)}, u32[]{:S(2)}) collective-permute-start(bf16[64,4096]{1,0:T(8,128)(2,1)} %get-tuple-element.79), channel_id=1, source_target_pairs={{0,4},{1,5},{2,6},{3,7},{4,0},{5,1},{6,2},{7,3},{8,12},{9,13},{10,... | collective-permute-start | bytes 1572872 | tf_op jit(solution)/shard_map/ppermute | solution.py:632
  119.1 3.5 %all-to-all-done.3.gathered = f32[8,40,512]{2,1,0:T(8,128)S(1)} async-done(((f32[8,40,512]{2,1,0:T(8,128)}), f32[8,40,512]{2,1,0:T(8,128)S(1)}, u32[]{:S(2)}, u32[]{:S(2)}) %all-to-all-start.3) | async-done | bytes 655392 | tf_op jit(solution)/shard_map/all_to_all | solution.py:70
  123.6 7.4 %all-to-all-start.4 = ((f32[32,8,128]{2,1,0:T(8,128)}), f32[32,8,128]{2,1,0:T(8,128)S(1)}, u32[]{:S(2)}, u32[]{:S(2)}) async-start(f32[32,8,128]{2,1,0:T(8,128)} %get-tuple-element.78), calls=%async_computation.4 | async-start | bytes 262144 | tf_op jit(solution)/shard_map/all_to_all | solution.py:70
  133.5 6.6 %all-to-all-done.4.heard = f32[32,8,128]{2,1,0:T(8,128)S(1)} async-done(((f32[32,8,128]{2,1,0:T(8,128)}), f32[32,8,128]{2,1,0:T(8,128)S(1)}, u32[]{:S(2)}, u32[]{:S(2)}) %all-to-all-start.4) | async-done | bytes 131104 | tf_op jit(solution)/shard_map/all_to_all | solution.py:70
  142.9 4.0 %all-to-all-start.5 = ((bf16[8,32,512]{2,1,0:T(8,128)(2,1)}), bf16[8,32,512]{2,1,0:T(8,128)(2,1)S(1)}, u32[]{:S(2)}, u32[]{:S(2)}) async-start(bf16[8,32,512]{2,1,0:T(8,128)(2,1)} %get-tuple-element.85), calls=%async_computation.5 | async-start | bytes 524288 | tf_op jit(solution)/shard_map/all_to_all | solution.py:70
  146.9 3.9 %collective-permute-start.5 = (bf16[64,4096]{1,0:T(8,128)(2,1)}, bf16[64,4096]{1,0:T(8,128)(2,1)S(1)}, u32[]{:S(2)}, u32[]{:S(2)}) collective-permute-start(bf16[64,4096]{1,0:T(8,128)(2,1)} %get-tuple-element.104), channel_id=1, source_target_pairs={{0,5},{1,6},{2,7},{3,4},{4,1},{5,2},{6,3},{7,0},{8,13},{9,14},{10,... | collective-permute-start | bytes 1572872 | tf_op jit(solution)/shard_map/ppermute | solution.py:632
  152.0 2.5 %all-to-all-done.5.grads = bf16[8,32,512]{2,1,0:T(8,128)(2,1)S(1)} async-done(((bf16[8,32,512]{2,1,0:T(8,128)(2,1)}), bf16[8,32,512]{2,1,0:T(8,128)(2,1)S(1)}, u32[]{:S(2)}, u32[]{:S(2)}) %all-to-all-start.5) | async-done | bytes 262176 | tf_op jit(solution)/shard_map/all_to_all | solution.py:70
  154.5 6.8 %shard_map.108 = (f32[256,128]{1,0:T(8,128)}, f32[192,128]{1,0:T(8,128)}, f32[4,4096]{1,0:T(4,128)}) custom-call(bf16[8,32,512]{2,1,0:T(8,128)(2,1)S(1)} %all-to-all-done.5.grads, f32[1,4096]{1,0:T(1,128)S(1)} %bitcast.42, f32[192,4096]{1,0:T(8,128)} %get-tuple-element.59.x.summed_in.summed, bf16[384,4096]{1,0:T(8,128)(2,1)} %get-tuple-element.90.fetched_in, ...), custom_call_target="tpu_custom_call" | custom-call | tf_op jit(solution)/shard_map/pallas_call | solution.py:698
  161.3 3.5 %all-to-all-start.6 = ((f32[16,16,128]{2,1,0:T(8,128)}), f32[16,16,128]{2,1,0:T(8,128)S(1)}, u32[]{:S(2)}, u32[]{:S(2)}) async-start(f32[16,16,128]{2,1,0:T(8,128)} %bitcast.13), calls=%async_computation.6 | async-start | bytes 262144 | tf_op jit(solution)/shard_map/all_to_all | solution.py:70
  167.1 6.5 %shard_map.109 = bf16[192,4096]{1,0:T(8,128)(2,1)} custom-call(f32[192,4096]{1,0:T(8,128)} %get-tuple-element.59.x.summed_in.summed, f32[4,4096]{1,0:T(4,128)} %get-tuple-element.95.weighted, f32[192,128]{1,0:T(8,128)} %get-tuple-element.96.state, bf16[128,4096]{1,0:T(8,128)(2,1)S(1)} %pad.18.router), custom_call_target="tpu_custom_call" | custom-call | flops 201326592 | bytes 5242880 | tf_op jit(solution)/shard_map/pallas_call | solution.py:513
  174.2 11.6 %all-to-all-start.7 = ((f32[16,16,128]{2,1,0:T(8,128)}), f32[16,16,128]{2,1,0:T(8,128)S(1)}, u32[]{:S(2)}, u32[]{:S(2)}) async-start(f32[16,16,128]{2,1,0:T(8,128)} %broadcast_in_dim.101), calls=%async_computation.7 | async-start | bytes 262144 | tf_op jit(solution)/shard_map/all_to_all | solution.py:70
  187.0 7.7 %shard_map.110.rest_1_ = bf16[8,64,4096]{2,1,0:T(8,128)(2,1)} custom-call(s32[7]{0:T(128)S(1)} %stack.51.source, bf16[8,32,512]{2,1,0:T(8,128)(2,1)S(1)} %all-to-all-done.5.grads, f32[1,4096]{1,0:T(1,128)S(1)} %bitcast.43, f32[8,64,8]{2,1,0:T(8,128)S(1)} %pad.19.notes, bf16[64,4096]{1,0:T(8,128)(2,1)} %get-tuple-element.99.rest_0_, ...), custom_call_target="tpu_custom_call" | custom-call | flops 22020096 | bytes 7340032 | tf_op jit(solution)/shard_map/pallas_call | solution.py:573
  195.5 5.3 %all-to-all-start.8 = ((f32[16,16,128]{2,1,0:T(8,128)}), f32[16,16,128]{2,1,0:T(8,128)S(1)}, u32[]{:S(2)}, u32[]{:S(2)}) async-start(f32[16,16,128]{2,1,0:T(8,128)} %broadcast_in_dim.102), calls=%async_computation.8 | async-start | bytes 262144 | tf_op jit(solution)/shard_map/all_to_all | solution.py:70
  202.2 2.5 %shard_map.111 = bf16[8,64,4096]{2,1,0:T(8,128)(2,1)} custom-call(s32[1]{0:T(128)} %bitcast.23.source, bf16[8,32,512]{2,1,0:T(8,128)(2,1)S(1)} %all-to-all-done.5.grads, f32[1,4096]{1,0:T(1,128)S(1)} %bitcast.44, f32[8,64,8]{2,1,0:T(8,128)S(1)} %pad.19.notes, bf16[64,4096]{1,0:T(8,128)(2,1)} %copy-done.7, ...), custom_call_target="tpu_custom_call", output_to_operand_aliasing={{}: (5, {})} | custom-call | flops 3145728 | bytes 1048576 | tf_op jit(solution)/shard_map/pallas_call | solution.py:573
  204.8 3.4 %all-to-all-done.8 = f32[16,16,128]{2,1,0:T(8,128)S(1)} async-done(((f32[16,16,128]{2,1,0:T(8,128)}), f32[16,16,128]{2,1,0:T(8,128)S(1)}, u32[]{:S(2)}, u32[]{:S(2)}) %all-to-all-start.8) | async-done | bytes 131104 | tf_op jit(solution)/shard_map/all_to_all | solution.py:70
  (83 shorter events, 27.5 us)
Async XLA Ops:
  0.6 7.8 %copy-start = (bf16[192,4096]{1,0:T(8,128)(2,1)S(1)}, bf16[192,4096]{1,0:T(8,128)(2,1)}, u32[]{:S(2)}) copy-start(bf16[192,4096]{1,0:T(8,128)(2,1)} %tok_in.1) | copy-start | bytes 4718596
  0.7 7.8 %copy-start.8 = (bf16[4096,8]{0,1:T(8,128)(2,1)S(1)}, bf16[4096,8]{0,1:T(8,128)(2,1)}, u32[]{:S(2)}) copy-start(bf16[4096,8]{0,1:T(8,128)(2,1)} %param.11) | copy-start | bytes 196612
  0.7 56.4 %copy-start.1 = (f32[4096]{0:T(1024)S(1)}, f32[4096]{0:T(1024)}, u32[]{:S(2)}) copy-start(f32[4096]{0:T(1024)} %param.12) | copy-start | bytes 49156
  0.7 56.3 %all-to-all-start = ((bf16[8,64,4096]{2,1,0:T(8,128)(2,1)}), bf16[8,64,4096]{2,1,0:T(8,128)(2,1)}, u32[]{:S(2)}, u32[]{:S(2)}) async-start(bf16[8,64,4096]{2,1,0:T(8,128)(2,1)} %bitcast.46), calls=%async_computation | async-start | bytes 8388608 | tf_op jit(solution)/shard_map/all_to_all | solution.py:70
  65.2 21.2 %copy-start.10 = (s32[2]{0:T(128)S(1)}, s32[2]{0:T(128)}, u32[]{:S(2)}) copy-start(s32[2]{0:T(128)} %param.9) | copy-start | bytes 28
  65.2 11.8 %all-to-all-start.1 = ((bf16[8,4,512]{2,1,0:T(4,128)(2,1)}), bf16[8,4,512]{2,1,0:T(4,128)(2,1)S(1)}, u32[]{:S(2)}, u32[]{:S(2)}) async-start(bf16[8,4,512]{2,1,0:T(4,128)(2,1)} %get-tuple-element.58), calls=%async_computation.1 | async-start | bytes 65536 | tf_op jit(solution)/shard_map/all_to_all | solution.py:70
  77.9 21.1 %all-to-all-start.2 = ((bf16[16,32,512]{2,1,0:T(8,128)(2,1)}), bf16[16,32,512]{2,1,0:T(8,128)(2,1)S(1)}, u32[]{:S(2)}, u32[]{:S(2)}) async-start(bf16[16,32,512]{2,1,0:T(8,128)(2,1)} %broadcast_in_dim.89), calls=%async_computation.2 | async-start | bytes 1048576 | tf_op jit(solution)/shard_map/all_to_all | solution.py:70
  99.0 4.8 %collective-permute-start = (bf16[16,32,512]{2,1,0:T(8,128)(2,1)S(1)}, bf16[16,32,512]{2,1,0:T(8,128)(2,1)S(1)}, u32[]{:S(2)}, u32[]{:S(2)}) collective-permute-start(bf16[16,32,512]{2,1,0:T(8,128)(2,1)S(1)} %all-to-all-done.2), channel_id=1, source_target_pairs={{0,8},{8,0},{1,9},{9,1},{2,10},{10,2},{3,11},{11,3},{4,12},{12,4},... | collective-permute-start | bytes 1572872 | tf_op jit(solution)/shard_map/ppermute | solution.py:66
  105.4 17.2 %all-to-all-start.3 = ((f32[8,40,512]{2,1,0:T(8,128)}), f32[8,40,512]{2,1,0:T(8,128)S(1)}, u32[]{:S(2)}, u32[]{:S(2)}) async-start(f32[8,40,512]{2,1,0:T(8,128)} %shard_map.105), calls=%async_computation.3 | async-start | bytes 1310720 | tf_op jit(solution)/shard_map/all_to_all | solution.py:70
  111.9 21.5 %collective-permute-start.1 = (bf16[64,4096]{1,0:T(8,128)(2,1)}, bf16[64,4096]{1,0:T(8,128)(2,1)S(1)}, u32[]{:S(2)}, u32[]{:S(2)}) collective-permute-start(bf16[64,4096]{1,0:T(8,128)(2,1)} %get-tuple-element.79), channel_id=1, source_target_pairs={{0,4},{1,5},{2,6},{3,7},{4,0},{5,1},{6,2},{7,3},{8,12},{9,13},{10,... | collective-permute-start | bytes 1572872 | tf_op jit(solution)/shard_map/ppermute | solution.py:632
  114.9 37.1 %collective-permute-start.2 = (bf16[64,4096]{1,0:T(8,128)(2,1)}, bf16[64,4096]{1,0:T(8,128)(2,1)S(1)}, u32[]{:S(2)}, u32[]{:S(2)}) collective-permute-start(bf16[64,4096]{1,0:T(8,128)(2,1)} %get-tuple-element.86), channel_id=1, source_target_pairs={{0,1},{1,2},{2,3},{3,0},{4,5},{5,6},{6,7},{7,4},{8,9},{9,10},{10,1... | collective-permute-start | bytes 1572872 | tf_op jit(solution)/shard_map/ppermute | solution.py:632
  116.1 35.9 %collective-permute-start.3 = (bf16[64,4096]{1,0:T(8,128)(2,1)}, bf16[64,4096]{1,0:T(8,128)(2,1)S(1)}, u32[]{:S(2)}, u32[]{:S(2)}) collective-permute-start(bf16[64,4096]{1,0:T(8,128)(2,1)} %get-tuple-element.87), channel_id=1, source_target_pairs={{0,3},{1,0},{2,1},{3,2},{4,7},{5,4},{6,5},{7,6},{8,11},{9,8},{10,9... | collective-permute-start | bytes 1572872 | tf_op jit(solution)/shard_map/ppermute | solution.py:632
  117.6 34.4 %collective-permute-start.4 = (bf16[64,4096]{1,0:T(8,128)(2,1)}, bf16[64,4096]{1,0:T(8,128)(2,1)}, u32[]{:S(2)}, u32[]{:S(2)}) collective-permute-start(bf16[64,4096]{1,0:T(8,128)(2,1)} %get-tuple-element.88), channel_id=1, source_target_pairs={{0,2},{1,3},{2,0},{3,1},{4,6},{5,7},{6,4},{7,5},{8,10},{9,11},{10,... | collective-permute-start | bytes 1572872 | tf_op jit(solution)/shard_map/ppermute | solution.py:632
  123.6 16.5 %all-to-all-start.4 = ((f32[32,8,128]{2,1,0:T(8,128)}), f32[32,8,128]{2,1,0:T(8,128)S(1)}, u32[]{:S(2)}, u32[]{:S(2)}) async-start(f32[32,8,128]{2,1,0:T(8,128)} %get-tuple-element.78), calls=%async_computation.4 | async-start | bytes 262144 | tf_op jit(solution)/shard_map/all_to_all | solution.py:70
  133.5 27.8 %copy-start.3 = (bf16[64,4096]{1,0:T(8,128)(2,1)}, bf16[64,4096]{1,0:T(8,128)(2,1)S(1)}, u32[]{:S(2)}) copy-start(bf16[64,4096]{1,0:T(8,128)(2,1)S(1)} %collective-permute-done.1.rest_1_) | copy-start | bytes 1572868
  142.9 11.6 %all-to-all-start.5 = ((bf16[8,32,512]{2,1,0:T(8,128)(2,1)}), bf16[8,32,512]{2,1,0:T(8,128)(2,1)S(1)}, u32[]{:S(2)}, u32[]{:S(2)}) async-start(bf16[8,32,512]{2,1,0:T(8,128)(2,1)} %get-tuple-element.85), calls=%async_computation.5 | async-start | bytes 524288 | tf_op jit(solution)/shard_map/all_to_all | solution.py:70
  146.9 39.3 %collective-permute-start.5 = (bf16[64,4096]{1,0:T(8,128)(2,1)}, bf16[64,4096]{1,0:T(8,128)(2,1)S(1)}, u32[]{:S(2)}, u32[]{:S(2)}) collective-permute-start(bf16[64,4096]{1,0:T(8,128)(2,1)} %get-tuple-element.104), channel_id=1, source_target_pairs={{0,5},{1,6},{2,7},{3,4},{4,1},{5,2},{6,3},{7,0},{8,13},{9,14},{10,... | collective-permute-start | bytes 1572872 | tf_op jit(solution)/shard_map/ppermute | solution.py:632
  150.7 35.5 %collective-permute-start.6 = (bf16[64,4096]{1,0:T(8,128)(2,1)}, bf16[64,4096]{1,0:T(8,128)(2,1)}, u32[]{:S(2)}, u32[]{:S(2)}) collective-permute-start(bf16[64,4096]{1,0:T(8,128)(2,1)} %get-tuple-element.105), channel_id=1, source_target_pairs={{0,7},{1,4},{2,5},{3,6},{4,3},{5,0},{6,1},{7,2},{8,15},{9,12},{10,... | collective-permute-start | bytes 1572872 | tf_op jit(solution)/shard_map/ppermute | solution.py:632
  152.0 9.3 %copy-start.4 = (bf16[64,4096]{1,0:T(8,128)(2,1)}, bf16[64,4096]{1,0:T(8,128)(2,1)S(1)}, u32[]{:S(2)}) copy-start(bf16[64,4096]{1,0:T(8,128)(2,1)S(1)} %collective-permute-done.2.rest_2_) | copy-start | bytes 1572868
  152.0 9.3 %copy-start.5 = (bf16[64,4096]{1,0:T(8,128)(2,1)}, bf16[64,4096]{1,0:T(8,128)(2,1)S(1)}, u32[]{:S(2)}) copy-start(bf16[64,4096]{1,0:T(8,128)(2,1)S(1)} %collective-permute-done.3.rest_3_) | copy-start | bytes 1572868
  161.3 12.2 %all-to-all-start.6 = ((f32[16,16,128]{2,1,0:T(8,128)}), f32[16,16,128]{2,1,0:T(8,128)S(1)}, u32[]{:S(2)}, u32[]{:S(2)}) async-start(f32[16,16,128]{2,1,0:T(8,128)} %bitcast.13), calls=%async_computation.6 | async-start | bytes 262144 | tf_op jit(solution)/shard_map/all_to_all | solution.py:70
  164.9 36.5 %collective-permute-start.7 = (bf16[64,4096]{1,0:T(8,128)(2,1)}, bf16[64,4096]{1,0:T(8,128)(2,1)S(1)}, u32[]{:S(2)}, u32[]{:S(2)}) collective-permute-start(bf16[64,4096]{1,0:T(8,128)(2,1)} %get-tuple-element.107), channel_id=1, source_target_pairs={{0,6},{1,7},{2,4},{3,5},{4,2},{5,3},{6,0},{7,1},{8,14},{9,15},{10,... | collective-permute-start | bytes 1572872 | tf_op jit(solution)/shard_map/ppermute | solution.py:632
  174.2 20.5 %all-to-all-start.7 = ((f32[16,16,128]{2,1,0:T(8,128)}), f32[16,16,128]{2,1,0:T(8,128)S(1)}, u32[]{:S(2)}, u32[]{:S(2)}) async-start(f32[16,16,128]{2,1,0:T(8,128)} %broadcast_in_dim.101), calls=%async_computation.7 | async-start | bytes 262144 | tf_op jit(solution)/shard_map/all_to_all | solution.py:70
  195.5 12.7 %all-to-all-start.8 = ((f32[16,16,128]{2,1,0:T(8,128)}), f32[16,16,128]{2,1,0:T(8,128)S(1)}, u32[]{:S(2)}, u32[]{:S(2)}) async-start(f32[16,16,128]{2,1,0:T(8,128)} %broadcast_in_dim.102), calls=%async_computation.8 | async-start | bytes 262144 | tf_op jit(solution)/shard_map/all_to_all | solution.py:70
  (4 other events, 10.2 us)

commit v14 on v13

--- a/solution.py
+++ b/solution.py
@@ -20,7 +20,7 @@
 SMEM = pl.BlockSpec(memory_space=pltpu.SMEM)
 HBM = pl.BlockSpec(memory_space=pltpu.HBM)
 NT = (((1,), (1,)), ((), ()))
-TURNS = ((4, 1, 3, 2), (5, 7), (6,))
+TURNS = ((4, 1, 3, 2), (5, 6), (7,))
 HALVES, RING = 2, 4
 
 

time: 213 us -> 211 us (level)
  transfers between devices with their start and end apart: 17 -> 17, of which waited for: 9 -> 9; matrix products, arithmetic and copies ran while one was open for 3% -> 3% of each run, Pallas kernels for 19% -> 20%
where the time goes in v14:
time: 211 us; the launch traced here: 209 us
  starting transfers between devices  76.9 us (36%)
  waiting for transfers between devices  67.5 us (32%)
  Pallas kernels  50.5 us (24%)
  local copies, waits for them, and re-layouts  7.33 us (3%)
  between operations  3.48 us (2%)
  other arithmetic  2.2 us (1%)
    all_to_all x9, waiting for transfers between devices, exchange(): return lax.all_to_all(x, axes, split_axis=0, concat_axis=0, tiled=True)  64.9 us
    all_to_all x9, starting transfers between devices, exchange(): return lax.all_to_all(x, axes, split_axis=0, concat_axis=0, tiled=True)  57.5 us
    ppermute x7, starting transfers between devices, move(): backs[r] = lax.ppermute(x, 'expert', pairs)  16.1 us
    pallas_call x2, Pallas kernels, expert_rows(): pl.pallas_call(functools.partial(expert_kernel, count), grid_spec=pltpu.P...  10.3 us
    pallas_call x1, Pallas kernels, overlaps(): pl.pallas_call(functools.partial(overlap_kernel, experts), grid=(experts,...  8.56 us
    pallas_call x1, Pallas kernels, forward(): pl.pallas_call(functools.partial(forward_kernel, experts), grid=(experts,...  8.12 us
    pallas_call x1, Pallas kernels, shards(): pl.pallas_call(router_kernel, in_specs=[VMEM] * 2 + [HBM] * 4, out_specs=...  6.8 us
    pallas_call x1, Pallas kernels, token_rows(): pl.pallas_call(functools.partial(token_kernel, experts), grid=(experts,),...  6.47 us
  transfers between devices with their start and end apart: 17, of which 9 were waited for; matrix products, arithmetic and copies ran while one was open for 3% of the time, Pallas kernels for 20%

profile of v14, /device:TPU:1, one launch (start us, length us, event | category | flops | bytes accessed | tf_op | source)
XLA Modules:
  0.0 208.5 jit_solution(13711521916043135714)
XLA Ops:
  0.7 7.6 %all-to-all-start = ((bf16[8,64,4096]{2,1,0:T(8,128)(2,1)}), bf16[8,64,4096]{2,1,0:T(8,128)(2,1)}, u32[]{:S(2)}, u32[]{:S(2)}) async-start(bf16[8,64,4096]{2,1,0:T(8,128)(2,1)} %bitcast.46), calls=%async_computation | async-start | bytes 8388608 | tf_op jit(solution)/shard_map/all_to_all | solution.py:70
  9.8 47.2 %all-to-all-done = bf16[8,64,4096]{2,1,0:T(8,128)(2,1)} async-done(((bf16[8,64,4096]{2,1,0:T(8,128)(2,1)}), bf16[8,64,4096]{2,1,0:T(8,128)(2,1)}, u32[]{:S(2)}, u32[]{:S(2)}) %all-to-all-start) | async-done | bytes 4194336 | tf_op jit(solution)/shard_map/all_to_all | solution.py:70
  57.0 8.1 %shard_map.102 = (f32[192,4096]{1,0:T(8,128)}, bf16[8,4,512]{2,1,0:T(4,128)(2,1)}, f32[192,1]{1,0:T(8,128)S(1)}) custom-call(bf16[192,4096]{1,0:T(8,128)(2,1)S(1)} %copy-done, bf16[512,4096]{1,0:T(8,128)(2,1)} %bitcast.2.rec, s32[192,2]{1,0:T(8,128)S(1)} %add.101.slot, f32[192,2]{1,0:T(8,128)S(1)} %exponential_divide_fusion.gate, f32[1,4096]{1,0:T(1,128)S(1)} %bitcast.41), custom_call_target="tpu_custom_call" | custom-call | flops 1610612736 | bytes 10485760 | tf_op jit(solution)/shard_map/pallas_call | solution.py:142
  65.2 5.2 %all-to-all-start.1 = ((bf16[8,4,512]{2,1,0:T(4,128)(2,1)}), bf16[8,4,512]{2,1,0:T(4,128)(2,1)S(1)}, u32[]{:S(2)}, u32[]{:S(2)}) async-start(bf16[8,4,512]{2,1,0:T(4,128)(2,1)} %get-tuple-element.58), calls=%async_computation.1 | async-start | bytes 65536 | tf_op jit(solution)/shard_map/all_to_all | solution.py:70
  70.4 5.8 %shard_map.103 = (bf16[64,4096]{1,0:T(8,128)(2,1)}, bf16[64,4096]{1,0:T(8,128)(2,1)}, bf16[64,4096]{1,0:T(8,128)(2,1)}, bf16[64,4096]{1,0:T(8,128)(2,1)}, bf16[6...) custom-call(s32[1]{0:T(128)} %bitcast.4.place, ...), custom_call_target="tpu_custom_call" | custom-call | flops 805306368 | bytes 7340032 | tf_op jit(solution)/shard_map/pallas_call | solution.py:211
  77.9 8.3 %all-to-all-start.2 = ((bf16[16,32,512]{2,1,0:T(8,128)(2,1)}), bf16[16,32,512]{2,1,0:T(8,128)(2,1)S(1)}, u32[]{:S(2)}, u32[]{:S(2)}) async-start(bf16[16,32,512]{2,1,0:T(8,128)(2,1)} %broadcast_in_dim.89), calls=%async_computation.2 | async-start | bytes 1048576 | tf_op jit(solution)/shard_map/all_to_all | solution.py:70
  88.4 8.6 %shard_map.104 = (f32[192,128]{1,0:T(8,128)}, bf16[384,4096]{1,0:T(8,128)(2,1)}) custom-call(f32[192,4096]{1,0:T(8,128)} %get-tuple-element.59.x.summed_in.summed, bf16[512,4096]{1,0:T(8,128)(2,1)} %bitcast.2.rec, s32[192,2]{1,0:T(8,128)S(1)} %add.101.slot, f32[192,128]{1,0:T(8,128)S(1)} %pad.16.facts), custom_call_target="tpu_custom_call" | custom-call | flops 1610612736 | bytes 10485760 | tf_op jit(solution)/shard_map/pallas_call | solution.py:263
  99.0 3.3 %collective-permute-start = (bf16[16,32,512]{2,1,0:T(8,128)(2,1)S(1)}, bf16[16,32,512]{2,1,0:T(8,128)(2,1)S(1)}, u32[]{:S(2)}, u32[]{:S(2)}) collective-permute-start(bf16[16,32,512]{2,1,0:T(8,128)(2,1)S(1)} %all-to-all-done.2), channel_id=1, source_target_pairs={{0,8},{8,0},{1,9},{9,1},{2,10},{10,2},{3,11},{11,3},{4,12},{12,4},... | collective-permute-start | bytes 1572872 | tf_op jit(solution)/shard_map/ppermute | solution.py:66
  105.4 6.5 %all-to-all-start.3 = ((f32[8,40,512]{2,1,0:T(8,128)}), f32[8,40,512]{2,1,0:T(8,128)S(1)}, u32[]{:S(2)}, u32[]{:S(2)}) async-start(f32[8,40,512]{2,1,0:T(8,128)} %shard_map.105), calls=%async_computation.3 | async-start | bytes 1310720 | tf_op jit(solution)/shard_map/all_to_all | solution.py:70
  111.9 3.0 %collective-permute-start.1 = (bf16[64,4096]{1,0:T(8,128)(2,1)}, bf16[64,4096]{1,0:T(8,128)(2,1)S(1)}, u32[]{:S(2)}, u32[]{:S(2)}) collective-permute-start(bf16[64,4096]{1,0:T(8,128)(2,1)} %get-tuple-element.79), channel_id=1, source_target_pairs={{0,4},{1,5},{2,6},{3,7},{4,0},{5,1},{6,2},{7,3},{8,12},{9,13},{10,... | collective-permute-start | bytes 1572872 | tf_op jit(solution)/shard_map/ppermute | solution.py:632
  119.1 3.5 %all-to-all-done.3.gathered = f32[8,40,512]{2,1,0:T(8,128)S(1)} async-done(((f32[8,40,512]{2,1,0:T(8,128)}), f32[8,40,512]{2,1,0:T(8,128)S(1)}, u32[]{:S(2)}, u32[]{:S(2)}) %all-to-all-start.3) | async-done | bytes 655392 | tf_op jit(solution)/shard_map/all_to_all | solution.py:70
  123.6 7.4 %all-to-all-start.4 = ((f32[32,8,128]{2,1,0:T(8,128)}), f32[32,8,128]{2,1,0:T(8,128)S(1)}, u32[]{:S(2)}, u32[]{:S(2)}) async-start(f32[32,8,128]{2,1,0:T(8,128)} %get-tuple-element.78), calls=%async_computation.4 | async-start | bytes 262144 | tf_op jit(solution)/shard_map/all_to_all | solution.py:70
  133.5 6.6 %all-to-all-done.4.heard = f32[32,8,128]{2,1,0:T(8,128)S(1)} async-done(((f32[32,8,128]{2,1,0:T(8,128)}), f32[32,8,128]{2,1,0:T(8,128)S(1)}, u32[]{:S(2)}, u32[]{:S(2)}) %all-to-all-start.4) | async-done | bytes 131104 | tf_op jit(solution)/shard_map/all_to_all | solution.py:70
  142.9 4.0 %all-to-all-start.5 = ((bf16[8,32,512]{2,1,0:T(8,128)(2,1)}), bf16[8,32,512]{2,1,0:T(8,128)(2,1)S(1)}, u32[]{:S(2)}, u32[]{:S(2)}) async-start(bf16[8,32,512]{2,1,0:T(8,128)(2,1)} %get-tuple-element.85), calls=%async_computation.5 | async-start | bytes 524288 | tf_op jit(solution)/shard_map/all_to_all | solution.py:70
  146.9 3.9 %collective-permute-start.5 = (bf16[64,4096]{1,0:T(8,128)(2,1)}, bf16[64,4096]{1,0:T(8,128)(2,1)S(1)}, u32[]{:S(2)}, u32[]{:S(2)}) collective-permute-start(bf16[64,4096]{1,0:T(8,128)(2,1)} %get-tuple-element.104), channel_id=1, source_target_pairs={{0,5},{1,6},{2,7},{3,4},{4,1},{5,2},{6,3},{7,0},{8,13},{9,14},{10,... | collective-permute-start | bytes 1572872 | tf_op jit(solution)/shard_map/ppermute | solution.py:632
  154.5 6.8 %shard_map.108 = (f32[256,128]{1,0:T(8,128)}, f32[192,128]{1,0:T(8,128)}, f32[4,4096]{1,0:T(4,128)}) custom-call(bf16[8,32,512]{2,1,0:T(8,128)(2,1)S(1)} %all-to-all-done.5.grads, f32[1,4096]{1,0:T(1,128)S(1)} %bitcast.42, f32[192,4096]{1,0:T(8,128)} %get-tuple-element.59.x.summed_in.summed, bf16[384,4096]{1,0:T(8,128)(2,1)} %get-tuple-element.90.fetched_in, ...), custom_call_target="tpu_custom_call" | custom-call | tf_op jit(solution)/shard_map/pallas_call | solution.py:698
  161.3 3.5 %all-to-all-start.6 = ((f32[16,16,128]{2,1,0:T(8,128)}), f32[16,16,128]{2,1,0:T(8,128)S(1)}, u32[]{:S(2)}, u32[]{:S(2)}) async-start(f32[16,16,128]{2,1,0:T(8,128)} %bitcast.13), calls=%async_computation.6 | async-start | bytes 262144 | tf_op jit(solution)/shard_map/all_to_all | solution.py:70
  164.9 2.7 %collective-permute-start.7 = (bf16[64,4096]{1,0:T(8,128)(2,1)}, bf16[64,4096]{1,0:T(8,128)(2,1)S(1)}, u32[]{:S(2)}, u32[]{:S(2)}) collective-permute-start(bf16[64,4096]{1,0:T(8,128)(2,1)} %get-tuple-element.107), channel_id=1, source_target_pairs={{0,7},{1,4},{2,5},{3,6},{4,3},{5,0},{6,1},{7,2},{8,15},{9,12},{10,... | collective-permute-start | bytes 1572872 | tf_op jit(solution)/shard_map/ppermute | solution.py:632
  167.7 6.5 %shard_map.109 = bf16[192,4096]{1,0:T(8,128)(2,1)} custom-call(f32[192,4096]{1,0:T(8,128)} %get-tuple-element.59.x.summed_in.summed, f32[4,4096]{1,0:T(4,128)} %get-tuple-element.95.weighted, f32[192,128]{1,0:T(8,128)} %get-tuple-element.96.state, bf16[128,4096]{1,0:T(8,128)(2,1)S(1)} %pad.18.router), custom_call_target="tpu_custom_call" | custom-call | flops 201326592 | bytes 5242880 | tf_op jit(solution)/shard_map/pallas_call | solution.py:513
  174.8 11.0 %all-to-all-start.7 = ((f32[16,16,128]{2,1,0:T(8,128)}), f32[16,16,128]{2,1,0:T(8,128)S(1)}, u32[]{:S(2)}, u32[]{:S(2)}) async-start(f32[16,16,128]{2,1,0:T(8,128)} %broadcast_in_dim.101), calls=%async_computation.7 | async-start | bytes 262144 | tf_op jit(solution)/shard_map/all_to_all | solution.py:70
  187.0 7.7 %shard_map.110.rest_1_ = bf16[8,64,4096]{2,1,0:T(8,128)(2,1)} custom-call(s32[7]{0:T(128)S(1)} %stack.51.source, bf16[8,32,512]{2,1,0:T(8,128)(2,1)S(1)} %all-to-all-done.5.grads, f32[1,4096]{1,0:T(1,128)S(1)} %bitcast.43, f32[8,64,8]{2,1,0:T(8,128)S(1)} %pad.19.notes, bf16[64,4096]{1,0:T(8,128)(2,1)} %get-tuple-element.99.rest_0_, ...), custom_call_target="tpu_custom_call" | custom-call | flops 22020096 | bytes 7340032 | tf_op jit(solution)/shard_map/pallas_call | solution.py:573
  195.5 3.9 %all-to-all-start.8 = ((f32[16,16,128]{2,1,0:T(8,128)}), f32[16,16,128]{2,1,0:T(8,128)S(1)}, u32[]{:S(2)}, u32[]{:S(2)}) async-start(f32[16,16,128]{2,1,0:T(8,128)} %broadcast_in_dim.102), calls=%async_computation.8 | async-start | bytes 262144 | tf_op jit(solution)/shard_map/all_to_all | solution.py:70
  200.8 2.5 %shard_map.111 = bf16[8,64,4096]{2,1,0:T(8,128)(2,1)} custom-call(s32[1]{0:T(128)} %bitcast.23.source, bf16[8,32,512]{2,1,0:T(8,128)(2,1)S(1)} %all-to-all-done.5.grads, f32[1,4096]{1,0:T(1,128)S(1)} %bitcast.44, f32[8,64,8]{2,1,0:T(8,128)S(1)} %pad.19.notes, bf16[64,4096]{1,0:T(8,128)(2,1)} %copy-done.7, ...), custom_call_target="tpu_custom_call", output_to_operand_aliasing={{}: (5, {})} | custom-call | flops 3145728 | bytes 1048576 | tf_op jit(solution)/shard_map/pallas_call | solution.py:573
  203.3 3.4 %all-to-all-done.8 = f32[16,16,128]{2,1,0:T(8,128)S(1)} async-done(((f32[16,16,128]{2,1,0:T(8,128)}), f32[16,16,128]{2,1,0:T(8,128)S(1)}, u32[]{:S(2)}, u32[]{:S(2)}) %all-to-all-start.8) | async-done | bytes 131104 | tf_op jit(solution)/shard_map/all_to_all | solution.py:70
  (83 shorter events, 27.9 us)
Async XLA Ops:
  0.6 7.8 %copy-start = (bf16[192,4096]{1,0:T(8,128)(2,1)S(1)}, bf16[192,4096]{1,0:T(8,128)(2,1)}, u32[]{:S(2)}) copy-start(bf16[192,4096]{1,0:T(8,128)(2,1)} %tok_in.1) | copy-start | bytes 4718596
  0.7 7.8 %copy-start.8 = (bf16[4096,8]{0,1:T(8,128)(2,1)S(1)}, bf16[4096,8]{0,1:T(8,128)(2,1)}, u32[]{:S(2)}) copy-start(bf16[4096,8]{0,1:T(8,128)(2,1)} %param.11) | copy-start | bytes 196612
  0.7 56.4 %copy-start.1 = (f32[4096]{0:T(1024)S(1)}, f32[4096]{0:T(1024)}, u32[]{:S(2)}) copy-start(f32[4096]{0:T(1024)} %param.12) | copy-start | bytes 49156
  0.7 56.3 %all-to-all-start = ((bf16[8,64,4096]{2,1,0:T(8,128)(2,1)}), bf16[8,64,4096]{2,1,0:T(8,128)(2,1)}, u32[]{:S(2)}, u32[]{:S(2)}) async-start(bf16[8,64,4096]{2,1,0:T(8,128)(2,1)} %bitcast.46), calls=%async_computation | async-start | bytes 8388608 | tf_op jit(solution)/shard_map/all_to_all | solution.py:70
  65.2 21.2 %copy-start.10 = (s32[2]{0:T(128)S(1)}, s32[2]{0:T(128)}, u32[]{:S(2)}) copy-start(s32[2]{0:T(128)} %param.9) | copy-start | bytes 28
  65.2 11.8 %all-to-all-start.1 = ((bf16[8,4,512]{2,1,0:T(4,128)(2,1)}), bf16[8,4,512]{2,1,0:T(4,128)(2,1)S(1)}, u32[]{:S(2)}, u32[]{:S(2)}) async-start(bf16[8,4,512]{2,1,0:T(4,128)(2,1)} %get-tuple-element.58), calls=%async_computation.1 | async-start | bytes 65536 | tf_op jit(solution)/shard_map/all_to_all | solution.py:70
  77.9 21.1 %all-to-all-start.2 = ((bf16[16,32,512]{2,1,0:T(8,128)(2,1)}), bf16[16,32,512]{2,1,0:T(8,128)(2,1)S(1)}, u32[]{:S(2)}, u32[]{:S(2)}) async-start(bf16[16,32,512]{2,1,0:T(8,128)(2,1)} %broadcast_in_dim.89), calls=%async_computation.2 | async-start | bytes 1048576 | tf_op jit(solution)/shard_map/all_to_all | solution.py:70
  99.0 4.8 %collective-permute-start = (bf16[16,32,512]{2,1,0:T(8,128)(2,1)S(1)}, bf16[16,32,512]{2,1,0:T(8,128)(2,1)S(1)}, u32[]{:S(2)}, u32[]{:S(2)}) collective-permute-start(bf16[16,32,512]{2,1,0:T(8,128)(2,1)S(1)} %all-to-all-done.2), channel_id=1, source_target_pairs={{0,8},{8,0},{1,9},{9,1},{2,10},{10,2},{3,11},{11,3},{4,12},{12,4},... | collective-permute-start | bytes 1572872 | tf_op jit(solution)/shard_map/ppermute | solution.py:66
  105.4 17.2 %all-to-all-start.3 = ((f32[8,40,512]{2,1,0:T(8,128)}), f32[8,40,512]{2,1,0:T(8,128)S(1)}, u32[]{:S(2)}, u32[]{:S(2)}) async-start(f32[8,40,512]{2,1,0:T(8,128)} %shard_map.105), calls=%async_computation.3 | async-start | bytes 1310720 | tf_op jit(solution)/shard_map/all_to_all | solution.py:70
  111.9 21.5 %collective-permute-start.1 = (bf16[64,4096]{1,0:T(8,128)(2,1)}, bf16[64,4096]{1,0:T(8,128)(2,1)S(1)}, u32[]{:S(2)}, u32[]{:S(2)}) collective-permute-start(bf16[64,4096]{1,0:T(8,128)(2,1)} %get-tuple-element.79), channel_id=1, source_target_pairs={{0,4},{1,5},{2,6},{3,7},{4,0},{5,1},{6,2},{7,3},{8,12},{9,13},{10,... | collective-permute-start | bytes 1572872 | tf_op jit(solution)/shard_map/ppermute | solution.py:632
  114.9 38.2 %collective-permute-start.2 = (bf16[64,4096]{1,0:T(8,128)(2,1)}, bf16[64,4096]{1,0:T(8,128)(2,1)S(1)}, u32[]{:S(2)}, u32[]{:S(2)}) collective-permute-start(bf16[64,4096]{1,0:T(8,128)(2,1)} %get-tuple-element.86), channel_id=1, source_target_pairs={{0,1},{1,2},{2,3},{3,0},{4,5},{5,6},{6,7},{7,4},{8,9},{9,10},{10,1... | collective-permute-start | bytes 1572872 | tf_op jit(solution)/shard_map/ppermute | solution.py:632
  116.1 37.1 %collective-permute-start.3 = (bf16[64,4096]{1,0:T(8,128)(2,1)}, bf16[64,4096]{1,0:T(8,128)(2,1)S(1)}, u32[]{:S(2)}, u32[]{:S(2)}) collective-permute-start(bf16[64,4096]{1,0:T(8,128)(2,1)} %get-tuple-element.87), channel_id=1, source_target_pairs={{0,3},{1,0},{2,1},{3,2},{4,7},{5,4},{6,5},{7,6},{8,11},{9,8},{10,9... | collective-permute-start | bytes 1572872 | tf_op jit(solution)/shard_map/ppermute | solution.py:632
  117.6 35.6 %collective-permute-start.4 = (bf16[64,4096]{1,0:T(8,128)(2,1)}, bf16[64,4096]{1,0:T(8,128)(2,1)}, u32[]{:S(2)}, u32[]{:S(2)}) collective-permute-start(bf16[64,4096]{1,0:T(8,128)(2,1)} %get-tuple-element.88), channel_id=1, source_target_pairs={{0,2},{1,3},{2,0},{3,1},{4,6},{5,7},{6,4},{7,5},{8,10},{9,11},{10,... | collective-permute-start | bytes 1572872 | tf_op jit(solution)/shard_map/ppermute | solution.py:632
  123.6 16.5 %all-to-all-start.4 = ((f32[32,8,128]{2,1,0:T(8,128)}), f32[32,8,128]{2,1,0:T(8,128)S(1)}, u32[]{:S(2)}, u32[]{:S(2)}) async-start(f32[32,8,128]{2,1,0:T(8,128)} %get-tuple-element.78), calls=%async_computation.4 | async-start | bytes 262144 | tf_op jit(solution)/shard_map/all_to_all | solution.py:70
  133.5 27.8 %copy-start.3 = (bf16[64,4096]{1,0:T(8,128)(2,1)}, bf16[64,4096]{1,0:T(8,128)(2,1)S(1)}, u32[]{:S(2)}) copy-start(bf16[64,4096]{1,0:T(8,128)(2,1)S(1)} %collective-permute-done.1.rest_1_) | copy-start | bytes 1572868
  142.9 11.6 %all-to-all-start.5 = ((bf16[8,32,512]{2,1,0:T(8,128)(2,1)}), bf16[8,32,512]{2,1,0:T(8,128)(2,1)S(1)}, u32[]{:S(2)}, u32[]{:S(2)}) async-start(bf16[8,32,512]{2,1,0:T(8,128)(2,1)} %get-tuple-element.85), calls=%async_computation.5 | async-start | bytes 524288 | tf_op jit(solution)/shard_map/all_to_all | solution.py:70
  146.9 39.3 %collective-permute-start.5 = (bf16[64,4096]{1,0:T(8,128)(2,1)}, bf16[64,4096]{1,0:T(8,128)(2,1)S(1)}, u32[]{:S(2)}, u32[]{:S(2)}) collective-permute-start(bf16[64,4096]{1,0:T(8,128)(2,1)} %get-tuple-element.104), channel_id=1, source_target_pairs={{0,5},{1,6},{2,7},{3,4},{4,1},{5,2},{6,3},{7,0},{8,13},{9,14},{10,... | collective-permute-start | bytes 1572872 | tf_op jit(solution)/shard_map/ppermute | solution.py:632
  150.7 35.5 %collective-permute-start.6 = (bf16[64,4096]{1,0:T(8,128)(2,1)}, bf16[64,4096]{1,0:T(8,128)(2,1)}, u32[]{:S(2)}, u32[]{:S(2)}) collective-permute-start(bf16[64,4096]{1,0:T(8,128)(2,1)} %get-tuple-element.105), channel_id=1, source_target_pairs={{0,6},{1,7},{2,4},{3,5},{4,2},{5,3},{6,0},{7,1},{8,14},{9,15},{10,... | collective-permute-start | bytes 1572872 | tf_op jit(solution)/shard_map/ppermute | solution.py:632
  153.1 8.2 %copy-start.4 = (bf16[64,4096]{1,0:T(8,128)(2,1)}, bf16[64,4096]{1,0:T(8,128)(2,1)S(1)}, u32[]{:S(2)}) copy-start(bf16[64,4096]{1,0:T(8,128)(2,1)S(1)} %collective-permute-done.2.rest_2_) | copy-start | bytes 1572868
  153.1 8.2 %copy-start.5 = (bf16[64,4096]{1,0:T(8,128)(2,1)}, bf16[64,4096]{1,0:T(8,128)(2,1)S(1)}, u32[]{:S(2)}) copy-start(bf16[64,4096]{1,0:T(8,128)(2,1)S(1)} %collective-permute-done.3.rest_3_) | copy-start | bytes 1572868
  161.3 12.8 %all-to-all-start.6 = ((f32[16,16,128]{2,1,0:T(8,128)}), f32[16,16,128]{2,1,0:T(8,128)S(1)}, u32[]{:S(2)}, u32[]{:S(2)}) async-start(f32[16,16,128]{2,1,0:T(8,128)} %bitcast.13), calls=%async_computation.6 | async-start | bytes 262144 | tf_op jit(solution)/shard_map/all_to_all | solution.py:70
  164.9 35.1 %collective-permute-start.7 = (bf16[64,4096]{1,0:T(8,128)(2,1)}, bf16[64,4096]{1,0:T(8,128)(2,1)S(1)}, u32[]{:S(2)}, u32[]{:S(2)}) collective-permute-start(bf16[64,4096]{1,0:T(8,128)(2,1)} %get-tuple-element.107), channel_id=1, source_target_pairs={{0,7},{1,4},{2,5},{3,6},{4,3},{5,0},{6,1},{7,2},{8,15},{9,12},{10,... | collective-permute-start | bytes 1572872 | tf_op jit(solution)/shard_map/ppermute | solution.py:632
  174.8 19.9 %all-to-all-start.7 = ((f32[16,16,128]{2,1,0:T(8,128)}), f32[16,16,128]{2,1,0:T(8,128)S(1)}, u32[]{:S(2)}, u32[]{:S(2)}) async-start(f32[16,16,128]{2,1,0:T(8,128)} %broadcast_in_dim.101), calls=%async_computation.7 | async-start | bytes 262144 | tf_op jit(solution)/shard_map/all_to_all | solution.py:70
  195.5 11.3 %all-to-all-start.8 = ((f32[16,16,128]{2,1,0:T(8,128)}), f32[16,16,128]{2,1,0:T(8,128)S(1)}, u32[]{:S(2)}, u32[]{:S(2)}) async-start(f32[16,16,128]{2,1,0:T(8,128)} %broadcast_in_dim.102), calls=%async_computation.8 | async-start | bytes 262144 | tf_op jit(solution)/shard_map/all_to_all | solution.py:70
  (4 other events, 10.2 us)
